TPU v7x, 32 devices: a whole 2x2x4 slice. The times are simulated.
32 devices in a mesh: section: 2 (over y), dp: 4 (over z), tensor: 4 (over x, core).
Axes of the slice: x: 2, y: 2, z: 4, core: 2. Of those that a mesh axis runs over, the one named last changes fastest.
Arguments:
- frames: bfloat16 [2, 2, 4, 1024, 768], P('section', None, 'dp', 'tensor'), may hold values from -6 to 6
- lengths: int32 [2, 2, 4], P(None, None, 'dp'), may hold values from 128 to 1024, as said below
- bucket_of: int32 [2, 2047], P('section'), may hold values from 0 to 319
- rel_table: float32 [2, 320, 12], P('section', None, 'tensor'), may hold values from -4 to 4
- norms: float32 [2, 3, 2, 768], P('section')
- attn_in: bfloat16 [2, 3, 768, 768], P('section', None, None, 'tensor'), may hold values from -0.21875 to 0.21875
- attn_out: bfloat16 [2, 768, 768], P('section', 'tensor'), may hold values from -3.5 to 3.5
- cross_pair: bfloat16 [2, 2, 768, 768], P('section', None, None, 'tensor')
- ffn_in: bfloat16 [2, 768, 3072], P('section', None, 'tensor'), may hold values from -0.21875 to 0.21875
- ffn_out: bfloat16 [2, 3072, 768], P('section', 'tensor'), may hold values from -0.109375 to 0.109375
- cotangent: bfloat16 [2, 2, 4, 1024, 768], P('section', None, 'dp', 'tensor'), may hold values from -6 to 6
Outputs:
- section_out: bfloat16 [2, 2, 4, 1024, 768], P('section', None, 'dp', 'tensor')
- frames_grad: float32 [2, 2, 4, 1024, 768], P('section', None, 'dp', 'tensor')
- rel_table_grad: float32 [2, 320, 12], P('section', None, 'tensor')
- norms_grad: float32 [2, 3, 2, 768], P('section')
- attn_in_grad: float32 [2, 3, 768, 768], P('section', None, None, 'tensor')
- attn_out_grad: float32 [2, 768, 768], P('section', 'tensor')
- cross_pair_grad: float32 [2, 2, 768, 768], P('section', None, None, 'tensor')
- ffn_in_grad: float32 [2, 768, 3072], P('section', None, 'tensor')
- ffn_out_grad: float32 [2, 3072, 768], P('section', 'tensor')
- stats: float32 [2], P('section')
Inputs may be any that keep to these rules, and one draw needn't show every extreme that they name: `lengths`: in each section and micro-batch, one sequence has all 1024 frames valid.
All inputs are finite; a program needn't handle non-finite values.
Results may differ from a plain program's by a relative error of at most 0.015.
Values may be sent and summed in bfloat16 or wider, within the bound.
No kernel may reach another device: no remote copies, remote signals or barrier semaphores. Data moves between devices by JAX's collectives and lax.ppermute only.
A program may use at most 896 MiB of HBM per device.

v0:
```python
import jax
import jax.numpy as jnp
from jax import lax
from jax.sharding import PartitionSpec as P

HEAD_DIM = 64


epsilon = 1e-05
masked_score = -1000000000.0
highest = lax.Precision.HIGHEST


def passed_along(value, axis, steps):
    count = lax.axis_size(axis)
    initial, last = (max(0, -steps), min(count, count - steps))
    return lax.ppermute(value, axis, [(source, source + steps) for source in range(initial, last)])


def norm_forward(values, gain_row, shift_row):
    centred = values - jnp.mean(values, -1, keepdims=True)
    reciprocal_factor = lax.rsqrt(jnp.mean(centred * centred, -1, keepdims=True) + epsilon)
    unit_rows = centred * reciprocal_factor
    return (unit_rows * gain_row + shift_row, unit_rows, reciprocal_factor)


def norm_backward(upstream, unit_rows, reciprocal_factor, gain_row):
    scaled = upstream * gain_row
    inner_term = (
        scaled
        - jnp.mean(scaled, -1, keepdims=True)
        - unit_rows * jnp.mean(scaled * unit_rows, -1, keepdims=True)
    )
    return (
        reciprocal_factor * inner_term,
        jnp.sum(upstream * unit_rows, (0, 1)),
        jnp.sum(upstream, (0, 1)),
    )


def gelu_slope(hidden_rows):
    return (
        0.5 * (1.0 + lax.erf(hidden_rows * 0.7071067811865476))
        + hidden_rows * jnp.exp(-0.5 * hidden_rows * hidden_rows) * 0.3989422804014327
    )


def split_heads(block):
    shaped = block.reshape(block.shape[:-1] + (block.shape[-1] // HEAD_DIM, HEAD_DIM))
    return jnp.moveaxis(shaped, -2, -3)


def join_heads(block):
    moved = jnp.moveaxis(block, -3, -2)
    return moved.reshape(moved.shape[:-2] + (moved.shape[-2] * moved.shape[-1],))


def unskew_sum(score_total):
    head_count, length = (score_total.shape[0], score_total.shape[1])
    padded = jnp.pad(score_total, ((0, 0), (0, 0), (length - 1, 0)))
    flat = jnp.pad(padded.reshape(head_count, length * (2 * length - 1)), ((0, 0), (0, length)))
    return jnp.sum(flat.reshape(head_count, length, 2 * length), 1)[:, : 2 * length - 1]


def score_block(queries, keys, bias, allowed):
    raw = jnp.einsum(
        "hid,hjd->hij", queries, keys, preferred_element_type=jnp.float32
    ) * HEAD_DIM ** (-0.5)
    return jnp.where(allowed, raw + bias, masked_score)


def attend_forward(queries, keys, values, bias, allowed):
    scores = score_block(queries, keys, bias, allowed)
    peak = jnp.max(scores, -1, keepdims=True)
    lifted = jnp.exp(scores - peak)
    total = jnp.sum(lifted, -1, keepdims=True)
    log_total = peak + jnp.log(total)
    weights = (lifted / total).astype(jnp.bfloat16)
    result = jnp.einsum("hij,hjd->hid", weights, values, preferred_element_type=jnp.float32)
    return (result.astype(jnp.bfloat16), log_total[..., 0])


def attend_backward(queries, keys, values, bias, allowed, log_total, upstream):
    scores = score_block(queries, keys, bias, allowed)
    probs = jnp.exp(scores - log_total[..., None])
    d_values = jnp.einsum(
        "hij,hid->hjd", probs.astype(jnp.bfloat16), upstream, preferred_element_type=jnp.float32
    )
    d_probs = jnp.einsum("hid,hjd->hij", upstream, values, preferred_element_type=jnp.float32)
    d_scores = probs * (d_probs - jnp.sum(d_probs * probs, -1, keepdims=True))
    rounded_values = d_scores.astype(jnp.bfloat16)
    d_queries = jnp.einsum(
        "hij,hjd->hid", rounded_values, keys, preferred_element_type=jnp.float32
    ) * HEAD_DIM ** (-0.5)
    d_keys = jnp.einsum(
        "hij,hid->hjd", rounded_values, queries, preferred_element_type=jnp.float32
    ) * HEAD_DIM ** (-0.5)
    return (
        d_queries.astype(jnp.bfloat16),
        d_keys.astype(jnp.bfloat16),
        d_values.astype(jnp.bfloat16),
        d_scores,
    )


def pick_entries(block):
    return lax.all_gather(block, "tensor", axis=1, tiled=True)


def sum_rows(block):
    return lax.psum_scatter(block, "tensor", scatter_dimension=1, tiled=True)


def gather_grads(block):
    return lax.all_gather(block, "tensor", axis=1, tiled=True)


def sum_grads(block):
    return lax.psum_scatter(block, "tensor", scatter_dimension=1, tiled=True)


def feed_forward(collected_rows, up_weight, down_weight):
    hidden_rows = jnp.einsum(
        "jua,ai->jui", collected_rows, up_weight, preferred_element_type=jnp.float32
    )
    activated_rows = jax.nn.gelu(hidden_rows, approximate=False).astype(jnp.bfloat16)
    return (
        jnp.einsum("jry,yx->jrx", activated_rows, down_weight, preferred_element_type=jnp.float32),
        hidden_rows,
        activated_rows,
    )


def feed_backward(
    rounded_values, collected_rows, hidden_rows, activated_rows, up_weight, down_weight
):
    down_weight_gradient = jnp.einsum(
        "nxv,nxt->vt", activated_rows, rounded_values, preferred_element_type=jnp.float32
    )
    activated_gradient = jnp.einsum(
        "hot,pt->hop", rounded_values, down_weight, preferred_element_type=jnp.float32
    )
    hidden_gradient = (activated_gradient * gelu_slope(hidden_rows)).astype(jnp.bfloat16)
    up_weight_gradient = jnp.einsum(
        "qwk,qwz->kz", collected_rows, hidden_gradient, preferred_element_type=jnp.float32
    )
    branch_portion = jnp.einsum(
        "knu,zu->knz", hidden_gradient, up_weight, preferred_element_type=jnp.float32
    )
    return (branch_portion, up_weight_gradient, down_weight_gradient)


def layer_forward(inputs16, keys_values, weights, context):
    norm_gains, input_weight, result_matrix, cross_weight, up_weight, down_weight = weights
    decoder, self_bias, self_allowed, cross_allowed, row_mask = context
    heads_here = input_weight.shape[2] // HEAD_DIM
    inputs = inputs16.astype(jnp.float32)
    normed, unit_one, inverse_one = norm_forward(inputs, norm_gains[0, 0], norm_gains[0, 1])
    gathered_single = pick_entries(normed.astype(jnp.bfloat16))
    seq_count, length = (gathered_single.shape[0], gathered_single.shape[1])
    projected = split_heads(
        jnp.einsum(
            "fgh,whn->wfgn", gathered_single, input_weight, preferred_element_type=jnp.float32
        ).astype(jnp.bfloat16)
    )

    def self_one(member):
        return attend_forward(member[0], member[1], member[2], self_bias, member[3])

    result_heads, lse_one = lax.map(
        self_one, (projected[0], projected[1], projected[2], self_allowed)
    )
    outcome_first = join_heads(result_heads)
    after_one = inputs + sum_rows(
        jnp.einsum("fpr,rg->fpg", outcome_first, result_matrix, preferred_element_type=jnp.float32)
    )
    normed, unit_two, inverse_two = norm_forward(after_one, norm_gains[1, 0], norm_gains[1, 1])
    collected_two = pick_entries(normed.astype(jnp.bfloat16))
    hidden_zeros = jnp.zeros((seq_count, length, up_weight.shape[1]), jnp.float32)

    def cross_one(member):
        return attend_forward(member[0], member[1], member[2], 0.0, member[3])

    def cross_branch(collected_rows):
        queries = split_heads(
            jnp.einsum(
                "uzm,my->uzy", collected_rows, cross_weight[0], preferred_element_type=jnp.float32
            ).astype(jnp.bfloat16)
        )
        sources = split_heads(keys_values)
        result_cross, lse_cross = lax.map(
            cross_one, (queries, sources[0], sources[1], cross_allowed)
        )
        merged_heads = join_heads(result_cross)
        branch_portion = jnp.einsum(
            "upj,tj->upt", merged_heads, cross_weight[1], preferred_element_type=jnp.float32
        )
        return (
            branch_portion,
            queries,
            merged_heads,
            lse_cross,
            hidden_zeros,
            hidden_zeros.astype(jnp.bfloat16),
        )

    def feed_branch(collected_rows):
        branch_portion, hidden_rows, activated_rows = feed_forward(
            collected_rows, up_weight, down_weight
        )
        query_zeros = jnp.zeros((seq_count, heads_here, length, HEAD_DIM), jnp.bfloat16)
        joined_zeros = jnp.zeros((seq_count, length, input_weight.shape[2]), jnp.bfloat16)
        lse_zeros = jnp.zeros((seq_count, heads_here, length), jnp.float32)
        return (branch_portion, query_zeros, joined_zeros, lse_zeros, hidden_rows, activated_rows)

    part_two, queries, merged_heads_two, lse_two, hidden_two, active_two = lax.cond(
        decoder, cross_branch, feed_branch, collected_two
    )
    after_two = after_one + sum_rows(part_two)
    normed, unit_three, inverse_three = norm_forward(after_two, norm_gains[2, 0], norm_gains[2, 1])
    normed = jnp.where(decoder, normed, normed * row_mask)
    collected_three = pick_entries(normed.astype(jnp.bfloat16))
    kv_zeros = jnp.zeros((2, seq_count, length, input_weight.shape[2]), jnp.bfloat16)

    def feed_third(collected_rows):
        branch_portion, hidden_rows, activated_rows = feed_forward(
            collected_rows, up_weight, down_weight
        )
        return (branch_portion, hidden_rows, activated_rows, kv_zeros)

    def project_third(collected_rows):
        kv_new = jnp.einsum(
            "fgh,whn->wfgn", collected_rows, cross_weight, preferred_element_type=jnp.float32
        ).astype(jnp.bfloat16)
        return (jnp.zeros(collected_rows.shape, jnp.float32), hidden_two, active_two, kv_new)

    part_three, hidden_used, active_used, kv_new = lax.cond(
        decoder, feed_third, project_third, collected_three
    )
    after_three = after_two + sum_rows(part_three)
    result = jnp.where(decoder, after_three * row_mask, normed)
    saved = (
        unit_one,
        inverse_one,
        gathered_single,
        projected,
        outcome_first,
        lse_one,
        unit_two,
        inverse_two,
        collected_two,
        queries,
        merged_heads_two,
        lse_two,
        unit_three,
        inverse_three,
        collected_three,
        hidden_used,
        active_used,
    )
    return (result, saved, kv_new)


def layer_backward(saved, upstream, returned_key_value, keys_values, weights, context):
    norm_gains, input_weight, result_matrix, cross_weight, up_weight, down_weight = weights
    decoder, self_bias, self_allowed, cross_allowed, row_mask = context
    (
        unit_one,
        inverse_one,
        gathered_single,
        projected,
        outcome_first,
        lse_one,
        unit_two,
        inverse_two,
        collected_two,
        queries,
        merged_heads_two,
        lse_two,
        unit_three,
        inverse_three,
        collected_three,
        hidden_used,
        active_used,
    ) = saved
    cross_zeros = jnp.zeros(cross_weight.shape, jnp.float32)
    up_zeros = jnp.zeros(up_weight.shape, jnp.float32)
    down_zeros = jnp.zeros(down_weight.shape, jnp.float32)
    cot_masked = upstream * row_mask
    incoming = gather_grads(jnp.where(decoder, cot_masked, 0.0).astype(jnp.bfloat16))

    def decoder_first(collected_rows):
        branch_portion, up_weight_gradient, down_weight_gradient = feed_backward(
            collected_rows, collected_three, hidden_used, active_used, up_weight, down_weight
        )
        return (branch_portion, cross_zeros, up_weight_gradient, down_weight_gradient)

    def encoder_first(collected_rows):
        branch_portion = jnp.einsum(
            "mgky,mty->gkt", returned_key_value, cross_weight, preferred_element_type=jnp.float32
        )
        d_cross = jnp.einsum(
            "wxn,rwxo->rno", collected_three, returned_key_value, preferred_element_type=jnp.float32
        )
        return (branch_portion, d_cross, up_zeros, down_zeros)

    part_first, cross_first, expand_leading, down_first = lax.cond(
        decoder, decoder_first, encoder_first, incoming
    )
    summed_first = sum_grads(part_first)
    upstream_first = jnp.where(decoder, summed_first, (upstream + summed_first) * row_mask)
    norm_first, gain_first, shift_first = norm_backward(
        upstream_first, unit_three, inverse_three, norm_gains[2, 0]
    )
    grad_two = jnp.where(decoder, cot_masked, 0.0) + norm_first
    gathered_grad_two = gather_grads(grad_two.astype(jnp.bfloat16))

    def cross_back(member):
        d_query, d_key, d_value, d_scores = attend_backward(
            member[0], member[1], member[2], 0.0, member[3], member[4], member[5]
        )
        return (d_query, d_key, d_value)

    def decoder_second(collected_rows):
        d_out_w = jnp.einsum(
            "vhg,vhr->gr", collected_rows, merged_heads_two, preferred_element_type=jnp.float32
        )
        d_joined = split_heads(
            jnp.einsum(
                "uzm,my->uzy", collected_rows, cross_weight[1], preferred_element_type=jnp.float32
            ).astype(jnp.bfloat16)
        )
        sources = split_heads(keys_values)
        d_query, d_key, d_value = lax.map(
            cross_back, (queries, sources[0], sources[1], cross_allowed, lse_two, d_joined)
        )
        flattened_query = join_heads(d_query)
        d_query_w = jnp.einsum(
            "vhg,vhr->gr", collected_two, flattened_query, preferred_element_type=jnp.float32
        )
        branch_portion = jnp.einsum(
            "upj,tj->upt", flattened_query, cross_weight[0], preferred_element_type=jnp.float32
        )
        kv_grad = jnp.stack([join_heads(d_key), join_heads(d_value)])
        return (branch_portion, jnp.stack([d_query_w, d_out_w]), up_zeros, down_zeros, kv_grad)

    def encoder_second(collected_rows):
        branch_portion, up_weight_gradient, down_weight_gradient = feed_backward(
            collected_rows, collected_two, hidden_used, active_used, up_weight, down_weight
        )
        return (
            branch_portion,
            cross_zeros,
            up_weight_gradient,
            down_weight_gradient,
            jnp.zeros(keys_values.shape, jnp.bfloat16),
        )

    part_second, cross_second, up_second, down_second, kv_grad = lax.cond(
        decoder, decoder_second, encoder_second, gathered_grad_two
    )
    summed_second = sum_grads(part_second)
    norm_second, gain_second, shift_second = norm_backward(
        summed_second, unit_two, inverse_two, norm_gains[1, 0]
    )
    grad_one = grad_two + norm_second
    gathered_derivative_single = gather_grads(grad_one.astype(jnp.bfloat16))

    def self_back(member):
        return attend_backward(
            member[0], member[1], member[2], self_bias, member[3], member[4], member[5]
        )

    d_attn_out = jnp.einsum(
        "rnb,rnx->bx", outcome_first, gathered_derivative_single, preferred_element_type=jnp.float32
    )
    d_joined = split_heads(
        jnp.einsum(
            "lus,ts->lut",
            gathered_derivative_single,
            result_matrix,
            preferred_element_type=jnp.float32,
        ).astype(jnp.bfloat16)
    )
    d_query, d_key, d_value, d_scores = lax.map(
        self_back, (projected[0], projected[1], projected[2], self_allowed, lse_one, d_joined)
    )
    projection_gradient = jnp.stack([join_heads(d_query), join_heads(d_key), join_heads(d_value)])
    d_attn_in = jnp.einsum(
        "wxn,rwxo->rno", gathered_single, projection_gradient, preferred_element_type=jnp.float32
    )
    summed_third = sum_grads(
        jnp.einsum(
            "mgky,mty->gkt", projection_gradient, input_weight, preferred_element_type=jnp.float32
        )
    )
    norm_third, gain_third, shift_third = norm_backward(
        summed_third, unit_one, inverse_one, norm_gains[0, 0]
    )
    grad_input = grad_one + norm_third
    gain_grads = jnp.stack(
        [
            jnp.stack([gain_third, shift_third]),
            jnp.stack([gain_second, shift_second]),
            jnp.stack([gain_first, shift_first]),
        ]
    )
    tick_grads = (
        jnp.sum(d_scores, 0),
        gain_grads,
        d_attn_in,
        d_attn_out,
        cross_first + cross_second,
        expand_leading + up_second,
        down_first + down_second,
    )
    return (grad_input, kv_grad, tick_grads)


def put_block(store, block_index, value):
    return lax.dynamic_update_index_in_dim(store, value, block_index, 0)


def body(
    frames,
    lengths,
    bucket_of,
    rel_table,
    norms,
    attn_in,
    attn_out,
    cross_pair,
    ffn_in,
    ffn_out,
    cotangent,
):
    section_index = lax.axis_index("section")
    decoder = section_index == 1
    micro_count = frames.shape[1]
    seq_count = frames.shape[2]
    quarter = frames.shape[3]
    model_width = frames.shape[4]
    length = quarter * lax.axis_size("tensor")
    head_width = attn_in.shape[3]
    bucket_count = rel_table.shape[1]
    weights = (norms[0], attn_in[0], attn_out[0], cross_pair[0], ffn_in[0], ffn_out[0])
    row_index = lax.broadcasted_iota(jnp.int32, (length, length), 0)
    col_index = lax.broadcasted_iota(jnp.int32, (length, length), 1)
    offsets = col_index - row_index + length - 1
    one_hot = (
        bucket_of[0][:, None] == lax.broadcasted_iota(jnp.int32, (1, bucket_count), 1)
    ).astype(jnp.float32)
    distance_bias = jnp.dot(
        one_hot, rel_table[0], precision=highest, preferred_element_type=jnp.float32
    )
    self_bias = distance_bias.T[:, offsets]
    own_lengths = lax.dynamic_index_in_dim(lengths, section_index, 0, keepdims=False)
    positions = lax.axis_index("tensor") * quarter + lax.broadcasted_iota(
        jnp.int32, (1, quarter, 1), 1
    )

    def context_of(block_index):
        own_length = lax.dynamic_index_in_dim(own_lengths, block_index, 0, keepdims=False)
        source_length = lax.dynamic_index_in_dim(lengths[0], block_index, 0, keepdims=False)
        keys_ok = col_index[None] < own_length[:, None, None]
        causal = (col_index <= row_index)[None] | jnp.logical_not(decoder)
        self_allowed = (keys_ok & causal)[:, None]
        cross_allowed = (col_index[None] < source_length[:, None, None])[:, None]
        row_mask = (positions < own_length[:, None, None]).astype(jnp.float32)
        return (decoder, self_bias, self_allowed, cross_allowed, row_mask)

    slot_count = micro_count + 1
    empty_kv = jnp.zeros((2, seq_count, length, head_width), jnp.bfloat16)
    received = empty_kv
    kv_store = jnp.zeros((micro_count,) + empty_kv.shape, jnp.bfloat16)
    out_store = jnp.zeros((slot_count, seq_count, quarter, model_width), jnp.float32)
    saved_store = None
    for tick_number in range(micro_count + 1):
        raw_index = tick_number - section_index
        is_valid = (raw_index >= 0) & (raw_index < micro_count)
        block_index = jnp.clip(raw_index, 0, micro_count - 1)
        write_index = jnp.where(is_valid, block_index, micro_count)
        context = context_of(block_index)
        inputs16 = lax.dynamic_index_in_dim(frames[0], block_index, 0, keepdims=False)
        result, saved, kv_new = layer_forward(inputs16, received, weights, context)
        kv_store = put_block(kv_store, block_index, received)
        out_store = put_block(out_store, write_index, result)
        if saved_store is None:
            saved_store = jax.tree.map(
                lambda array_leaf: jnp.zeros((slot_count,) + array_leaf.shape, array_leaf.dtype),
                saved,
            )
        saved_store = jax.tree.map(
            lambda saved_tree_node, array_leaf: put_block(saved_tree_node, write_index, array_leaf),
            saved_store,
            saved,
        )
        if tick_number < micro_count:
            received = passed_along(kv_new, "section", 1)
    returned = empty_kv
    grads_store = jnp.zeros((slot_count, seq_count, quarter, model_width), jnp.float32)
    totals = None
    for tick_number in range(micro_count + 1):
        raw_index = tick_number - 1 + section_index
        is_valid = (raw_index >= 0) & (raw_index < micro_count)
        block_index = jnp.clip(raw_index, 0, micro_count - 1)
        write_index = jnp.where(is_valid, block_index, micro_count)
        context = context_of(block_index)
        keys_values = lax.dynamic_index_in_dim(kv_store, block_index, 0, keepdims=False)
        saved = jax.tree.map(
            lambda saved_tree_node: lax.dynamic_index_in_dim(
                saved_tree_node, block_index, 0, keepdims=False
            ),
            saved_store,
        )
        upstream = lax.dynamic_index_in_dim(cotangent[0], block_index, 0, keepdims=False).astype(
            jnp.float32
        )
        grad_input, kv_grad, tick_grads = layer_backward(
            saved, upstream, returned, keys_values, weights, context
        )
        grads_store = put_block(grads_store, write_index, grad_input)
        tick_grads = jax.tree.map(
            lambda array_leaf: jnp.where(is_valid, array_leaf, 0.0), tick_grads
        )
        totals = tick_grads if totals is None else jax.tree.map(jnp.add, totals, tick_grads)
        if tick_number < micro_count:
            returned = passed_along(kv_grad, "section", -1)
    out_final = out_store[:micro_count]
    grads_final = grads_store[:micro_count]
    spread = unskew_sum(totals[0])
    squares = jnp.sum(out_final * out_final)
    valid_rows = jnp.sum((positions[None] < own_lengths[:, :, None, None]).astype(jnp.float32))
    gain_total, square_total, count_total = lax.psum(
        (totals[1], squares, valid_rows), ("dp", "tensor")
    )
    stats = jnp.sqrt(square_total / (count_total * model_width)).reshape(1)
    local_shape = (1, micro_count, seq_count, quarter, model_width)
    return (
        out_final.reshape(local_shape).astype(jnp.bfloat16),
        grads_final.reshape(local_shape),
        lax.psum(
            jnp.dot(
                one_hot.T, spread.T, precision=highest, preferred_element_type=jnp.float32
            ).astype(jnp.bfloat16),
            "dp",
        ).astype(jnp.float32)[None],
        gain_total[None],
        lax.psum(totals[2].astype(jnp.bfloat16), "dp").astype(jnp.float32)[None],
        lax.psum(totals[3].astype(jnp.bfloat16), "dp").astype(jnp.float32)[None],
        lax.psum(totals[4].astype(jnp.bfloat16), "dp").astype(jnp.float32)[None],
        lax.psum(totals[5].astype(jnp.bfloat16), "dp").astype(jnp.float32)[None],
        lax.psum(totals[6].astype(jnp.bfloat16), "dp").astype(jnp.float32)[None],
        stats,
    )


def solution(mesh):
    in_specs = (
        P("section", None, "dp", "tensor", None),
        P(None, None, "dp"),
        P("section", None),
        P("section", None, "tensor"),
        P("section", None, None, None),
        P("section", None, None, "tensor"),
        P("section", "tensor", None),
        P("section", None, None, "tensor"),
        P("section", None, "tensor"),
        P("section", "tensor", None),
        P("section", None, "dp", "tensor", None),
    )
    out_specs = (
        P("section", None, "dp", "tensor", None),
        P("section", None, "dp", "tensor", None),
        P("section", None, "tensor"),
        P("section", None, None, None),
        P("section", None, None, "tensor"),
        P("section", "tensor", None),
        P("section", None, None, "tensor"),
        P("section", None, "tensor"),
        P("section", "tensor", None),
        P("section"),
    )
    return jax.shard_map(body, mesh=mesh, in_specs=in_specs, out_specs=out_specs, check_vma=False)
```

profile of v0, /device:TPU:0, one launch (start us, length us, event | category | flops | bytes accessed | tf_op | source)
XLA Modules:
  0.0 6155.5 jit_solution(5146509848207890749)
XLA Ops:
  25.6 3794.1 %gather_fusion = f32[1048576,3]{1,0:T(8,128)} fusion(f32[3,2047]{0,1:T(8,128)S(1)} %copy.247, s32[1048576]{0:T(1024)} %broadcast_clamp_fusion), kind=kCustom, calls=%fused_computation | custom fusion | bytes 29360128 | tf_op jit(solution)/shard_map/gather | solution.py:456
  3819.6 280.7 %copy.249 = f32[1024,1024,3]{0,1,2:T(8,128)} copy(f32[1024,1024,3]{2,1,0:T(8,128)} %bitcast.254) | data formatting | bytes 25165824 | tf_op jit(solution)/shard_map/gather | solution.py:456
  4105.7 7.1 fusion.667
  4123.4 7.5 fusion.668
  4140.5 7.1 fusion.669
  4160.3 40.5 reduce-scatter.25.cloned.1.call-done
  4200.8 40.4 reduce-scatter.19.cloned.1.call-done
  4246.4 18.9 all-gather.21.cloned.1.call-done
  4267.4 15.7 conditional.12
  4267.4 9.4 fusion.2
  4284.5 53.1 reduce-scatter.21.cloned.1.call-done
  4341.5 19.2 all-gather.23.cloned.1.call-done
  4366.1 15.0 collective-permute-start
  4382.3 15.4 collective-permute-done
  4398.1 16.0 conditional.14
  4398.1 9.4 fusion.55
  4414.9 56.0 reduce-scatter.27.cloned.1.call-done
  4474.9 19.0 all-gather.29.cloned.1.call-done
  4499.5 15.0 collective-permute-start.1
  4515.9 15.3 collective-permute-done.1
  4531.4 15.8 conditional.16
  4531.5 9.4 fusion.104
  4548.1 56.1 reduce-scatter.33.cloned.1.call-done
  4612.0 15.2 all-gather.35.cloned.1.call-done
  4652.9 7.9 conditional.18
  4664.1 24.7 reduce-scatter.23.cloned.1.call-done
  4691.9 37.4 reduce-scatter.29.cloned.1.call-done
  4732.7 37.1 reduce-scatter.35.cloned.1.call-done
  4772.4 37.9 reduce-scatter.37.cloned.1.call-done
  4844.2 22.3 conditional.19
  4867.8 42.8 collective-permute-done.2
  4910.6 7.5 conditional.20
  4918.2 43.3 reduce-scatter.43.cloned.1.call-done
  4967.1 19.0 all-gather.45.cloned.1.call-done
  4989.6 22.1 conditional.21
  5013.0 43.2 collective-permute-done.3
  5056.2 7.7 conditional.22
  5064.0 43.3 reduce-scatter.49.cloned.1.call-done
  5113.8 18.3 all-gather.51.cloned.1.call-done
  5135.1 20.3 conditional.23
  5155.6 8.3 all-gather.41.cloned.1.call-start
  5195.5 17.8 reduce-scatter.45.cloned.1.call-done
  5213.3 40.3 reduce-scatter.51.cloned.1.call-done
  5260.0 13.7 fusion.379
  5275.8 13.4 fusion.370
  5318.7 7.3 fusion.450
  5326.0 11.3 multiply_reduce_fusion.5
  5337.3 7.5 multiply_reduce_fusion.4
  5346.9 11.2 multiply_reduce_fusion.3
  5358.1 36.4 select_add_fusion
  5455.3 12.8 copy.370
  5468.1 15.6 pad.8.clone
  5483.7 35.0 reshape.3296
  5518.8 492.0 %while.1 = (u32[]{:T(128)}, f32[6288384]{0:T(1024)}, f32[1,3,2096128]{2,1,0:T(4,128)}, u32[]{}, u32[]{}, /*index=5*/u32[]{}, u32[]{}, u32[]{}) while((u32[]{:T(128)}, f32[6288384]{0:T(1024)}, f32[1,3,2096128]{2,1,0:T(4,128)}, u32[]{}, u32[]{}, /*index=5*/u32[]{}, u32[]{}, u32[]{}) %tuple.436), condition=%wide.cond, body=%wide.body.sunk | while | flops 9 | bytes 50307256
  5523.2 9.0 reshape.3299
  5532.2 151.4 %dynamic-update-slice.2 = f32[1,3,2096128]{2,1,0:T(4,128)} dynamic-update-slice(f32[1,3,2096128]{2,1,0:T(4,128)} %get-tuple-element.1693, f32[1,1,2096128]{2,1,0:T(1,128)} %reshape.3299, u32[]{:T(128)S(6)} %multiply.296, u32[]{:T(128)S(6)} %multiply.298, u32[]{} %constant.1939..sunk) | dynamic-update-slice | bytes 16769028
  5687.4 9.0 reshape.3299
  5696.4 150.8 %dynamic-update-slice.2 = f32[1,3,2096128]{2,1,0:T(4,128)} dynamic-update-slice(f32[1,3,2096128]{2,1,0:T(4,128)} %get-tuple-element.1693, f32[1,1,2096128]{2,1,0:T(1,128)} %reshape.3299, u32[]{:T(128)S(6)} %multiply.296, u32[]{:T(128)S(6)} %multiply.298, u32[]{} %constant.1939..sunk) | dynamic-update-slice | bytes 16769028
  5851.0 9.0 reshape.3299
  5859.9 150.8 %dynamic-update-slice.2 = f32[1,3,2096128]{2,1,0:T(4,128)} dynamic-update-slice(f32[1,3,2096128]{2,1,0:T(4,128)} %get-tuple-element.1693, f32[1,1,2096128]{2,1,0:T(1,128)} %reshape.3299, u32[]{:T(128)S(6)} %multiply.296, u32[]{:T(128)S(6)} %multiply.298, u32[]{} %constant.1939..sunk) | dynamic-update-slice | bytes 16769028
  6010.7 22.6 pad.9
  6033.4 26.3 bitcast_reduce_fusion
  6060.9 11.7 psum.63
  6088.1 57.7 all-reduce.2
  (810 shorter events, 465.3 us)
Async XLA Ops:
  7.2 4095.8 %copy-start = (bf16[1,3,768,192]{2,3,1,0:T(8,128)(2,1)S(1)}, bf16[1,3,768,192]{2,3,1,0:T(8,128)(2,1)}, u32[]{:S(2)}) copy-start(bf16[1,3,768,192]{2,3,1,0:T(8,128)(2,1)} %param.40) | copy-start | bytes 2654212
  7.2 4095.8 %all-gather.31.cloned.1.call-start = ((), (), s32[]{:S(2)}) async-start(), calls=%async_computation.30 | async-start | bytes 1966080 | tf_op jit(solution)/shard_map/all_gather | solution.py:107
  13.7 4106.9 %all-gather.25.cloned.1.call-start = ((), (), s32[]{:S(2)}) async-start(), calls=%async_computation.24 | async-start | bytes 1966080 | tf_op jit(solution)/shard_map/all_gather | solution.py:107
  14.4 4123.3 %all-gather.19.cloned.1.call-start = ((), (), s32[]{:S(2)}) async-start(), calls=%async_computation.18 | async-start | bytes 1966080 | tf_op jit(solution)/shard_map/all_gather | solution.py:107
  15.2 4145.1 %reduce-scatter.31.cloned.1.call-start = ((), (), s32[]{:S(2)}) async-start(), calls=%async_computation.31 | async-start | bytes 3932160 | tf_op jit(solution)/shard_map/reduce_scatter | solution.py:111
  3819.6 280.7 %copy-start.169 = (s32[2,2,1]{1,2,0:T(1,128)S(1)}, s32[2,2,1]{1,2,0:T(1,128)}, u32[]{:S(2)}) copy-start(s32[2,2,1]{1,2,0:T(1,128)} %param.36) | copy-start | bytes 52
  4119.3 81.5 %reduce-scatter.25.cloned.1.call-start = ((), (), s32[]{:S(2)}) async-start(), calls=%async_computation.25 | async-start | bytes 3932160 | tf_op jit(solution)/shard_map/reduce_scatter | solution.py:111
  4137.3 103.9 %reduce-scatter.19.cloned.1.call-start = ((), (), s32[]{:S(2)}) async-start(), calls=%async_computation.19 | async-start | bytes 3932160 | tf_op jit(solution)/shard_map/reduce_scatter | solution.py:111
  4151.7 89.5 %copy-start.5 = (bf16[1,2,1,256,768]{4,3,2,1,0:T(8,128)(2,1)S(1)}, bf16[1,2,1,256,768]{4,3,2,1,0:T(8,128)(2,1)}, u32[]{:S(2)}) copy-start(bf16[1,2,1,256,768]{4,3,2,1,0:T(8,128)(2,1)} %param.35) | copy-start | bytes 2359300
  4154.0 90.0 %copy-start.133 = (f32[768]{0:T(1024)S(1)}, f32[768]{0:T(1024)}, u32[]{:S(2)}) copy-start(f32[768]{0:T(1024)} %get-tuple-element.1413) | copy-start | bytes 9220
  4154.0 90.0 %copy-start.182 = (f32[768]{0:T(1024)S(1)}, f32[768]{0:T(1024)}, u32[]{:S(2)}) copy-start(f32[768]{0:T(1024)} %get-tuple-element.1412) | copy-start | bytes 9220
  4154.1 111.3 %all-gather.21.cloned.1.call-start = ((), (), s32[]{:S(2)}) async-start(), calls=%async_computation.20 | async-start | bytes 1966080 | tf_op jit(solution)/shard_map/all_gather | solution.py:107
  4243.1 94.5 %copy-start.18 = (f32[1,256,768]{2,1,0:T(8,128)}, f32[1,256,768]{2,1,0:T(8,128)S(1)}, u32[]{:S(2)}) copy-start(f32[1,256,768]{2,1,0:T(8,128)S(1)} %get-tuple-element.1512) | copy-start | bytes 2359300
  4245.5 92.1 %reduce-scatter.21.cloned.1.call-start = ((), (), s32[]{:S(2)}) async-start(), calls=%async_computation.21 | async-start | bytes 3932160 | tf_op jit(solution)/shard_map/reduce_scatter | solution.py:111
  4283.7 56.0 copy-start.116
  4283.8 56.0 copy-start.124
  4283.8 76.9 %all-gather.23.cloned.1.call-start = ((), (), s32[]{:S(2)}) async-start(), calls=%async_computation.22 | async-start | bytes 1966080 | tf_op jit(solution)/shard_map/all_gather | solution.py:107
  4284.5 76.2 %copy-start.195 = (f32[256]{0:T(256)}, f32[256]{0:T(256)S(1)}, u32[]{:S(2)}) copy-start(f32[256]{0:T(256)S(1)} %compare_convert_fusion.6) | copy-start | bytes 3076
  4340.8 41.5 all-gather.27.cloned.1.call-start
  4341.4 129.5 %reduce-scatter.27.cloned.1.call-start = ((), (), s32[]{:S(2)}) async-start(), calls=%async_computation.27 | async-start | bytes 3932160 | tf_op jit(solution)/shard_map/reduce_scatter | solution.py:111
  4366.1 31.6 collective-permute-start
  4414.1 58.4 copy-start.143
  4414.1 56.8 copy-start.16
  4414.1 79.8 %all-gather.29.cloned.1.call-start = ((), (), s32[]{:S(2)}) async-start(), calls=%async_computation.28 | async-start | bytes 1966080 | tf_op jit(solution)/shard_map/all_gather | solution.py:107
  4414.9 79.0 %copy-start.197 = (f32[256]{0:T(256)}, f32[256]{0:T(256)S(1)}, u32[]{:S(2)}) copy-start(f32[256]{0:T(256)S(1)} %compare_convert_fusion.5) | copy-start | bytes 3076
  4474.1 41.7 all-gather.33.cloned.1.call-start
  4474.9 129.3 %reduce-scatter.33.cloned.1.call-start = ((), (), s32[]{:S(2)}) async-start(), calls=%async_computation.33 | async-start | bytes 3932160 | tf_op jit(solution)/shard_map/reduce_scatter | solution.py:111
  4499.5 31.6 collective-permute-start.1
  4547.2 57.0 copy-start.13
  4547.3 62.2 %copy-start.23 = (bf16[1,2,1,256,768]{4,3,2,1,0:T(8,128)(2,1)S(1)}, bf16[1,2,1,256,768]{4,3,2,1,0:T(8,128)(2,1)}, u32[]{:S(2)}) copy-start(bf16[1,2,1,256,768]{4,3,2,1,0:T(8,128)(2,1)} %param.45) | copy-start | bytes 2359300
  4547.3 80.0 %all-gather.35.cloned.1.call-start = ((), (), s32[]{:S(2)}) async-start(), calls=%async_computation.34 | async-start | bytes 1966080 | tf_op jit(solution)/shard_map/all_gather | solution.py:107
  4607.4 45.4 all-gather.37.cloned.1.call-start
  4610.8 78.0 %reduce-scatter.23.cloned.1.call-start = ((), (), s32[]{:S(2)}) async-start(), calls=%async_computation.23 | async-start | bytes 3932160 | tf_op jit(solution)/shard_map/reduce_scatter | solution.py:111
  4611.4 117.9 %reduce-scatter.29.cloned.1.call-start = ((), (), s32[]{:S(2)}) async-start(), calls=%async_computation.29 | async-start | bytes 3932160 | tf_op jit(solution)/shard_map/reduce_scatter | solution.py:111
  4612.0 157.8 %reduce-scatter.35.cloned.1.call-start = ((), (), s32[]{:S(2)}) async-start(), calls=%async_computation.35 | async-start | bytes 3932160 | tf_op jit(solution)/shard_map/reduce_scatter | solution.py:111
  4629.6 180.7 %reduce-scatter.37.cloned.1.call-start = ((), (), s32[]{:S(2)}) async-start(), calls=%async_computation.37 | async-start | bytes 3932160 | tf_op jit(solution)/shard_map/reduce_scatter | solution.py:119
  4660.8 180.0 %all-gather.39.cloned.1.call-start = ((), (), s32[]{:S(2)}) async-start(), calls=%async_computation.38 | async-start | bytes 1966080 | tf_op jit(solution)/shard_map/all_gather | solution.py:115
  4661.4 27.5 copy-start.196
  4663.0 28.8 copy-start.168
  4663.0 66.2 %copy-start.154 = (f32[256]{0:T(256)S(1)}, f32[256]{0:T(256)}, u32[]{:S(2)}) copy-start(f32[256]{0:T(256)} %copy-done.153) | copy-start | bytes 3076
  4663.0 66.2 %copy-start.198 = (f32[256]{0:T(256)S(1)}, f32[256]{0:T(256)}, u32[]{:S(2)}) copy-start(f32[256]{0:T(256)} %copy-done.197) | copy-start | bytes 3076
  4691.8 78.0 %copy-start.26 = (f32[1,256,768]{2,1,0:T(8,128)S(1)}, f32[1,256,768]{2,1,0:T(8,128)}, u32[]{:S(2)}) copy-start(f32[1,256,768]{2,1,0:T(8,128)} %copy-done.25) | copy-start | bytes 2359300
  4815.2 52.6 all-gather.43.cloned.1.call-start
  4816.0 145.5 %reduce-scatter.43.cloned.1.call-start = ((), (), s32[]{:S(2)}) async-start(), calls=%async_computation.43 | async-start | bytes 3932160 | tf_op jit(solution)/shard_map/reduce_scatter | solution.py:119
  4866.5 44.1 collective-permute-start.2
  4918.1 43.4 copy-start.152
  4918.1 68.1 %all-gather.45.cloned.1.call-start = ((), (), s32[]{:S(2)}) async-start(), calls=%async_computation.44 | async-start | bytes 1966080 | tf_op jit(solution)/shard_map/all_gather | solution.py:115
  4966.4 46.6 all-gather.49.cloned.1.call-start
  4967.1 140.2 %reduce-scatter.49.cloned.1.call-start = ((), (), s32[]{:S(2)}) async-start(), calls=%async_computation.49 | async-start | bytes 3932160 | tf_op jit(solution)/shard_map/reduce_scatter | solution.py:119
  5011.7 44.5 collective-permute-start.3
  5063.9 43.4 copy-start.150
  5063.9 45.8 copy-start.199
  5063.9 68.1 %all-gather.51.cloned.1.call-start = ((), (), s32[]{:S(2)}) async-start(), calls=%async_computation.50 | async-start | bytes 1966080 | tf_op jit(solution)/shard_map/all_gather | solution.py:115
  5112.2 83.3 %reduce-scatter.39.cloned.1.call-start = ((), (), s32[]{:S(2)}) async-start(), calls=%async_computation.39 | async-start | bytes 3932160 | tf_op jit(solution)/shard_map/reduce_scatter | solution.py:119
  5113.0 100.3 %reduce-scatter.45.cloned.1.call-start = ((), (), s32[]{:S(2)}) async-start(), calls=%async_computation.45 | async-start | bytes 3932160 | tf_op jit(solution)/shard_map/reduce_scatter | solution.py:119
  5113.7 139.9 %reduce-scatter.51.cloned.1.call-start = ((), (), s32[]{:S(2)}) async-start(), calls=%async_computation.51 | async-start | bytes 3932160 | tf_op jit(solution)/shard_map/reduce_scatter | solution.py:119
  5155.6 159.0 %all-gather.41.cloned.1.call-start = ((), (), s32[]{:S(2)}) async-start(), calls=%async_computation.40 | async-start | bytes 1966080 | tf_op jit(solution)/shard_map/all_gather | solution.py:115
  5194.1 59.6 copy-start.134
  5258.0 58.6 all-gather.47.cloned.1.call-start
  5275.6 69.2 %all-gather.53.cloned.1.call-start = ((), (), s32[]{:S(2)}) async-start(), calls=%async_computation.52 | async-start | bytes 1966080 | tf_op jit(solution)/shard_map/all_gather | solution.py:115
  5314.2 758.9 %all-reduce.6.cloned.1.call-start = ((), (), s32[]{:S(2)}) async-start(), calls=%async_computation.54 | async-start | bytes 8257536 | tf_op jit(solution)/shard_map/psum | solution.py:549
  5436.9 645.1 %reduce-scatter.41.cloned.1.call-start = ((), (), s32[]{:S(2)}) async-start(), calls=%async_computation.41 | async-start | bytes 3932160 | tf_op jit(solution)/shard_map/reduce_scatter | solution.py:119
  5441.2 640.8 %reduce-scatter.53.cloned.1.call-start = ((), (), s32[]{:S(2)}) async-start(), calls=%async_computation.53 | async-start | bytes 3932160 | tf_op jit(solution)/shard_map/reduce_scatter | solution.py:119
  5445.3 636.7 %reduce-scatter.47.cloned.1.call-start = ((), (), s32[]{:S(2)}) async-start(), calls=%async_computation.47 | async-start | bytes 3932160 | tf_op jit(solution)/shard_map/reduce_scatter | solution.py:119
  (176 other events, 1027.4 us)
Sparse Core Ops, SparseCore 0:
  13.8 22.3 all-gather.30
  38.3 19.6 all-gather.24
  60.2 19.6 all-gather.18
  4119.4 40.8 reduce-scatter.30
  4162.8 37.9 reduce-scatter.24
  4203.2 37.9 reduce-scatter.18
  4245.6 19.6 all-gather.20
  4283.9 53.6 reduce-scatter.20
  4340.9 19.6 all-gather.22
  4362.6 19.6 all-gather.26
  4414.2 56.6 reduce-scatter.26
  4474.3 19.6 all-gather.28
  4496.2 19.6 all-gather.32
  4547.4 56.7 reduce-scatter.32
  4607.5 19.6 all-gather.34
  4628.7 19.6 all-gather.36
  4650.7 37.9 reduce-scatter.22
  4691.3 37.9 reduce-scatter.28
  4731.8 37.9 reduce-scatter.34
  4772.3 37.9 reduce-scatter.36
  4815.3 19.6 all-gather.38
  4836.6 19.6 all-gather.42
  4918.2 43.1 reduce-scatter.42
  4966.5 19.6 all-gather.44
  4987.8 19.6 all-gather.48
  5064.1 43.1 reduce-scatter.48
  5112.3 19.6 all-gather.50
  5134.6 37.9 reduce-scatter.38
  5175.3 37.9 reduce-scatter.44
  5215.7 37.9 reduce-scatter.50
  5258.1 19.6 all-gather.40
  5279.5 19.6 all-gather.46
  5314.4 19.6 all-gather.52
  5437.0 154.1 all-reduce.5
  5593.8 36.8 reduce-scatter.40
  5633.2 37.9 reduce-scatter.52
  5673.6 37.9 reduce-scatter.46
where the time goes:
time: 6260 us; the launch traced here: 6160 us
  local copies, waits for them, and re-layouts  4800 us (77%)
  waiting for transfers between devices  770 us (12%)
  matrix products  283 us (5%)
  other arithmetic  164 us (3%)
  blocking collectives  69.3 us (1%)
    gather x2, local copies, waits for them, and re-layouts, body(): self_bias = distance_bias.T[:, offsets]  4070 us
    unnamed x385, local copies, waits for them, and re-layouts  582 us
    reduce_scatter x9, waiting for transfers between devices, sum_rows(): return lax.psum_scatter(block, 'tensor', scatter_dimension=1, tiled=True)  352 us
    reduce_scatter x9, waiting for transfers between devices, sum_grads(): return lax.psum_scatter(block, 'tensor', scatter_dimension=1, tiled=True)  183 us
  transfers between devices with their start and end apart: 41, of which 26 were waited for; matrix products, arithmetic and copies ran while one was open for 82% of the time, Pallas kernels for 0%

commit v1 on v0

--- a/solution.py
+++ b/solution.py
@@ -1,6 +1,8 @@
 import jax
 import jax.numpy as jnp
 from jax import lax
+from jax.experimental import pallas as pl
+from jax.experimental.pallas import tpu as pltpu
 from jax.sharding import PartitionSpec as P
 
 HEAD_DIM = 64
@@ -55,11 +57,55 @@
     return moved.reshape(moved.shape[:-2] + (moved.shape[-2] * moved.shape[-1],))
 
 
+def skew_kernel(distance_ref, table_ref):
+    width = table_ref.shape[2]
+    for head in range(distance_ref.shape[0]):
+        row = jnp.broadcast_to(distance_ref[head : head + 1, :], (128, width))
+        table_ref[head] = pltpu.roll(row, width - 127, 1, stride=1, stride_axis=0)
+
+
+def unskew_kernel(band_ref, total_ref):
+    width = band_ref.shape[2]
+    amount = 127 - lax.broadcasted_iota(jnp.int32, (128, width), 0)
+    for head in range(band_ref.shape[0]):
+        rows = band_ref[head]
+        for bit in range(7):
+            rows = jnp.where(((amount >> bit) & 1) == 1, pltpu.roll(rows, 1 << bit, 1), rows)
+        total_ref[head : head + 1, :] = jnp.sum(rows, 0, keepdims=True)
+
+
+def whole():
+    return pl.BlockSpec(memory_space=pltpu.VMEM)
+
+
+def bias_of(distance_bias, length):
+    padded = jnp.pad(distance_bias.T, ((0, 0), (0, 1)))
+    heads = padded.shape[0]
+    table = pl.pallas_call(
+        skew_kernel,
+        out_shape=jax.ShapeDtypeStruct((heads, 128, 2 * length), jnp.float32),
+        in_specs=[whole()],
+        out_specs=whole(),
+    )(padded)
+    starts = [length - 128 - 128 * block for block in range(length // 128)]
+    blocks = [table[:, :, start : start + length] for start in starts]
+    return jnp.concatenate(blocks, 1)
+
+
 def unskew_sum(score_total):
-    head_count, length = (score_total.shape[0], score_total.shape[1])
-    padded = jnp.pad(score_total, ((0, 0), (0, 0), (length - 1, 0)))
-    flat = jnp.pad(padded.reshape(head_count, length * (2 * length - 1)), ((0, 0), (0, length)))
-    return jnp.sum(flat.reshape(head_count, length, 2 * length), 1)[:, : 2 * length - 1]
+    heads, length = (score_total.shape[0], score_total.shape[1])
+    band = jnp.zeros((heads, 128, 2 * length), jnp.float32)
+    for block in range(length // 128):
+        start = length - 128 - 128 * block
+        rows = score_total[:, 128 * block : 128 * block + 128]
+        band = band + jnp.pad(rows, ((0, 0), (0, 0), (start, length - start)))
+    total = pl.pallas_call(
+        unskew_kernel,
+        out_shape=jax.ShapeDtypeStruct((heads, 2 * length), jnp.float32),
+        in_specs=[whole()],
+        out_specs=whole(),
+    )(band)
+    return total[:, : 2 * length - 1]
 
 
 def score_block(queries, keys, bias, allowed):
@@ -446,14 +492,13 @@
     weights = (norms[0], attn_in[0], attn_out[0], cross_pair[0], ffn_in[0], ffn_out[0])
     row_index = lax.broadcasted_iota(jnp.int32, (length, length), 0)
     col_index = lax.broadcasted_iota(jnp.int32, (length, length), 1)
-    offsets = col_index - row_index + length - 1
     one_hot = (
         bucket_of[0][:, None] == lax.broadcasted_iota(jnp.int32, (1, bucket_count), 1)
     ).astype(jnp.float32)
     distance_bias = jnp.dot(
         one_hot, rel_table[0], precision=highest, preferred_element_type=jnp.float32
     )
-    self_bias = distance_bias.T[:, offsets]
+    self_bias = bias_of(distance_bias, length)
     own_lengths = lax.dynamic_index_in_dim(lengths, section_index, 0, keepdims=False)
     positions = lax.axis_index("tensor") * quarter + lax.broadcasted_iota(
         jnp.int32, (1, quarter, 1), 1

time: 6260 us -> 1790 us (0.29); the launches traced: 6160 us -> 1780 us
  local copies, waits for them, and re-layouts: 4800 us -> 171 us
  waiting for transfers between devices: 770 us -> 1030 us
    gather x2 -> x0, local copies, waits for them, and re-layouts: 4070 us -> none  [body(): self_bias = distance_bias.T[:, offsets]]
    unnamed x385 -> x372, local copies, waits for them, and re-layouts: 582 us -> 47.2 us
    reduce_scatter x9, waiting for transfers between devices: 183 us -> 299 us  [sum_grads(): return lax.psum_scatter(block, 'tensor', scatter_dimension=1, tiled=True)]
    psum x1, waiting for transfers between devices: 0.01 us -> 98.1 us  [body(): lax.psum(totals[2].astype(jnp.bfloat16), 'dp').astype(jnp.float32)[None]]
  transfers between devices with their start and end apart: 41 -> 41, of which waited for: 26 -> 31; matrix products, arithmetic and copies ran while one was open for 82% -> 21% of each run, Pallas kernels for 0% -> 1%
where the time goes in v1:
time: 1790 us; the launch traced here: 1780 us
  waiting for transfers between devices  1030 us (58%)
  matrix products  281 us (16%)
  local copies, waits for them, and re-layouts  171 us (10%)
  other arithmetic  141 us (8%)
  blocking collectives  72.6 us (4%)
  starting transfers between devices  45.4 us (3%)
  between operations  20.3 us (1%)
    reduce_scatter x9, waiting for transfers between devices, sum_rows(): return lax.psum_scatter(block, 'tensor', scatter_dimension=1, tiled=True)  376 us
    reduce_scatter x9, waiting for transfers between devices, sum_grads(): return lax.psum_scatter(block, 'tensor', scatter_dimension=1, tiled=True)  299 us
    ppermute x4, waiting for transfers between devices, passed_along(): lax.ppermute(value, axis, [(source, source + steps) for source in range(i...  141 us
    psum x1, waiting for transfers between devices, body(): lax.psum(totals[2].astype(jnp.bfloat16), 'dp').astype(jnp.float32)[None]  98.1 us
    all_gather x9, waiting for transfers between devices, pick_entries(): return lax.all_gather(block, 'tensor', axis=1, tiled=True)  76.9 us
    psum x1, blocking collectives, body(): lax.psum((totals[1], squares, valid_rows), ('dp', 'tensor'))  60.3 us
    dot_general x6, matrix products, score_block(): jnp.einsum('hid,hjd->hij', queries, keys, preferred_element_type=jnp.floa...  48.4 us
    unnamed x372, local copies, waits for them, and re-layouts  47.2 us
  transfers between devices with their start and end apart: 41, of which 31 were waited for; matrix products, arithmetic and copies ran while one was open for 21% of the time, Pallas kernels for 1%

profile of v1, /device:TPU:0, one launch (start us, length us, event | category | flops | bytes accessed | tf_op | source)
XLA Modules:
  0.0 1781.6 jit_solution(13150722289957379604)
XLA Ops:
  40.8 6.4 fusion.655
  62.6 6.5 fusion.656
  83.1 6.8 fusion.657
  98.5 22.3 %reduce-scatter.31.cloned.1.call-done = f32[1,256,768]{2,1,0:T(8,128)} async-done(((f32[1,1024,768]{2,1,0:T(8,128)}), f32[1,256,768]{2,1,0:T(8,128)}) %reduce-scatter.31.cloned.1.call-update) | async-done | bytes 786448 | tf_op jit(solution)/shard_map/reduce_scatter | solution.py:157
  120.7 40.5 %reduce-scatter.25.cloned.1.call-done = f32[1,256,768]{2,1,0:T(8,128)} async-done(((f32[1,1024,768]{2,1,0:T(8,128)}), f32[1,256,768]{2,1,0:T(8,128)}) %reduce-scatter.25.cloned.1.call-update) | async-done | bytes 786448 | tf_op jit(solution)/shard_map/reduce_scatter | solution.py:157
  161.2 40.4 %reduce-scatter.19.cloned.1.call-done = f32[1,256,768]{2,1,0:T(8,128)} async-done(((f32[1,1024,768]{2,1,0:T(8,128)}), f32[1,256,768]{2,1,0:T(8,128)}) %reduce-scatter.19.cloned.1.call-update) | async-done | bytes 786448 | tf_op jit(solution)/shard_map/reduce_scatter | solution.py:157
  206.8 18.9 %all-gather.21.cloned.1.call-done = bf16[1,1024,768]{2,1,0:T(8,128)(2,1)} async-done(((bf16[1,256,768]{2,1,0:T(8,128)(2,1)}), bf16[1,1024,768]{2,1,0:T(8,128)(2,1)}) %all-gather.21.cloned.1.call-update) | async-done | bytes 1572880 | tf_op jit(solution)/shard_map/all_gather | solution.py:153
  229.3 15.9 conditional.12
  229.7 9.4 fusion.2
  246.8 55.9 %reduce-scatter.21.cloned.1.call-done = f32[1,256,768]{2,1,0:T(8,128)} async-done(((f32[1,1024,768]{2,1,0:T(8,128)}), f32[1,256,768]{2,1,0:T(8,128)}) %reduce-scatter.21.cloned.1.call-update) | async-done | bytes 786448 | tf_op jit(solution)/shard_map/reduce_scatter | solution.py:157
  306.6 19.2 %all-gather.23.cloned.1.call-done = bf16[1,1024,768]{2,1,0:T(8,128)(2,1)} async-done(((bf16[1,256,768]{2,1,0:T(8,128)(2,1)}), bf16[1,1024,768]{2,1,0:T(8,128)(2,1)}) %all-gather.23.cloned.1.call-update) | async-done | bytes 1572880 | tf_op jit(solution)/shard_map/all_gather | solution.py:153
  325.8 5.3 conditional.13
  331.1 15.0 collective-permute-start
  347.4 15.3 collective-permute-done
  365.0 15.7 conditional.14
  365.0 9.4 fusion.55
  381.5 60.0 %reduce-scatter.27.cloned.1.call-done = f32[1,256,768]{2,1,0:T(8,128)} async-done(((f32[1,1024,768]{2,1,0:T(8,128)}), f32[1,256,768]{2,1,0:T(8,128)}) %reduce-scatter.27.cloned.1.call-update) | async-done | bytes 786448 | tf_op jit(solution)/shard_map/reduce_scatter | solution.py:157
  445.4 19.0 %all-gather.29.cloned.1.call-done = bf16[1,1024,768]{2,1,0:T(8,128)(2,1)} async-done(((bf16[1,256,768]{2,1,0:T(8,128)(2,1)}), bf16[1,1024,768]{2,1,0:T(8,128)(2,1)}) %all-gather.29.cloned.1.call-update) | async-done | bytes 1572880 | tf_op jit(solution)/shard_map/all_gather | solution.py:153
  464.4 5.6 conditional.15
  470.1 15.1 collective-permute-start.1
  486.3 15.4 collective-permute-done.1
  504.0 15.7 conditional.16
  504.0 9.4 fusion.104
  520.5 59.9 %reduce-scatter.33.cloned.1.call-done = f32[1,256,768]{2,1,0:T(8,128)} async-done(((f32[1,1024,768]{2,1,0:T(8,128)}), f32[1,256,768]{2,1,0:T(8,128)}) %reduce-scatter.33.cloned.1.call-update) | async-done | bytes 786448 | tf_op jit(solution)/shard_map/reduce_scatter | solution.py:157
  588.2 15.2 all-gather.35.cloned.1.call-done
  629.5 9.3 conditional.18
  642.1 22.8 %reduce-scatter.23.cloned.1.call-done = f32[1,256,768]{2,1,0:T(8,128)} async-done(((f32[1,1024,768]{2,1,0:T(8,128)}), f32[1,256,768]{2,1,0:T(8,128)}) %reduce-scatter.23.cloned.1.call-update) | async-done | bytes 786448 | tf_op jit(solution)/shard_map/reduce_scatter | solution.py:157
  668.0 37.4 %reduce-scatter.29.cloned.1.call-done = f32[1,256,768]{2,1,0:T(8,128)} async-done(((f32[1,1024,768]{2,1,0:T(8,128)}), f32[1,256,768]{2,1,0:T(8,128)}) %reduce-scatter.29.cloned.1.call-update) | async-done | bytes 786448 | tf_op jit(solution)/shard_map/reduce_scatter | solution.py:157
  708.8 37.2 %reduce-scatter.35.cloned.1.call-done = f32[1,256,768]{2,1,0:T(8,128)} async-done(((f32[1,1024,768]{2,1,0:T(8,128)}), f32[1,256,768]{2,1,0:T(8,128)}) %reduce-scatter.35.cloned.1.call-update) | async-done | bytes 786448 | tf_op jit(solution)/shard_map/reduce_scatter | solution.py:157
  748.5 38.0 %reduce-scatter.37.cloned.1.call-done = f32[1,256,768]{2,1,0:T(8,128)} async-done(((f32[1,1024,768]{2,1,0:T(8,128)}), f32[1,256,768]{2,1,0:T(8,128)}) %reduce-scatter.37.cloned.1.call-update) | async-done | bytes 786448 | tf_op jit(solution)/shard_map/reduce_scatter | solution.py:165
  820.2 19.3 %conditional.19 = (f32[2,768,192]{1,2,0:T(8,128)}, f32[768,768]{1,0:T(8,128)}, f32[768,768]{1,0:T(8,128)}, bf16[2,1,1024,192]{2,3,1,0:T(8,128)(2,1)S(1)}, f32[1024,768]{1,0:T(8,128)}) conditional(s32[]{:T(128)} %convert_element_type.760, (bf16[1,1024,768]{2,1,0:T(8,128)(2,1)S(1)}, bf16[768,768]{1,0:T(8,128)(2,1)}, f32[1,1024,768]{2,1,0:T(8,128)}, ...), branch_computations={%region_56.57_spmd, %region_57.59_spmd} | conditional | flops 4839702528 | bytes 193029920 | solution.py:405
  841.7 54.7 %collective-permute-done.2 = bf16[2,1,1024,192]{2,3,0,1:T(8,128)(2,1)S(1)} collective-permute-done((bf16[2,1,1024,192]{2,3,0,1:T(8,128)(2,1)}, bf16[2,1,1024,192]{2,3,0,1:T(8,128)(2,1)S(1)}, u32[]{:S(2)}, u32[]{:S(2)}) %collective-permute-start.2) | collective-permute-done | bytes 786464 | tf_op jit(solution)/shard_map/ppermute | solution.py:19
  896.4 9.3 conditional.20
  905.8 42.0 %reduce-scatter.43.cloned.1.call-done = f32[1,256,768]{2,1,0:T(8,128)} async-done(((f32[1,1024,768]{2,1,0:T(8,128)}), f32[1,256,768]{2,1,0:T(8,128)}) %reduce-scatter.43.cloned.1.call-update) | async-done | bytes 786448 | tf_op jit(solution)/shard_map/reduce_scatter | solution.py:165
  953.5 19.0 %all-gather.45.cloned.1.call-done = bf16[1,1024,768]{2,1,0:T(8,128)(2,1)} async-done(((bf16[1,256,768]{2,1,0:T(8,128)(2,1)}), bf16[1,1024,768]{2,1,0:T(8,128)(2,1)}) %all-gather.45.cloned.1.call-update) | async-done | bytes 1572880 | tf_op jit(solution)/shard_map/all_gather | solution.py:161
  976.0 19.3 %conditional.21 = (f32[2,768,192]{1,2,0:T(8,128)}, f32[768,768]{1,0:T(8,128)}, f32[768,768]{1,0:T(8,128)}, bf16[2,1,1024,192]{2,3,1,0:T(8,128)(2,1)S(1)}, f32[1024,768]{1,0:T(8,128)}) conditional(s32[]{:T(128)} %convert_element_type.760, (bf16[1,1024,768]{2,1,0:T(8,128)(2,1)S(1)}, bf16[768,768]{1,0:T(8,128)(2,1)}, f32[1,1024,768]{2,1,0:T(8,128)}, ...), branch_computations={%region_71.72_spmd, %region_72.74_spmd} | conditional | flops 4839702528 | bytes 193029920 | solution.py:405
  997.5 55.1 %collective-permute-done.3 = bf16[2,1,1024,192]{2,3,0,1:T(8,128)(2,1)S(1)} collective-permute-done((bf16[2,1,1024,192]{2,3,0,1:T(8,128)(2,1)}, bf16[2,1,1024,192]{2,3,0,1:T(8,128)(2,1)S(1)}, u32[]{:S(2)}, u32[]{:S(2)}) %collective-permute-start.3) | collective-permute-done | bytes 786464 | tf_op jit(solution)/shard_map/ppermute | solution.py:19
  1052.6 9.3 conditional.22
  1062.0 41.9 %reduce-scatter.49.cloned.1.call-done = f32[1,256,768]{2,1,0:T(8,128)} async-done(((f32[1,1024,768]{2,1,0:T(8,128)}), f32[1,256,768]{2,1,0:T(8,128)}) %reduce-scatter.49.cloned.1.call-update) | async-done | bytes 786448 | tf_op jit(solution)/shard_map/reduce_scatter | solution.py:165
  1110.4 18.3 %all-gather.51.cloned.1.call-done = bf16[1,1024,768]{2,1,0:T(8,128)(2,1)} async-done(((bf16[1,256,768]{2,1,0:T(8,128)(2,1)}), bf16[1,1024,768]{2,1,0:T(8,128)(2,1)}) %all-gather.51.cloned.1.call-update) | async-done | bytes 1572880 | tf_op jit(solution)/shard_map/all_gather | solution.py:161
  1132.1 18.1 %conditional.23 = (f32[2,768,192]{1,2,0:T(8,128)}, f32[768,768]{1,0:T(8,128)S(1)}, f32[768,768]{1,0:T(8,128)}, f32[1024,768]{1,0:T(8,128)}) conditional(s32[]{:T(128)} %convert_element_type.760, (bf16[1,1024,768]{2,1,0:T(8,128)(2,1)S(1)}, bf16[768,768]{1,0:T(8,128)(2,1)}, f32[1,1024,768]{2,1,0:T(8,128)}, bf16[768,768]{1,0:T(8,128)(2,1)}, ...), branch_computations={%region_86.87_spmd, %region_87.89_spmd} | conditional | flops 4839702528 | bytes 114119856 | solution.py:405
  1150.3 10.2 all-gather.47.cloned.1.call-start
  1185.2 24.7 %reduce-scatter.45.cloned.1.call-done = f32[1,256,768]{2,1,0:T(8,128)} async-done(((f32[1,1024,768]{2,1,0:T(8,128)}), f32[1,256,768]{2,1,0:T(8,128)}) %reduce-scatter.45.cloned.1.call-update) | async-done | bytes 786448 | tf_op jit(solution)/shard_map/reduce_scatter | solution.py:165
  1209.9 40.3 %reduce-scatter.51.cloned.1.call-done = f32[1,256,768]{2,1,0:T(8,128)} async-done(((f32[1,1024,768]{2,1,0:T(8,128)}), f32[1,256,768]{2,1,0:T(8,128)}) %reduce-scatter.51.cloned.1.call-update) | async-done | bytes 786448 | tf_op jit(solution)/shard_map/reduce_scatter | solution.py:165
  1255.4 9.6 subtract_exponential_fusion.6
  1265.0 9.6 subtract_exponential_fusion.8
  1276.0 9.5 subtract_exponential_fusion.7
  1298.1 7.3 fusion.468
  1312.5 5.9 fusion.440
  1320.5 6.0 fusion.437
  1326.5 11.3 multiply_reduce_fusion.5
  1337.8 7.4 multiply_reduce_fusion.4
  1347.4 5.8 fusion.443
  1353.2 11.1 multiply_reduce_fusion.3
  1364.3 35.5 %select_add_fusion = (f32[3,1024,1024]{2,1,0:T(8,128)}, bf16[3,1024,1024]{2,1,0:T(8,128)(2,1)}, bf16[3,1024,1024]{2,1,0:T(8,128)(2,1)}, bf16[3,1024,1024]{2,1,0:T(8,128)(2,1)}) fusion(pred[]{:T(512)S(6)} %and.79, pred[]{:T(512)S(6)} %and.77, pred[]{:T(512)S(6)} %and.75, f32[3,1024,1024]{2,1,0:T(8,128)} %subtract_exponential_fusion.8, ...), kind=kLoop, calls=%fused_computation.454 | loop fusion | flops 44040192 | bytes 106991616 | tf_op jit(solution)/shard_map/add | solution.py:571
  1448.9 8.7 fusion.654
  1457.6 5.2 pad_add_fusion.band_ref
  1462.8 9.4 shard_map.187
  1474.1 12.4 psum.63
  1487.1 98.1 %all-reduce.13.cloned.1.call-done = (bf16[1,3,768,192]{2,3,1,0:T(8,128)(2,1)}, bf16[1,192,768]{2,1,0:T(8,128)(2,1)}, bf16[1,2,768,192]{2,3,1,0:T(8,128)(2,1)}, b...) async-done(((bf16[1,3,768,192]{2,3,1,0:T(8,128)(2,1)}, bf16[1,192,768]{2,1,0:T(8,128)(2,1)}, bf16[1,2,768,192]{2,3,1,0:T(8,128)(2,1)}, bf16[1,768,768]{2,1,0:T(8,128)(2,1)}, ...) | async-done | bytes 4128784 | tf_op jit(solution)/shard_map/psum | solution.py:594
  1594.0 30.7 %reduce-scatter.41.cloned.1.call-done = f32[1,256,768]{2,1,0:T(8,128)} async-done(((f32[1,1024,768]{2,1,0:T(8,128)}), f32[1,256,768]{2,1,0:T(8,128)}) %reduce-scatter.41.cloned.1.call-update) | async-done | bytes 786448 | tf_op jit(solution)/shard_map/reduce_scatter | solution.py:165
  1624.6 40.5 %reduce-scatter.53.cloned.1.call-done = f32[1,256,768]{2,1,0:T(8,128)} async-done(((f32[1,1024,768]{2,1,0:T(8,128)}), f32[1,256,768]{2,1,0:T(8,128)}) %reduce-scatter.53.cloned.1.call-update) | async-done | bytes 786448 | tf_op jit(solution)/shard_map/reduce_scatter | solution.py:165
  1665.2 40.4 %reduce-scatter.47.cloned.1.call-done = f32[1,256,768]{2,1,0:T(8,128)} async-done(((f32[1,1024,768]{2,1,0:T(8,128)}), f32[1,256,768]{2,1,0:T(8,128)}) %reduce-scatter.47.cloned.1.call-update) | async-done | bytes 786448 | tf_op jit(solution)/shard_map/reduce_scatter | solution.py:165
  1711.6 60.3 %all-reduce.9 = (f32[1,3,2,768]{3,2,1,0:T(2,128)}, f32[]{:T(128)}, f32[]{:T(128)}) all-reduce(f32[1,3,2,768]{3,2,1,0:T(2,128)S(1)} %fusion.616, f32[]{:T(128)} %multiply_reduce_fusion.6, f32[]{:T(128)} %fusion.622), channel_id=1, replica_groups=mesh['section'=2,'dp'=4,'tensor'=4] {'dp','tensor'}, use_global_device_ids=true, to_apply=%region_115.116 | all-reduce | flops 4610 | bytes 36880 | tf_op jit(solution)/shard_map/psum | solution.py:579
  (772 shorter events, 433.8 us)
Async XLA Ops:
  7.2 29.6 %copy-start = (bf16[1,3,768,192]{2,3,1,0:T(8,128)(2,1)S(1)}, bf16[1,3,768,192]{2,3,1,0:T(8,128)(2,1)}, u32[]{:S(2)}) copy-start(bf16[1,3,768,192]{2,3,1,0:T(8,128)(2,1)} %param.40) | copy-start | bytes 2654212
  7.2 29.5 %all-gather.31.cloned.1.call-start = ((), (), s32[]{:S(2)}) async-start(), calls=%async_computation.30 | async-start | bytes 1966080 | tf_op jit(solution)/shard_map/all_gather | solution.py:153
  12.1 192.2 %copy-start.122 = (f32[768]{0:T(1024)}, f32[768]{0:T(1024)S(1)}, u32[]{:S(2)}) copy-start(f32[768]{0:T(1024)S(1)} %get-tuple-element.1408) | copy-start | bytes 9220
  14.2 44.4 %all-gather.25.cloned.1.call-start = ((), (), s32[]{:S(2)}) async-start(), calls=%async_computation.24 | async-start | bytes 1966080 | tf_op jit(solution)/shard_map/all_gather | solution.py:153
  14.9 65.4 %all-gather.19.cloned.1.call-start = ((), (), s32[]{:S(2)}) async-start(), calls=%async_computation.18 | async-start | bytes 1966080 | tf_op jit(solution)/shard_map/all_gather | solution.py:153
  15.7 105.0 %reduce-scatter.31.cloned.1.call-start = ((), (), s32[]{:S(2)}) async-start(), calls=%async_computation.31 | async-start | bytes 3932160 | tf_op jit(solution)/shard_map/reduce_scatter | solution.py:157
  56.5 104.8 %reduce-scatter.25.cloned.1.call-start = ((), (), s32[]{:S(2)}) async-start(), calls=%async_computation.25 | async-start | bytes 3932160 | tf_op jit(solution)/shard_map/reduce_scatter | solution.py:157
  78.2 123.4 %reduce-scatter.19.cloned.1.call-start = ((), (), s32[]{:S(2)}) async-start(), calls=%async_computation.19 | async-start | bytes 3932160 | tf_op jit(solution)/shard_map/reduce_scatter | solution.py:157
  98.4 127.3 %all-gather.21.cloned.1.call-start = ((), (), s32[]{:S(2)}) async-start(), calls=%async_computation.20 | async-start | bytes 1966080 | tf_op jit(solution)/shard_map/all_gather | solution.py:153
  203.5 99.2 %copy-start.15 = (f32[1,256,768]{2,1,0:T(8,128)}, f32[1,256,768]{2,1,0:T(8,128)S(1)}, u32[]{:S(2)}) copy-start(f32[1,256,768]{2,1,0:T(8,128)S(1)} %get-tuple-element.1509) | copy-start | bytes 2359300
  205.9 96.8 %reduce-scatter.21.cloned.1.call-start = ((), (), s32[]{:S(2)}) async-start(), calls=%async_computation.21 | async-start | bytes 3932160 | tf_op jit(solution)/shard_map/reduce_scatter | solution.py:157
  245.8 59.1 %copy-start.103 = (f32[768]{0:T(1024)S(1)}, f32[768]{0:T(1024)}, u32[]{:S(2)}) copy-start(f32[768]{0:T(1024)} %get-tuple-element.1405) | copy-start | bytes 9220
  245.8 59.1 %copy-start.113 = (f32[768]{0:T(1024)S(1)}, f32[768]{0:T(1024)}, u32[]{:S(2)}) copy-start(f32[768]{0:T(1024)} %get-tuple-element.1406) | copy-start | bytes 9220
  245.9 79.9 %all-gather.23.cloned.1.call-start = ((), (), s32[]{:S(2)}) async-start(), calls=%async_computation.22 | async-start | bytes 1966080 | tf_op jit(solution)/shard_map/all_gather | solution.py:153
  246.8 79.0 %copy-start.183 = (f32[256]{0:T(256)}, f32[256]{0:T(256)S(1)}, u32[]{:S(2)}) copy-start(f32[256]{0:T(256)S(1)} %compare_convert_fusion.6) | copy-start | bytes 3076
  304.0 21.7 %copy-start.134 = (f32[256]{0:T(256)}, f32[256]{0:T(256)S(1)}, u32[]{:S(2)}) copy-start(f32[256]{0:T(256)S(1)} %broadcast_multiply_fusion.24) | copy-start | bytes 3076
  305.9 41.5 %all-gather.27.cloned.1.call-start = ((), (), s32[]{:S(2)}) async-start(), calls=%async_computation.26 | async-start | bytes 1966080 | tf_op jit(solution)/shard_map/all_gather | solution.py:153
  306.5 134.9 %reduce-scatter.27.cloned.1.call-start = ((), (), s32[]{:S(2)}) async-start(), calls=%async_computation.27 | async-start | bytes 3932160 | tf_op jit(solution)/shard_map/reduce_scatter | solution.py:157
  331.1 31.6 %collective-permute-start = (bf16[2,1,1024,192]{2,3,0,1:T(8,128)(2,1)}, bf16[2,1,1024,192]{2,3,0,1:T(8,128)(2,1)}, u32[]{:S(2)}, u32[]{:S(2)}) collective-permute-start(bf16[2,1,1024,192]{2,3,0,1:T(8,128)(2,1)} %get-tuple-element.1348), channel_id=1, source_target_pairs={{0,16},{1,17},{2,18},{3,19},{4,20},{5,21},{6,22},{7,23},{8,24},{9,... | collective-permute-start | bytes 2359304 | tf_op jit(solution)/shard_map/ppermute | solution.py:19
  380.7 62.3 %copy-start.132 = (f32[1,1,3,1024]{3,2,1,0:T(4,128)}, f32[1,1,3,1024]{3,2,1,0:T(4,128)S(1)}, u32[]{:S(2)}) copy-start(f32[1,1,3,1024]{3,2,1,0:T(4,128)S(1)} %get-tuple-element.1057) | copy-start | bytes 36868
  380.7 60.7 %copy-start.13 = (f32[1,256,768]{2,1,0:T(8,128)S(1)}, f32[1,256,768]{2,1,0:T(8,128)}, u32[]{:S(2)}) copy-start(f32[1,256,768]{2,1,0:T(8,128)} %copy-done.12) | copy-start | bytes 2359300
  380.8 83.7 %all-gather.29.cloned.1.call-start = ((), (), s32[]{:S(2)}) async-start(), calls=%async_computation.28 | async-start | bytes 1966080 | tf_op jit(solution)/shard_map/all_gather | solution.py:153
  381.4 83.0 %copy-start.185 = (f32[256]{0:T(256)}, f32[256]{0:T(256)S(1)}, u32[]{:S(2)}) copy-start(f32[256]{0:T(256)S(1)} %compare_convert_fusion.5) | copy-start | bytes 3076
  444.6 41.7 %all-gather.33.cloned.1.call-start = ((), (), s32[]{:S(2)}) async-start(), calls=%async_computation.32 | async-start | bytes 1966080 | tf_op jit(solution)/shard_map/all_gather | solution.py:153
  445.4 135.0 %reduce-scatter.33.cloned.1.call-start = ((), (), s32[]{:S(2)}) async-start(), calls=%async_computation.33 | async-start | bytes 3932160 | tf_op jit(solution)/shard_map/reduce_scatter | solution.py:157
  470.1 31.7 %collective-permute-start.1 = (bf16[2,1,1024,192]{2,3,0,1:T(8,128)(2,1)}, bf16[2,1,1024,192]{2,3,0,1:T(8,128)(2,1)}, u32[]{:S(2)}, u32[]{:S(2)}) collective-permute-start(bf16[2,1,1024,192]{2,3,0,1:T(8,128)(2,1)} %get-tuple-element.1350), channel_id=1, source_target_pairs={{0,16},{1,17},{2,18},{3,19},{4,20},{5,21},{6,22},{7,23},{8,24},{9,... | collective-permute-start | bytes 2359304 | tf_op jit(solution)/shard_map/ppermute | solution.py:19
  519.7 60.7 %copy-start.10 = (f32[1,256,768]{2,1,0:T(8,128)S(1)}, f32[1,256,768]{2,1,0:T(8,128)}, u32[]{:S(2)}) copy-start(f32[1,256,768]{2,1,0:T(8,128)} %copy-done.9) | copy-start | bytes 2359300
  519.7 65.9 %copy-start.17 = (bf16[1,2,1,256,768]{4,3,2,1,0:T(8,128)(2,1)S(1)}, bf16[1,2,1,256,768]{4,3,2,1,0:T(8,128)(2,1)}, u32[]{:S(2)}) copy-start(bf16[1,2,1,256,768]{4,3,2,1,0:T(8,128)(2,1)} %param.45) | copy-start | bytes 2359300
  519.7 83.7 %all-gather.35.cloned.1.call-start = ((), (), s32[]{:S(2)}) async-start(), calls=%async_computation.34 | async-start | bytes 1966080 | tf_op jit(solution)/shard_map/all_gather | solution.py:153
  583.6 45.9 %all-gather.37.cloned.1.call-start = ((), (), s32[]{:S(2)}) async-start(), calls=%async_computation.36 | async-start | bytes 1966080 | tf_op jit(solution)/shard_map/all_gather | solution.py:161
  586.9 78.0 %reduce-scatter.23.cloned.1.call-start = ((), (), s32[]{:S(2)}) async-start(), calls=%async_computation.23 | async-start | bytes 3932160 | tf_op jit(solution)/shard_map/reduce_scatter | solution.py:157
  587.5 117.9 %reduce-scatter.29.cloned.1.call-start = ((), (), s32[]{:S(2)}) async-start(), calls=%async_computation.29 | async-start | bytes 3932160 | tf_op jit(solution)/shard_map/reduce_scatter | solution.py:157
  588.1 157.8 %reduce-scatter.35.cloned.1.call-start = ((), (), s32[]{:S(2)}) async-start(), calls=%async_computation.35 | async-start | bytes 3932160 | tf_op jit(solution)/shard_map/reduce_scatter | solution.py:157
  605.7 180.7 %reduce-scatter.37.cloned.1.call-start = ((), (), s32[]{:S(2)}) async-start(), calls=%async_computation.37 | async-start | bytes 3932160 | tf_op jit(solution)/shard_map/reduce_scatter | solution.py:165
  638.8 177.9 %all-gather.39.cloned.1.call-start = ((), (), s32[]{:S(2)}) async-start(), calls=%async_computation.38 | async-start | bytes 1966080 | tf_op jit(solution)/shard_map/all_gather | solution.py:161
  639.5 25.6 %copy-start.184 = (f32[256]{0:T(256)S(1)}, f32[256]{0:T(256)}, u32[]{:S(2)}) copy-start(f32[256]{0:T(256)} %copy-done.183) | copy-start | bytes 3076
  641.1 26.9 %copy-start.157 = (f32[256]{0:T(256)S(1)}, f32[256]{0:T(256)}, u32[]{:S(2)}) copy-start(f32[256]{0:T(256)} %copy-done.156) | copy-start | bytes 3076
  641.1 64.4 %copy-start.143 = (f32[256]{0:T(256)S(1)}, f32[256]{0:T(256)}, u32[]{:S(2)}) copy-start(f32[256]{0:T(256)} %copy-done.142) | copy-start | bytes 3076
  641.1 64.4 %copy-start.186 = (f32[256]{0:T(256)S(1)}, f32[256]{0:T(256)}, u32[]{:S(2)}) copy-start(f32[256]{0:T(256)} %copy-done.185) | copy-start | bytes 3076
  668.0 78.0 %copy-start.20 = (f32[1,256,768]{2,1,0:T(8,128)S(1)}, f32[1,256,768]{2,1,0:T(8,128)}, u32[]{:S(2)}) copy-start(f32[1,256,768]{2,1,0:T(8,128)} %copy-done.19) | copy-start | bytes 2359300
  791.4 50.4 %all-gather.43.cloned.1.call-start = ((), (), s32[]{:S(2)}) async-start(), calls=%async_computation.42 | async-start | bytes 1966080 | tf_op jit(solution)/shard_map/all_gather | solution.py:161
  792.1 155.7 %reduce-scatter.43.cloned.1.call-start = ((), (), s32[]{:S(2)}) async-start(), calls=%async_computation.43 | async-start | bytes 3932160 | tf_op jit(solution)/shard_map/reduce_scatter | solution.py:165
  840.4 56.0 %collective-permute-start.2 = (bf16[2,1,1024,192]{2,3,0,1:T(8,128)(2,1)}, bf16[2,1,1024,192]{2,3,0,1:T(8,128)(2,1)S(1)}, u32[]{:S(2)}, u32[]{:S(2)}) collective-permute-start(bf16[2,1,1024,192]{2,3,0,1:T(8,128)(2,1)} %bitcast.1524), channel_id=1, source_target_pairs={{16,0},{17,1},{18,2},{19,3},{20,4},{21,5},{22,6},{23,7},{24,8},{25... | collective-permute-start | bytes 2359304 | tf_op jit(solution)/shard_map/ppermute | solution.py:19
  905.7 42.1 %copy-start.141 = (f32[256]{0:T(256)S(1)}, f32[256]{0:T(256)}, u32[]{:S(2)}) copy-start(f32[256]{0:T(256)} %copy-done.140) | copy-start | bytes 3076
  905.8 66.8 %all-gather.45.cloned.1.call-start = ((), (), s32[]{:S(2)}) async-start(), calls=%async_computation.44 | async-start | bytes 1966080 | tf_op jit(solution)/shard_map/all_gather | solution.py:161
  952.7 44.7 %all-gather.49.cloned.1.call-start = ((), (), s32[]{:S(2)}) async-start(), calls=%async_computation.48 | async-start | bytes 1966080 | tf_op jit(solution)/shard_map/all_gather | solution.py:161
  953.5 150.5 %reduce-scatter.49.cloned.1.call-start = ((), (), s32[]{:S(2)}) async-start(), calls=%async_computation.49 | async-start | bytes 3932160 | tf_op jit(solution)/shard_map/reduce_scatter | solution.py:165
  996.2 56.4 %collective-permute-start.3 = (bf16[2,1,1024,192]{2,3,0,1:T(8,128)(2,1)}, bf16[2,1,1024,192]{2,3,0,1:T(8,128)(2,1)S(1)}, u32[]{:S(2)}, u32[]{:S(2)}) collective-permute-start(bf16[2,1,1024,192]{2,3,0,1:T(8,128)(2,1)} %bitcast.1525), channel_id=1, source_target_pairs={{16,0},{17,1},{18,2},{19,3},{20,4},{21,5},{22,6},{23,7},{24,8},{25... | collective-permute-start | bytes 2359304 | tf_op jit(solution)/shard_map/ppermute | solution.py:19
  1061.9 42.0 %copy-start.139 = (f32[256]{0:T(256)S(1)}, f32[256]{0:T(256)}, u32[]{:S(2)}) copy-start(f32[256]{0:T(256)} %copy-done.138) | copy-start | bytes 3076
  1061.9 44.5 %copy-start.187 = (f32[1,1,256,1]{2,3,1,0:T(1,128)S(1)}, f32[1,1,256,1]{2,3,1,0:T(1,128)}, u32[]{:S(2)}) copy-start(f32[1,1,256,1]{2,3,1,0:T(1,128)} %get-tuple-element.1522) | copy-start | bytes 3076
  1062.0 66.8 %all-gather.51.cloned.1.call-start = ((), (), s32[]{:S(2)}) async-start(), calls=%async_computation.50 | async-start | bytes 1966080 | tf_op jit(solution)/shard_map/all_gather | solution.py:161
  1108.9 76.3 %reduce-scatter.39.cloned.1.call-start = ((), (), s32[]{:S(2)}) async-start(), calls=%async_computation.39 | async-start | bytes 3932160 | tf_op jit(solution)/shard_map/reduce_scatter | solution.py:165
  1109.6 100.3 %reduce-scatter.45.cloned.1.call-start = ((), (), s32[]{:S(2)}) async-start(), calls=%async_computation.45 | async-start | bytes 3932160 | tf_op jit(solution)/shard_map/reduce_scatter | solution.py:165
  1110.4 139.9 %reduce-scatter.51.cloned.1.call-start = ((), (), s32[]{:S(2)}) async-start(), calls=%async_computation.51 | async-start | bytes 3932160 | tf_op jit(solution)/shard_map/reduce_scatter | solution.py:165
  1150.3 160.0 %all-gather.47.cloned.1.call-start = ((), (), s32[]{:S(2)}) async-start(), calls=%async_computation.46 | async-start | bytes 1966080 | tf_op jit(solution)/shard_map/all_gather | solution.py:161
  1182.4 67.9 %copy-start.123 = (f32[768]{0:T(1024)S(1)}, f32[768]{0:T(1024)}, u32[]{:S(2)}) copy-start(f32[768]{0:T(1024)} %copy-done.122) | copy-start | bytes 9220
  1255.3 63.1 %all-gather.41.cloned.1.call-start = ((), (), s32[]{:S(2)}) async-start(), calls=%async_computation.40 | async-start | bytes 1966080 | tf_op jit(solution)/shard_map/all_gather | solution.py:161
  1275.9 69.4 %all-gather.53.cloned.1.call-start = ((), (), s32[]{:S(2)}) async-start(), calls=%async_computation.52 | async-start | bytes 1966080 | tf_op jit(solution)/shard_map/all_gather | solution.py:161
  1309.9 275.3 %all-reduce.13.cloned.1.call-start = ((), (), s32[]{:S(2)}) async-start(), calls=%async_computation.54 | async-start | bytes 8257536 | tf_op jit(solution)/shard_map/psum | solution.py:594
  1430.3 194.4 %reduce-scatter.41.cloned.1.call-start = ((), (), s32[]{:S(2)}) async-start(), calls=%async_computation.41 | async-start | bytes 3932160 | tf_op jit(solution)/shard_map/reduce_scatter | solution.py:165
  1434.7 230.5 %reduce-scatter.53.cloned.1.call-start = ((), (), s32[]{:S(2)}) async-start(), calls=%async_computation.53 | async-start | bytes 3932160 | tf_op jit(solution)/shard_map/reduce_scatter | solution.py:165
  1438.7 266.8 %reduce-scatter.47.cloned.1.call-start = ((), (), s32[]{:S(2)}) async-start(), calls=%async_computation.47 | async-start | bytes 3932160 | tf_op jit(solution)/shard_map/reduce_scatter | solution.py:165
  1590.8 114.8 %copy-start.6 = (f32[3,1,256,768]{3,2,0,1:T(8,128)S(1)}, f32[3,1,256,768]{3,2,0,1:T(8,128)}, u32[]{:S(2)}) copy-start(f32[3,1,256,768]{3,2,0,1:T(8,128)} %copy-done.5) | copy-start | bytes 7077892
  1590.8 114.8 %copy-start.115 = (f32[768]{0:T(1024)S(1)}, f32[768]{0:T(1024)}, u32[]{:S(2)}) copy-start(f32[768]{0:T(1024)} %copy-done.114) | copy-start | bytes 9220
  (162 other events, 853.6 us)
Sparse Core Ops, SparseCore 0:
  14.3 22.3 all-gather.30
  38.8 19.6 all-gather.24
  60.7 19.6 all-gather.18
  82.8 37.9 reduce-scatter.30
  123.3 37.9 reduce-scatter.24
  163.6 37.9 reduce-scatter.18
  206.0 19.6 all-gather.20
  246.0 56.6 reduce-scatter.20
  306.0 19.6 all-gather.22
  327.7 19.6 all-gather.26
  380.9 60.5 reduce-scatter.26
  444.8 19.6 all-gather.28
  466.6 19.6 all-gather.32
  519.9 60.4 reduce-scatter.32
  583.7 19.6 all-gather.34
  604.8 19.6 all-gather.36
  626.9 37.9 reduce-scatter.22
  667.4 37.9 reduce-scatter.28
  708.0 37.9 reduce-scatter.34
  748.5 37.9 reduce-scatter.36
  791.5 19.6 all-gather.38
  812.7 19.6 all-gather.42
  905.9 41.8 reduce-scatter.42
  952.9 19.6 all-gather.44
  974.2 19.6 all-gather.48
  1062.1 41.8 reduce-scatter.48
  1109.0 19.6 all-gather.50
  1131.3 37.9 reduce-scatter.38
  1171.9 37.9 reduce-scatter.44
  1212.3 37.9 reduce-scatter.50
  1255.5 19.6 all-gather.46
  1277.4 19.6 all-gather.40
  1310.0 19.8 all-gather.52
  1430.4 154.8 all-reduce.12
  1587.8 36.8 reduce-scatter.40
  1627.2 37.9 reduce-scatter.52
  1667.6 37.9 reduce-scatter.46

commit v2 on v0

v2 whole, which is shorter than its diff:
```python
import functools
import math

import jax
import jax.numpy as jnp
from jax import lax
from jax.experimental import pallas as pl
from jax.experimental.pallas import tpu as pltpu
from jax.sharding import PartitionSpec as P

HEAD_DIM = 64
SCALE = HEAD_DIM ** (-0.5)
EPSILON = 1e-05
MASKED = -1000000000.0
HIGHEST = lax.Precision.HIGHEST
BF = jnp.bfloat16
F32 = jnp.float32
NN = (((1,), (0,)), ((), ()))
NT = (((1,), (1,)), ((), ()))
TN = (((0,), (0,)), ((), ()))
TILE = 256
BAND = 128
ENCODER, DECODER = 0, 1
ROLE, OWN_LEN, SOURCE_LEN, CORE, START = 0, 1, 2, 3, 4
VMEM_BYTES = 58 * 1024 * 1024


def mm(left, right, dims):
    return lax.dot_general(left, right, dims, preferred_element_type=F32)


def whole():
    return pl.BlockSpec(memory_space=pltpu.VMEM)


def scalars():
    return pl.BlockSpec(memory_space=pltpu.SMEM)


def shape(dims, dtype):
    return jax.ShapeDtypeStruct(dims, dtype)


def cost(flops, nbytes, exps=0):
    return pl.CostEstimate(flops=int(flops), bytes_accessed=int(nbytes), transcendentals=int(exps))


def params(**extra):
    return pltpu.CompilerParams(vmem_limit_bytes=VMEM_BYTES, **extra)


def norm_of(values, norm_ref):
    centred = values - jnp.mean(values, -1, keepdims=True)
    factor = lax.rsqrt(jnp.mean(centred * centred, -1, keepdims=True) + EPSILON)
    return centred * factor * norm_ref[0:1, :] + norm_ref[1:2, :]


def enter_kernel(info, mine, core_mine, far, core_far, norm_ref, rows_ref, normed_ref):
    quarter = mine.shape[0]
    for step, piece in enumerate((mine, core_mine, far, core_far)):
        start = pl.multiple_of(info[START + step], quarter)
        values = piece[...]
        rows_ref[pl.ds(start, quarter), :] = values
        normed_ref[pl.ds(start, quarter), :] = norm_of(values.astype(F32), norm_ref).astype(BF)


def enter(info, pieces, norm):
    quarter, width = pieces[0].shape
    out = shape((4 * quarter, width), BF)
    return pl.pallas_call(
        enter_kernel,
        out_shape=(out, out),
        in_specs=[scalars()] + [whole()] * 5,
        out_specs=(whole(), whole()),
        compiler_params=params(),
        cost_estimate=cost(16 * quarter * width * 4, quarter * width * 24),
    )(info, *pieces, norm)


def masked_kernel(info, mine, core_mine, far, core_far, rows_ref):
    quarter = mine.shape[0]
    for step, piece in enumerate((mine, core_mine, far, core_far)):
        start = pl.multiple_of(info[START + step], quarter)
        row = start + lax.broadcasted_iota(jnp.int32, (quarter, 1), 0)
        values = jnp.where(row < info[OWN_LEN], piece[...].astype(F32), 0.0)
        rows_ref[pl.ds(start, quarter), :] = values.astype(BF)


def masked_rows(info, pieces):
    quarter, width = pieces[0].shape
    return pl.pallas_call(
        masked_kernel,
        out_shape=shape((4 * quarter, width), BF),
        in_specs=[scalars()] + [whole()] * 4,
        out_specs=whole(),
        compiler_params=params(),
        cost_estimate=cost(quarter * width * 8, quarter * width * 16),
    )(info, *pieces)


def skew_kernel(distance_ref, table_ref):
    width = table_ref.shape[2]
    for head in range(distance_ref.shape[0]):
        row = jnp.broadcast_to(distance_ref[head : head + 1, :], (BAND, width))
        table_ref[head] = pltpu.roll(row, width - (BAND - 1), 1, stride=1, stride_axis=0)


def skew(distances):
    heads, width = distances.shape
    return pl.pallas_call(
        skew_kernel,
        out_shape=shape((heads, BAND, width), F32),
        in_specs=[whole()],
        out_specs=whole(),
        compiler_params=params(),
        cost_estimate=cost(heads * BAND * width, heads * BAND * width * 4),
    )(distances)


def unskewed(band):
    width = band.shape[1]
    amount = (BAND - 1) - lax.broadcasted_iota(jnp.int32, (BAND, width), 0)
    for bit in range(7):
        band = jnp.where(((amount >> bit) & 1) == 1, pltpu.roll(band, 1 << bit, 1), band)
    return jnp.sum(band, 0, keepdims=True)


def lane_limit(info, row_start, rows, causal, length_at):
    last = info[length_at] - 1
    if not causal:
        return last
    row = row_start + lax.broadcasted_iota(jnp.int32, (rows, 1), 0)
    free = jnp.where(info[ROLE] == DECODER, 0, 1 << 20)
    return jnp.minimum(row + free, last)


def bias_block(table_ref, head, row_start, length):
    blocks = []
    for part in range(TILE // BAND):
        offset = pl.multiple_of(length - BAND - row_start - part * BAND, BAND)
        blocks.append(table_ref[head, :, pl.ds(offset, length)])
    return jnp.concatenate(blocks, 0)


def attend_loop(info, qkv_ref, table_ref, out_ref, lse_ref, length_at):
    length, width = out_ref.shape
    causal = table_ref is not None

    def block(index, carry):
        start = pl.multiple_of(index * TILE, TILE)
        rows = pl.ds(start, TILE)
        limit = lane_limit(info, start, TILE, causal, length_at)
        allowed = lax.broadcasted_iota(jnp.int32, (TILE, length), 1) <= limit
        for head in range(width // HEAD_DIM):
            span = slice(head * HEAD_DIM, (head + 1) * HEAD_DIM)
            queries = qkv_ref[0, rows, span] * jnp.asarray(SCALE, BF)
            scores = mm(queries, qkv_ref[1, :, span], NT)
            if causal:
                scores = scores + bias_block(table_ref, head, start, length)
            scores = jnp.where(allowed, scores, MASKED)
            peak = jnp.max(scores, -1, keepdims=True)
            lifted = jnp.exp(scores - peak)
            total = jnp.sum(lifted, -1, keepdims=True)
            mixed = mm(lifted.astype(BF), qkv_ref[2, :, span], NN)
            out_ref[rows, span] = (mixed / total).astype(BF)
            lse_ref[rows, head : head + 1] = peak + jnp.log(total)
        return carry

    lax.fori_loop(0, length // TILE, block, 0)


def by_rows(count, body):
    def step(index, carry):
        body(pl.ds(pl.multiple_of(index * TILE, TILE), TILE))
        return carry

    lax.fori_loop(0, count // TILE, step, 0)


def self_forward_kernel(has_sum, info, normed, weights, project, table, *refs):
    previous = refs[0] if has_sum else None
    sum_ref, qkv_ref, out_ref, lse_ref = refs[1 if has_sum else 0 :]
    length = out_ref.shape[0]

    def inputs(rows):
        block = normed[rows, :]
        for place in range(3):
            qkv_ref[place, rows, :] = mm(block, weights[place], NN).astype(BF)

    by_rows(length, inputs)
    attend_loop(info, qkv_ref, table, out_ref, lse_ref, OWN_LEN)

    def outputs(rows):
        value = mm(out_ref[rows, :], project[...], NN)
        if has_sum:
            value = value + previous[rows, :]
        sum_ref[rows, :] = value.astype(sum_ref.dtype)

    by_rows(length, outputs)


def attention_cost(length, width, model, matmuls, projections):
    heads = width // HEAD_DIM
    return cost(
        heads * length * length * HEAD_DIM * 2 * matmuls * 4 + projections * 2 * length * model * width,
        length * model * 8,
        heads * length * length,
    )


def self_forward(info, normed, weights, project, table, previous):
    length, model = normed.shape
    width = project.shape[0]
    has_sum = previous is not None
    operands = [info, normed, weights, project, table] + ([previous] if has_sum else [])
    return pl.pallas_call(
        functools.partial(self_forward_kernel, has_sum),
        out_shape=(
            shape((length, model), BF if has_sum else F32),
            shape((3, length, width), BF),
            shape((length, width), BF),
            shape((length, 128), F32),
        ),
        in_specs=[scalars()] + [whole()] * (len(operands) - 1),
        out_specs=(whole(),) * 4,
        compiler_params=params(),
        cost_estimate=attention_cost(length, width, model, 2, 4),
    )(*operands)


def cross_forward_kernel(has_sum, info, normed, near, far, query_pair, source_pair, *refs):
    previous = refs[0] if has_sum else None
    sum_ref, qkv_ref, out_ref, lse_ref = refs[1 if has_sum else 0 :]
    length = out_ref.shape[0]
    half = near.shape[0]

    @pl.when(info[ROLE] == DECODER)
    def _():
        def queries(rows):
            qkv_ref[0, rows, :] = mm(normed[rows, :], query_pair[0], NN).astype(BF)

        by_rows(length, queries)
        for piece, side in ((near, info[CORE]), (far, 1 - info[CORE])):
            base = side * half

            def sources(index, carry, piece=piece, base=base):
                local = pl.multiple_of(index * TILE, TILE)
                block = piece[pl.ds(local, TILE), :]
                rows = pl.ds(pl.multiple_of(base + local, TILE), TILE)
                for place in range(2):
                    qkv_ref[1 + place, rows, :] = mm(block, source_pair[place], NN).astype(BF)
                return carry

            lax.fori_loop(0, half // TILE, sources, 0)
        attend_loop(info, qkv_ref, None, out_ref, lse_ref, SOURCE_LEN)

        def outputs(rows):
            value = mm(out_ref[rows, :], query_pair[1], NT)
            if has_sum:
                value = value + previous[rows, :]
            sum_ref[rows, :] = value.astype(sum_ref.dtype)

        by_rows(length, outputs)


def cross_forward(info, normed, near, far, query_pair, source_pair, previous):
    length, model = normed.shape
    width = query_pair.shape[2]
    has_sum = previous is not None
    operands = [info, normed, near, far, query_pair, source_pair]
    operands += [previous] if has_sum else []
    return pl.pallas_call(
        functools.partial(cross_forward_kernel, has_sum),
        out_shape=(
            shape((length, model), BF if has_sum else F32),
            shape((3, length, width), BF),
            shape((length, width), BF),
            shape((length, 128), F32),
        ),
        in_specs=[scalars()] + [whole()] * (len(operands) - 1),
        out_specs=(whole(),) * 4,
        compiler_params=params(),
        cost_estimate=attention_cost(length, width, model, 2, 4),
    )(*operands)


def attend_back_loop(
    info, qkv_ref, table_ref, lse_ref, upstream, grads_ref, key_sum, value_sum, band, length_at
):
    length, width = upstream.shape
    causal = table_ref is not None
    key_sum[...] = jnp.zeros_like(key_sum)
    value_sum[...] = jnp.zeros_like(value_sum)
    if causal:
        band[...] = jnp.zeros_like(band)

    def block(index, carry):
        start = pl.multiple_of(index * TILE, TILE)
        rows = pl.ds(start, TILE)
        limit = lane_limit(info, start, TILE, causal, length_at)
        allowed = lax.broadcasted_iota(jnp.int32, (TILE, length), 1) <= limit
        for head in range(width // HEAD_DIM):
            span = slice(head * HEAD_DIM, (head + 1) * HEAD_DIM)
            queries = qkv_ref[0, rows, span] * jnp.asarray(SCALE, BF)
            keys = qkv_ref[1, :, span]
            scores = mm(queries, keys, NT)
            if causal:
                scores = scores + bias_block(table_ref, head, start, length)
            probs = jnp.where(allowed, jnp.exp(scores - lse_ref[rows, head : head + 1]), 0.0)
            above = upstream[rows, span]
            d_probs = mm(above, qkv_ref[2, :, span], NT)
            inner = jnp.sum(d_probs * probs, -1, keepdims=True)
            d_scores = probs * (d_probs - inner)
            low = d_scores.astype(BF)
            grads_ref[0, rows, span] = (mm(low, keys, NN) * SCALE).astype(BF)
            key_sum[span, :] += mm(queries, low, TN)
            value_sum[span, :] += mm(above, probs.astype(BF), TN)
            if causal:
                for part in range(TILE // BAND):
                    offset = pl.multiple_of(length - BAND - start - part * BAND, BAND)
                    cols = pl.ds(offset, length)
                    band[head, :, cols] += d_scores[part * BAND : (part + 1) * BAND, :]
        return carry

    lax.fori_loop(0, length // TILE, block, 0)
    grads_ref[1] = key_sum[...].T.astype(BF)
    grads_ref[2] = value_sum[...].T.astype(BF)


def self_backward_kernel(has_sum, info, qkv, lse, above, weights, project, table, *refs):
    previous = refs[0] if has_sum else None
    sum_ref, grads_ref, spread_ref, upstream, key_sum, value_sum, band = refs[1 if has_sum else 0 :]
    length = above.shape[0]

    def entering(rows):
        upstream[rows, :] = mm(above[rows, :], project[...], NT).astype(BF)

    by_rows(length, entering)
    attend_back_loop(
        info, qkv, table, lse, upstream, grads_ref, key_sum, value_sum, band, OWN_LEN
    )

    def leaving(rows):
        value = mm(grads_ref[0, rows, :], weights[0], NT)
        for place in (1, 2):
            value = value + mm(grads_ref[place, rows, :], weights[place], NT)
        if has_sum:
            value = value + previous[rows, :]
        sum_ref[rows, :] = value.astype(sum_ref.dtype)

    by_rows(length, leaving)
    for head in range(table.shape[0]):
        spread_ref[head : head + 1, :] = unskewed(band[head])


def self_backward(info, qkv, lse, above, weights, project, table, previous):
    length, model = above.shape
    width = project.shape[0]
    has_sum = previous is not None
    operands = [info, qkv, lse, above, weights, project, table]
    operands += [previous] if has_sum else []
    return pl.pallas_call(
        functools.partial(self_backward_kernel, has_sum),
        out_shape=(
            shape((length, model), BF if has_sum else F32),
            shape((3, length, width), BF),
            shape((table.shape[0], table.shape[2]), F32),
        ),
        in_specs=[scalars()] + [whole()] * (len(operands) - 1),
        out_specs=(whole(),) * 3,
        scratch_shapes=[
            pltpu.VMEM((length, width), BF),
            pltpu.VMEM((width, length), F32),
            pltpu.VMEM((width, length), F32),
            pltpu.VMEM(table.shape, F32),
        ],
        compiler_params=params(),
        cost_estimate=attention_cost(length, width, model, 5, 4),
    )(*operands)


def cross_backward_kernel(has_sum, info, qkv, lse, above, query_pair, source_pair, *refs):
    before = refs[:2] if has_sum else (None, None)
    sum_ref, source_ref, grads_ref, upstream, key_sum, value_sum = refs[2 if has_sum else 0 :]
    length = above.shape[0]

    @pl.when(info[ROLE] == DECODER)
    def _():
        def entering(rows):
            upstream[rows, :] = mm(above[rows, :], query_pair[1], NN).astype(BF)

        by_rows(length, entering)
        attend_back_loop(
            info, qkv, None, lse, upstream, grads_ref, key_sum, value_sum, None, SOURCE_LEN
        )

        def leaving(rows):
            value = mm(grads_ref[0, rows, :], query_pair[0], NT)
            source = mm(grads_ref[1, rows, :], source_pair[0], NT)
            source = source + mm(grads_ref[2, rows, :], source_pair[1], NT)
            if has_sum:
                value = value + before[0][rows, :]
                source = source + before[1][rows, :]
            sum_ref[rows, :] = value.astype(sum_ref.dtype)
            source_ref[rows, :] = source.astype(source_ref.dtype)

        by_rows(length, leaving)


def cross_backward(info, qkv, lse, above, query_pair, source_pair, before):
    length, model = above.shape
    width = query_pair.shape[2]
    has_sum = before is not None
    operands = [info, qkv, lse, above, query_pair, source_pair] + (list(before) if has_sum else [])
    out = shape((length, model), BF if has_sum else F32)
    return pl.pallas_call(
        functools.partial(cross_backward_kernel, has_sum),
        out_shape=(out, out, shape((3, length, width), BF)),
        in_specs=[scalars()] + [whole()] * (len(operands) - 1),
        out_specs=(whole(),) * 3,
        scratch_shapes=[
            pltpu.VMEM((length, width), BF),
            pltpu.VMEM((width, length), F32),
            pltpu.VMEM((width, length), F32),
        ],
        compiler_params=params(),
        cost_estimate=attention_cost(length, width, model, 5, 4),
    )(*operands)


def row_spec(width):
    return pl.BlockSpec((TILE, width), lambda index: (index, 0))


def fixed_spec(dims):
    return pl.BlockSpec(dims, lambda index: (0,) * len(dims))


def add_norm_kernel(stream, near, far, norm_ref, sum_ref, normed_ref):
    value = stream[...].astype(F32) + (near[...].astype(F32) + far[...].astype(F32))
    sum_ref[...] = value
    normed_ref[...] = norm_of(value, norm_ref).astype(BF)


def add_norm(stream, near, far, norm):
    length, model = stream.shape
    return pl.pallas_call(
        add_norm_kernel,
        grid=(length // TILE,),
        out_shape=(shape((length, model), F32), shape((length, model), BF)),
        in_specs=[row_spec(model)] * 3 + [fixed_spec((2, model))],
        out_specs=(row_spec(model),) * 2,
        compiler_params=params(),
        cost_estimate=cost(length * model * 12, length * model * 14),
    )(stream, near, far, norm)


def row_mask(info, index, at):
    row = index * TILE + lax.broadcasted_iota(jnp.int32, (TILE, 1), 0)
    return row < info[at]


def squares_of(value):
    return jnp.sum(jnp.sum(value * value, 0, keepdims=True), 1, keepdims=True)


def source_kernel(info, stream, near, far, norm_ref, sum_ref, sent_ref, square_ref):
    index = pl.program_id(0)
    value = stream[...] + (near[...].astype(F32) + far[...].astype(F32))
    sum_ref[...] = value
    result = jnp.where(row_mask(info, index, OWN_LEN), norm_of(value, norm_ref), 0.0)
    sent_ref[...] = result.astype(BF)

    @pl.when(index == 0)
    def _():
        square_ref[...] = jnp.zeros_like(square_ref)

    square_ref[...] += squares_of(result)


def source_out(info, stream, near, far, norm):
    length, model = stream.shape
    return pl.pallas_call(
        source_kernel,
        grid=(length // TILE,),
        out_shape=(shape((length, model), F32), shape((length, model), BF), shape((8, 128), F32)),
        in_specs=[scalars()] + [row_spec(model)] * 3 + [fixed_spec((2, model))],
        out_specs=(row_spec(model), row_spec(model), fixed_spec((8, 128))),
        compiler_params=params(),
        cost_estimate=cost(length * model * 14, length * model * 14),
    )(info, stream, near, far, norm)


def finish_kernel(info, stream, near, far, sent, square, out_ref, square_ref):
    index = pl.program_id(0)

    @pl.when(info[ROLE] == DECODER)
    def _():
        value = stream[...] + (near[...].astype(F32) + far[...].astype(F32))
        value = jnp.where(row_mask(info, index, OWN_LEN), value, 0.0)
        out_ref[...] = value.astype(BF)

        @pl.when(index == 0)
        def _():
            square_ref[...] = jnp.zeros_like(square_ref)

        square_ref[...] += squares_of(value)

    @pl.when(info[ROLE] == ENCODER)
    def _():
        out_ref[...] = sent[...]
        square_ref[...] = square[...]


def finish(info, stream, near, far, sent, square):
    length, model = stream.shape
    return pl.pallas_call(
        finish_kernel,
        grid=(length // TILE,),
        out_shape=(shape((length, model), BF), shape((8, 128), F32)),
        in_specs=[scalars()] + [row_spec(model)] * 4 + [fixed_spec((8, 128))],
        out_specs=(row_spec(model), fixed_spec((8, 128))),
        compiler_params=params(),
        cost_estimate=cost(length * model * 6, length * model * 12),
    )(info, stream, near, far, sent, square)


def norm_back(upstream, values, norm_ref):
    centred = values - jnp.mean(values, -1, keepdims=True)
    factor = lax.rsqrt(jnp.mean(centred * centred, -1, keepdims=True) + EPSILON)
    unit = centred * factor
    scaled = upstream * norm_ref[0:1, :]
    inner = scaled - jnp.mean(scaled, -1, keepdims=True)
    inner = inner - unit * jnp.mean(scaled * unit, -1, keepdims=True)
    gain = jnp.sum(upstream * unit, 0, keepdims=True)
    shift = jnp.sum(upstream, 0, keepdims=True)
    return factor * inner, gain, shift


def norm_back_kernel(residual, near, far, values, norm_ref, grad_ref, low_ref, norm_grad_ref):
    upstream = near[...].astype(F32) + far[...].astype(F32)
    grad, gain, shift = norm_back(upstream, values[...].astype(F32), norm_ref)
    grad = residual[...].astype(F32) + grad
    grad_ref[...] = grad
    low_ref[...] = grad.astype(BF)

    @pl.when(pl.program_id(0) == 0)
    def _():
        norm_grad_ref[...] = jnp.zeros_like(norm_grad_ref)

    norm_grad_ref[0:1, :] += gain
    norm_grad_ref[1:2, :] += shift


def norm_backward(residual, near, far, values, norm):
    length, model = values.shape
    return pl.pallas_call(
        norm_back_kernel,
        grid=(length // TILE,),
        out_shape=(shape((length, model), F32), shape((length, model), BF), shape((2, model), F32)),
        in_specs=[row_spec(model)] * 4 + [fixed_spec((2, model))],
        out_specs=(row_spec(model), row_spec(model), fixed_spec((2, model))),
        compiler_params=params(),
        cost_estimate=cost(length * model * 20, length * model * 18),
    )(residual, near, far, values, norm)


def source_back_kernel(
    info, cot, returned, values, norm_ref, kept, kept_low, kept_norm, grad_ref, low_ref, norm_grad_ref
):
    index = pl.program_id(0)

    @pl.when(info[ROLE] == ENCODER)
    def _():
        upstream = cot[...].astype(F32) + returned[...].astype(F32)
        upstream = jnp.where(row_mask(info, index, OWN_LEN), upstream, 0.0)
        grad, gain, shift = norm_back(upstream, values[...], norm_ref)
        grad_ref[...] = grad
        low_ref[...] = grad.astype(BF)

        @pl.when(index == 0)
        def _():
            norm_grad_ref[...] = jnp.zeros_like(norm_grad_ref)

        norm_grad_ref[0:1, :] += gain
        norm_grad_ref[1:2, :] += shift

    @pl.when(info[ROLE] == DECODER)
    def _():
        grad_ref[...] = kept[...]
        low_ref[...] = kept_low[...]
        norm_grad_ref[...] = kept_norm[...]


def source_back(info, cot, returned, values, norm, kept):
    length, model = values.shape
    return pl.pallas_call(
        source_back_kernel,
        grid=(length // TILE,),
        out_shape=(shape((length, model), F32), shape((length, model), BF), shape((2, model), F32)),
        in_specs=[scalars()]
        + [row_spec(model)] * 3
        + [fixed_spec((2, model)), row_spec(model), row_spec(model), fixed_spec((2, model))],
        out_specs=(row_spec(model), row_spec(model), fixed_spec((2, model))),
        compiler_params=params(),
        cost_estimate=cost(length * model * 20, length * model * 18),
    )(info, cot, returned, values, norm, *kept)


def gelu_parts(hidden):
    half = 0.5 * (1.0 + lax.erf(hidden * math.sqrt(0.5)))
    slope = half + hidden * jnp.exp(-0.5 * hidden * hidden) * (1.0 / math.sqrt(2.0 * math.pi))
    return hidden * half, slope


def feed_forward_kernel(has_sum, info, normed, up, down, *refs):
    previous = refs[0] if has_sum else None
    sum_ref, active_ref, slope_ref = refs[1 if has_sum else 0 :]

    @pl.when(info[ROLE] == ENCODER)
    def _():
        active, slope = gelu_parts(mm(normed[...], up[...], NN))
        active = active.astype(BF)
        active_ref[...] = active
        slope_ref[...] = slope
        value = mm(active, down[...], NN)
        if has_sum:
            value = value + previous[...]
        sum_ref[...] = value.astype(sum_ref.dtype)


def feed_forward(info, normed, up, down, previous):
    length, model = normed.shape
    hidden = up.shape[1]
    has_sum = previous is not None
    operands = [info, normed, up, down] + ([previous] if has_sum else [])
    return pl.pallas_call(
        functools.partial(feed_forward_kernel, has_sum),
        grid=(length // TILE,),
        out_shape=(
            shape((length, model), BF if has_sum else F32),
            shape((length, hidden), BF),
            shape((length, hidden), F32),
        ),
        in_specs=[scalars(), row_spec(model), fixed_spec(up.shape), fixed_spec(down.shape)]
        + ([row_spec(model)] if has_sum else []),
        out_specs=(row_spec(model), row_spec(hidden), row_spec(hidden)),
        compiler_params=params(),
        cost_estimate=cost(4 * length * model * hidden, length * model * 12, length * hidden),
    )(*operands)


def feed_both_kernel(has_sum, info, normed, cot, up, down, passed, *refs):
    before = refs[:2] if has_sum else (None, None)
    sum_ref, back_ref, active_ref, hidden_grad_ref = refs[2 if has_sum else 0 :]

    @pl.when(info[ROLE] == DECODER)
    def _():
        active, slope = gelu_parts(mm(normed[...], up[...], NN))
        active = active.astype(BF)
        active_ref[...] = active
        value = mm(active, down[...], NN)
        grad = (mm(cot[...], down[...], NT) * slope).astype(BF)
        hidden_grad_ref[...] = grad
        back = mm(grad, up[...], NT)
        if has_sum:
            value = value + before[0][...]
            back = back + before[1][...]
        sum_ref[...] = value.astype(sum_ref.dtype)
        back_ref[...] = back.astype(back_ref.dtype)

    @pl.when(info[ROLE] == ENCODER)
    def _():
        active_ref[...] = passed[...]


def feed_both(info, normed, cot, up, down, passed, before):
    length, model = normed.shape
    hidden = up.shape[1]
    has_sum = before is not None
    operands = [info, normed, cot, up, down, passed] + (list(before) if has_sum else [])
    out = shape((length, model), BF if has_sum else F32)
    return pl.pallas_call(
        functools.partial(feed_both_kernel, has_sum),
        grid=(length // TILE,),
        out_shape=(out, out, shape((length, hidden), BF), shape((length, hidden), BF)),
        in_specs=[
            scalars(),
            row_spec(model),
            row_spec(model),
            fixed_spec(up.shape),
            fixed_spec(down.shape),
            row_spec(hidden),
        ]
        + ([row_spec(model)] * 2 if has_sum else []),
        out_specs=(row_spec(model), row_spec(model), row_spec(hidden), row_spec(hidden)),
        compiler_params=params(),
        cost_estimate=cost(8 * length * model * hidden, length * model * 16, length * hidden),
    )(*operands)


def feed_back_kernel(has_sum, info, above, slope, up, down, passed, *refs):
    before, passed_sum = refs[:2] if has_sum else (None, None)
    back_ref, hidden_grad_ref = refs[2 if has_sum else 0 :]

    @pl.when(info[ROLE] == ENCODER)
    def _():
        grad = (mm(above[...], down[...], NT) * slope[...]).astype(BF)
        hidden_grad_ref[...] = grad
        back = mm(grad, up[...], NT)
        if has_sum:
            back = back + before[...]
        back_ref[...] = back.astype(back_ref.dtype)

    @pl.when(info[ROLE] == DECODER)
    def _():
        hidden_grad_ref[...] = passed[...]
        if has_sum:
            back_ref[...] = passed_sum[...]


def feed_back(info, above, slope, up, down, passed, before):
    length, model = above.shape
    hidden = up.shape[1]
    has_sum = before is not None
    operands = [info, above, slope, up, down, passed] + (list(before) if has_sum else [])
    return pl.pallas_call(
        functools.partial(feed_back_kernel, has_sum),
        grid=(length // TILE,),
        out_shape=(shape((length, model), BF if has_sum else F32), shape((length, hidden), BF)),
        in_specs=[
            scalars(),
            row_spec(model),
            row_spec(hidden),
            fixed_spec(up.shape),
            fixed_spec(down.shape),
            row_spec(hidden),
        ]
        + ([row_spec(model)] * 2 if has_sum else []),
        out_specs=(row_spec(model), row_spec(hidden)),
        compiler_params=params(),
        cost_estimate=cost(4 * length * model * hidden, length * model * 12),
    )(*operands)


def across(value):
    return lax.ppermute(value, "tensor", [(0, 2), (1, 3), (2, 0), (3, 1)])


def across_in(value, role):
    links = [(0, 2), (1, 3), (2, 0), (3, 1)]
    return lax.ppermute(
        value, ("section", "tensor"), [(role * 4 + a, role * 4 + b) for a, b in links]
    )


def beside(value):
    return lax.ppermute(value, "tensor", [(0, 1), (1, 0), (2, 3), (3, 2)])


def to_decoder(value):
    return lax.ppermute(value, "section", [(ENCODER, DECODER)])


def to_encoder(value):
    return lax.ppermute(value, "section", [(DECODER, ENCODER)])


def total_over_sequences(value):
    if lax.axis_size("dp") != 4:
        return lax.psum(value, "dp")
    place = lax.axis_index("dp")
    inner = (place == 1) | (place == 2)
    value = value + lax.ppermute(value, "dp", [(0, 1), (3, 2)])
    value = value + lax.ppermute(value, "dp", [(1, 2), (2, 1)])
    return jnp.where(inner, value, lax.ppermute(value, "dp", [(1, 0), (2, 3)]))


def weight_total(own, other):
    value = (own + across(other.astype(BF)).astype(F32)).astype(BF)
    return total_over_sequences(value).astype(F32)


def after(value, done):
    return lax.optimization_barrier((value, done))[0]


def rows_product(left, right):
    return lax.dot_general(left, right, TN, preferred_element_type=F32)


def body(
    frames,
    lengths,
    bucket_of,
    rel_table,
    norms,
    attn_in,
    attn_out,
    cross_pair,
    ffn_in,
    ffn_out,
    cotangent,
):
    section = lax.axis_index("section")
    tensor = lax.axis_index("tensor")
    pair, core = tensor // 2, tensor % 2
    decoder = section == DECODER
    quarter, model = frames.shape[3], frames.shape[4]
    length = 4 * quarter
    half = length // 2
    width = attn_in.shape[3]
    heads = width // HEAD_DIM
    buckets = rel_table.shape[1]

    own_length = lengths[section, pair, 0]
    source_length = lengths[ENCODER, pair, 0]
    starts = [(tensor ^ step) * quarter for step in range(4)]
    info = jnp.stack([section, own_length, source_length, core] + starts).astype(jnp.int32)

    def pick(array, index):
        return lax.dynamic_index_in_dim(array[0, :, 0], index, 0, keepdims=False)

    def quarters(array):
        mine = pick(array, pair)
        far = across(pick(array, 1 - pair))
        both = beside(jnp.stack([mine, far]))
        return mine, both[0], far, both[1]

    frame_pieces = quarters(frames)
    rel_far = across(rel_table[0])
    in_near, out_near, up_near, down_near = attn_in[0], attn_out[0], ffn_in[0], ffn_out[0]
    in_far = across(in_near)
    out_far = across(out_near)
    pair_near = cross_pair[0]
    up_far_e = across_in(up_near, ENCODER)
    down_far_e = across_in(down_near, ENCODER)
    source_near = to_decoder(pair_near)
    pair_far = across_in(pair_near, DECODER)
    source_far = across_in(source_near, DECODER)
    cot_pieces = quarters(cotangent)
    up_far_d = across_in(up_near, DECODER)
    down_far_d = across_in(down_near, DECODER)

    buckets_here = jnp.pad(bucket_of[0], (0, 1), constant_values=-1)
    one_hot = (lax.broadcasted_iota(jnp.int32, (buckets, 2 * length), 0) == buckets_here[None]).astype(F32)
    distances = lax.dot_general(
        jnp.concatenate([rel_table[0], rel_far], 1),
        one_hot,
        TN,
        precision=HIGHEST,
        preferred_element_type=F32,
    )
    table_near = skew(distances[:heads])
    table_far = skew(distances[heads:])

    rows, normed_one = enter(info, frame_pieces, norms[0, 0])
    part, qkv_near, mixed_near, lse_near = self_forward(
        info, normed_one, in_near, out_near, table_near, None
    )
    part, qkv_far, mixed_far, lse_far = self_forward(
        info, normed_one, in_far, out_far, table_far, part
    )
    stream_one, normed_two = add_norm(rows, part, beside(part), norms[0, 1])
    cot = masked_rows(info, cot_pieces)

    part, active_near, slope_near = feed_forward(info, normed_two, up_near, down_near, None)
    part, active_far, slope_far = feed_forward(info, normed_two, up_far_e, down_far_e, part)
    stream_e, sent, squares = source_out(info, stream_one, part, beside(part), norms[0, 2])
    sent_near = to_decoder(lax.dynamic_slice_in_dim(sent, core * half, half, 0))
    sent_far = beside(sent_near)

    part, cross_near, joined_near, cross_lse_near = cross_forward(
        info, normed_two, sent_near, sent_far, pair_near, source_near, None
    )
    part, cross_far, joined_far, cross_lse_far = cross_forward(
        info, normed_two, sent_near, sent_far, pair_far, source_far, part
    )
    stream_d, normed_three = add_norm(stream_one, part, beside(part), norms[0, 2])
    part, back, active_near, grad_near = feed_both(
        info, normed_three, cot, up_near, down_near, active_near, None
    )
    part_d, back, active_far, grad_far = feed_both(
        info, normed_three, cot, up_far_d, down_far_d, active_far, (part, back)
    )
    kept = norm_backward(cot, back, beside(back), stream_d, norms[0, 2])
    above_two = kept[1]
    back, returned, d_cross_near = cross_backward(
        info, cross_near, cross_lse_near, above_two, pair_near, source_near, None
    )
    back, returned, d_cross_far = cross_backward(
        info, cross_far, cross_lse_far, above_two, pair_far, source_far, (back, returned)
    )
    returned_mine = lax.dynamic_slice_in_dim(returned, core * half, half, 0)
    returned_theirs = lax.dynamic_slice_in_dim(returned, (1 - core) * half, half, 0)
    returned = returned_mine.astype(F32) + beside(returned_theirs).astype(F32)
    returned = to_encoder(returned.astype(BF))
    returned_theirs = beside(returned)
    returned = jnp.where(
        core == 0,
        jnp.concatenate([returned, returned_theirs]),
        jnp.concatenate([returned_theirs, returned]),
    )

    grad_two, above_e, norm_grad_three = source_back(
        info, cot, returned, stream_e, norms[0, 2], kept
    )
    back_e, grad_near = feed_back(info, above_e, slope_near, up_near, down_near, grad_near, None)
    back, grad_far = feed_back(
        info, above_e, slope_far, up_far_e, down_far_e, grad_far, (back_e, back)
    )
    grad_one, above_one, norm_grad_two = norm_backward(
        grad_two, back, beside(back), stream_one, norms[0, 1]
    )

    normed_feed = jnp.where(decoder, normed_three, normed_two)
    above_feed = jnp.where(decoder, cot, above_e)
    d_ffn_out = weight_total(
        rows_product(active_near, above_feed), rows_product(active_far, above_feed)
    )
    d_ffn_in = weight_total(
        rows_product(normed_feed, grad_near), rows_product(normed_feed, grad_far)
    )

    back, d_qkv_near, spread_near = self_backward(
        info, qkv_near, lse_near, above_one, in_near, out_near, table_near, None
    )
    back, d_qkv_far, spread_far = self_backward(
        info, qkv_far, lse_far, above_one, in_far, out_far, table_far, back
    )
    grad_rows, _, norm_grad_one = norm_backward(grad_one, back, beside(back), rows, norms[0, 0])

    def input_grads(normed, grads):
        return jnp.stack([rows_product(normed, grads[place]) for place in range(3)])

    d_attn_out = weight_total(
        rows_product(mixed_near, above_one), rows_product(mixed_far, above_one)
    )
    d_attn_in = weight_total(
        input_grads(normed_one, d_qkv_near), input_grads(normed_one, d_qkv_far)
    )

    sent_all = jnp.where(
        core == 0,
        jnp.concatenate([sent_near, sent_far]),
        jnp.concatenate([sent_far, sent_near]),
    )

    def cross_grads(grads, joined):
        return jnp.stack(
            [
                rows_product(sent_all, grads[1]),
                rows_product(sent_all, grads[2]),
                rows_product(normed_two, grads[0]),
                rows_product(above_two, joined),
            ]
        )

    d_far = across_in(cross_grads(d_cross_far, joined_far).astype(BF), DECODER)
    d_pair = (cross_grads(d_cross_near, joined_near) + d_far.astype(F32)).astype(BF)
    d_source = to_encoder(d_pair[:2])
    d_pair = jnp.where(decoder, d_pair[2:], d_source)
    d_pair = total_over_sequences(d_pair).astype(F32)

    result, squares = finish(info, stream_d, part_d, beside(part_d), sent, squares)

    def placed(value):
        mine = lax.dynamic_slice_in_dim(value, tensor * quarter, quarter, 0)
        theirs = lax.dynamic_slice_in_dim(value, (tensor ^ 2) * quarter, quarter, 0)
        other = across(theirs.astype(BF)).astype(value.dtype)
        stacked = jnp.where(pair == 0, jnp.stack([mine, other]), jnp.stack([other, mine]))
        return stacked[None, :, None]

    spreads = jnp.concatenate([spread_near, spread_far])
    d_table = lax.dot_general(
        one_hot, spreads, NT, precision=HIGHEST, preferred_element_type=F32
    )
    small = jnp.concatenate(
        [
            norm_grad_one,
            norm_grad_two,
            norm_grad_three,
            jnp.broadcast_to(squares[:1, :1], (1, model)),
            jnp.broadcast_to(own_length.astype(F32), (1, model)),
        ]
    )
    small = total_over_sequences(small + across(small))
    d_table = total_over_sequences(d_table[:, :heads] + across(d_table[:, heads:]))
    stats = jnp.sqrt(small[6, :1] / (small[7, :1] * model))
    return (
        placed(result),
        placed(grad_rows),
        d_table[None],
        small[:6].reshape(1, 3, 2, model),
        d_attn_in[None],
        d_attn_out[None],
        d_pair[None],
        d_ffn_in[None],
        d_ffn_out[None],
        stats,
    )


def solution(mesh):
    in_specs = (
        P("section", None, "dp", "tensor", None),
        P(None, None, "dp"),
        P("section", None),
        P("section", None, "tensor"),
        P("section", None, None, None),
        P("section", None, None, "tensor"),
        P("section", "tensor", None),
        P("section", None, None, "tensor"),
        P("section", None, "tensor"),
        P("section", "tensor", None),
        P("section", None, "dp", "tensor", None),
    )
    out_specs = (
        P("section", None, "dp", "tensor", None),
        P("section", None, "dp", "tensor", None),
        P("section", None, "tensor"),
        P("section", None, None, None),
        P("section", None, None, "tensor"),
        P("section", "tensor", None),
        P("section", None, None, "tensor"),
        P("section", None, "tensor"),
        P("section", "tensor", None),
        P("section"),
    )
    return jax.shard_map(body, mesh=mesh, in_specs=in_specs, out_specs=out_specs, check_vma=False)
```

time: 6260 us -> 774 us (0.12); the launches traced: 6160 us -> 764 us
  local copies, waits for them, and re-layouts: 4800 us -> 37.6 us
  waiting for transfers between devices: 770 us -> 346 us
  matrix products: 283 us -> 32.4 us
  Pallas kernels: 0 us -> 224 us
  other arithmetic: 164 us -> 35.5 us
  blocking collectives: 69.3 us -> 0 us
    gather x2 -> x0, local copies, waits for them, and re-layouts: 4070 us -> none  [body(): self_bias = distance_bias.T[:, offsets]]
    unnamed x385 -> x112, local copies, waits for them, and re-layouts: 582 us -> 11.7 us
    reduce_scatter x18 -> x0, waiting for transfers between devices: 534 us -> none  [the longest x9 352 us: sum_rows(): return lax.psum_scatter(block, 'tensor', scatter_dimension=1, tiled=True)]
    dot_general x64 -> x22, matrix products: 276 us -> 32.4 us  [the longest x20 30.3 us: rows_product(): return lax.dot_general(left, right, TN, preferred_element_type=F32)]
    ppermute x4 -> x57, waiting for transfers between devices: 117 us -> 346 us  [the longest x2 138 us: to_encoder(): return lax.ppermute(value, 'section', [(DECODER, ENCODER)])]
    pallas_call x0 -> x26, Pallas kernels: none -> 224 us  [the longest x2 56.8 us: self_backward(): pl.pallas_call(functools.partial(self_backward_kernel, has_sum), out_shap...]
    all_gather x18 -> x0, waiting for transfers between devices: 112 us -> none  [the longest x9 74.9 us: pick_entries(): return lax.all_gather(block, 'tensor', axis=1, tiled=True)]
    psum x2 -> x0, blocking collectives: 69.3 us -> none  [the longest x1 57.7 us: body(): lax.psum((totals[1], squares, valid_rows), ('dp', 'tensor'))]
  transfers between devices with their start and end apart: 41 -> 57, of which waited for: 26 -> 20; matrix products, arithmetic and copies ran while one was open for 82% -> 12% of each run, Pallas kernels for 0% -> 20%
where the time goes in v2:
time: 774 us; the launch traced here: 764 us
  waiting for transfers between devices  346 us (45%)
  Pallas kernels  224 us (29%)
  starting transfers between devices  83.5 us (11%)
  local copies, waits for them, and re-layouts  37.6 us (5%)
  other arithmetic  35.5 us (5%)
  matrix products  32.4 us (4%)
    ppermute x2, waiting for transfers between devices, to_encoder(): return lax.ppermute(value, 'section', [(DECODER, ENCODER)])  138 us
    ppermute x13, waiting for transfers between devices, across(): return lax.ppermute(value, 'tensor', [(0, 2), (1, 3), (2, 0), (3, 1)])  88 us
    pallas_call x2, Pallas kernels, self_backward(): pl.pallas_call(functools.partial(self_backward_kernel, has_sum), out_shap...  56.8 us
    ppermute x7, waiting for transfers between devices, total_over_sequences(): return jnp.where(inner, value, lax.ppermute(value, 'dp', [(1, 0), (2, 3)]))  46.6 us
    ppermute x7, waiting for transfers between devices, across_in(): lax.ppermute(value, ('section', 'tensor'), [(role * 4 + a, role * 4 + b)...  35.4 us
    ppermute x7, starting transfers between devices, total_over_sequences(): value = value + lax.ppermute(value, 'dp', [(0, 1), (3, 2)])  33.6 us
    pallas_call x2, Pallas kernels, self_forward(): pl.pallas_call(functools.partial(self_forward_kernel, has_sum), out_shape...  32.2 us
    dot_general x20, matrix products, rows_product(): return lax.dot_general(left, right, TN, preferred_element_type=F32)  30.3 us
  transfers between devices with their start and end apart: 57, of which 20 were waited for; matrix products, arithmetic and copies ran while one was open for 12% of the time, Pallas kernels for 20%

profile of v2, /device:TPU:0, one launch (start us, length us, event | category | flops | bytes accessed | tf_op | source)
XLA Modules:
  0.0 764.0 jit_solution(3268263759425287850)
XLA Ops:
  2.7 2.9 collective-permute-start
  7.8 7.8 %collective-permute-done.far = bf16[256,768]{1,0:T(8,128)(2,1)S(1)} collective-permute-done((bf16[256,768]{1,0:T(8,128)(2,1)S(1)}, bf16[256,768]{1,0:T(8,128)(2,1)S(1)}, u32[]{:S(2)}, u32[]{:S(2)}) %collective-permute-start) | collective-permute-done | bytes 393248 | tf_op jit(solution)/shard_map/ppermute | solution.py:747
  21.1 19.1 %collective-permute-done.4 = f32[320,3]{0,1:T(4,128)S(1)} collective-permute-done((f32[320,3]{0,1:T(4,128)S(1)}, f32[320,3]{0,1:T(4,128)S(1)}, u32[]{:S(2)}, u32[]{:S(2)}) %collective-permute-start.4) | collective-permute-done | bytes 3872 | tf_op jit(solution)/shard_map/ppermute | solution.py:747
  41.8 3.3 shard_map.187.table
  45.1 3.3 shard_map.188.table
  50.8 3.7 shard_map.186
  54.4 15.9 %shard_map.189 = (f32[1024,768]{1,0:T(8,128)}, bf16[3,1024,192]{2,1,0:T(8,128)(2,1)}, bf16[1024,192]{1,0:T(8,128)(2,1)}, f32[1024,128]{1,0:T(8,128)}) custom-call(s32[8]{0:T(128)} %stack.134.info, bf16[1024,768]{1,0:T(8,128)(2,1)} %get-tuple-element.79.normed, bf16[3,768,192]{2,1,0:T(8,128)(2,1)} %bitcast.163, bf16[192,768]{1,0:T(8,128)(2,1)} %bitcast.184, ...), custom_call_target="tpu_custom_call" | custom-call | flops 4429185024 | bytes 6291456 | tf_op jit(solution)/shard_map/pallas_call | solution.py:216
  70.3 16.3 %shard_map.190 = (bf16[1024,768]{1,0:T(8,128)(2,1)}, bf16[3,1024,192]{2,1,0:T(8,128)(2,1)}, bf16[1024,192]{1,0:T(8,128)(2,1)}, f32[1024,128]{1,0:T(8,128)}) custom-call(s32[8]{0:T(128)} %stack.134.info, bf16[1024,768]{1,0:T(8,128)(2,1)} %get-tuple-element.79.normed, bf16[3,768,192]{2,1,0:T(8,128)(2,1)} %copy.26.weights, ...), custom_call_target="tpu_custom_call" | custom-call | flops 4429185024 | bytes 6291456 | tf_op jit(solution)/shard_map/pallas_call | solution.py:216
  86.6 3.6 collective-permute-start.6
  90.3 2.4 collective-permute-start.7
  93.9 5.1 shard_map.191
  99.0 7.7 %shard_map.192 = (f32[1024,768]{1,0:T(8,128)}, bf16[1024,768]{1,0:T(8,128)(2,1)}, f32[1024,768]{1,0:T(8,128)}) custom-call(s32[8]{0:T(128)} %stack.134.info, bf16[1024,768]{1,0:T(8,128)(2,1)} %get-tuple-element.83.normed, bf16[768,768]{1,0:T(8,128)(2,1)} %bitcast.174, bf16[768,768]{1,0:T(8,128)(2,1)} %bitcast.180), custom_call_target="tpu_custom_call" | custom-call | flops 2415919104 | bytes 9437184 | tf_op jit(solution)/shard_map/pallas_call | solution.py:637
  106.7 10.5 %collective-permute-done.6.up = bf16[768,768]{1,0:T(8,128)(2,1)S(1)} collective-permute-done((bf16[768,768]{1,0:T(8,128)(2,1)S(1)}, bf16[768,768]{1,0:T(8,128)(2,1)S(1)}, u32[]{:S(2)}, u32[]{:S(2)}) %collective-permute-start.6) | collective-permute-done | bytes 1179680 | tf_op jit(solution)/shard_map/ppermute | solution.py:752
  117.3 24.9 %collective-permute-done.7.down = bf16[768,768]{1,0:T(8,128)(2,1)S(1)} collective-permute-done((bf16[768,768]{1,0:T(8,128)(2,1)}, bf16[768,768]{1,0:T(8,128)(2,1)S(1)}, u32[]{:S(2)}, u32[]{:S(2)}) %collective-permute-start.7) | collective-permute-done | bytes 1179680 | tf_op jit(solution)/shard_map/ppermute | solution.py:752
  143.2 8.2 %shard_map.193 = (bf16[1024,768]{1,0:T(8,128)(2,1)}, bf16[1024,768]{1,0:T(8,128)(2,1)}, f32[1024,768]{1,0:T(8,128)}) custom-call(s32[8]{0:T(128)} %stack.134.info, bf16[1024,768]{1,0:T(8,128)(2,1)} %get-tuple-element.83.normed, bf16[768,768]{1,0:T(8,128)(2,1)} %copy-done.18, bf16[768,768]{1,0:T(8,128)(2,1)} %copy-done.19, f32[1024,768]{1,0:T(8,128)} %get-tuple-element.84.refs_0_), custom_call_target="tpu_custom_call" | custom-call | flops 2415919104 | bytes 9437184 | tf_op jit(solution)/shard_map/pallas_call | solution.py:637
  151.4 3.6 collective-permute-done.8.far
  156.2 5.9 shard_map.194
  166.0 16.5 %collective-permute-done.9.near = bf16[512,768]{1,0:T(8,128)(2,1)S(1)} collective-permute-done((bf16[512,768]{1,0:T(8,128)(2,1)S(1)}, bf16[512,768]{1,0:T(8,128)(2,1)S(1)}, u32[]{:S(2)}, u32[]{:S(2)}) %collective-permute-start.9) | collective-permute-done | bytes 786464 | tf_op jit(solution)/shard_map/ppermute | solution.py:762
  183.2 11.5 %collective-permute-done.12 = bf16[2,768,192]{1,2,0:T(8,128)(2,1)S(1)} collective-permute-done((bf16[2,768,192]{1,2,0:T(8,128)(2,1)S(1)}, bf16[2,768,192]{1,2,0:T(8,128)(2,1)S(1)}, u32[]{:S(2)}, u32[]{:S(2)}) %collective-permute-start.12) | collective-permute-done | bytes 589856 | tf_op jit(solution)/shard_map/ppermute | solution.py:762
  200.0 4.8 shard_map.195
  204.8 5.4 shard_map.196
  212.9 9.8 %collective-permute-done.15.far = bf16[256,768]{1,0:T(8,128)(2,1)S(1)} collective-permute-done((bf16[256,768]{1,0:T(8,128)(2,1)S(1)}, bf16[256,768]{1,0:T(8,128)(2,1)S(1)}, u32[]{:S(2)}, u32[]{:S(2)}) %collective-permute-start.15) | collective-permute-done | bytes 393248 | tf_op jit(solution)/shard_map/ppermute | solution.py:747
  226.6 2.9 shard_map.198.cot.residual
  230.6 5.3 shard_map.197
  236.0 7.2 shard_map.199
  244.2 7.9 %shard_map.200 = (bf16[1024,768]{1,0:T(8,128)(2,1)}, bf16[1024,768]{1,0:T(8,128)(2,1)}, bf16[1024,768]{1,0:T(8,128)(2,1)}, bf16[1024,768]{1,0:T(8,128)(2,1)}) custom-call(s32[8]{0:T(128)} %stack.134.info, bf16[1024,768]{1,0:T(8,128)(2,1)} %get-tuple-element.90.normed, bf16[1024,768]{1,0:T(8,128)(2,1)} %shard_map.198.cot.residual, ...), custom_call_target="tpu_custom_call" | custom-call | flops 4831838208 | bytes 12582912 | tf_op jit(solution)/shard_map/pallas_call | solution.py:683
  252.7 3.2 collective-permute-done.21.far
  257.0 6.9 shard_map.202
  264.0 5.7 shard_map.203
  269.7 6.7 shard_map.204
  282.1 2.2 fusion.10
  286.8 2.2 convolution_bitcast_fusion.2
  294.8 119.5 %collective-permute-done.23 = bf16[512,768]{1,0:T(8,128)(2,1)S(1)} collective-permute-done((bf16[512,768]{1,0:T(8,128)(2,1)S(1)}, bf16[512,768]{1,0:T(8,128)(2,1)S(1)}, u32[]{:S(2)}, u32[]{:S(2)}) %collective-permute-start.23) | collective-permute-done | bytes 786464 | tf_op jit(solution)/shard_map/ppermute | solution.py:766
  414.8 18.6 %collective-permute-done.45 = bf16[2,768,192]{1,2,0:T(8,128)(2,1)} collective-permute-done((bf16[2,768,192]{1,2,0:T(8,128)(2,1)S(1)}, bf16[2,768,192]{1,2,0:T(8,128)(2,1)}, u32[]{:S(2)}, u32[]{:S(2)}) %collective-permute-start.45) | collective-permute-done | bytes 589856 | tf_op jit(solution)/shard_map/ppermute | solution.py:766
  434.5 3.8 collective-permute-start.46
  440.1 7.8 %shard_map.205 = (f32[1024,768]{1,0:T(8,128)}, bf16[1024,768]{1,0:T(8,128)(2,1)}, f32[2,768]{1,0:T(2,128)}) custom-call(s32[8]{0:T(128)} %stack.134.info, bf16[1024,768]{1,0:T(8,128)(2,1)} %shard_map.198.cot.residual, bf16[1024,768]{1,0:T(8,128)(2,1)} %maximum_select_fusion.returned, f32[1024,768]{1,0:T(8,128)} %get-tuple-element.107.values, ...), custom_call_target="tpu_custom_call" | custom-call | flops 15728640 | bytes 14155776 | tf_op jit(solution)/shard_map/pallas_call | solution.py:597
  448.0 8.2 %shard_map.206 = (f32[1024,768]{1,0:T(8,128)}, bf16[1024,768]{1,0:T(8,128)(2,1)}) custom-call(s32[8]{0:T(128)} %stack.134.info, bf16[1024,768]{1,0:T(8,128)(2,1)} %get-tuple-element.111.above, f32[1024,768]{1,0:T(8,128)} %get-tuple-element.114.slope, bf16[768,768]{1,0:T(8,128)(2,1)} %bitcast.176, bf16[768,768]{1,0:T(8,128)(2,1)} %bitcast.182, ...), custom_call_target="tpu_custom_call" | custom-call | flops 2415919104 | bytes 9437184 | tf_op jit(solution)/shard_map/pallas_call | solution.py:727
  456.2 9.0 %shard_map.207 = (bf16[1024,768]{1,0:T(8,128)(2,1)}, bf16[1024,768]{1,0:T(8,128)(2,1)}) custom-call(s32[8]{0:T(128)} %stack.134.info, bf16[1024,768]{1,0:T(8,128)(2,1)} %get-tuple-element.111.above, f32[1024,768]{1,0:T(8,128)} %get-tuple-element.112.slope, bf16[768,768]{1,0:T(8,128)(2,1)} %copy-done.18, bf16[768,768]{1,0:T(8,128)(2,1)} %copy-done.19, ...), custom_call_target="tpu_custom_call" | custom-call | flops 2415919104 | bytes 9437184 | tf_op jit(solution)/shard_map/pallas_call | solution.py:727
  465.3 4.6 convolution_convert_fusion.1
  471.4 2.5 convolution_convert_fusion
  475.3 4.8 shard_map.201
  480.2 2.2 dynamic-slice_bitcast_fusion.1
  484.9 14.2 %collective-permute-done.49 = bf16[768,768]{1,0:T(8,128)(2,1)} collective-permute-done((bf16[768,768]{1,0:T(8,128)(2,1)}, bf16[768,768]{1,0:T(8,128)(2,1)}, u32[]{:S(2)}, u32[]{:S(2)}) %collective-permute-start.49) | collective-permute-done | bytes 1179680 | tf_op jit(solution)/shard_map/ppermute | solution.py:747
  499.1 3.4 add_convert_fusion.1
  502.5 2.3 collective-permute-start.50
  504.9 19.5 %collective-permute-done.53 = bf16[768,768]{1,0:T(8,128)(2,1)} collective-permute-done((bf16[768,768]{1,0:T(8,128)(2,1)}, bf16[768,768]{1,0:T(8,128)(2,1)}, u32[]{:S(2)}, u32[]{:S(2)}) %collective-permute-start.53) | collective-permute-done | bytes 1179680 | tf_op jit(solution)/shard_map/ppermute | solution.py:747
  524.4 2.7 add_convert_fusion
  527.1 7.7 %shard_map.208 = (f32[1024,768]{1,0:T(8,128)}, bf16[1024,768]{1,0:T(8,128)(2,1)}, f32[2,768]{1,0:T(2,128)}) custom-call(f32[1024,768]{1,0:T(8,128)} %get-tuple-element.110.residual, bf16[1024,768]{1,0:T(8,128)(2,1)} %get-tuple-element.118.near, bf16[1024,768]{1,0:T(8,128)(2,1)} %collective-permute-done.25.far, f32[1024,768]{1,0:T(8,128)} %get-tuple-element.82.stream.values, ...), custom_call_target="tpu_custom_call" | custom-call | flops 15728640 | bytes 14155776 | tf_op jit(solution)/shard_map/pallas_call | solution.py:557
  534.8 27.8 %shard_map.209 = (f32[1024,768]{1,0:T(8,128)}, bf16[3,1024,192]{2,1,0:T(8,128)(2,1)}, f32[3,2048]{1,0:T(4,128)}) custom-call(s32[8]{0:T(128)} %stack.134.info, bf16[3,1024,192]{2,1,0:T(8,128)(2,1)} %get-tuple-element.123.qkv, f32[1024,128]{1,0:T(8,128)} %get-tuple-element.124.lse, bf16[1024,768]{1,0:T(8,128)(2,1)} %get-tuple-element.122.above, ...), custom_call_target="tpu_custom_call" | custom-call | flops 9261023232 | bytes 6291456 | tf_op jit(solution)/shard_map/pallas_call | solution.py:362
  562.7 29.0 %shard_map.210 = (bf16[1024,768]{1,0:T(8,128)(2,1)}, bf16[3,1024,192]{2,1,0:T(8,128)(2,1)}, f32[3,2048]{1,0:T(4,128)}) custom-call(s32[8]{0:T(128)} %stack.134.info, bf16[3,1024,192]{2,1,0:T(8,128)(2,1)} %get-tuple-element.120.qkv, f32[1024,128]{1,0:T(8,128)} %get-tuple-element.121.lse, bf16[1024,768]{1,0:T(8,128)(2,1)} %get-tuple-element.122.above, ...), custom_call_target="tpu_custom_call" | custom-call | flops 9261023232 | bytes 6291456 | tf_op jit(solution)/shard_map/pallas_call | solution.py:362
  603.4 17.5 %collective-permute-done.40 = bf16[192,768]{1,0:T(8,128)(2,1)S(1)} collective-permute-done((bf16[192,768]{1,0:T(8,128)(2,1)S(1)}, bf16[192,768]{1,0:T(8,128)(2,1)S(1)}, u32[]{:S(2)}, u32[]{:S(2)}) %collective-permute-start.40) | collective-permute-done | bytes 294944 | tf_op jit(solution)/shard_map/ppermute | solution.py:747
  625.3 5.3 collective-permute-start.41
  631.9 2.2 collective-permute-start.37
  635.6 2.5 collective-permute-done.41
  649.8 2.2 bitcast_convert_fusion.3
  655.4 7.1 shard_map.211
  665.2 2.9 fusion.68
  668.0 14.2 %collective-permute-done.31 = f32[320,3]{0,1:T(4,128)S(1)} collective-permute-done((f32[320,3]{0,1:T(4,128)S(1)}, f32[320,3]{0,1:T(4,128)S(1)}, u32[]{:S(2)}, u32[]{:S(2)}) %collective-permute-start.31) | collective-permute-done | bytes 3872 | tf_op jit(solution)/shard_map/ppermute | solution.py:776
  684.4 16.6 %collective-permute-start.33 = (f32[8,768]{1,0:T(8,128)S(1)}, f32[8,768]{1,0:T(8,128)S(1)}, u32[]{:S(2)}, u32[]{:S(2)}) collective-permute-start(f32[8,768]{1,0:T(8,128)S(1)} %add.115), channel_id=1, source_target_pairs={{0,4},{12,8},{1,5},{13,9},{2,6},{14,10},{3,7},{15,11},{16,20},{28,... | collective-permute-start | bytes 73736 | tf_op jit(solution)/shard_map/ppermute | solution.py:774
  715.4 18.5 %collective-permute-done.35 = f32[8,768]{1,0:T(8,128)S(1)} collective-permute-done((f32[8,768]{1,0:T(8,128)S(1)}, f32[8,768]{1,0:T(8,128)S(1)}, u32[]{:S(2)}, u32[]{:S(2)}) %collective-permute-start.35) | collective-permute-done | bytes 24608 | tf_op jit(solution)/shard_map/ppermute | solution.py:776
  741.7 2.8 bitcast_convert_fusion.1
  744.5 7.4 collective-permute-done.56
  751.9 2.8 bitcast_convert_fusion
  754.8 6.5 collective-permute-done.39
  (271 shorter events, 120.0 us)
Async XLA Ops:
  2.7 12.9 %collective-permute-start = (bf16[256,768]{1,0:T(8,128)(2,1)S(1)}, bf16[256,768]{1,0:T(8,128)(2,1)S(1)}, u32[]{:S(2)}, u32[]{:S(2)}) collective-permute-start(bf16[256,768]{1,0:T(8,128)(2,1)S(1)} %get-tuple-element.176), channel_id=1, source_target_pairs={{0,2},{1,3},{2,0},{3,1},{4,6},{5,7},{6,4},{7,5},{8,10},{9,11},{10,... | collective-permute-start | bytes 1179656 | tf_op jit(solution)/shard_map/ppermute | solution.py:747
  5.7 42.7 %collective-permute-start.2 = (bf16[3,768,192]{1,2,0:T(8,128)(2,1)S(1)}, bf16[3,768,192]{1,2,0:T(8,128)(2,1)S(1)}, u32[]{:S(2)}, u32[]{:S(2)}) collective-permute-start(bf16[3,768,192]{1,2,0:T(8,128)(2,1)S(1)} %bitcast.165), channel_id=1, source_target_pairs={{0,2},{1,3},{2,0},{3,1},{4,6},{5,7},{6,4},{7,5},{8,10},{9,11},{10,... | collective-permute-start | bytes 2654216 | tf_op jit(solution)/shard_map/ppermute | solution.py:747
  5.7 64.6 %collective-permute-start.3 = (bf16[192,768]{1,0:T(8,128)(2,1)S(1)}, bf16[192,768]{1,0:T(8,128)(2,1)}, u32[]{:S(2)}, u32[]{:S(2)}) collective-permute-start(bf16[192,768]{1,0:T(8,128)(2,1)S(1)} %bitcast.186), channel_id=1, source_target_pairs={{0,2},{1,3},{2,0},{3,1},{4,6},{5,7},{6,4},{7,5},{8,10},{9,11},{10,... | collective-permute-start | bytes 884744 | tf_op jit(solution)/shard_map/ppermute | solution.py:747
  7.7 32.5 %collective-permute-start.4 = (f32[320,3]{0,1:T(4,128)S(1)}, f32[320,3]{0,1:T(4,128)S(1)}, u32[]{:S(2)}, u32[]{:S(2)}) collective-permute-start(f32[320,3]{0,1:T(4,128)S(1)} %bitcast.172), channel_id=1, source_target_pairs={{0,2},{1,3},{2,0},{3,1},{4,6},{5,7},{6,4},{7,5},{8,10},{9,11},{10,... | collective-permute-start | bytes 11528 | tf_op jit(solution)/shard_map/ppermute | solution.py:747
  16.6 33.3 %collective-permute-start.1 = (bf16[2,256,768]{2,1,0:T(8,128)(2,1)}, bf16[2,256,768]{2,1,0:T(8,128)(2,1)S(1)}, u32[]{:S(2)}, u32[]{:S(2)}) collective-permute-start(bf16[2,256,768]{2,1,0:T(8,128)(2,1)} %pad_maximum_fusion.2), channel_id=1, source_target_pairs={{0,1},{1,0},{2,3},{3,2},{4,5},{5,4},{6,7},{7,6},{8,9},{9,8},{10,11... | collective-permute-start | bytes 2359304 | tf_op jit(solution)/shard_map/ppermute | solution.py:758
  86.6 6.1 collective-permute-start.5
  86.6 30.7 %collective-permute-start.6 = (bf16[768,768]{1,0:T(8,128)(2,1)S(1)}, bf16[768,768]{1,0:T(8,128)(2,1)S(1)}, u32[]{:S(2)}, u32[]{:S(2)}) collective-permute-start(bf16[768,768]{1,0:T(8,128)(2,1)S(1)} %bitcast.177), channel_id=1, source_target_pairs={{0,2},{1,3},{2,0},{3,1},{4,6},{5,7},{6,4},{7,5},{8,10},{9,11},{10,... | collective-permute-start | bytes 3538952 | tf_op jit(solution)/shard_map/ppermute | solution.py:752
  90.3 51.9 %collective-permute-start.7 = (bf16[768,768]{1,0:T(8,128)(2,1)}, bf16[768,768]{1,0:T(8,128)(2,1)S(1)}, u32[]{:S(2)}, u32[]{:S(2)}) collective-permute-start(bf16[768,768]{1,0:T(8,128)(2,1)} %bitcast.179), channel_id=1, source_target_pairs={{0,2},{1,3},{2,0},{3,1},{4,6},{5,7},{6,4},{7,5},{8,10},{9,11},{10,... | collective-permute-start | bytes 3538952 | tf_op jit(solution)/shard_map/ppermute | solution.py:752
  151.4 3.6 collective-permute-start.8
  163.3 19.1 %collective-permute-start.9 = (bf16[512,768]{1,0:T(8,128)(2,1)S(1)}, bf16[512,768]{1,0:T(8,128)(2,1)S(1)}, u32[]{:S(2)}, u32[]{:S(2)}) collective-permute-start(bf16[512,768]{1,0:T(8,128)(2,1)S(1)} %constant_dynamic-slice_fusion.2), channel_id=1, source_target_pairs={{0,16},{1,17},{2,18},{3,19},{4,20},{5,21},{6,22},{7,23},{8,24},{9,... | collective-permute-start | bytes 2359304 | tf_op jit(solution)/shard_map/ppermute | solution.py:762
  164.7 29.9 %collective-permute-start.12 = (bf16[2,768,192]{1,2,0:T(8,128)(2,1)S(1)}, bf16[2,768,192]{1,2,0:T(8,128)(2,1)S(1)}, u32[]{:S(2)}, u32[]{:S(2)}) collective-permute-start(bf16[2,768,192]{1,2,0:T(8,128)(2,1)S(1)} %bitcast.168), channel_id=1, source_target_pairs={{0,16},{1,17},{2,18},{3,19},{4,20},{5,21},{6,22},{7,23},{8,24},{9,... | collective-permute-start | bytes 1769480 | tf_op jit(solution)/shard_map/ppermute | solution.py:762
  182.5 17.5 %collective-permute-start.10 = (bf16[512,768]{1,0:T(8,128)(2,1)S(1)}, bf16[512,768]{1,0:T(8,128)(2,1)}, u32[]{:S(2)}, u32[]{:S(2)}) collective-permute-start(bf16[512,768]{1,0:T(8,128)(2,1)S(1)} %collective-permute-done.9.near), channel_id=1, source_target_pairs={{0,1},{1,0},{2,3},{3,2},{4,5},{5,4},{6,7},{7,6},{8,9},{9,8},{10,11... | collective-permute-start | bytes 2359304 | tf_op jit(solution)/shard_map/ppermute | solution.py:758
  182.5 15.2 %collective-permute-start.11 = (bf16[2,768,192]{1,2,0:T(8,128)(2,1)S(1)}, bf16[2,768,192]{1,2,0:T(8,128)(2,1)S(1)}, u32[]{:S(2)}, u32[]{:S(2)}) collective-permute-start(bf16[2,768,192]{1,2,0:T(8,128)(2,1)S(1)} %bitcast.169), channel_id=1, source_target_pairs={{16,18},{17,19},{18,16},{19,17},{20,22},{21,23},{22,20},{23,21},{2... | collective-permute-start | bytes 1769480 | tf_op jit(solution)/shard_map/ppermute | solution.py:752
  194.7 4.2 collective-permute-start.13
  210.2 19.3 %collective-permute-start.14 = (bf16[1024,768]{1,0:T(8,128)(2,1)}, bf16[1024,768]{1,0:T(8,128)(2,1)S(1)}, u32[]{:S(2)}, u32[]{:S(2)}) collective-permute-start(bf16[1024,768]{1,0:T(8,128)(2,1)} %get-tuple-element.88.near), channel_id=1, source_target_pairs={{0,1},{1,0},{2,3},{3,2},{4,5},{5,4},{6,7},{7,6},{8,9},{9,8},{10,11... | collective-permute-start | bytes 4718600 | tf_op jit(solution)/shard_map/ppermute | solution.py:758
  211.1 11.5 %collective-permute-start.15 = (bf16[256,768]{1,0:T(8,128)(2,1)S(1)}, bf16[256,768]{1,0:T(8,128)(2,1)S(1)}, u32[]{:S(2)}, u32[]{:S(2)}) collective-permute-start(bf16[256,768]{1,0:T(8,128)(2,1)S(1)} %get-tuple-element.171), channel_id=1, source_target_pairs={{0,2},{1,3},{2,0},{3,1},{4,6},{5,7},{6,4},{7,5},{8,10},{9,11},{10,... | collective-permute-start | bytes 1179656 | tf_op jit(solution)/shard_map/ppermute | solution.py:747
  222.7 2.9 collective-permute-start.16
  222.8 20.4 %collective-permute-start.17 = (bf16[768,768]{1,0:T(8,128)(2,1)S(1)}, bf16[768,768]{1,0:T(8,128)(2,1)S(1)}, u32[]{:S(2)}, u32[]{:S(2)}) collective-permute-start(bf16[768,768]{1,0:T(8,128)(2,1)S(1)} %bitcast.178), channel_id=1, source_target_pairs={{16,18},{17,19},{18,16},{19,17},{20,22},{21,23},{22,20},{23,21},{2... | collective-permute-start | bytes 3538952 | tf_op jit(solution)/shard_map/ppermute | solution.py:752
  223.5 19.7 %collective-permute-start.18 = (bf16[768,768]{1,0:T(8,128)(2,1)S(1)}, bf16[768,768]{1,0:T(8,128)(2,1)}, u32[]{:S(2)}, u32[]{:S(2)}) collective-permute-start(bf16[768,768]{1,0:T(8,128)(2,1)S(1)} %bitcast.183), channel_id=1, source_target_pairs={{16,18},{17,19},{18,16},{19,17},{20,22},{21,23},{22,20},{23,21},{2... | collective-permute-start | bytes 3538952 | tf_op jit(solution)/shard_map/ppermute | solution.py:752
  252.2 3.8 collective-permute-start.21
  277.7 11.2 %collective-permute-start.22 = (bf16[512,768]{1,0:T(8,128)(2,1)S(1)}, bf16[512,768]{1,0:T(8,128)(2,1)S(1)}, u32[]{:S(2)}, u32[]{:S(2)}) collective-permute-start(bf16[512,768]{1,0:T(8,128)(2,1)S(1)} %constant_dynamic-slice_fusion), channel_id=1, source_target_pairs={{0,1},{1,0},{2,3},{3,2},{4,5},{5,4},{6,7},{7,6},{8,9},{9,8},{10,11... | collective-permute-start | bytes 2359304 | tf_op jit(solution)/shard_map/ppermute | solution.py:758
  285.0 8.1 %collective-permute-start.44 = (bf16[4,768,192]{1,2,0:T(8,128)(2,1)S(1)}, bf16[4,768,192]{1,2,0:T(8,128)(2,1)S(1)}, u32[]{:S(2)}, u32[]{:S(2)}) collective-permute-start(bf16[4,768,192]{1,2,0:T(8,128)(2,1)S(1)} %pad_maximum_fusion), channel_id=1, source_target_pairs={{16,18},{17,19},{18,16},{19,17},{20,22},{21,23},{22,20},{23,21},{2... | collective-permute-start | bytes 3538952 | tf_op jit(solution)/shard_map/ppermute | solution.py:752
  289.2 125.1 %collective-permute-start.23 = (bf16[512,768]{1,0:T(8,128)(2,1)S(1)}, bf16[512,768]{1,0:T(8,128)(2,1)S(1)}, u32[]{:S(2)}, u32[]{:S(2)}) collective-permute-start(bf16[512,768]{1,0:T(8,128)(2,1)S(1)} %add_convert_fusion.2), channel_id=1, source_target_pairs={{16,0},{17,1},{18,2},{19,3},{20,4},{21,5},{22,6},{23,7},{24,8},{25... | collective-permute-start | bytes 2359304 | tf_op jit(solution)/shard_map/ppermute | solution.py:766
  293.5 139.9 %collective-permute-start.45 = (bf16[2,768,192]{1,2,0:T(8,128)(2,1)S(1)}, bf16[2,768,192]{1,2,0:T(8,128)(2,1)}, u32[]{:S(2)}, u32[]{:S(2)}) collective-permute-start(bf16[2,768,192]{1,2,0:T(8,128)(2,1)S(1)} %slice.131), channel_id=1, source_target_pairs={{16,0},{17,1},{18,2},{19,3},{20,4},{21,5},{22,6},{23,7},{24,8},{25... | collective-permute-start | bytes 1769480 | tf_op jit(solution)/shard_map/ppermute | solution.py:766
  414.3 24.0 %collective-permute-start.24 = (bf16[512,768]{1,0:T(8,128)(2,1)S(1)}, bf16[512,768]{1,0:T(8,128)(2,1)S(1)}, u32[]{:S(2)}, u32[]{:S(2)}) collective-permute-start(bf16[512,768]{1,0:T(8,128)(2,1)S(1)} %collective-permute-done.23), channel_id=1, source_target_pairs={{0,1},{1,0},{2,3},{3,2},{4,5},{5,4},{6,7},{7,6},{8,9},{9,8},{10,11... | collective-permute-start | bytes 2359304 | tf_op jit(solution)/shard_map/ppermute | solution.py:758
  414.3 61.0 %collective-permute-start.19 = (bf16[1024,768]{1,0:T(8,128)(2,1)}, bf16[1024,768]{1,0:T(8,128)(2,1)}, u32[]{:S(2)}, u32[]{:S(2)}) collective-permute-start(bf16[1024,768]{1,0:T(8,128)(2,1)} %get-tuple-element.95.near), channel_id=1, source_target_pairs={{0,1},{1,0},{2,3},{3,2},{4,5},{5,4},{6,7},{7,6},{8,9},{9,8},{10,11... | collective-permute-start | bytes 4718600 | tf_op jit(solution)/shard_map/ppermute | solution.py:758
  434.5 39.9 %collective-permute-start.46 = (bf16[2,768,192]{1,2,0:T(8,128)(2,1)S(1)}, bf16[2,768,192]{1,2,0:T(8,128)(2,1)S(1)}, u32[]{:S(2)}, u32[]{:S(2)}) collective-permute-start(bf16[2,768,192]{1,2,0:T(8,128)(2,1)S(1)} %slice_select_fusion), channel_id=1, source_target_pairs={{0,4},{12,8},{1,5},{13,9},{2,6},{14,10},{3,7},{15,11},{16,20},{28,... | collective-permute-start | bytes 1769480 | tf_op jit(solution)/shard_map/ppermute | solution.py:774
  469.9 29.2 %collective-permute-start.49 = (bf16[768,768]{1,0:T(8,128)(2,1)}, bf16[768,768]{1,0:T(8,128)(2,1)}, u32[]{:S(2)}, u32[]{:S(2)}) collective-permute-start(bf16[768,768]{1,0:T(8,128)(2,1)} %convolution_convert_fusion.1), channel_id=1, source_target_pairs={{0,2},{1,3},{2,0},{3,1},{4,6},{5,7},{6,4},{7,5},{8,10},{9,11},{10,... | collective-permute-start | bytes 3538952 | tf_op jit(solution)/shard_map/ppermute | solution.py:747
  473.9 50.5 %collective-permute-start.53 = (bf16[768,768]{1,0:T(8,128)(2,1)}, bf16[768,768]{1,0:T(8,128)(2,1)}, u32[]{:S(2)}, u32[]{:S(2)}) collective-permute-start(bf16[768,768]{1,0:T(8,128)(2,1)} %convolution_convert_fusion), channel_id=1, source_target_pairs={{0,2},{1,3},{2,0},{3,1},{4,6},{5,7},{6,4},{7,5},{8,10},{9,11},{10,... | collective-permute-start | bytes 3538952 | tf_op jit(solution)/shard_map/ppermute | solution.py:747
  474.5 9.4 %collective-permute-start.47 = (bf16[2,768,192]{1,2,0:T(8,128)(2,1)S(1)}, bf16[2,768,192]{1,2,0:T(8,128)(2,1)S(1)}, u32[]{:S(2)}, u32[]{:S(2)}) collective-permute-start(bf16[2,768,192]{1,2,0:T(8,128)(2,1)S(1)} %add.125), channel_id=1, source_target_pairs={{4,8},{8,4},{5,9},{9,5},{6,10},{10,6},{7,11},{11,7},{20,24},{24,20... | collective-permute-start | bytes 1769480 | tf_op jit(solution)/shard_map/ppermute | solution.py:775
  475.2 51.9 %collective-permute-start.25 = (bf16[1024,768]{1,0:T(8,128)(2,1)}, bf16[1024,768]{1,0:T(8,128)(2,1)}, u32[]{:S(2)}, u32[]{:S(2)}) collective-permute-start(bf16[1024,768]{1,0:T(8,128)(2,1)} %get-tuple-element.118.near), channel_id=1, source_target_pairs={{0,1},{1,0},{2,3},{3,2},{4,5},{5,4},{6,7},{7,6},{8,9},{9,8},{10,11... | collective-permute-start | bytes 4718600 | tf_op jit(solution)/shard_map/ppermute | solution.py:758
  482.4 119.5 %collective-permute-start.20 = (bf16[256,768]{1,0:T(8,128)(2,1)}, bf16[256,768]{1,0:T(8,128)(2,1)}, u32[]{:S(2)}, u32[]{:S(2)}) collective-permute-start(bf16[256,768]{1,0:T(8,128)(2,1)} %get-tuple-element.167), channel_id=1, source_target_pairs={{0,2},{1,3},{2,0},{3,1},{4,6},{5,7},{6,4},{7,5},{8,10},{9,11},{10,... | collective-permute-start | bytes 1179656 | tf_op jit(solution)/shard_map/ppermute | solution.py:747
  499.1 25.3 %copy-start.14 = (bf16[1024,768]{1,0:T(8,128)(2,1)S(1)}, bf16[1024,768]{1,0:T(8,128)(2,1)}, u32[]{:S(2)}) copy-start(bf16[1024,768]{1,0:T(8,128)(2,1)} %get-tuple-element.111.above) | copy-start | bytes 4718596
  499.1 25.3 %copy-start.50 = (bf16[1024,768]{1,0:T(8,128)(2,1)S(1)}, bf16[1024,768]{1,0:T(8,128)(2,1)}, u32[]{:S(2)}) copy-start(bf16[1024,768]{1,0:T(8,128)(2,1)} %get-tuple-element.144) | copy-start | bytes 4718596
  502.5 129.3 %collective-permute-start.50 = (bf16[768,768]{1,0:T(8,128)(2,1)S(1)}, bf16[768,768]{1,0:T(8,128)(2,1)}, u32[]{:S(2)}, u32[]{:S(2)}) collective-permute-start(bf16[768,768]{1,0:T(8,128)(2,1)S(1)} %add_convert_fusion.1), channel_id=1, source_target_pairs={{0,4},{12,8},{1,5},{13,9},{2,6},{14,10},{3,7},{15,11},{16,20},{28,... | collective-permute-start | bytes 3538952 | tf_op jit(solution)/shard_map/ppermute | solution.py:774
  527.1 74.8 %copy-start.16 = (bf16[768,768]{1,0:T(8,128)(2,1)}, bf16[768,768]{1,0:T(8,128)(2,1)S(1)}, u32[]{:S(2)}) copy-start(bf16[768,768]{1,0:T(8,128)(2,1)S(1)} %add_convert_fusion) | copy-start | bytes 3538948
  562.7 29.0 %copy-start.30 = (bf16[1024,768]{1,0:T(8,128)(2,1)S(1)}, bf16[1024,768]{1,0:T(8,128)(2,1)}, u32[]{:S(2)}) copy-start(bf16[1024,768]{1,0:T(8,128)(2,1)} %get-tuple-element.79.normed) | copy-start | bytes 4718596
  595.9 7.4 collective-permute-start.28
  598.0 32.7 %copy-start.2 = (f32[1,768,192]{1,2,0:T(8,128)}, f32[1,768,192]{1,2,0:T(8,128)S(1)}, u32[]{:S(2)}) copy-start(f32[1,768,192]{1,2,0:T(8,128)S(1)} %convolution_bitcast_fusion.4) | copy-start | bytes 1769476
  598.1 27.2 %collective-permute-start.36 = (bf16[3,768,192]{1,2,0:T(8,128)(2,1)S(1)}, bf16[3,768,192]{1,2,0:T(8,128)(2,1)S(1)}, u32[]{:S(2)}, u32[]{:S(2)}) collective-permute-start(bf16[3,768,192]{1,2,0:T(8,128)(2,1)S(1)} %pad_maximum_fusion.1), channel_id=1, source_target_pairs={{0,2},{1,3},{2,0},{3,1},{4,6},{5,7},{6,4},{7,5},{8,10},{9,11},{10,... | collective-permute-start | bytes 2654216 | tf_op jit(solution)/shard_map/ppermute | solution.py:747
  600.2 20.7 %collective-permute-start.40 = (bf16[192,768]{1,0:T(8,128)(2,1)S(1)}, bf16[192,768]{1,0:T(8,128)(2,1)S(1)}, u32[]{:S(2)}, u32[]{:S(2)}) collective-permute-start(bf16[192,768]{1,0:T(8,128)(2,1)S(1)} %convolution_convert_fusion.6), channel_id=1, source_target_pairs={{0,2},{1,3},{2,0},{3,1},{4,6},{5,7},{6,4},{7,5},{8,10},{9,11},{10,... | collective-permute-start | bytes 884744 | tf_op jit(solution)/shard_map/ppermute | solution.py:747
  601.3 30.5 %copy-start.3 = (f32[1,768,192]{1,2,0:T(8,128)}, f32[1,768,192]{1,2,0:T(8,128)S(1)}, u32[]{:S(2)}) copy-start(f32[1,768,192]{1,2,0:T(8,128)S(1)} %convolution_bitcast_fusion.5) | copy-start | bytes 1769476
  601.8 33.8 %copy-start.4 = (f32[1,768,192]{1,2,0:T(8,128)}, f32[1,768,192]{1,2,0:T(8,128)S(1)}, u32[]{:S(2)}) copy-start(f32[1,768,192]{1,2,0:T(8,128)S(1)} %convolution_bitcast_fusion.6) | copy-start | bytes 1769476
  601.9 38.0 %collective-permute-start.54 = (bf16[768,768]{1,0:T(8,128)(2,1)S(1)}, bf16[768,768]{1,0:T(8,128)(2,1)S(1)}, u32[]{:S(2)}, u32[]{:S(2)}) collective-permute-start(bf16[768,768]{1,0:T(8,128)(2,1)S(1)} %add_convert_fusion), channel_id=1, source_target_pairs={{0,4},{12,8},{1,5},{13,9},{2,6},{14,10},{3,7},{15,11},{16,20},{28,... | collective-permute-start | bytes 3538952 | tf_op jit(solution)/shard_map/ppermute | solution.py:774
  603.3 50.8 %collective-permute-start.26 = (bf16[1024,768]{1,0:T(8,128)(2,1)}, bf16[1024,768]{1,0:T(8,128)(2,1)}, u32[]{:S(2)}, u32[]{:S(2)}) collective-permute-start(bf16[1024,768]{1,0:T(8,128)(2,1)} %get-tuple-element.126.near), channel_id=1, source_target_pairs={{0,1},{1,0},{2,3},{3,2},{4,5},{5,4},{6,7},{7,6},{8,9},{9,8},{10,11... | collective-permute-start | bytes 4718600 | tf_op jit(solution)/shard_map/ppermute | solution.py:758
  620.9 3.1 collective-permute-start.29
  624.0 21.3 %collective-permute-start.48 = (bf16[2,768,192]{1,2,0:T(8,128)(2,1)}, bf16[2,768,192]{1,2,0:T(8,128)(2,1)}, u32[]{:S(2)}, u32[]{:S(2)}) collective-permute-start(bf16[2,768,192]{1,2,0:T(8,128)(2,1)} %add.126), channel_id=1, source_target_pairs={{4,0},{8,12},{5,1},{9,13},{6,2},{10,14},{7,3},{11,15},{20,16},{24,... | collective-permute-start | bytes 1769480 | tf_op jit(solution)/shard_map/ppermute | solution.py:776
  625.3 12.8 %collective-permute-start.41 = (bf16[192,768]{1,0:T(8,128)(2,1)S(1)}, bf16[192,768]{1,0:T(8,128)(2,1)S(1)}, u32[]{:S(2)}, u32[]{:S(2)}) collective-permute-start(bf16[192,768]{1,0:T(8,128)(2,1)S(1)} %fusion.6), channel_id=1, source_target_pairs={{0,4},{12,8},{1,5},{13,9},{2,6},{14,10},{3,7},{15,11},{16,20},{28,... | collective-permute-start | bytes 884744 | tf_op jit(solution)/shard_map/ppermute | solution.py:774
  631.9 32.1 %collective-permute-start.37 = (bf16[3,768,192]{1,2,0:T(8,128)(2,1)}, bf16[3,768,192]{1,2,0:T(8,128)(2,1)}, u32[]{:S(2)}, u32[]{:S(2)}) collective-permute-start(bf16[3,768,192]{1,2,0:T(8,128)(2,1)} %fusion.3), channel_id=1, source_target_pairs={{0,4},{12,8},{1,5},{13,9},{2,6},{14,10},{3,7},{15,11},{16,20},{28,... | collective-permute-start | bytes 2654216 | tf_op jit(solution)/shard_map/ppermute | solution.py:774
  638.1 62.8 %collective-permute-start.51 = (bf16[768,768]{1,0:T(8,128)(2,1)S(1)}, bf16[768,768]{1,0:T(8,128)(2,1)}, u32[]{:S(2)}, u32[]{:S(2)}) collective-permute-start(bf16[768,768]{1,0:T(8,128)(2,1)S(1)} %add.128), channel_id=1, source_target_pairs={{4,8},{8,4},{5,9},{9,5},{6,10},{10,6},{7,11},{11,7},{20,24},{24,20... | collective-permute-start | bytes 3538952 | tf_op jit(solution)/shard_map/ppermute | solution.py:775
  639.8 6.1 collective-permute-start.30
  645.3 6.7 collective-permute-start.42
  646.0 64.5 %collective-permute-start.55 = (bf16[768,768]{1,0:T(8,128)(2,1)S(1)}, bf16[768,768]{1,0:T(8,128)(2,1)}, u32[]{:S(2)}, u32[]{:S(2)}) collective-permute-start(bf16[768,768]{1,0:T(8,128)(2,1)S(1)} %add.131), channel_id=1, source_target_pairs={{4,8},{8,4},{5,9},{9,5},{6,10},{10,6},{7,11},{11,7},{20,24},{24,20... | collective-permute-start | bytes 3538952 | tf_op jit(solution)/shard_map/ppermute | solution.py:775
  652.0 30.2 %collective-permute-start.31 = (f32[320,3]{0,1:T(4,128)S(1)}, f32[320,3]{0,1:T(4,128)S(1)}, u32[]{:S(2)}, u32[]{:S(2)}) collective-permute-start(f32[320,3]{0,1:T(4,128)S(1)} %add.114), channel_id=1, source_target_pairs={{4,0},{8,12},{5,1},{9,13},{6,2},{10,14},{7,3},{11,15},{20,16},{24,... | collective-permute-start | bytes 11528 | tf_op jit(solution)/shard_map/ppermute | solution.py:776
  654.1 49.7 %collective-permute-start.43 = (bf16[192,768]{1,0:T(8,128)(2,1)}, bf16[192,768]{1,0:T(8,128)(2,1)}, u32[]{:S(2)}, u32[]{:S(2)}) collective-permute-start(bf16[192,768]{1,0:T(8,128)(2,1)} %add.123), channel_id=1, source_target_pairs={{4,0},{8,12},{5,1},{9,13},{6,2},{10,14},{7,3},{11,15},{20,16},{24,... | collective-permute-start | bytes 884744 | tf_op jit(solution)/shard_map/ppermute | solution.py:776
  664.0 20.4 %collective-permute-start.32 = (f32[8,768]{1,0:T(8,128)S(1)}, f32[8,768]{1,0:T(8,128)S(1)}, u32[]{:S(2)}, u32[]{:S(2)}) collective-permute-start(f32[8,768]{1,0:T(8,128)S(1)} %concatenate.53), channel_id=1, source_target_pairs={{0,2},{1,3},{2,0},{3,1},{4,6},{5,7},{6,4},{7,5},{8,10},{9,11},{10,... | collective-permute-start | bytes 73736 | tf_op jit(solution)/shard_map/ppermute | solution.py:747
  682.2 54.2 %collective-permute-start.38 = (bf16[3,768,192]{1,2,0:T(8,128)(2,1)}, bf16[3,768,192]{1,2,0:T(8,128)(2,1)}, u32[]{:S(2)}, u32[]{:S(2)}) collective-permute-start(bf16[3,768,192]{1,2,0:T(8,128)(2,1)} %fusion.68), channel_id=1, source_target_pairs={{4,8},{8,4},{5,9},{9,5},{6,10},{10,6},{7,11},{11,7},{20,24},{24,20... | collective-permute-start | bytes 2654216 | tf_op jit(solution)/shard_map/ppermute | solution.py:775
  684.4 21.3 %collective-permute-start.33 = (f32[8,768]{1,0:T(8,128)S(1)}, f32[8,768]{1,0:T(8,128)S(1)}, u32[]{:S(2)}, u32[]{:S(2)}) collective-permute-start(f32[8,768]{1,0:T(8,128)S(1)} %add.115), channel_id=1, source_target_pairs={{0,4},{12,8},{1,5},{13,9},{2,6},{14,10},{3,7},{15,11},{16,20},{28,... | collective-permute-start | bytes 73736 | tf_op jit(solution)/shard_map/ppermute | solution.py:774
  702.5 39.2 %collective-permute-start.52 = (bf16[768,768]{1,0:T(8,128)(2,1)S(1)}, bf16[768,768]{1,0:T(8,128)(2,1)}, u32[]{:S(2)}, u32[]{:S(2)}) collective-permute-start(bf16[768,768]{1,0:T(8,128)(2,1)S(1)} %add.129), channel_id=1, source_target_pairs={{4,0},{8,12},{5,1},{9,13},{6,2},{10,14},{7,3},{11,15},{20,16},{24,... | collective-permute-start | bytes 3538952 | tf_op jit(solution)/shard_map/ppermute | solution.py:776
  705.7 3.5 collective-permute-start.34
  708.3 31.1 %collective-permute-start.27 = (bf16[256,768]{1,0:T(8,128)(2,1)}, bf16[256,768]{1,0:T(8,128)(2,1)}, u32[]{:S(2)}, u32[]{:S(2)}) collective-permute-start(bf16[256,768]{1,0:T(8,128)(2,1)} %dynamic-slice_convert_fusion), channel_id=1, source_target_pairs={{0,2},{1,3},{2,0},{3,1},{4,6},{5,7},{6,4},{7,5},{8,10},{9,11},{10,... | collective-permute-start | bytes 1179656 | tf_op jit(solution)/shard_map/ppermute | solution.py:747
  709.2 24.7 %collective-permute-start.35 = (f32[8,768]{1,0:T(8,128)S(1)}, f32[8,768]{1,0:T(8,128)S(1)}, u32[]{:S(2)}, u32[]{:S(2)}) collective-permute-start(f32[8,768]{1,0:T(8,128)S(1)} %add.117), channel_id=1, source_target_pairs={{4,0},{8,12},{5,1},{9,13},{6,2},{10,14},{7,3},{11,15},{20,16},{24,... | collective-permute-start | bytes 73736 | tf_op jit(solution)/shard_map/ppermute | solution.py:776
  712.0 39.9 %collective-permute-start.56 = (bf16[768,768]{1,0:T(8,128)(2,1)S(1)}, bf16[768,768]{1,0:T(8,128)(2,1)}, u32[]{:S(2)}, u32[]{:S(2)}) collective-permute-start(bf16[768,768]{1,0:T(8,128)(2,1)S(1)} %add.132), channel_id=1, source_target_pairs={{4,0},{8,12},{5,1},{9,13},{6,2},{10,14},{7,3},{11,15},{20,16},{24,... | collective-permute-start | bytes 3538952 | tf_op jit(solution)/shard_map/ppermute | solution.py:776
  738.1 23.2 %collective-permute-start.39 = (bf16[3,768,192]{1,2,0:T(8,128)(2,1)S(1)}, bf16[3,768,192]{1,2,0:T(8,128)(2,1)S(1)}, u32[]{:S(2)}, u32[]{:S(2)}) collective-permute-start(bf16[3,768,192]{1,2,0:T(8,128)(2,1)S(1)} %add.120), channel_id=1, source_target_pairs={{4,0},{8,12},{5,1},{9,13},{6,2},{10,14},{7,3},{11,15},{20,16},{24,... | collective-permute-start | bytes 2654216 | tf_op jit(solution)/shard_map/ppermute | solution.py:776
  (47 other events, 274.9 us)

commit v3 on v2

v3 whole, which is shorter than its diff:
```python
import functools
import math

import jax
import jax.numpy as jnp
from jax import lax
from jax.experimental import pallas as pl
from jax.experimental.pallas import tpu as pltpu
from jax.sharding import PartitionSpec as P

HEAD_DIM = 64
SCALE = HEAD_DIM ** (-0.5)
EPSILON = 1e-05
MASKED = -1000000000.0
HIGHEST = lax.Precision.HIGHEST
BF = jnp.bfloat16
F32 = jnp.float32
NN = (((1,), (0,)), ((), ()))
NT = (((1,), (1,)), ((), ()))
TN = (((0,), (0,)), ((), ()))
TILE = 256
QUERIES = 512
BAND = 128
ENCODER, DECODER = 0, 1
ROLE, OWN_LEN, SOURCE_LEN, CORE, START = 0, 1, 2, 3, 4
HIDES_LITTLE = 0.02
HIDES_MUCH = 2.0


def mm(left, right, dims):
    return lax.dot_general(left, right, dims, preferred_element_type=F32)


def whole():
    return pl.BlockSpec(memory_space=pltpu.VMEM)


def scalars():
    return pl.BlockSpec(memory_space=pltpu.SMEM)


def shape(dims, dtype):
    return jax.ShapeDtypeStruct(dims, dtype)


def cost(flops, nbytes, weight=HIDES_LITTLE):
    return pl.CostEstimate(
        flops=int(flops * weight), bytes_accessed=int(nbytes * weight), transcendentals=0
    )


def params(megabytes=28):
    return pltpu.CompilerParams(vmem_limit_bytes=megabytes * 1024 * 1024)


def norm_of(values, norm_ref):
    centred = values - jnp.mean(values, -1, keepdims=True)
    factor = lax.rsqrt(jnp.mean(centred * centred, -1, keepdims=True) + EPSILON)
    return centred * factor * norm_ref[0:1, :] + norm_ref[1:2, :]


def enter_kernel(info, mine, core_mine, far, core_far, norm_ref, rows_ref, normed_ref):
    quarter = mine.shape[0]
    for step, piece in enumerate((mine, core_mine, far, core_far)):
        start = pl.multiple_of(info[START + step], quarter)
        values = piece[...]
        rows_ref[pl.ds(start, quarter), :] = values
        normed_ref[pl.ds(start, quarter), :] = norm_of(values.astype(F32), norm_ref).astype(BF)


def enter(info, pieces, norm):
    quarter, width = pieces[0].shape
    out = shape((4 * quarter, width), BF)
    return pl.pallas_call(
        enter_kernel,
        out_shape=(out, out),
        in_specs=[scalars()] + [whole()] * 5,
        out_specs=(whole(), whole()),
        compiler_params=params(),
        cost_estimate=cost(16 * quarter * width * 4, quarter * width * 24),
    )(info, *pieces, norm)


def masked_kernel(info, mine, core_mine, far, core_far, rows_ref):
    quarter = mine.shape[0]
    for step, piece in enumerate((mine, core_mine, far, core_far)):
        start = pl.multiple_of(info[START + step], quarter)
        row = start + lax.broadcasted_iota(jnp.int32, (quarter, 1), 0)
        values = jnp.where(row < info[OWN_LEN], piece[...].astype(F32), 0.0)
        rows_ref[pl.ds(start, quarter), :] = values.astype(BF)


def masked_rows(info, pieces):
    quarter, width = pieces[0].shape
    return pl.pallas_call(
        masked_kernel,
        out_shape=shape((4 * quarter, width), BF),
        in_specs=[scalars()] + [whole()] * 4,
        out_specs=whole(),
        compiler_params=params(),
        cost_estimate=cost(quarter * width * 8, quarter * width * 16),
    )(info, *pieces)


def skew_kernel(distance_ref, table_ref):
    width = table_ref.shape[2]
    for head in range(distance_ref.shape[0]):
        row = jnp.broadcast_to(distance_ref[head : head + 1, :], (BAND, width))
        table_ref[head] = pltpu.roll(row, width - (BAND - 1), 1, stride=1, stride_axis=0)


def skew(distances):
    heads, width = distances.shape
    return pl.pallas_call(
        skew_kernel,
        out_shape=shape((heads, BAND, width), F32),
        in_specs=[whole()],
        out_specs=whole(),
        compiler_params=params(),
        cost_estimate=cost(heads * BAND * width, heads * BAND * width * 4),
    )(distances)


def unskewed(band):
    width = band.shape[1]
    amount = (BAND - 1) - lax.broadcasted_iota(jnp.int32, (BAND, width), 0)
    for bit in range(7):
        band = jnp.where(((amount >> bit) & 1) == 1, pltpu.roll(band, 1 << bit, 1), band)
    return jnp.sum(band, 0, keepdims=True)


def by_blocks(count, body):
    def step(index, carry):
        body(pl.ds(pl.multiple_of(index * TILE, TILE), TILE))
        return carry

    lax.fori_loop(0, count // TILE, step, 0)


def head_span(head):
    return slice(head * HEAD_DIM, (head + 1) * HEAD_DIM)


def allowed_keys(info, start, length, causal, length_at):
    key = lax.broadcasted_iota(jnp.int32, (length, QUERIES), 0)
    last = info[length_at] - 1
    if not causal:
        return key <= last
    query = start + lax.broadcasted_iota(jnp.int32, (1, QUERIES), 1)
    free = jnp.where(info[ROLE] == DECODER, 0, 1 << 20)
    return key <= jnp.minimum(query + free, last)


def bias_block(table_ref, head, start, length):
    blocks = []
    for band in range(length // BAND):
        offset = pl.multiple_of(length - BAND - band * BAND + start, BAND)
        blocks.append(table_ref[head, :, pl.ds(offset, QUERIES)])
    return jnp.concatenate(blocks, 0)


def upright(source, place, target):
    def step(cols):
        block = source[place, :, cols].astype(F32).T
        for head in range(target.shape[0]):
            target[head, cols, :] = block[:, head_span(head)].astype(BF)

    by_blocks(source.shape[2], step)


def attend_loop(info, qkv_ref, keys_ref, table_ref, out_ref, lse_ref, length_at):
    width, length = out_ref.shape
    causal = table_ref is not None

    def block(index, carry):
        start = pl.multiple_of(index * QUERIES, QUERIES)
        cols = pl.ds(start, QUERIES)
        allowed = allowed_keys(info, start, length, causal, length_at)
        for head in range(width // HEAD_DIM):
            span = head_span(head)
            queries = qkv_ref[0, span, cols] * jnp.asarray(SCALE, BF)
            scores = mm(keys_ref[head], queries, NN)
            if causal:
                scores = scores + bias_block(table_ref, head, start, length)
            scores = jnp.where(allowed, scores, MASKED)
            peak = jnp.max(scores, 0, keepdims=True)
            lifted = jnp.exp(scores - peak)
            total = jnp.sum(lifted, 0, keepdims=True)
            mixed = mm(qkv_ref[2, span, :], lifted.astype(BF), NN)
            out_ref[span, cols] = mixed / total
            lse_ref[head : head + 1, cols] = peak + jnp.log(total)
        return carry

    lax.fori_loop(0, length // QUERIES, block, 0)


def self_forward_kernel(has_sum, info, normed, weights, table, *refs):
    previous = refs[0] if has_sum else None
    sum_ref, qkv_ref, out_ref, lse_ref, keys = refs[1 if has_sum else 0 :]
    length = out_ref.shape[1]

    def inputs(cols):
        block = normed[cols, :]
        for place in range(3):
            qkv_ref[place, :, cols] = mm(weights[place], block, NT).astype(BF)

    by_blocks(length, inputs)
    upright(qkv_ref, 1, keys)
    attend_loop(info, qkv_ref, keys, table, out_ref, lse_ref, OWN_LEN)

    def outputs(cols):
        value = mm(out_ref[:, cols].astype(BF), weights[3], TN)
        if has_sum:
            value = value + previous[cols, :]
        sum_ref[cols, :] = value.astype(sum_ref.dtype)

    by_blocks(length, outputs)


def attention_cost(length, width, model, matmuls, projections, weight=HIDES_LITTLE):
    heads = width // HEAD_DIM
    return cost(
        heads * length * length * HEAD_DIM * 2 * matmuls * 4 + projections * 2 * length * model * width,
        length * model * 8,
        weight,
    )


def saved_shapes(length, width):
    return (shape((3, width, length), BF), shape((width, length), F32), shape((8, length), F32))


def self_forward(info, normed, weights, table, previous):
    length, model = normed.shape
    width = weights.shape[1]
    has_sum = previous is not None
    operands = [info, normed, weights, table] + ([previous] if has_sum else [])
    return pl.pallas_call(
        functools.partial(self_forward_kernel, has_sum),
        out_shape=(shape((length, model), BF if has_sum else F32),) + saved_shapes(length, width),
        in_specs=[scalars()] + [whole()] * (len(operands) - 1),
        out_specs=(whole(),) * 4,
        scratch_shapes=[pltpu.VMEM((width // HEAD_DIM, length, HEAD_DIM), BF)],
        compiler_params=params(),
        cost_estimate=attention_cost(length, width, model, 2, 4, HIDES_MUCH),
    )(*operands)


def cross_forward_kernel(info, normed, near, far, weights_near, weights_far, *refs):
    sum_ref, keys = refs[0], refs[7]
    length = normed.shape[0]
    half = near.shape[0]
    sides = ((weights_near, refs[1:4]), (weights_far, refs[4:7]))

    @pl.when(info[ROLE] == DECODER)
    def _():
        for weights, (qkv_ref, out_ref, lse_ref) in sides:

            def queries(cols, weights=weights, qkv_ref=qkv_ref):
                qkv_ref[0, :, cols] = mm(weights[0], normed[cols, :], NT).astype(BF)

            by_blocks(length, queries)
            for piece, side in ((near, info[CORE]), (far, 1 - info[CORE])):
                base = side * half

                def sources(index, carry, piece=piece, base=base, weights=weights, qkv_ref=qkv_ref):
                    local = pl.multiple_of(index * TILE, TILE)
                    block = piece[pl.ds(local, TILE), :]
                    cols = pl.ds(pl.multiple_of(base + local, TILE), TILE)
                    for place in (1, 2):
                        qkv_ref[place, :, cols] = mm(weights[1 + place], block, NT).astype(BF)
                    return carry

                lax.fori_loop(0, half // TILE, sources, 0)
            upright(qkv_ref, 1, keys)
            attend_loop(info, qkv_ref, keys, None, out_ref, lse_ref, SOURCE_LEN)

        def outputs(cols):
            value = mm(refs[2][:, cols].astype(BF), weights_near[1], TN)
            value = value + mm(refs[5][:, cols].astype(BF), weights_far[1], TN)
            sum_ref[cols, :] = value.astype(sum_ref.dtype)

        by_blocks(length, outputs)


def cross_forward(info, normed, near, far, weights_near, weights_far):
    length, model = normed.shape
    width = weights_near.shape[1]
    saved = saved_shapes(length, width)
    results = pl.pallas_call(
        cross_forward_kernel,
        out_shape=(shape((length, model), BF),) + saved + saved,
        in_specs=[scalars()] + [whole()] * 5,
        out_specs=(whole(),) * 7,
        scratch_shapes=[pltpu.VMEM((width // HEAD_DIM, length, HEAD_DIM), BF)],
        compiler_params=params(),
        cost_estimate=attention_cost(length, 2 * width, model, 2, 4),
    )(info, normed, near, far, weights_near, weights_far)
    return results[0], results[1:4], results[4:7]


def attend_back_loop(
    info, saved, table_ref, upstream, grads_ref, upright_refs, key_sum, value_sum, band, length_at
):
    qkv_ref, out_ref, lse_ref = saved
    width, length = out_ref.shape
    causal = table_ref is not None
    keys_up, values_up, queries_up, above_up = upright_refs
    upright(qkv_ref, 1, keys_up)
    upright(qkv_ref, 2, values_up)
    upright(qkv_ref, 0, queries_up)
    upright(upstream, 0, above_up)
    key_sum[...] = jnp.zeros_like(key_sum)
    value_sum[...] = jnp.zeros_like(value_sum)
    if causal:
        band[...] = jnp.zeros_like(band)

    def block(index, carry):
        start = pl.multiple_of(index * QUERIES, QUERIES)
        cols = pl.ds(start, QUERIES)
        allowed = allowed_keys(info, start, length, causal, length_at)
        for head in range(width // HEAD_DIM):
            span = head_span(head)
            queries = qkv_ref[0, span, cols] * jnp.asarray(SCALE, BF)
            scores = mm(keys_up[head], queries, NN)
            if causal:
                scores = scores + bias_block(table_ref, head, start, length)
            scores = jnp.where(allowed, scores, MASKED)
            probs = jnp.exp(scores - lse_ref[head : head + 1, cols])
            above = upstream[0, span, cols]
            d_probs = mm(values_up[head], above, NN)
            inner = above.astype(F32) * out_ref[span, cols]
            inner = jnp.sum(inner, 0, keepdims=True)
            d_scores = probs * (d_probs - inner)
            low = d_scores.astype(BF)
            grads_ref[0, span, cols] = (mm(qkv_ref[1, span, :], low, NN) * SCALE).astype(BF)
            key_sum[head] += mm(low, queries_up[head, cols, :], NN)
            value_sum[head] += mm(probs.astype(BF), above_up[head, cols, :], NN)
            if causal:
                for part in range(length // BAND):
                    offset = pl.multiple_of(length - BAND - part * BAND + start, BAND)
                    place = pl.ds(offset, QUERIES)
                    band[head, :, place] += d_scores[part * BAND : (part + 1) * BAND, :]
        return carry

    lax.fori_loop(0, length // QUERIES, block, 0)
    for head in range(width // HEAD_DIM):
        span = head_span(head)
        grads_ref[1, span, :] = (key_sum[head] * SCALE).T.astype(BF)
        grads_ref[2, span, :] = value_sum[head].T.astype(BF)


def back_scratch(length, width):
    heads = width // HEAD_DIM
    return [
        pltpu.VMEM((1, width, length), BF),
        *[pltpu.VMEM((heads, length, HEAD_DIM), BF) for _ in range(4)],
        pltpu.VMEM((heads, length, HEAD_DIM), F32),
        pltpu.VMEM((heads, length, HEAD_DIM), F32),
    ]


def self_backward_kernel(has_sum, info, qkv, out, lse, above, normed, weights, table, *refs):
    previous = refs[0] if has_sum else None
    refs = refs[1 if has_sum else 0 :]
    sum_ref, weight_ref, spread_ref, upstream = refs[:4]
    upright_refs, key_sum, value_sum, band, grads_ref = refs[4:8], refs[8], refs[9], refs[10], refs[11]
    length = above.shape[0]

    def entering(cols):
        upstream[0, :, cols] = mm(weights[3], above[cols, :], NT).astype(BF)

    by_blocks(length, entering)
    attend_back_loop(
        info,
        (qkv, out, lse),
        table,
        upstream,
        grads_ref,
        upright_refs,
        key_sum,
        value_sum,
        band,
        OWN_LEN,
    )

    def leaving(cols):
        value = mm(grads_ref[0, :, cols], weights[0], TN)
        for place in (1, 2):
            value = value + mm(grads_ref[place, :, cols], weights[place], TN)
        if has_sum:
            value = value + previous[cols, :]
        sum_ref[cols, :] = value.astype(sum_ref.dtype)

    by_blocks(length, leaving)
    for place in range(3):
        weight_ref[place] = mm(grads_ref[place], normed[...], NN).astype(weight_ref.dtype)
    weight_ref[3] = mm(out[...].astype(BF), above[...], NN).astype(weight_ref.dtype)
    for head in range(table.shape[0]):
        spread_ref[head : head + 1, :] = unskewed(band[head])


def self_backward(info, saved, above, normed, weights, table, previous, weight_type):
    length, model = above.shape
    width = weights.shape[1]
    has_sum = previous is not None
    operands = [info, *saved, above, normed, weights, table] + ([previous] if has_sum else [])
    return pl.pallas_call(
        functools.partial(self_backward_kernel, has_sum),
        out_shape=(
            shape((length, model), BF if has_sum else F32),
            shape((4, width, model), weight_type),
            shape((table.shape[0], table.shape[2]), F32),
        ),
        in_specs=[scalars()] + [whole()] * (len(operands) - 1),
        out_specs=(whole(),) * 3,
        scratch_shapes=back_scratch(length, width)
        + [pltpu.VMEM(table.shape, F32), pltpu.VMEM((3, width, length), BF)],
        compiler_params=params(),
        cost_estimate=attention_cost(length, width, model, 5, 8),
    )(*operands)


def cross_backward_kernel(info, *refs):
    saved_near, saved_far, (above, weights_near, weights_far) = refs[:3], refs[3:6], refs[6:9]
    sum_ref, source_ref, grads_near, grads_far, upstream = refs[9:14]
    upright_refs, key_sum, value_sum = refs[14:18], refs[18], refs[19]
    length = above.shape[0]

    @pl.when(info[ROLE] == DECODER)
    def _():
        for saved, weights, grads_ref in (
            (saved_near, weights_near, grads_near),
            (saved_far, weights_far, grads_far),
        ):

            def entering(cols, weights=weights):
                upstream[0, :, cols] = mm(weights[1], above[cols, :], NT).astype(BF)

            by_blocks(length, entering)
            attend_back_loop(
                info,
                saved,
                None,
                upstream,
                grads_ref,
                upright_refs,
                key_sum,
                value_sum,
                None,
                SOURCE_LEN,
            )

        def leaving(cols):
            value = mm(grads_near[0, :, cols], weights_near[0], TN)
            value = value + mm(grads_far[0, :, cols], weights_far[0], TN)
            sum_ref[cols, :] = value.astype(BF)
            source = None
            for grads_ref, weights in ((grads_near, weights_near), (grads_far, weights_far)):
                for place in (1, 2):
                    term = mm(grads_ref[place, :, cols], weights[1 + place], TN)
                    source = term if source is None else source + term
            source_ref[cols, :] = source.astype(BF)

        by_blocks(length, leaving)


def cross_backward(info, saved_near, saved_far, above, weights_near, weights_far):
    length, model = above.shape
    width = weights_near.shape[1]
    out, grads = shape((length, model), BF), shape((3, width, length), BF)
    return pl.pallas_call(
        cross_backward_kernel,
        out_shape=(out, out, grads, grads),
        in_specs=[scalars()] + [whole()] * 9,
        out_specs=(whole(),) * 4,
        scratch_shapes=back_scratch(length, width),
        compiler_params=params(),
        cost_estimate=attention_cost(length, 2 * width, model, 5, 4),
    )(info, *saved_near, *saved_far, above, weights_near, weights_far)


def cross_weights_kernel(info, grads_near, grads_far, out_near, out_far, normed, above, *refs):
    near, far, weight_near, weight_far = refs
    half = near.shape[0]

    @pl.when(info[ROLE] == DECODER)
    def _():
        start = pl.multiple_of(info[CORE] * half, half)
        other = pl.multiple_of((1 - info[CORE]) * half, half)
        for grads, out, target in (
            (grads_near, out_near, weight_near),
            (grads_far, out_far, weight_far),
        ):
            target[0] = mm(grads[0], normed[...], NN).astype(target.dtype)
            target[1] = mm(out[...].astype(BF), above[...], NN).astype(target.dtype)
            for place in (1, 2):
                value = mm(grads[place, :, pl.ds(start, half)], near[...], NN)
                value = value + mm(grads[place, :, pl.ds(other, half)], far[...], NN)
                target[1 + place] = value.astype(target.dtype)


def cross_weights(info, grads_near, grads_far, out_near, out_far, normed, above, near, far):
    length, model = above.shape
    width = out_near.shape[0]
    return pl.pallas_call(
        cross_weights_kernel,
        out_shape=(shape((4, width, model), F32), shape((4, width, model), BF)),
        in_specs=[scalars()] + [whole()] * 8,
        out_specs=(whole(),) * 2,
        compiler_params=params(),
        cost_estimate=cost(16 * length * model * width, length * model * 16),
    )(info, grads_near, grads_far, out_near, out_far, normed, above, near, far)


def row_spec(width):
    return pl.BlockSpec((TILE, width), lambda index: (index, 0))


def fixed_spec(dims):
    return pl.BlockSpec(dims, lambda index: (0,) * len(dims))


def add_norm_kernel(stream, near, far, norm_ref, sum_ref, normed_ref):
    value = stream[...].astype(F32) + (near[...].astype(F32) + far[...].astype(F32))
    sum_ref[...] = value
    normed_ref[...] = norm_of(value, norm_ref).astype(BF)


def add_norm(stream, near, far, norm):
    length, model = stream.shape
    return pl.pallas_call(
        add_norm_kernel,
        grid=(length // TILE,),
        out_shape=(shape((length, model), F32), shape((length, model), BF)),
        in_specs=[row_spec(model)] * 3 + [fixed_spec((2, model))],
        out_specs=(row_spec(model),) * 2,
        compiler_params=params(),
        cost_estimate=cost(length * model * 12, length * model * 14),
    )(stream, near, far, norm)


def row_mask(info, index, at):
    row = index * TILE + lax.broadcasted_iota(jnp.int32, (TILE, 1), 0)
    return row < info[at]


def squares_of(value):
    return jnp.sum(jnp.sum(value * value, 0, keepdims=True), 1, keepdims=True)


def source_kernel(info, stream, near, far, norm_ref, sum_ref, sent_ref, square_ref):
    index = pl.program_id(0)
    value = stream[...] + (near[...].astype(F32) + far[...].astype(F32))
    sum_ref[...] = value
    result = jnp.where(row_mask(info, index, OWN_LEN), norm_of(value, norm_ref), 0.0)
    sent_ref[...] = result.astype(BF)

    @pl.when(index == 0)
    def _():
        square_ref[...] = jnp.zeros_like(square_ref)

    square_ref[...] += squares_of(result)


def source_out(info, stream, near, far, norm):
    length, model = stream.shape
    return pl.pallas_call(
        source_kernel,
        grid=(length // TILE,),
        out_shape=(shape((length, model), F32), shape((length, model), BF), shape((8, 128), F32)),
        in_specs=[scalars()] + [row_spec(model)] * 3 + [fixed_spec((2, model))],
        out_specs=(row_spec(model), row_spec(model), fixed_spec((8, 128))),
        compiler_params=params(),
        cost_estimate=cost(length * model * 14, length * model * 14),
    )(info, stream, near, far, norm)


def finish_kernel(info, stream, near, far, sent, square, out_ref, square_ref):
    index = pl.program_id(0)

    @pl.when(info[ROLE] == DECODER)
    def _():
        value = stream[...] + (near[...].astype(F32) + far[...].astype(F32))
        value = jnp.where(row_mask(info, index, OWN_LEN), value, 0.0)
        out_ref[...] = value.astype(BF)

        @pl.when(index == 0)
        def _():
            square_ref[...] = jnp.zeros_like(square_ref)

        square_ref[...] += squares_of(value)

    @pl.when(info[ROLE] == ENCODER)
    def _():
        out_ref[...] = sent[...]
        square_ref[...] = square[...]


def finish(info, stream, near, far, sent, square):
    length, model = stream.shape
    return pl.pallas_call(
        finish_kernel,
        grid=(length // TILE,),
        out_shape=(shape((length, model), BF), shape((8, 128), F32)),
        in_specs=[scalars()] + [row_spec(model)] * 4 + [fixed_spec((8, 128))],
        out_specs=(row_spec(model), fixed_spec((8, 128))),
        compiler_params=params(),
        cost_estimate=cost(length * model * 6, length * model * 12),
    )(info, stream, near, far, sent, square)


def norm_back(upstream, values, norm_ref):
    centred = values - jnp.mean(values, -1, keepdims=True)
    factor = lax.rsqrt(jnp.mean(centred * centred, -1, keepdims=True) + EPSILON)
    unit = centred * factor
    scaled = upstream * norm_ref[0:1, :]
    inner = scaled - jnp.mean(scaled, -1, keepdims=True)
    inner = inner - unit * jnp.mean(scaled * unit, -1, keepdims=True)
    gain = jnp.sum(upstream * unit, 0, keepdims=True)
    shift = jnp.sum(upstream, 0, keepdims=True)
    return factor * inner, gain, shift


def norm_back_kernel(residual, near, far, values, norm_ref, grad_ref, low_ref, norm_grad_ref):
    upstream = near[...].astype(F32) + far[...].astype(F32)
    grad, gain, shift = norm_back(upstream, values[...].astype(F32), norm_ref)
    grad = residual[...].astype(F32) + grad
    grad_ref[...] = grad
    low_ref[...] = grad.astype(BF)

    @pl.when(pl.program_id(0) == 0)
    def _():
        norm_grad_ref[...] = jnp.zeros_like(norm_grad_ref)

    norm_grad_ref[0:1, :] += gain
    norm_grad_ref[1:2, :] += shift


def norm_backward(residual, near, far, values, norm):
    length, model = values.shape
    return pl.pallas_call(
        norm_back_kernel,
        grid=(length // TILE,),
        out_shape=(shape((length, model), F32), shape((length, model), BF), shape((2, model), F32)),
        in_specs=[row_spec(model)] * 4 + [fixed_spec((2, model))],
        out_specs=(row_spec(model), row_spec(model), fixed_spec((2, model))),
        compiler_params=params(),
        cost_estimate=cost(length * model * 20, length * model * 18),
    )(residual, near, far, values, norm)


def source_back_kernel(
    info, cot, near, far, values, norm_ref, grad_ref, low_ref, norm_grad_ref
):
    index = pl.program_id(0)
    blocks = near.shape[0] // TILE
    rows = pl.ds(pl.multiple_of(lax.rem(index, blocks) * TILE, TILE), TILE)
    mine = (index >= blocks).astype(jnp.int32) == info[CORE]
    returned = jnp.where(mine, near[rows, :].astype(F32), far[rows, :].astype(F32))
    upstream = cot[...].astype(F32) + returned
    upstream = jnp.where(row_mask(info, index, OWN_LEN), upstream, 0.0)
    grad, gain, shift = norm_back(upstream, values[...], norm_ref)
    grad_ref[...] = grad
    low_ref[...] = grad.astype(BF)

    @pl.when(index == 0)
    def _():
        norm_grad_ref[...] = jnp.zeros_like(norm_grad_ref)

    norm_grad_ref[0:1, :] += gain
    norm_grad_ref[1:2, :] += shift


def source_back(info, cot, near, far, values, norm):
    length, model = values.shape
    return pl.pallas_call(
        source_back_kernel,
        grid=(length // TILE,),
        out_shape=(shape((length, model), F32), shape((length, model), BF), shape((2, model), F32)),
        in_specs=[scalars(), row_spec(model), fixed_spec(near.shape), fixed_spec(far.shape)]
        + [row_spec(model), fixed_spec((2, model))],
        out_specs=(row_spec(model), row_spec(model), fixed_spec((2, model))),
        compiler_params=params(),
        cost_estimate=cost(length * model * 20, length * model * 18),
    )(info, cot, near, far, values, norm)


def gelu_parts(hidden):
    half = 0.5 * (1.0 + lax.erf(hidden * math.sqrt(0.5)))
    slope = half + hidden * jnp.exp(-0.5 * hidden * hidden) * (1.0 / math.sqrt(2.0 * math.pi))
    return hidden * half, slope


def feed_forward_kernel(has_sum, info, normed, pack, *refs):
    previous = refs[0] if has_sum else None
    sum_ref, active_ref, slope_ref = refs[1 if has_sum else 0 :]

    @pl.when(info[ROLE] == ENCODER)
    def _():
        active, slope = gelu_parts(mm(normed[...], pack[0], NN))
        active = active.astype(BF)
        active_ref[...] = active
        slope_ref[...] = slope
        value = mm(active, pack[1], NN)
        if has_sum:
            value = value + previous[...]
        sum_ref[...] = value.astype(sum_ref.dtype)


def feed_forward(info, normed, pack, previous):
    length, model = normed.shape
    hidden = pack.shape[2]
    has_sum = previous is not None
    operands = [info, normed, pack] + ([previous] if has_sum else [])
    return pl.pallas_call(
        functools.partial(feed_forward_kernel, has_sum),
        grid=(length // TILE,),
        out_shape=(
            shape((length, model), BF if has_sum else F32),
            shape((length, hidden), BF),
            shape((length, hidden), F32),
        ),
        in_specs=[scalars(), row_spec(model), fixed_spec(pack.shape)]
        + ([row_spec(model)] if has_sum else []),
        out_specs=(row_spec(model), row_spec(hidden), row_spec(hidden)),
        compiler_params=params(),
        cost_estimate=cost(4 * length * model * hidden, length * model * 12),
    )(*operands)


def feed_both_kernel(info, normed, cot, pack_near, pack_far, *refs):
    sum_ref, back_ref = refs[:2]

    @pl.when(info[ROLE] == DECODER)
    def _():
        value, back = None, None
        for pack, active_ref, grad_ref in ((pack_near, *refs[2:4]), (pack_far, *refs[4:6])):
            active, slope = gelu_parts(mm(normed[...], pack[0], NN))
            active = active.astype(BF)
            active_ref[...] = active
            term = mm(active, pack[1], NN)
            value = term if value is None else value + term
            grad = (mm(cot[...], pack[1], NT) * slope).astype(BF)
            grad_ref[...] = grad
            term = mm(grad, pack[0], NT)
            back = term if back is None else back + term
        sum_ref[...] = value.astype(BF)
        back_ref[...] = back.astype(BF)


def feed_both(info, normed, cot, pack_near, pack_far):
    length, model = normed.shape
    hidden = pack_near.shape[2]
    out, unit = shape((length, model), BF), shape((length, hidden), BF)
    return pl.pallas_call(
        feed_both_kernel,
        grid=(length // TILE,),
        out_shape=(out, out, unit, unit, unit, unit),
        in_specs=[
            scalars(),
            row_spec(model),
            row_spec(model),
            fixed_spec(pack_near.shape),
            fixed_spec(pack_far.shape),
        ],
        out_specs=(row_spec(model),) * 2 + (row_spec(hidden),) * 4,
        compiler_params=params(),
        cost_estimate=cost(16 * length * model * hidden, length * model * 20),
    )(info, normed, cot, pack_near, pack_far)


def feed_back_kernel(above, slope_near, slope_far, pack_near, pack_far, back_ref, *grad_refs):
    back = None
    for pack, slope, grad_ref in (
        (pack_near, slope_near, grad_refs[0]),
        (pack_far, slope_far, grad_refs[1]),
    ):
        grad = (mm(above[...], pack[1], NT) * slope[...]).astype(BF)
        grad_ref[...] = grad
        term = mm(grad, pack[0], NT)
        back = term if back is None else back + term
    back_ref[...] = back.astype(BF)


def feed_back(above, slope_near, slope_far, pack_near, pack_far):
    length, model = above.shape
    hidden = pack_near.shape[2]
    unit = shape((length, hidden), BF)
    return pl.pallas_call(
        feed_back_kernel,
        grid=(length // TILE,),
        out_shape=(shape((length, model), BF), unit, unit),
        in_specs=[
            row_spec(model),
            row_spec(hidden),
            row_spec(hidden),
            fixed_spec(pack_near.shape),
            fixed_spec(pack_far.shape),
        ],
        out_specs=(row_spec(model), row_spec(hidden), row_spec(hidden)),
        compiler_params=params(),
        cost_estimate=cost(8 * length * model * hidden, length * model * 16),
    )(above, slope_near, slope_far, pack_near, pack_far)


def product_kernel(left_near, left_far, right_near, right_far, near_ref, far_ref):
    near_ref[...] = mm(left_near[...], right_near[...], TN)
    far_ref[...] = mm(left_far[...], right_far[...], TN).astype(BF)


def feed_weights(left_near, left_far, right_near, right_far):
    length, rows = left_near.shape
    columns = right_near.shape[1]
    left = pl.BlockSpec((length, TILE), lambda index: (0, index))
    right = pl.BlockSpec((length, columns), lambda index: (0, 0))
    out = row_spec(columns)
    return pl.pallas_call(
        product_kernel,
        grid=(rows // TILE,),
        out_shape=(shape((rows, columns), F32), shape((rows, columns), BF)),
        in_specs=[left, left, right, right],
        out_specs=(out, out),
        compiler_params=params(),
        cost_estimate=cost(4 * length * rows * columns, length * rows * 12),
    )(left_near, left_far, right_near, right_far)


def across(value):
    return lax.ppermute(value, "tensor", [(0, 2), (1, 3), (2, 0), (3, 1)])


def across_in(value, role):
    links = [(0, 2), (1, 3), (2, 0), (3, 1)]
    return lax.ppermute(
        value, ("section", "tensor"), [(role * 4 + a, role * 4 + b) for a, b in links]
    )


def beside(value):
    return lax.ppermute(value, "tensor", [(0, 1), (1, 0), (2, 3), (3, 2)])


def to_decoder(value):
    return lax.ppermute(value, "section", [(ENCODER, DECODER)])


def to_encoder(value):
    return lax.ppermute(value, "section", [(DECODER, ENCODER)])


def line_total(value):
    if lax.axis_size("dp") != 4:
        return lax.psum(value, "dp")
    place = lax.axis_index("dp")
    inner = (place == 1) | (place == 2)
    value = value + lax.ppermute(value, "dp", [(0, 1), (3, 2)])
    value = value + lax.ppermute(value, "dp", [(1, 2), (2, 1)])
    return jnp.where(inner, value, lax.ppermute(value, "dp", [(1, 0), (2, 3)]))


def exchange_total(value):
    if lax.axis_size("dp") != value.shape[0]:
        return lax.psum(value, "dp")
    parts = lax.all_to_all(value, "dp", 0, 0, tiled=True)
    total = jnp.sum(parts.astype(F32), 0, keepdims=True).astype(BF)
    return lax.all_to_all(jnp.broadcast_to(total, value.shape), "dp", 0, 0, tiled=True)


def far_added(own, other):
    return (own + across(other).astype(F32)).astype(BF)


def after(value, done):
    return lax.optimization_barrier((value, done))[0]


def body(
    frames,
    lengths,
    bucket_of,
    rel_table,
    norms,
    attn_in,
    attn_out,
    cross_pair,
    ffn_in,
    ffn_out,
    cotangent,
):
    section = lax.axis_index("section")
    tensor = lax.axis_index("tensor")
    pair, core = tensor // 2, tensor % 2
    decoder = section == DECODER
    quarter, model = frames.shape[3], frames.shape[4]
    length = 4 * quarter
    half = length // 2
    width = attn_in.shape[3]
    heads = width // HEAD_DIM
    buckets = rel_table.shape[1]

    own_length = lengths[section, pair, 0]
    source_length = lengths[ENCODER, pair, 0]
    starts = [(tensor ^ step) * quarter for step in range(4)]
    info = jnp.stack([section, own_length, source_length, core] + starts).astype(jnp.int32)

    def pick(array, index):
        return lax.dynamic_index_in_dim(array[0, :, 0], index, 0, keepdims=False)

    self_near = jnp.concatenate([jnp.swapaxes(attn_in[0], 1, 2), attn_out[0][None]])
    feed_near = jnp.stack([ffn_in[0], ffn_out[0]])
    pair_own = jnp.swapaxes(cross_pair[0], 1, 2)
    frame_mine = pick(frames, pair)
    frame_far = across(pick(frames, 1 - pair))
    rel_far = across(rel_table[0])
    self_far = across(after(self_near, frame_far))
    pair_source = to_decoder(pair_own)
    feed_far_e = across_in(after(feed_near, self_far), ENCODER)
    cross_near = jnp.concatenate([pair_own, after(pair_source, self_far)])
    cross_far = across_in(cross_near, DECODER)
    cot_far = across(after(pick(cotangent, 1 - pair), cross_far))
    feed_far_d = across_in(after(feed_near, cot_far), DECODER)

    def quarters(mine, far):
        both = beside(jnp.stack([mine, far]))
        return mine, both[0], far, both[1]

    buckets_here = jnp.pad(bucket_of[0][::-1], (0, 1), constant_values=-1)
    one_hot = (lax.broadcasted_iota(jnp.int32, (buckets, 2 * length), 0) == buckets_here[None]).astype(F32)
    distances = lax.dot_general(
        jnp.concatenate([rel_table[0], rel_far], 1),
        one_hot,
        TN,
        precision=HIGHEST,
        preferred_element_type=F32,
    )
    table_near = skew(distances[:heads])
    table_far = skew(distances[heads:])

    rows, normed_one = enter(info, quarters(frame_mine, frame_far), norms[0, 0])
    part, *saved_near = self_forward(info, normed_one, self_near, table_near, None)
    part, *saved_far = self_forward(
        info, normed_one, after(self_far, pair_source), table_far, part
    )
    stream_one, normed_two = add_norm(rows, part, beside(part), norms[0, 1])

    part, active_e_near, slope_near = feed_forward(
        info, after(normed_two, cross_far), feed_near, None
    )
    part, active_e_far, slope_far = feed_forward(info, normed_two, feed_far_e, part)
    cot = masked_rows(info, quarters(pick(cotangent, pair), cot_far))
    stream_e, sent, squares = source_out(
        info, after(stream_one, cot), part, beside(part), norms[0, 2]
    )
    sent_near = to_decoder(lax.dynamic_slice_in_dim(sent, core * half, half, 0))
    sent_far = beside(sent_near)
    normed_cross = after(normed_two, feed_far_d)

    part, joint_near, joint_far = cross_forward(
        info, normed_cross, sent_near, sent_far, cross_near, cross_far
    )
    stream_d, normed_three = add_norm(stream_one, part, beside(part), norms[0, 2])
    part_d, back, active_d_near, hidden_d_near, active_d_far, hidden_d_far = feed_both(
        info, normed_three, cot, feed_near, feed_far_d
    )
    grad_d, above_d, norm_d = norm_backward(cot, back, beside(back), stream_d, norms[0, 2])
    back_d, returned, d_joint_near, d_joint_far = cross_backward(
        info, joint_near, joint_far, above_d, cross_near, cross_far
    )
    returned_mine = lax.dynamic_slice_in_dim(returned, core * half, half, 0)
    returned_theirs = lax.dynamic_slice_in_dim(returned, (1 - core) * half, half, 0)
    returned = returned_mine.astype(F32) + beside(returned_theirs).astype(F32)
    returned = returned.astype(BF)
    returned_near = to_encoder(returned)
    returned_far = beside(returned_near)

    pair_near, pair_far = cross_weights(
        info,
        d_joint_near,
        d_joint_far,
        joint_near[1],
        joint_far[1],
        normed_two,
        after(above_d, returned),
        sent_near,
        sent_far,
    )
    d_pair = (pair_near + across_in(pair_far, DECODER).astype(F32)).astype(BF)
    d_source = to_encoder(d_pair[2:])

    grad_two, above_e, norm_grad_three = lax.cond(
        decoder,
        lambda: (grad_d, above_d, norm_d),
        lambda: source_back(info, cot, returned_near, returned_far, stream_e, norms[0, 2]),
    )
    down_near, down_far = lax.cond(
        decoder,
        lambda: feed_weights(active_d_near, active_d_far, cot, cot),
        lambda: feed_weights(active_e_near, active_e_far, above_e, above_e),
    )
    d_down = far_added(down_near, down_far)
    d_ffn_out = line_total(d_down).astype(F32)
    back, hidden_near, hidden_far = lax.cond(
        decoder,
        lambda: (back_d, hidden_d_near, hidden_d_far),
        lambda: feed_back(above_e, slope_near, slope_far, feed_near, feed_far_e),
    )
    grad_one, above_one, norm_grad_two = norm_backward(
        grad_two, back, beside(back), stream_one, norms[0, 1]
    )
    up_near, up_far = lax.cond(
        decoder,
        lambda: feed_weights(normed_three, normed_three, hidden_near, hidden_far),
        lambda: feed_weights(normed_two, normed_two, hidden_near, hidden_far),
    )
    d_up = far_added(up_near, up_far)
    d_ffn_in = line_total(d_up).astype(F32)

    back, attn_far, spread_far = self_backward(
        info, saved_far, above_one, normed_one, self_far, table_far, None, BF
    )
    back, attn_near, spread_near = self_backward(
        info, saved_near, after(above_one, d_down), normed_one, self_near, table_near, back, F32
    )
    grad_rows, _, norm_grad_one = norm_backward(grad_one, back, beside(back), rows, norms[0, 0])
    d_attn = exchange_total(far_added(attn_near, attn_far)).astype(F32)
    d_pair = jnp.where(decoder, d_pair[:2], d_source)
    d_pair = line_total(d_pair).astype(F32)

    part_d = after(part_d, returned)
    result, squares = finish(info, stream_d, part_d, beside(part_d), sent, squares)

    def placed(value):
        mine = lax.dynamic_slice_in_dim(value, tensor * quarter, quarter, 0)
        theirs = lax.dynamic_slice_in_dim(value, (tensor ^ 2) * quarter, quarter, 0)
        other = across(theirs.astype(BF)).astype(value.dtype)
        stacked = jnp.where(pair == 0, jnp.stack([mine, other]), jnp.stack([other, mine]))
        return stacked[None, :, None]

    spreads = jnp.concatenate([spread_near, spread_far])
    d_table = lax.dot_general(
        one_hot, spreads, NT, precision=HIGHEST, preferred_element_type=F32
    )
    def table_rows(value):
        rows_used = -(-buckets * heads // model)
        padded = jnp.pad(value.reshape(-1), (0, rows_used * model - buckets * heads))
        return padded.reshape(rows_used, model)

    shared = jnp.concatenate(
        [
            norm_grad_one,
            norm_grad_two,
            norm_grad_three,
            jnp.broadcast_to(squares[:1, :1], (1, model)),
            jnp.broadcast_to(own_length.astype(F32), (1, model)),
        ]
    )
    small = jnp.concatenate([shared, table_rows(d_table[:, :heads])])
    small = small + across(jnp.concatenate([shared, table_rows(d_table[:, heads:])]))
    small = line_total(small)
    d_table = small[8:].reshape(-1)[: buckets * heads].reshape(buckets, heads)
    stats = jnp.sqrt(small[6, :1] / (small[7, :1] * model))
    return (
        placed(result),
        placed(grad_rows),
        d_table[None],
        small[:6].reshape(1, 3, 2, model),
        jnp.swapaxes(d_attn[:3], 1, 2)[None],
        d_attn[3][None],
        jnp.swapaxes(d_pair, 1, 2)[None],
        d_ffn_in[None],
        d_ffn_out[None],
        stats,
    )


def solution(mesh):
    in_specs = (
        P("section", None, "dp", "tensor", None),
        P(None, None, "dp"),
        P("section", None),
        P("section", None, "tensor"),
        P("section", None, None, None),
        P("section", None, None, "tensor"),
        P("section", "tensor", None),
        P("section", None, None, "tensor"),
        P("section", None, "tensor"),
        P("section", "tensor", None),
        P("section", None, "dp", "tensor", None),
    )
    out_specs = (
        P("section", None, "dp", "tensor", None),
        P("section", None, "dp", "tensor", None),
        P("section", None, "tensor"),
        P("section", None, None, None),
        P("section", None, None, "tensor"),
        P("section", "tensor", None),
        P("section", None, None, "tensor"),
        P("section", None, "tensor"),
        P("section", "tensor", None),
        P("section"),
    )
    return jax.shard_map(body, mesh=mesh, in_specs=in_specs, out_specs=out_specs, check_vma=False)
```

time: 774 us -> 576 us (0.74)
  waiting for transfers between devices: 346 us -> 232 us
  Pallas kernels: 224 us -> 165 us
  matrix products: 32.4 us -> 2.13 us
    ppermute x13 -> x10, waiting for transfers between devices: 88 us -> 24.2 us  [across(): return lax.ppermute(value, 'tensor', [(0, 2), (1, 3), (2, 0), (3, 1)])]
    ppermute x2, waiting for transfers between devices: 138 us -> 96.6 us  [to_encoder(): return lax.ppermute(value, 'section', [(DECODER, ENCODER)])]
    dot_general x20 -> x0, matrix products: 30.3 us -> none  [rows_product(): return lax.dot_general(left, right, TN, preferred_element_type=F32)]
    pallas_call x8 -> x7, Pallas kernels: 55 us -> 34.8 us  [the longest x1 11 us: feed_back(): pl.pallas_call(feed_back_kernel, grid=(length // TILE,), out_shape=(shape...]
    ppermute x21 -> x12, starting transfers between devices: 50.2 us -> 39.2 us  [the longest x4 28.2 us: line_total(): value = value + lax.ppermute(value, 'dp', [(0, 1), (3, 2)])]
    ppermute x2, waiting for transfers between devices: 27.9 us -> 17.3 us  [to_decoder(): return lax.ppermute(value, 'section', [(ENCODER, DECODER)])]
    ppermute x7 -> x4, waiting for transfers between devices: 35.4 us -> 24.9 us  [across_in(): lax.ppermute(value, ('section', 'tensor'), [(role * 4 + a, role * 4 + b)...]
    unnamed x112 -> x169, local copies, waits for them, and re-layouts: 11.7 us -> 22 us
  transfers between devices with their start and end apart: 57 -> 44, of which waited for: 20 -> 17; matrix products, arithmetic and copies ran while one was open for 12% -> 11% of each run, Pallas kernels for 20% -> 25%
where the time goes in v3:
time: 576 us; the launch traced here: 565 us
  waiting for transfers between devices  232 us (40%)
  Pallas kernels  165 us (29%)
  starting transfers between devices  80.1 us (14%)
  local copies, waits for them, and re-layouts  42.9 us (7%)
  other arithmetic  37.3 us (6%)
    ppermute x2, waiting for transfers between devices, to_encoder(): return lax.ppermute(value, 'section', [(DECODER, ENCODER)])  96.6 us
    pallas_call x2, Pallas kernels, self_backward(): pl.pallas_call(functools.partial(self_backward_kernel, has_sum), out_shap...  52.1 us
    ppermute x4, waiting for transfers between devices, line_total(): return jnp.where(inner, value, lax.ppermute(value, 'dp', [(1, 0), (2, 3)]))  42.9 us
    ppermute x4, starting transfers between devices, line_total(): value = value + lax.ppermute(value, 'dp', [(0, 1), (3, 2)])  28.2 us
    ppermute x4, waiting for transfers between devices, across_in(): lax.ppermute(value, ('section', 'tensor'), [(role * 4 + a, role * 4 + b)...  24.9 us
    ppermute x10, waiting for transfers between devices, across(): return lax.ppermute(value, 'tensor', [(0, 2), (1, 3), (2, 0), (3, 1)])  24.2 us
    pallas_call x2, Pallas kernels, self_forward(): pl.pallas_call(functools.partial(self_forward_kernel, has_sum), out_shape...  22.9 us
    unnamed x169, local copies, waits for them, and re-layouts  22 us
  transfers between devices with their start and end apart: 44, of which 17 were waited for; matrix products, arithmetic and copies ran while one was open for 11% of the time, Pallas kernels for 25%

profile of v3, /device:TPU:0, one launch (start us, length us, event | category | flops | bytes accessed | tf_op | source)
XLA Modules:
  0.0 564.5 jit_solution(8856899584784556042)
XLA Ops:
  2.0 3.0 collective-permute-start
  5.0 4.2 collective-permute-start.3
  11.6 2.6 collective-permute-done.far
  19.4 1.8 collective-permute-start.2
  24.8 11.4 %shard_map.189 = (f32[1024,768]{1,0:T(8,128)S(1)}, bf16[3,192,1024]{2,1,0:T(8,128)(2,1)S(1)}, f32[192,1024]{1,0:T(8,128)S(1)}, f32[8,1024]{1,0:T(8,128)S(1)}) custom-call(s32[8]{0:T(128)S(1)} %stack.74.info, bf16[1024,768]{1,0:T(8,128)(2,1)S(1)} %get-tuple-element.170.normed, bf16[4,192,768]{2,1,0:T(8,128)(2,1)S(1)} %pad_maximum_fusion.weights, ...), custom_call_target="tpu_custom_call" | custom-call | flops 8858370048 | bytes 12582912 | tf_op jit(solution)/shard_map/pallas_call | solution.py:238
  38.2 9.6 %collective-permute-done.2.weights = bf16[4,192,768]{2,1,0:T(8,128)(2,1)S(1)} collective-permute-done((bf16[4,192,768]{2,1,0:T(8,128)(2,1)S(1)}, bf16[4,192,768]{2,1,0:T(8,128)(2,1)S(1)}, u32[]{:S(2)}, u32[]{:S(2)}) %collective-permute-start.2) | collective-permute-done | bytes 1179680 | tf_op jit(solution)/shard_map/ppermute | solution.py:830
  47.8 4.2 collective-permute-start.10
  52.0 11.4 %shard_map.190 = (bf16[1024,768]{1,0:T(8,128)(2,1)S(1)}, bf16[3,192,1024]{2,1,0:T(8,128)(2,1)S(1)}, f32[192,1024]{1,0:T(8,128)S(1)}, f32[8,1024]{1,0:T(8,128)S(1)}) custom-call(s32[8]{0:T(128)S(1)} %stack.74.info, bf16[1024,768]{1,0:T(8,128)(2,1)S(1)} %get-tuple-element.170.normed, bf16[4,192,768]{2,1,0:T(8,128)(2,1)S(1)} %collective-permute-done.2.weights, ...), custom_call_target="tpu_custom_call" | custom-call | flops 8858370048 | bytes 12582912 | tf_op jit(solution)/shard_map/pallas_call | solution.py:238
  63.6 2.0 pad_maximum_fusion.1.weights_near.refs_7_
  67.0 2.6 shard_map.191
  70.6 7.2 %shard_map.193 = (f32[1024,768]{1,0:T(8,128)S(1)}, bf16[1024,768]{1,0:T(8,128)(2,1)}, f32[1024,768]{1,0:T(8,128)}) custom-call(s32[8]{0:T(128)S(1)} %stack.74.info, bf16[1024,768]{1,0:T(8,128)(2,1)} %get-tuple-element.183.normed, bf16[2,768,768]{2,1,0:T(8,128)(2,1)} %constant_dynamic-update-slice_fusion.pack.pack_near), custom_call_target="tpu_custom_call" | custom-call | flops 48318384 | bytes 188743 | tf_op jit(solution)/shard_map/pallas_call | solution.py:716
  77.8 24.9 %collective-permute-done.10.pack = bf16[2,768,768]{2,1,0:T(8,128)(2,1)S(1)} collective-permute-done((bf16[2,768,768]{2,1,0:T(8,128)(2,1)}, bf16[2,768,768]{2,1,0:T(8,128)(2,1)S(1)}, u32[]{:S(2)}, u32[]{:S(2)}) %collective-permute-start.10) | collective-permute-done | bytes 2359328 | tf_op jit(solution)/shard_map/ppermute | solution.py:835
  102.8 7.1 %shard_map.194 = (bf16[1024,768]{1,0:T(8,128)(2,1)}, bf16[1024,768]{1,0:T(8,128)(2,1)}, f32[1024,768]{1,0:T(8,128)}) custom-call(s32[8]{0:T(128)S(1)} %stack.74.info, bf16[1024,768]{1,0:T(8,128)(2,1)} %get-tuple-element.183.normed, bf16[2,768,768]{2,1,0:T(8,128)(2,1)S(1)} %collective-permute-done.10.pack, f32[1024,768]{1,0:T(8,128)S(1)} %get-tuple-element.184.refs_0_), custom_call_target="tpu_custom_call" | custom-call | flops 48318384 | bytes 188743 | tf_op jit(solution)/shard_map/pallas_call | solution.py:716
  110.0 1.8 collective-permute-start.7
  111.8 9.8 %collective-permute-done.7.far = bf16[256,768]{1,0:T(8,128)(2,1)S(1)} collective-permute-done((bf16[256,768]{1,0:T(8,128)(2,1)S(1)}, bf16[256,768]{1,0:T(8,128)(2,1)S(1)}, u32[]{:S(2)}, u32[]{:S(2)}) %collective-permute-start.7) | collective-permute-done | bytes 393248 | tf_op jit(solution)/shard_map/ppermute | solution.py:830
  123.3 2.0 collective-permute-start.8
  128.3 5.5 shard_map.195
  136.3 17.3 %collective-permute-done.12.near.refs_0_ = bf16[512,768]{1,0:T(8,128)(2,1)S(1)} collective-permute-done((bf16[512,768]{1,0:T(8,128)(2,1)S(1)}, bf16[512,768]{1,0:T(8,128)(2,1)S(1)}, u32[]{:S(2)}, u32[]{:S(2)}) %collective-permute-start.12) | collective-permute-done | bytes 786464 | tf_op jit(solution)/shard_map/ppermute | solution.py:845
  153.7 2.3 collective-permute-done.13.far.refs_1_
  156.0 1.9 shard_map.196
  160.9 3.3 collective-permute-done.14.far
  167.3 6.6 %shard_map.198 = (bf16[1024,768]{1,0:T(8,128)(2,1)}, bf16[1024,768]{1,0:T(8,128)(2,1)}, bf16[1024,768]{1,0:T(8,128)(2,1)}, bf16[1024,768]{1,0:T(8,128)(2,1)}, bf...) custom-call(s32[8]{0:T(128)S(1)} %copy-done.74, bf16[1024,768]{1,0:T(8,128)(2,1)S(1)} %get-tuple-element.189.normed, ...), custom_call_target="tpu_custom_call" | custom-call | flops 193273536 | bytes 314572 | tf_op jit(solution)/shard_map/pallas_call | solution.py:756
  174.1 3.6 collective-permute-done.15.far
  177.7 1.9 copy-done.1
  179.7 6.6 %shard_map.199 = (f32[1024,768]{1,0:T(8,128)}, bf16[1024,768]{1,0:T(8,128)(2,1)S(1)}, f32[2,768]{1,0:T(2,128)S(1)}) custom-call(bf16[1024,768]{1,0:T(8,128)(2,1)} %copy-done.55, bf16[1024,768]{1,0:T(8,128)(2,1)} %get-tuple-element.197.near, bf16[1024,768]{1,0:T(8,128)(2,1)} %collective-permute-done.15.far, f32[1024,768]{1,0:T(8,128)S(1)} %copy-done.1, ...), custom_call_target="tpu_custom_call" | custom-call | flops 314572 | bytes 283115 | tf_op jit(solution)/shard_map/pallas_call | solution.py:642
  186.3 1.9 shard_map.200
  188.6 2.1 collective-permute-done.16
  192.2 96.6 %collective-permute-done.19 = bf16[512,768]{1,0:T(8,128)(2,1)} collective-permute-done((bf16[512,768]{1,0:T(8,128)(2,1)S(1)}, bf16[512,768]{1,0:T(8,128)(2,1)}, u32[]{:S(2)}, u32[]{:S(2)}) %collective-permute-start.19) | collective-permute-done | bytes 786464 | tf_op jit(solution)/shard_map/ppermute | solution.py:849
  288.8 2.8 shard_map.206
  294.7 7.4 %conditional.4 = ((f32[1024,768]{1,0:T(8,128)}, bf16[1024,768]{1,0:T(8,128)(2,1)}, f32[2,768]{1,0:T(2,128)S(1)})) conditional(s32[]{:T(128)} %convert_element_type.69, (f32[1,3,2,768]{3,2,1,0:T(2,128)}, s32[8]{0:T(128)S(1)}, bf16[1024,768]{1,0:T(8,128)(2,1)}, bf16[512,768]{1,0:T(8,128)(2,1)}, bf16[512,768]{1,0:T(8,128)(2,1)}, ...), branch_computations={%region_0.1_spmd, %region_1.2_spmd} | conditional | flops 314572 | bytes 295411 | solution.py:991
  295.4 6.7 %branch_0_fun.4 = (f32[1024,768]{1,0:T(8,128)}, bf16[1024,768]{1,0:T(8,128)(2,1)}, f32[2,768]{1,0:T(2,128)S(1)}) custom-call(s32[8]{0:T(128)S(1)} %get-tuple-element.58.info, bf16[1024,768]{1,0:T(8,128)(2,1)} %get-tuple-element.59.cot, bf16[512,768]{1,0:T(8,128)(2,1)} %get-tuple-element.60.near, bf16[512,768]{1,0:T(8,128)(2,1)} %get-tuple-element.61.far, ...), custom_call_target="tpu_custom_call" | custom-call | flops 314572 | bytes 283115 | tf_op jit(solution)/shard_map/cond/branch_0_fun/pallas_call | solution.py:677
  302.1 11.0 %conditional.5 = ((bf16[1024,768]{1,0:T(8,128)(2,1)}, bf16[1024,768]{1,0:T(8,128)(2,1)}, bf16[1024,768]{1,0:T(8,128)(2,1)})) conditional(s32[]{:T(128)} %convert_element_type.69, (bf16[1024,768]{1,0:T(8,128)(2,1)}, f32[1024,768]{1,0:T(8,128)}, f32[1024,768]{1,0:T(8,128)}, bf16[2,768,768]{2,1,0:T(8,128)(2,1)}, ...), branch_computations={%region_2.3_spmd, %region_3.4_spmd} | conditional | flops 96636768 | bytes 3145760 | solution.py:1003
  302.1 11.0 %branch_0_fun.5 = (bf16[1024,768]{1,0:T(8,128)(2,1)}, bf16[1024,768]{1,0:T(8,128)(2,1)}, bf16[1024,768]{1,0:T(8,128)(2,1)}) custom-call(bf16[1024,768]{1,0:T(8,128)(2,1)} %get-tuple-element.64.above, f32[1024,768]{1,0:T(8,128)} %get-tuple-element.65.slope_near, f32[1024,768]{1,0:T(8,128)} %get-tuple-element.66.slope_far, ...), custom_call_target="tpu_custom_call" | custom-call | flops 96636768 | bytes 251658 | tf_op jit(solution)/shard_map/cond/branch_0_fun/pallas_call | solution.py:790
  313.7 6.4 %conditional.7 = ((f32[768,768]{1,0:T(8,128)}, bf16[768,768]{1,0:T(8,128)(2,1)})) conditional(s32[]{:T(128)} %convert_element_type.69, (bf16[1024,768]{1,0:T(8,128)(2,1)}, bf16[1024,768]{1,0:T(8,128)(2,1)}, bf16[1024,768]{1,0:T(8,128)(2,1)}) %tuple.60, (bf16[1024,768]{1,0:T(8,128)(2,1)}, bf16[1024,768]{1,0:T(8,128)(2,1)}, ...), branch_computations={%region_7.8_spmd, %region_8.9_spmd} | conditional | flops 48318384 | bytes 188751 | solution.py:1011
  313.7 6.4 %branch_0_fun.7 = (f32[768,768]{1,0:T(8,128)}, bf16[768,768]{1,0:T(8,128)(2,1)}) custom-call(bf16[1024,768]{1,0:T(8,128)(2,1)} %get-tuple-element.75.left_near.left_far, bf16[1024,768]{1,0:T(8,128)(2,1)} %get-tuple-element.75.left_near.left_far, bf16[1024,768]{1,0:T(8,128)(2,1)} %get-tuple-element.76.right_near, bf16[1024,768]{1,0:T(8,128)(2,1)} %get-tuple-element.77.right_far), custom_call_target="tpu_custom_call" | custom-call | flops 48318384 | bytes 188743 | tf_op jit(solution)/shard_map/cond/branch_0_fun/pallas_call | solution.py:818
  321.6 2.4 add_convert_fusion.1
  326.2 4.2 conditional.6
  326.2 4.0 branch_0_fun.6
  331.0 5.6 shard_map.202
  336.7 25.3 %shard_map.203 = (f32[1024,768]{1,0:T(8,128)S(1)}, bf16[4,192,768]{2,1,0:T(8,128)(2,1)S(1)}, f32[3,2048]{1,0:T(4,128)S(1)}) custom-call(s32[8]{0:T(128)S(1)} %copy-done.75, bf16[3,192,1024]{2,1,0:T(8,128)(2,1)S(1)} %copy-done.39, f32[192,1024]{1,0:T(8,128)S(1)} %copy-done.47, f32[8,1024]{1,0:T(8,128)S(1)} %copy-done.54, ...), custom_call_target="tpu_custom_call" | custom-call | flops 209379648 | bytes 125829 | tf_op jit(solution)/shard_map/pallas_call | solution.py:408
  364.8 4.3 collective-permute-start.32
  372.1 2.2 collective-permute-done.22
  375.7 4.7 collective-permute-start.39
  380.4 26.8 %shard_map.204 = (bf16[1024,768]{1,0:T(8,128)(2,1)}, f32[4,192,768]{2,1,0:T(8,128)S(1)}, f32[3,2048]{1,0:T(4,128)S(1)}) custom-call(s32[8]{0:T(128)S(1)} %copy-done.75, bf16[3,192,1024]{2,1,0:T(8,128)(2,1)S(1)} %copy-done.35, f32[192,1024]{1,0:T(8,128)S(1)} %copy-done.45, f32[8,1024]{1,0:T(8,128)S(1)} %copy-done.52, ...), custom_call_target="tpu_custom_call" | custom-call | flops 209379648 | bytes 125829 | tf_op jit(solution)/shard_map/pallas_call | solution.py:408
  408.4 4.3 all-to-all-start
  412.8 2.0 add.98
  417.6 1.8 collective-permute-start.37
  419.5 13.1 %collective-permute-done.39 = bf16[768,768]{1,0:T(8,128)(2,1)} collective-permute-done((bf16[768,768]{1,0:T(8,128)(2,1)}, bf16[768,768]{1,0:T(8,128)(2,1)}, u32[]{:S(2)}, u32[]{:S(2)}) %collective-permute-start.39) | collective-permute-done | bytes 1179680 | tf_op jit(solution)/shard_map/ppermute | solution.py:857
  432.6 2.9 add.103
  439.4 2.6 shard_map.201
  447.7 1.9 copy-done.22
  449.6 5.3 shard_map.205
  458.8 2.1 maximum_select_fusion.1
  461.4 17.8 %collective-permute-start.26 = (f32[10,768]{1,0:T(8,128)S(1)}, f32[10,768]{1,0:T(8,128)S(1)}, u32[]{:S(2)}, u32[]{:S(2)}) collective-permute-start(f32[10,768]{1,0:T(8,128)S(1)} %add.93), channel_id=1, source_target_pairs={{0,4},{12,8},{1,5},{13,9},{2,6},{14,10},{3,7},{15,11},{16,20},{28,... | collective-permute-start | bytes 92168 | tf_op jit(solution)/shard_map/ppermute | solution.py:857
  479.2 1.9 add.102
  485.1 4.9 all-to-all-start.1
  490.0 2.2 convert_bitcast_fusion
  492.8 1.9 dynamic-slice_convert_fusion
  497.0 1.9 add.104
  500.2 2.1 dynamic-slice_bitcast_fusion
  502.3 31.4 %collective-permute-done.28 = f32[10,768]{1,0:T(8,128)S(1)} collective-permute-done((f32[10,768]{1,0:T(8,128)S(1)}, f32[10,768]{1,0:T(8,128)S(1)}, u32[]{:S(2)}, u32[]{:S(2)}) %collective-permute-start.28) | collective-permute-done | bytes 30752 | tf_op jit(solution)/shard_map/ppermute | solution.py:859
  543.7 2.8 bitcast_convert_fusion.1
  546.6 11.4 %collective-permute-done.41 = bf16[768,768]{1,0:T(8,128)(2,1)} collective-permute-done((bf16[768,768]{1,0:T(8,128)(2,1)S(1)}, bf16[768,768]{1,0:T(8,128)(2,1)}, u32[]{:S(2)}, u32[]{:S(2)}) %collective-permute-start.41) | collective-permute-done | bytes 1179680 | tf_op jit(solution)/shard_map/ppermute | solution.py:859
  558.0 2.8 bitcast_convert_fusion
  (293 shorter events, 84.2 us)
Async XLA Ops:
  2.0 12.2 %collective-permute-start = (bf16[256,768]{1,0:T(8,128)(2,1)S(1)}, bf16[256,768]{1,0:T(8,128)(2,1)S(1)}, u32[]{:S(2)}, u32[]{:S(2)}) collective-permute-start(bf16[256,768]{1,0:T(8,128)(2,1)S(1)} %get-tuple-element.267), channel_id=1, source_target_pairs={{0,2},{1,3},{2,0},{3,1},{4,6},{5,7},{6,4},{7,5},{8,10},{9,11},{10,... | collective-permute-start | bytes 1179656 | tf_op jit(solution)/shard_map/ppermute | solution.py:830
  5.0 33.2 %collective-permute-start.3 = (bf16[2,192,768]{2,1,0:T(8,128)(2,1)}, bf16[2,192,768]{2,1,0:T(8,128)(2,1)}, u32[]{:S(2)}, u32[]{:S(2)}) collective-permute-start(bf16[2,192,768]{2,1,0:T(8,128)(2,1)} %bitcast.19), channel_id=1, source_target_pairs={{0,16},{1,17},{2,18},{3,19},{4,20},{5,21},{6,22},{7,23},{8,24},{9,... | collective-permute-start | bytes 1769480 | tf_op jit(solution)/shard_map/ppermute | solution.py:845
  9.3 9.2 %collective-permute-start.4 = (f32[320,3]{0,1:T(4,128)S(1)}, f32[320,3]{0,1:T(4,128)S(1)}, u32[]{:S(2)}, u32[]{:S(2)}) collective-permute-start(f32[320,3]{0,1:T(4,128)S(1)} %bitcast.78), channel_id=1, source_target_pairs={{0,2},{1,3},{2,0},{3,1},{4,6},{5,7},{6,4},{7,5},{8,10},{9,11},{10,... | collective-permute-start | bytes 11528 | tf_op jit(solution)/shard_map/ppermute | solution.py:830
  11.6 13.2 %copy-start.14 = (bf16[4,192,768]{2,1,0:T(8,128)(2,1)}, bf16[4,192,768]{2,1,0:T(8,128)(2,1)S(1)}, u32[]{:S(2)}) copy-start(bf16[4,192,768]{2,1,0:T(8,128)(2,1)S(1)} %pad_maximum_fusion.weights) | copy-start | bytes 3538948
  11.6 55.4 %copy-start.49 = (f32[2,768]{1,0:T(2,128)}, f32[2,768]{1,0:T(2,128)S(1)}, u32[]{:S(2)}) copy-start(f32[2,768]{1,0:T(2,128)S(1)} %get-tuple-element.274.norm_ref) | copy-start | bytes 18436
  15.1 7.8 %collective-permute-start.1 = (bf16[2,256,768]{2,1,0:T(8,128)(2,1)}, bf16[2,256,768]{2,1,0:T(8,128)(2,1)S(1)}, u32[]{:S(2)}, u32[]{:S(2)}) collective-permute-start(bf16[2,256,768]{2,1,0:T(8,128)(2,1)} %pad_maximum_fusion.2), channel_id=1, source_target_pairs={{0,1},{1,0},{2,3},{3,2},{4,5},{5,4},{6,7},{7,6},{8,9},{9,8},{10,11... | collective-permute-start | bytes 2359304 | tf_op jit(solution)/shard_map/ppermute | solution.py:841
  18.5 84.3 %copy-start.73 = (s32[8]{0:T(128)}, s32[8]{0:T(128)S(1)}, u32[]{:S(2)}) copy-start(s32[8]{0:T(128)S(1)} %stack.74.info) | copy-start | bytes 100
  19.4 28.4 %collective-permute-start.2 = (bf16[4,192,768]{2,1,0:T(8,128)(2,1)S(1)}, bf16[4,192,768]{2,1,0:T(8,128)(2,1)S(1)}, u32[]{:S(2)}, u32[]{:S(2)}) collective-permute-start(bf16[4,192,768]{2,1,0:T(8,128)(2,1)S(1)} %pad_maximum_fusion.weights), channel_id=1, source_target_pairs={{0,2},{1,3},{2,0},{3,1},{4,6},{5,7},{6,4},{7,5},{8,10},{9,11},{10,... | collective-permute-start | bytes 3538952 | tf_op jit(solution)/shard_map/ppermute | solution.py:830
  22.1 29.9 %copy-start.5 = (f32[3,128,2048]{2,1,0:T(8,128)}, f32[3,128,2048]{2,1,0:T(8,128)S(1)}, u32[]{:S(2)}) copy-start(f32[3,128,2048]{2,1,0:T(8,128)S(1)} %shard_map.187.table) | copy-start | bytes 9437188
  24.8 27.2 %copy-start.10 = (bf16[1024,768]{1,0:T(8,128)(2,1)}, bf16[1024,768]{1,0:T(8,128)(2,1)S(1)}, u32[]{:S(2)}) copy-start(bf16[1024,768]{1,0:T(8,128)(2,1)S(1)} %get-tuple-element.170.normed) | copy-start | bytes 4718596
  24.8 42.2 %copy-start.12 = (bf16[1024,768]{1,0:T(8,128)(2,1)}, bf16[1024,768]{1,0:T(8,128)(2,1)S(1)}, u32[]{:S(2)}) copy-start(bf16[1024,768]{1,0:T(8,128)(2,1)S(1)} %get-tuple-element.169.stream.values) | copy-start | bytes 4718596
  38.2 25.2 %copy-start.51 = (f32[8,1024]{1,0:T(8,128)}, f32[8,1024]{1,0:T(8,128)S(1)}, u32[]{:S(2)}) copy-start(f32[8,1024]{1,0:T(8,128)S(1)} %get-tuple-element.215.lse) | copy-start | bytes 98308
  47.8 15.7 %copy-start.36 = (bf16[4,192,768]{2,1,0:T(8,128)(2,1)}, bf16[4,192,768]{2,1,0:T(8,128)(2,1)S(1)}, u32[]{:S(2)}) copy-start(bf16[4,192,768]{2,1,0:T(8,128)(2,1)S(1)} %collective-permute-done.2.weights) | copy-start | bytes 3538948
  47.8 55.0 %collective-permute-start.10 = (bf16[2,768,768]{2,1,0:T(8,128)(2,1)}, bf16[2,768,768]{2,1,0:T(8,128)(2,1)S(1)}, u32[]{:S(2)}, u32[]{:S(2)}) collective-permute-start(bf16[2,768,768]{2,1,0:T(8,128)(2,1)} %constant_dynamic-update-slice_fusion.pack.pack_near), channel_id=1, source_target_pairs={{0,2},{1,3},{2,0},{3,1},{4,6},{5,7},{6,4},{7,5},{8,10},{9,11},{10,... | collective-permute-start | bytes 7077896 | tf_op jit(solution)/shard_map/ppermute | solution.py:835
  63.5 3.5 collective-permute-start.5
  65.6 4.0 collective-permute-start.6
  109.9 18.4 %collective-permute-start.11 = (bf16[1024,768]{1,0:T(8,128)(2,1)}, bf16[1024,768]{1,0:T(8,128)(2,1)}, u32[]{:S(2)}, u32[]{:S(2)}) collective-permute-start(bf16[1024,768]{1,0:T(8,128)(2,1)} %get-tuple-element.185.near), channel_id=1, source_target_pairs={{0,1},{1,0},{2,3},{3,2},{4,5},{5,4},{6,7},{7,6},{8,9},{9,8},{10,11... | collective-permute-start | bytes 4718600 | tf_op jit(solution)/shard_map/ppermute | solution.py:841
  110.0 11.6 %collective-permute-start.7 = (bf16[256,768]{1,0:T(8,128)(2,1)S(1)}, bf16[256,768]{1,0:T(8,128)(2,1)S(1)}, u32[]{:S(2)}, u32[]{:S(2)}) collective-permute-start(bf16[256,768]{1,0:T(8,128)(2,1)S(1)} %get-tuple-element.178), channel_id=1, source_target_pairs={{0,2},{1,3},{2,0},{3,1},{4,6},{5,7},{6,4},{7,5},{8,10},{9,11},{10,... | collective-permute-start | bytes 1179656 | tf_op jit(solution)/shard_map/ppermute | solution.py:830
  123.3 2.6 collective-permute-start.9
  123.3 30.4 %collective-permute-start.8 = (bf16[2,768,768]{2,1,0:T(8,128)(2,1)}, bf16[2,768,768]{2,1,0:T(8,128)(2,1)}, u32[]{:S(2)}, u32[]{:S(2)}) collective-permute-start(bf16[2,768,768]{2,1,0:T(8,128)(2,1)} %constant_dynamic-update-slice_fusion.pack.pack_near), channel_id=1, source_target_pairs={{16,18},{17,19},{18,16},{19,17},{20,22},{21,23},{22,20},{23,21},{2... | collective-permute-start | bytes 7077896 | tf_op jit(solution)/shard_map/ppermute | solution.py:835
  128.3 39.0 %copy-start.55 = (bf16[1024,768]{1,0:T(8,128)(2,1)}, bf16[1024,768]{1,0:T(8,128)(2,1)S(1)}, u32[]{:S(2)}) copy-start(bf16[1024,768]{1,0:T(8,128)(2,1)S(1)} %shard_map.192.cot.residual) | copy-start | bytes 4718596
  128.3 27.7 %copy-start.17 = (bf16[4,192,768]{2,1,0:T(8,128)(2,1)S(1)}, bf16[4,192,768]{2,1,0:T(8,128)(2,1)}, u32[]{:S(2)}) copy-start(bf16[4,192,768]{2,1,0:T(8,128)(2,1)} %copy-done.16) | copy-start | bytes 3538948
  133.8 22.2 %copy-start.8 = (bf16[4,192,768]{2,1,0:T(8,128)(2,1)S(1)}, bf16[4,192,768]{2,1,0:T(8,128)(2,1)}, u32[]{:S(2)}) copy-start(bf16[4,192,768]{2,1,0:T(8,128)(2,1)} %copy-done.7) | copy-start | bytes 3538948
  135.0 18.6 %collective-permute-start.12 = (bf16[512,768]{1,0:T(8,128)(2,1)S(1)}, bf16[512,768]{1,0:T(8,128)(2,1)S(1)}, u32[]{:S(2)}, u32[]{:S(2)}) collective-permute-start(bf16[512,768]{1,0:T(8,128)(2,1)S(1)} %constant_dynamic-slice_fusion.2), channel_id=1, source_target_pairs={{0,16},{1,17},{2,18},{3,19},{4,20},{5,21},{6,22},{7,23},{8,24},{9,... | collective-permute-start | bytes 2359304 | tf_op jit(solution)/shard_map/ppermute | solution.py:845
  153.7 2.3 collective-permute-start.13
  160.8 3.4 collective-permute-start.14
  173.9 3.8 collective-permute-start.15
  186.3 102.5 %copy-start.56 = (bf16[1024,768]{1,0:T(8,128)(2,1)}, bf16[1024,768]{1,0:T(8,128)(2,1)S(1)}, u32[]{:S(2)}) copy-start(bf16[1024,768]{1,0:T(8,128)(2,1)S(1)} %get-tuple-element.240.refs_6_.above) | copy-start | bytes 4718596
  188.3 100.5 %copy-start.24 = (bf16[512,768]{1,0:T(8,128)(2,1)S(1)}, bf16[512,768]{1,0:T(8,128)(2,1)}, u32[]{:S(2)}) copy-start(bf16[512,768]{1,0:T(8,128)(2,1)} %copy-done.23) | copy-start | bytes 2359300
  188.3 100.5 %copy-start.26 = (bf16[512,768]{1,0:T(8,128)(2,1)S(1)}, bf16[512,768]{1,0:T(8,128)(2,1)}, u32[]{:S(2)}) copy-start(bf16[512,768]{1,0:T(8,128)(2,1)} %copy-done.25) | copy-start | bytes 2359300
  188.4 2.4 collective-permute-start.16
  190.9 97.9 %collective-permute-start.19 = (bf16[512,768]{1,0:T(8,128)(2,1)S(1)}, bf16[512,768]{1,0:T(8,128)(2,1)}, u32[]{:S(2)}, u32[]{:S(2)}) collective-permute-start(bf16[512,768]{1,0:T(8,128)(2,1)S(1)} %add_convert_fusion.4), channel_id=1, source_target_pairs={{16,0},{17,1},{18,2},{19,3},{20,4},{21,5},{22,6},{23,7},{24,8},{25... | collective-permute-start | bytes 2359304 | tf_op jit(solution)/shard_map/ppermute | solution.py:849
  288.8 5.9 %collective-permute-start.20 = (bf16[512,768]{1,0:T(8,128)(2,1)}, bf16[512,768]{1,0:T(8,128)(2,1)}, u32[]{:S(2)}, u32[]{:S(2)}) collective-permute-start(bf16[512,768]{1,0:T(8,128)(2,1)} %collective-permute-done.19), channel_id=1, source_target_pairs={{0,1},{1,0},{2,3},{3,2},{4,5},{5,4},{6,7},{7,6},{8,9},{9,8},{10,11... | collective-permute-start | bytes 2359304 | tf_op jit(solution)/shard_map/ppermute | solution.py:841
  293.1 28.5 %collective-permute-start.30 = (bf16[4,192,768]{2,1,0:T(8,128)(2,1)}, bf16[4,192,768]{2,1,0:T(8,128)(2,1)}, u32[]{:S(2)}, u32[]{:S(2)}) collective-permute-start(bf16[4,192,768]{2,1,0:T(8,128)(2,1)} %get-tuple-element.242), channel_id=1, source_target_pairs={{16,18},{17,19},{18,16},{19,17},{20,22},{21,23},{22,20},{23,21},{2... | collective-permute-start | bytes 3538952 | tf_op jit(solution)/shard_map/ppermute | solution.py:835
  313.2 17.8 %collective-permute-start.21 = (bf16[1024,768]{1,0:T(8,128)(2,1)}, bf16[1024,768]{1,0:T(8,128)(2,1)}, u32[]{:S(2)}, u32[]{:S(2)}) collective-permute-start(bf16[1024,768]{1,0:T(8,128)(2,1)} %get-tuple-element.211.near), channel_id=1, source_target_pairs={{0,1},{1,0},{2,3},{3,2},{4,5},{5,4},{6,7},{7,6},{8,9},{9,8},{10,11... | collective-permute-start | bytes 4718600 | tf_op jit(solution)/shard_map/ppermute | solution.py:841
  320.1 49.0 %collective-permute-start.35 = (bf16[768,768]{1,0:T(8,128)(2,1)}, bf16[768,768]{1,0:T(8,128)(2,1)}, u32[]{:S(2)}, u32[]{:S(2)}) collective-permute-start(bf16[768,768]{1,0:T(8,128)(2,1)} %get-tuple-element.246), channel_id=1, source_target_pairs={{0,2},{1,3},{2,0},{3,1},{4,6},{5,7},{6,4},{7,5},{8,10},{9,11},{10,... | collective-permute-start | bytes 3538952 | tf_op jit(solution)/shard_map/ppermute | solution.py:830
  324.8 38.8 %collective-permute-start.31 = (bf16[2,192,768]{2,1,0:T(8,128)(2,1)}, bf16[2,192,768]{2,1,0:T(8,128)(2,1)}, u32[]{:S(2)}, u32[]{:S(2)}) collective-permute-start(bf16[2,192,768]{2,1,0:T(8,128)(2,1)} %slice.105), channel_id=1, source_target_pairs={{16,0},{17,1},{18,2},{19,3},{20,4},{21,5},{22,6},{23,7},{24,8},{25... | collective-permute-start | bytes 1769480 | tf_op jit(solution)/shard_map/ppermute | solution.py:849
  330.4 44.0 %collective-permute-start.22 = (bf16[768,768]{1,0:T(8,128)(2,1)}, bf16[768,768]{1,0:T(8,128)(2,1)S(1)}, u32[]{:S(2)}, u32[]{:S(2)}) collective-permute-start(bf16[768,768]{1,0:T(8,128)(2,1)} %get-tuple-element.222), channel_id=1, source_target_pairs={{0,2},{1,3},{2,0},{3,1},{4,6},{5,7},{6,4},{7,5},{8,10},{9,11},{10,... | collective-permute-start | bytes 3538952 | tf_op jit(solution)/shard_map/ppermute | solution.py:830
  336.7 25.4 %copy-start.21 = (f32[1024,768]{1,0:T(8,128)}, f32[1024,768]{1,0:T(8,128)S(1)}, u32[]{:S(2)}) copy-start(f32[1024,768]{1,0:T(8,128)S(1)} %get-tuple-element.212.residual) | copy-start | bytes 9437188
  336.7 26.9 %copy-start.61 = (bf16[4,192,768]{2,1,0:T(8,128)(2,1)S(1)}, bf16[4,192,768]{2,1,0:T(8,128)(2,1)}, u32[]{:S(2)}) copy-start(bf16[4,192,768]{2,1,0:T(8,128)(2,1)} %copy-done.60) | copy-start | bytes 3538948
  336.7 32.4 %copy-start.63 = (f32[768,768]{1,0:T(8,128)S(1)}, f32[768,768]{1,0:T(8,128)}, u32[]{:S(2)}) copy-start(f32[768,768]{1,0:T(8,128)} %get-tuple-element.245) | copy-start | bytes 7077892
  362.1 45.1 %collective-permute-start.29 = (bf16[4,192,768]{2,1,0:T(8,128)(2,1)S(1)}, bf16[4,192,768]{2,1,0:T(8,128)(2,1)S(1)}, u32[]{:S(2)}, u32[]{:S(2)}) collective-permute-start(bf16[4,192,768]{2,1,0:T(8,128)(2,1)S(1)} %get-tuple-element.237), channel_id=1, source_target_pairs={{0,2},{1,3},{2,0},{3,1},{4,6},{5,7},{6,4},{7,5},{8,10},{9,11},{10,... | collective-permute-start | bytes 3538952 | tf_op jit(solution)/shard_map/ppermute | solution.py:830
  363.6 74.3 %collective-permute-start.17 = (bf16[1024,768]{1,0:T(8,128)(2,1)}, bf16[1024,768]{1,0:T(8,128)(2,1)}, u32[]{:S(2)}, u32[]{:S(2)}) collective-permute-start(bf16[1024,768]{1,0:T(8,128)(2,1)} %get-tuple-element.200.near), channel_id=1, source_target_pairs={{0,1},{1,0},{2,3},{3,2},{4,5},{5,4},{6,7},{7,6},{8,9},{9,8},{10,11... | collective-permute-start | bytes 4718600 | tf_op jit(solution)/shard_map/ppermute | solution.py:841
  364.8 48.0 %collective-permute-start.32 = (bf16[2,192,768]{2,1,0:T(8,128)(2,1)S(1)}, bf16[2,192,768]{2,1,0:T(8,128)(2,1)}, u32[]{:S(2)}, u32[]{:S(2)}) collective-permute-start(bf16[2,192,768]{2,1,0:T(8,128)(2,1)S(1)} %slice_select_fusion), channel_id=1, source_target_pairs={{0,4},{12,8},{1,5},{13,9},{2,6},{14,10},{3,7},{15,11},{16,20},{28,... | collective-permute-start | bytes 1769480 | tf_op jit(solution)/shard_map/ppermute | solution.py:857
  369.1 11.3 %copy-start.35 = (bf16[3,192,1024]{2,1,0:T(8,128)(2,1)S(1)}, bf16[3,192,1024]{2,1,0:T(8,128)(2,1)}, u32[]{:S(2)}) copy-start(bf16[3,192,1024]{2,1,0:T(8,128)(2,1)} %copy-done.34) | copy-start | bytes 3538948
  369.1 11.3 %copy-start.45 = (f32[192,1024]{1,0:T(8,128)S(1)}, f32[192,1024]{1,0:T(8,128)}, u32[]{:S(2)}) copy-start(f32[192,1024]{1,0:T(8,128)} %copy-done.44) | copy-start | bytes 2359300
  370.8 45.6 %collective-permute-start.36 = (bf16[768,768]{1,0:T(8,128)(2,1)S(1)}, bf16[768,768]{1,0:T(8,128)(2,1)S(1)}, u32[]{:S(2)}, u32[]{:S(2)}) collective-permute-start(bf16[768,768]{1,0:T(8,128)(2,1)S(1)} %add_convert_fusion), channel_id=1, source_target_pairs={{0,4},{12,8},{1,5},{13,9},{2,6},{14,10},{3,7},{15,11},{16,20},{28,... | collective-permute-start | bytes 3538952 | tf_op jit(solution)/shard_map/ppermute | solution.py:857
  375.7 56.9 %collective-permute-start.39 = (bf16[768,768]{1,0:T(8,128)(2,1)}, bf16[768,768]{1,0:T(8,128)(2,1)}, u32[]{:S(2)}, u32[]{:S(2)}) collective-permute-start(bf16[768,768]{1,0:T(8,128)(2,1)} %add_convert_fusion.3), channel_id=1, source_target_pairs={{0,4},{12,8},{1,5},{13,9},{2,6},{14,10},{3,7},{15,11},{16,20},{28,... | collective-permute-start | bytes 3538952 | tf_op jit(solution)/shard_map/ppermute | solution.py:857
  408.4 74.0 %all-to-all-start = ((bf16[4,192,768]{2,1,0:T(8,128)(2,1)}), bf16[4,192,768]{2,1,0:T(8,128)(2,1)}, u32[]{:S(2)}, u32[]{:S(2)}) async-start(bf16[4,192,768]{2,1,0:T(8,128)(2,1)} %add_convert_fusion.2), calls=%async_computation | async-start | bytes 2359296 | tf_op jit(solution)/shard_map/all_to_all | solution.py:865
  412.7 34.9 %collective-permute-start.23 = (bf16[1024,768]{1,0:T(8,128)(2,1)}, bf16[1024,768]{1,0:T(8,128)(2,1)}, u32[]{:S(2)}, u32[]{:S(2)}) collective-permute-start(bf16[1024,768]{1,0:T(8,128)(2,1)} %get-tuple-element.228.near), channel_id=1, source_target_pairs={{0,1},{1,0},{2,3},{3,2},{4,5},{5,4},{6,7},{7,6},{8,9},{9,8},{10,11... | collective-permute-start | bytes 4718600 | tf_op jit(solution)/shard_map/ppermute | solution.py:841
  414.8 27.2 %collective-permute-start.33 = (bf16[2,192,768]{2,1,0:T(8,128)(2,1)}, bf16[2,192,768]{2,1,0:T(8,128)(2,1)}, u32[]{:S(2)}, u32[]{:S(2)}) collective-permute-start(bf16[2,192,768]{2,1,0:T(8,128)(2,1)} %add.98), channel_id=1, source_target_pairs={{4,8},{8,4},{5,9},{9,5},{6,10},{10,6},{7,11},{11,7},{20,24},{24,20... | collective-permute-start | bytes 1769480 | tf_op jit(solution)/shard_map/ppermute | solution.py:858
  417.6 20.3 %copy-start.2 = (f32[1024,768]{1,0:T(8,128)S(1)}, f32[1024,768]{1,0:T(8,128)}, u32[]{:S(2)}) copy-start(f32[1024,768]{1,0:T(8,128)} %copy-done) | copy-start | bytes 9437188
  417.6 61.6 %collective-permute-start.37 = (bf16[768,768]{1,0:T(8,128)(2,1)}, bf16[768,768]{1,0:T(8,128)(2,1)}, u32[]{:S(2)}, u32[]{:S(2)}) collective-permute-start(bf16[768,768]{1,0:T(8,128)(2,1)} %add.101), channel_id=1, source_target_pairs={{4,8},{8,4},{5,9},{9,5},{6,10},{10,6},{7,11},{11,7},{20,24},{24,20... | collective-permute-start | bytes 3538952 | tf_op jit(solution)/shard_map/ppermute | solution.py:858
  435.5 61.5 %collective-permute-start.40 = (bf16[768,768]{1,0:T(8,128)(2,1)}, bf16[768,768]{1,0:T(8,128)(2,1)}, u32[]{:S(2)}, u32[]{:S(2)}) collective-permute-start(bf16[768,768]{1,0:T(8,128)(2,1)} %add.103), channel_id=1, source_target_pairs={{4,8},{8,4},{5,9},{9,5},{6,10},{10,6},{7,11},{11,7},{20,24},{24,20... | collective-permute-start | bytes 3538952 | tf_op jit(solution)/shard_map/ppermute | solution.py:858
  443.4 46.6 %collective-permute-start.34 = (bf16[2,192,768]{2,1,0:T(8,128)(2,1)S(1)}, bf16[2,192,768]{2,1,0:T(8,128)(2,1)}, u32[]{:S(2)}, u32[]{:S(2)}) collective-permute-start(bf16[2,192,768]{2,1,0:T(8,128)(2,1)S(1)} %add.99), channel_id=1, source_target_pairs={{4,0},{8,12},{5,1},{9,13},{6,2},{10,14},{7,3},{11,15},{20,16},{24,... | collective-permute-start | bytes 1769480 | tf_op jit(solution)/shard_map/ppermute | solution.py:859
  444.9 13.9 %collective-permute-start.18 = (bf16[256,768]{1,0:T(8,128)(2,1)S(1)}, bf16[256,768]{1,0:T(8,128)(2,1)}, u32[]{:S(2)}, u32[]{:S(2)}) collective-permute-start(bf16[256,768]{1,0:T(8,128)(2,1)S(1)} %get-tuple-element.258), channel_id=1, source_target_pairs={{0,2},{1,3},{2,0},{3,1},{4,6},{5,7},{6,4},{7,5},{8,10},{9,11},{10,... | collective-permute-start | bytes 1179656 | tf_op jit(solution)/shard_map/ppermute | solution.py:830
  457.2 4.1 collective-permute-start.25
  461.4 30.8 %collective-permute-start.26 = (f32[10,768]{1,0:T(8,128)S(1)}, f32[10,768]{1,0:T(8,128)S(1)}, u32[]{:S(2)}, u32[]{:S(2)}) collective-permute-start(f32[10,768]{1,0:T(8,128)S(1)} %add.93), channel_id=1, source_target_pairs={{0,4},{12,8},{1,5},{13,9},{2,6},{14,10},{3,7},{15,11},{16,20},{28,... | collective-permute-start | bytes 92168 | tf_op jit(solution)/shard_map/ppermute | solution.py:857
  481.1 62.6 %collective-permute-start.38 = (bf16[768,768]{1,0:T(8,128)(2,1)S(1)}, bf16[768,768]{1,0:T(8,128)(2,1)}, u32[]{:S(2)}, u32[]{:S(2)}) collective-permute-start(bf16[768,768]{1,0:T(8,128)(2,1)S(1)} %add.102), channel_id=1, source_target_pairs={{4,0},{8,12},{5,1},{9,13},{6,2},{10,14},{7,3},{11,15},{20,16},{24,... | collective-permute-start | bytes 3538952 | tf_op jit(solution)/shard_map/ppermute | solution.py:859
  485.1 75.8 %all-to-all-start.1 = ((bf16[4,192,768]{2,1,0:T(8,128)(2,1)}), bf16[4,192,768]{2,1,0:T(8,128)(2,1)S(1)}, u32[]{:S(2)}, u32[]{:S(2)}) async-start(bf16[4,192,768]{2,1,0:T(8,128)(2,1)} %broadcast_in_dim.43), calls=%async_computation.1 | async-start | bytes 2359296 | tf_op jit(solution)/shard_map/all_to_all | solution.py:867
  492.2 3.5 collective-permute-start.27
  494.8 46.7 %collective-permute-start.24 = (bf16[256,768]{1,0:T(8,128)(2,1)}, bf16[256,768]{1,0:T(8,128)(2,1)}, u32[]{:S(2)}, u32[]{:S(2)}) collective-permute-start(bf16[256,768]{1,0:T(8,128)(2,1)} %dynamic-slice_convert_fusion), channel_id=1, source_target_pairs={{0,2},{1,3},{2,0},{3,1},{4,6},{5,7},{6,4},{7,5},{8,10},{9,11},{10,... | collective-permute-start | bytes 1179656 | tf_op jit(solution)/shard_map/ppermute | solution.py:830
  495.7 38.0 %collective-permute-start.28 = (f32[10,768]{1,0:T(8,128)S(1)}, f32[10,768]{1,0:T(8,128)S(1)}, u32[]{:S(2)}, u32[]{:S(2)}) collective-permute-start(f32[10,768]{1,0:T(8,128)S(1)} %add.95), channel_id=1, source_target_pairs={{4,0},{8,12},{5,1},{9,13},{6,2},{10,14},{7,3},{11,15},{20,16},{24,... | collective-permute-start | bytes 92168 | tf_op jit(solution)/shard_map/ppermute | solution.py:859
  498.9 59.1 %collective-permute-start.41 = (bf16[768,768]{1,0:T(8,128)(2,1)S(1)}, bf16[768,768]{1,0:T(8,128)(2,1)}, u32[]{:S(2)}, u32[]{:S(2)}) collective-permute-start(bf16[768,768]{1,0:T(8,128)(2,1)S(1)} %add.104), channel_id=1, source_target_pairs={{4,0},{8,12},{5,1},{9,13},{6,2},{10,14},{7,3},{11,15},{20,16},{24,... | collective-permute-start | bytes 3538952 | tf_op jit(solution)/shard_map/ppermute | solution.py:859
  (62 other events, 262.6 us)

commit v4 on v3

--- a/solution.py
+++ b/solution.py
@@ -19,7 +19,6 @@
 NT = (((1,), (1,)), ((), ()))
 TN = (((0,), (0,)), ((), ()))
 TILE = 256
-QUERIES = 512
 BAND = 128
 ENCODER, DECODER = 0, 1
 ROLE, OWN_LEN, SOURCE_LEN, CORE, START = 0, 1, 2, 3, 4
@@ -122,9 +121,12 @@
 
 
 def unskewed(band):
-    width = band.shape[1]
-    amount = (BAND - 1) - lax.broadcasted_iota(jnp.int32, (BAND, width), 0)
-    for bit in range(7):
+    rows, width = band.shape
+    while rows > 8:
+        rows //= 2
+        band = pltpu.roll(band[:rows], rows, 1) + band[rows:]
+    amount = (rows - 1) - lax.broadcasted_iota(jnp.int32, (rows, width), 0)
+    for bit in range(3):
         band = jnp.where(((amount >> bit) & 1) == 1, pltpu.roll(band, 1 << bit, 1), band)
     return jnp.sum(band, 0, keepdims=True)
 
@@ -141,62 +143,44 @@
     return slice(head * HEAD_DIM, (head + 1) * HEAD_DIM)
 
 
-def allowed_keys(info, start, length, causal, length_at):
-    key = lax.broadcasted_iota(jnp.int32, (length, QUERIES), 0)
+def allowed_keys(info, length, causal, length_at):
+    key = lax.broadcasted_iota(jnp.int32, (length, length), 0)
     last = info[length_at] - 1
     if not causal:
         return key <= last
-    query = start + lax.broadcasted_iota(jnp.int32, (1, QUERIES), 1)
+    query = lax.broadcasted_iota(jnp.int32, (1, length), 1)
     free = jnp.where(info[ROLE] == DECODER, 0, 1 << 20)
     return key <= jnp.minimum(query + free, last)
 
 
-def bias_block(table_ref, head, start, length):
-    blocks = []
-    for band in range(length // BAND):
-        offset = pl.multiple_of(length - BAND - band * BAND + start, BAND)
-        blocks.append(table_ref[head, :, pl.ds(offset, QUERIES)])
-    return jnp.concatenate(blocks, 0)
-
-
-def upright(source, place, target):
-    def step(cols):
-        block = source[place, :, cols].astype(F32).T
-        for head in range(target.shape[0]):
-            target[head, cols, :] = block[:, head_span(head)].astype(BF)
-
-    by_blocks(source.shape[2], step)
-
-
-def attend_loop(info, qkv_ref, keys_ref, table_ref, out_ref, lse_ref, length_at):
+def scores_of(queries, keys, allowed, table_ref, head):
+    scores = mm(keys, queries, TN)
+    if table_ref is not None:
+        length = scores.shape[0]
+        starts = range(length - BAND, -BAND, -BAND)
+        bands = [table_ref[head, :, start : start + length] for start in starts]
+        scores = scores + jnp.concatenate(bands, 0)
+    return jnp.where(allowed, scores, MASKED)
+
+
+def attend(info, qkv_ref, table_ref, out_ref, lse_ref, length_at):
     width, length = out_ref.shape
-    causal = table_ref is not None
-
-    def block(index, carry):
-        start = pl.multiple_of(index * QUERIES, QUERIES)
-        cols = pl.ds(start, QUERIES)
-        allowed = allowed_keys(info, start, length, causal, length_at)
-        for head in range(width // HEAD_DIM):
-            span = head_span(head)
-            queries = qkv_ref[0, span, cols] * jnp.asarray(SCALE, BF)
-            scores = mm(keys_ref[head], queries, NN)
-            if causal:
-                scores = scores + bias_block(table_ref, head, start, length)
-            scores = jnp.where(allowed, scores, MASKED)
-            peak = jnp.max(scores, 0, keepdims=True)
-            lifted = jnp.exp(scores - peak)
-            total = jnp.sum(lifted, 0, keepdims=True)
-            mixed = mm(qkv_ref[2, span, :], lifted.astype(BF), NN)
-            out_ref[span, cols] = mixed / total
-            lse_ref[head : head + 1, cols] = peak + jnp.log(total)
-        return carry
-
-    lax.fori_loop(0, length // QUERIES, block, 0)
+    allowed = allowed_keys(info, length, table_ref is not None, length_at)
+    for head in range(width // HEAD_DIM):
+        span = head_span(head)
+        queries = qkv_ref[0, span, :] * jnp.asarray(SCALE, BF)
+        scores = scores_of(queries, qkv_ref[1, span, :], allowed, table_ref, head)
+        peak = jnp.max(scores, 0, keepdims=True)
+        lifted = jnp.exp(scores - peak)
+        total = jnp.sum(lifted, 0, keepdims=True)
+        mixed = mm(qkv_ref[2, span, :], lifted.astype(BF), NN)
+        out_ref[span, :] = mixed / total
+        lse_ref[head : head + 1, :] = peak + jnp.log(total)
 
 
 def self_forward_kernel(has_sum, info, normed, weights, table, *refs):
     previous = refs[0] if has_sum else None
-    sum_ref, qkv_ref, out_ref, lse_ref, keys = refs[1 if has_sum else 0 :]
+    sum_ref, qkv_ref, out_ref, lse_ref = refs[1 if has_sum else 0 :]
     length = out_ref.shape[1]
 
     def inputs(cols):
@@ -205,8 +189,7 @@
             qkv_ref[place, :, cols] = mm(weights[place], block, NT).astype(BF)
 
     by_blocks(length, inputs)
-    upright(qkv_ref, 1, keys)
-    attend_loop(info, qkv_ref, keys, table, out_ref, lse_ref, OWN_LEN)
+    attend(info, qkv_ref, table, out_ref, lse_ref, OWN_LEN)
 
     def outputs(cols):
         value = mm(out_ref[:, cols].astype(BF), weights[3], TN)
@@ -240,15 +223,18 @@
         out_shape=(shape((length, model), BF if has_sum else F32),) + saved_shapes(length, width),
         in_specs=[scalars()] + [whole()] * (len(operands) - 1),
         out_specs=(whole(),) * 4,
-        scratch_shapes=[pltpu.VMEM((width // HEAD_DIM, length, HEAD_DIM), BF)],
         compiler_params=params(),
         cost_estimate=attention_cost(length, width, model, 2, 4, HIDES_MUCH),
     )(*operands)
 
 
+def rows_of(ref, place, width):
+    return ref[place * width : (place + 1) * width, :]
+
+
 def cross_forward_kernel(info, normed, near, far, weights_near, weights_far, *refs):
-    sum_ref, keys = refs[0], refs[7]
-    length = normed.shape[0]
+    sum_ref = refs[0]
+    length, width = normed.shape[0], weights_near.shape[0] // 4
     half = near.shape[0]
     sides = ((weights_near, refs[1:4]), (weights_far, refs[4:7]))
 
@@ -257,7 +243,7 @@
         for weights, (qkv_ref, out_ref, lse_ref) in sides:
 
             def queries(cols, weights=weights, qkv_ref=qkv_ref):
-                qkv_ref[0, :, cols] = mm(weights[0], normed[cols, :], NT).astype(BF)
+                qkv_ref[0, :, cols] = mm(rows_of(weights, 0, width), normed[cols, :], NT).astype(BF)
 
             by_blocks(length, queries)
             for piece, side in ((near, info[CORE]), (far, 1 - info[CORE])):
@@ -268,16 +254,15 @@
                     block = piece[pl.ds(local, TILE), :]
                     cols = pl.ds(pl.multiple_of(base + local, TILE), TILE)
                     for place in (1, 2):
-                        qkv_ref[place, :, cols] = mm(weights[1 + place], block, NT).astype(BF)
+                        qkv_ref[place, :, cols] = mm(rows_of(weights, 1 + place, width), block, NT).astype(BF)
                     return carry
 
                 lax.fori_loop(0, half // TILE, sources, 0)
-            upright(qkv_ref, 1, keys)
-            attend_loop(info, qkv_ref, keys, None, out_ref, lse_ref, SOURCE_LEN)
+            attend(info, qkv_ref, None, out_ref, lse_ref, SOURCE_LEN)
 
         def outputs(cols):
-            value = mm(refs[2][:, cols].astype(BF), weights_near[1], TN)
-            value = value + mm(refs[5][:, cols].astype(BF), weights_far[1], TN)
+            value = mm(refs[2][:, cols].astype(BF), rows_of(weights_near, 1, width), TN)
+            value = value + mm(refs[5][:, cols].astype(BF), rows_of(weights_far, 1, width), TN)
             sum_ref[cols, :] = value.astype(sum_ref.dtype)
 
         by_blocks(length, outputs)
@@ -285,104 +270,56 @@
 
 def cross_forward(info, normed, near, far, weights_near, weights_far):
     length, model = normed.shape
-    width = weights_near.shape[1]
+    width = weights_near.shape[0] // 4
     saved = saved_shapes(length, width)
     results = pl.pallas_call(
         cross_forward_kernel,
         out_shape=(shape((length, model), BF),) + saved + saved,
         in_specs=[scalars()] + [whole()] * 5,
         out_specs=(whole(),) * 7,
-        scratch_shapes=[pltpu.VMEM((width // HEAD_DIM, length, HEAD_DIM), BF)],
         compiler_params=params(),
         cost_estimate=attention_cost(length, 2 * width, model, 2, 4),
     )(info, normed, near, far, weights_near, weights_far)
     return results[0], results[1:4], results[4:7]
 
 
-def attend_back_loop(
-    info, saved, table_ref, upstream, grads_ref, upright_refs, key_sum, value_sum, band, length_at
-):
+def attend_back(info, saved, table_ref, upstream, grads_ref, band, length_at):
     qkv_ref, out_ref, lse_ref = saved
     width, length = out_ref.shape
-    causal = table_ref is not None
-    keys_up, values_up, queries_up, above_up = upright_refs
-    upright(qkv_ref, 1, keys_up)
-    upright(qkv_ref, 2, values_up)
-    upright(qkv_ref, 0, queries_up)
-    upright(upstream, 0, above_up)
-    key_sum[...] = jnp.zeros_like(key_sum)
-    value_sum[...] = jnp.zeros_like(value_sum)
-    if causal:
+    allowed = allowed_keys(info, length, table_ref is not None, length_at)
+    if table_ref is not None:
         band[...] = jnp.zeros_like(band)
-
-    def block(index, carry):
-        start = pl.multiple_of(index * QUERIES, QUERIES)
-        cols = pl.ds(start, QUERIES)
-        allowed = allowed_keys(info, start, length, causal, length_at)
-        for head in range(width // HEAD_DIM):
-            span = head_span(head)
-            queries = qkv_ref[0, span, cols] * jnp.asarray(SCALE, BF)
-            scores = mm(keys_up[head], queries, NN)
-            if causal:
-                scores = scores + bias_block(table_ref, head, start, length)
-            scores = jnp.where(allowed, scores, MASKED)
-            probs = jnp.exp(scores - lse_ref[head : head + 1, cols])
-            above = upstream[0, span, cols]
-            d_probs = mm(values_up[head], above, NN)
-            inner = above.astype(F32) * out_ref[span, cols]
-            inner = jnp.sum(inner, 0, keepdims=True)
-            d_scores = probs * (d_probs - inner)
-            low = d_scores.astype(BF)
-            grads_ref[0, span, cols] = (mm(qkv_ref[1, span, :], low, NN) * SCALE).astype(BF)
-            key_sum[head] += mm(low, queries_up[head, cols, :], NN)
-            value_sum[head] += mm(probs.astype(BF), above_up[head, cols, :], NN)
-            if causal:
-                for part in range(length // BAND):
-                    offset = pl.multiple_of(length - BAND - part * BAND + start, BAND)
-                    place = pl.ds(offset, QUERIES)
-                    band[head, :, place] += d_scores[part * BAND : (part + 1) * BAND, :]
-        return carry
-
-    lax.fori_loop(0, length // QUERIES, block, 0)
     for head in range(width // HEAD_DIM):
         span = head_span(head)
-        grads_ref[1, span, :] = (key_sum[head] * SCALE).T.astype(BF)
-        grads_ref[2, span, :] = value_sum[head].T.astype(BF)
-
-
-def back_scratch(length, width):
-    heads = width // HEAD_DIM
-    return [
-        pltpu.VMEM((1, width, length), BF),
-        *[pltpu.VMEM((heads, length, HEAD_DIM), BF) for _ in range(4)],
-        pltpu.VMEM((heads, length, HEAD_DIM), F32),
-        pltpu.VMEM((heads, length, HEAD_DIM), F32),
-    ]
+        queries = qkv_ref[0, span, :] * jnp.asarray(SCALE, BF)
+        keys, above = qkv_ref[1, span, :], upstream[span, :]
+        scores = scores_of(queries, keys, allowed, table_ref, head)
+        probs = jnp.exp(scores - lse_ref[head : head + 1, :])
+        inner = jnp.sum(above.astype(F32) * out_ref[span, :], 0, keepdims=True)
+        d_scores = probs * (mm(qkv_ref[2, span, :], above, TN) - inner)
+        low = d_scores.astype(BF)
+        grads_ref[0, span, :] = (mm(keys, low, NN) * SCALE).astype(BF)
+        grads_ref[1, span, :] = mm(queries, low, NT).astype(BF)
+        grads_ref[2, span, :] = mm(above, probs.astype(BF), NT).astype(BF)
+        if table_ref is not None:
+            for part in range(length // BAND):
+                start = length - BAND - part * BAND
+                rows = slice(part * BAND, (part + 1) * BAND)
+                band[head, :, start : start + length] += d_scores[rows, :]
 
 
 def self_backward_kernel(has_sum, info, qkv, out, lse, above, normed, weights, table, *refs):
     previous = refs[0] if has_sum else None
     refs = refs[1 if has_sum else 0 :]
     sum_ref, weight_ref, spread_ref, upstream = refs[:4]
-    upright_refs, key_sum, value_sum, band, grads_ref = refs[4:8], refs[8], refs[9], refs[10], refs[11]
+    band, grads_ref = refs[4:6]
     length = above.shape[0]
 
     def entering(cols):
-        upstream[0, :, cols] = mm(weights[3], above[cols, :], NT).astype(BF)
+        upstream[:, cols] = mm(weights[3], above[cols, :], NT).astype(BF)
 
     by_blocks(length, entering)
-    attend_back_loop(
-        info,
-        (qkv, out, lse),
-        table,
-        upstream,
-        grads_ref,
-        upright_refs,
-        key_sum,
-        value_sum,
-        band,
-        OWN_LEN,
-    )
+    attend_back(info, (qkv, out, lse), table, upstream, grads_ref, band, OWN_LEN)
 
     def leaving(cols):
         value = mm(grads_ref[0, :, cols], weights[0], TN)
@@ -414,18 +351,20 @@
         ),
         in_specs=[scalars()] + [whole()] * (len(operands) - 1),
         out_specs=(whole(),) * 3,
-        scratch_shapes=back_scratch(length, width)
-        + [pltpu.VMEM(table.shape, F32), pltpu.VMEM((3, width, length), BF)],
-        compiler_params=params(),
-        cost_estimate=attention_cost(length, width, model, 5, 8),
+        scratch_shapes=[
+            pltpu.VMEM((width, length), BF),
+            pltpu.VMEM(table.shape, F32),
+            pltpu.VMEM((3, width, length), BF),
+        ],
+        compiler_params=params(),
+        cost_estimate=attention_cost(length, width, model, 5, 8, HIDES_MUCH),
     )(*operands)
 
 
 def cross_backward_kernel(info, *refs):
     saved_near, saved_far, (above, weights_near, weights_far) = refs[:3], refs[3:6], refs[6:9]
     sum_ref, source_ref, grads_near, grads_far, upstream = refs[9:14]
-    upright_refs, key_sum, value_sum = refs[14:18], refs[18], refs[19]
-    length = above.shape[0]
+    length, width = above.shape[0], weights_near.shape[0] // 4
 
     @pl.when(info[ROLE] == DECODER)
     def _():
@@ -435,30 +374,19 @@
         ):
 
             def entering(cols, weights=weights):
-                upstream[0, :, cols] = mm(weights[1], above[cols, :], NT).astype(BF)
+                upstream[:, cols] = mm(rows_of(weights, 1, width), above[cols, :], NT).astype(BF)
 
             by_blocks(length, entering)
-            attend_back_loop(
-                info,
-                saved,
-                None,
-                upstream,
-                grads_ref,
-                upright_refs,
-                key_sum,
-                value_sum,
-                None,
-                SOURCE_LEN,
-            )
+            attend_back(info, saved, None, upstream, grads_ref, None, SOURCE_LEN)
 
         def leaving(cols):
-            value = mm(grads_near[0, :, cols], weights_near[0], TN)
-            value = value + mm(grads_far[0, :, cols], weights_far[0], TN)
+            value = mm(grads_near[0, :, cols], rows_of(weights_near, 0, width), TN)
+            value = value + mm(grads_far[0, :, cols], rows_of(weights_far, 0, width), TN)
             sum_ref[cols, :] = value.astype(BF)
             source = None
             for grads_ref, weights in ((grads_near, weights_near), (grads_far, weights_far)):
                 for place in (1, 2):
-                    term = mm(grads_ref[place, :, cols], weights[1 + place], TN)
+                    term = mm(grads_ref[place, :, cols], rows_of(weights, 1 + place, width), TN)
                     source = term if source is None else source + term
             source_ref[cols, :] = source.astype(BF)
 
@@ -467,14 +395,14 @@
 
 def cross_backward(info, saved_near, saved_far, above, weights_near, weights_far):
     length, model = above.shape
-    width = weights_near.shape[1]
+    width = weights_near.shape[0] // 4
     out, grads = shape((length, model), BF), shape((3, width, length), BF)
     return pl.pallas_call(
         cross_backward_kernel,
         out_shape=(out, out, grads, grads),
         in_specs=[scalars()] + [whole()] * 9,
         out_specs=(whole(),) * 4,
-        scratch_shapes=back_scratch(length, width),
+        scratch_shapes=[pltpu.VMEM((width, length), BF)],
         compiler_params=params(),
         cost_estimate=attention_cost(length, 2 * width, model, 5, 4),
     )(info, *saved_near, *saved_far, above, weights_near, weights_far)
@@ -517,6 +445,10 @@
     return pl.BlockSpec((TILE, width), lambda index: (index, 0))
 
 
+def pack_spec(place, width):
+    return pl.BlockSpec((width, width), lambda index: (place, 0))
+
+
 def fixed_spec(dims):
     return pl.BlockSpec(dims, lambda index: (0,) * len(dims))
 
@@ -650,9 +582,145 @@
     )(residual, near, far, values, norm)
 
 
-def source_back_kernel(
-    info, cot, near, far, values, norm_ref, grad_ref, low_ref, norm_grad_ref
-):
+def gelu_parts(hidden):
+    half = 0.5 * (1.0 + lax.erf(hidden * math.sqrt(0.5)))
+    slope = half + hidden * jnp.exp(-0.5 * hidden * hidden) * (1.0 / math.sqrt(2.0 * math.pi))
+    return hidden * half, slope
+
+
+def feed_forward_kernel(has_sum, info, normed, pack, *refs):
+    previous = refs[0] if has_sum else None
+    sum_ref, active_ref, slope_ref = refs[1 if has_sum else 0 :]
+
+    @pl.when(info[ROLE] == ENCODER)
+    def _():
+        active, slope = gelu_parts(mm(normed[...], pack[0], NN))
+        active = active.astype(BF)
+        active_ref[...] = active
+        slope_ref[...] = slope.astype(BF)
+        value = mm(active, pack[1], NN)
+        if has_sum:
+            value = value + previous[...]
+        sum_ref[...] = value.astype(sum_ref.dtype)
+
+
+def feed_forward(info, normed, pack, previous):
+    length, model = normed.shape
+    hidden = pack.shape[2]
+    has_sum = previous is not None
+    operands = [info, normed, pack] + ([previous] if has_sum else [])
+    return pl.pallas_call(
+        functools.partial(feed_forward_kernel, has_sum),
+        grid=(length // TILE,),
+        out_shape=(
+            shape((length, model), BF if has_sum else F32),
+            shape((length, hidden), BF),
+            shape((length, hidden), BF),
+        ),
+        in_specs=[scalars(), row_spec(model), fixed_spec(pack.shape)]
+        + ([row_spec(model)] if has_sum else []),
+        out_specs=(row_spec(model), row_spec(hidden), row_spec(hidden)),
+        compiler_params=params(),
+        cost_estimate=cost(4 * length * model * hidden, length * model * 12),
+    )(*operands)
+
+
+def feed_above_kernel(info, cot, down_near, down_far, near_ref, far_ref):
+    @pl.when(info[ROLE] == DECODER)
+    def _():
+        near_ref[...] = mm(cot[...], down_near[...], NT)
+        far_ref[...] = mm(cot[...], down_far[...], NT)
+
+
+def feed_above(info, cot, down_near, down_far):
+    length, model = cot.shape
+    hidden = down_near.shape[0]
+    unit = shape((length, hidden), F32)
+    return pl.pallas_call(
+        feed_above_kernel,
+        grid=(length // TILE,),
+        out_shape=(unit, unit),
+        in_specs=[
+            scalars(),
+            row_spec(model),
+            fixed_spec(down_near.shape),
+            pack_spec(1, model),
+        ],
+        out_specs=(row_spec(hidden),) * 2,
+        compiler_params=params(),
+        cost_estimate=cost(4 * length * model * hidden, length * model * 10),
+    )(info, cot, down_near, down_far)
+
+
+def feed_both_kernel(info, normed, above_near, above_far, up_near, up_far, back_ref, *refs):
+    @pl.when(info[ROLE] == DECODER)
+    def _():
+        back = None
+        for up, above, active_ref, grad_ref in (
+            (up_near, above_near, *refs[0:2]),
+            (up_far, above_far, *refs[2:4]),
+        ):
+            active, slope = gelu_parts(mm(normed[...], up[...], NN))
+            active_ref[...] = active.astype(BF)
+            grad = (above[...] * slope).astype(BF)
+            grad_ref[...] = grad
+            term = mm(grad, up[...], NT)
+            back = term if back is None else back + term
+        back_ref[...] = back.astype(BF)
+
+
+def feed_both(info, normed, above, up_near, up_far):
+    length, model = normed.shape
+    hidden = up_near.shape[1]
+    out, unit = shape((length, model), BF), shape((length, hidden), BF)
+    return pl.pallas_call(
+        feed_both_kernel,
+        grid=(length // TILE,),
+        out_shape=(out, unit, unit, unit, unit),
+        in_specs=[
+            scalars(),
+            row_spec(model),
+            row_spec(hidden),
+            row_spec(hidden),
+            fixed_spec(up_near.shape),
+            fixed_spec(up_far.shape),
+        ],
+        out_specs=(row_spec(model),) + (row_spec(hidden),) * 4,
+        compiler_params=params(),
+        cost_estimate=cost(8 * length * model * hidden, length * model * 20),
+    )(info, normed, *above, up_near, up_far)
+
+
+def feed_value_kernel(info, active_near, active_far, down_near, down_far, sum_ref):
+    @pl.when(info[ROLE] == DECODER)
+    def _():
+        value = mm(active_near[...], down_near[...], NN) + mm(active_far[...], down_far[...], NN)
+        sum_ref[...] = value.astype(BF)
+
+
+def feed_value(info, active_near, active_far, down_near, down_far):
+    length, hidden = active_near.shape
+    model = down_near.shape[1]
+    return pl.pallas_call(
+        feed_value_kernel,
+        grid=(length // TILE,),
+        out_shape=shape((length, model), BF),
+        in_specs=[
+            scalars(),
+            row_spec(hidden),
+            row_spec(hidden),
+            fixed_spec(down_near.shape),
+            pack_spec(1, model),
+        ],
+        out_specs=row_spec(model),
+        compiler_params=params(),
+        cost_estimate=cost(4 * length * model * hidden, length * model * 6),
+    )(info, active_near, active_far, down_near, down_far)
+
+
+def source_back_kernel(info, cot, near, far, values, norm_ref, *refs):
+    slope_near, slope_far, pack_near, pack_far, grad_ref, low_ref, norm_grad_ref = refs[:7]
+    back_ref, hidden_near, hidden_far = refs[7:]
     index = pl.program_id(0)
     blocks = near.shape[0] // TILE
     rows = pl.ds(pl.multiple_of(lax.rem(index, blocks) * TILE, TILE), TILE)
@@ -661,8 +729,9 @@
     upstream = cot[...].astype(F32) + returned
     upstream = jnp.where(row_mask(info, index, OWN_LEN), upstream, 0.0)
     grad, gain, shift = norm_back(upstream, values[...], norm_ref)
+    low = grad.astype(BF)
     grad_ref[...] = grad
-    low_ref[...] = grad.astype(BF)
+    low_ref[...] = low
 
     @pl.when(index == 0)
     def _():
@@ -670,138 +739,56 @@
 
     norm_grad_ref[0:1, :] += gain
     norm_grad_ref[1:2, :] += shift
-
-
-def source_back(info, cot, near, far, values, norm):
+    back = None
+    for pack, slope, hidden_ref in (
+        (pack_near, slope_near, hidden_near),
+        (pack_far, slope_far, hidden_far),
+    ):
+        hidden = (mm(low, pack[1], NT) * slope[...].astype(F32)).astype(BF)
+        hidden_ref[...] = hidden
+        term = mm(hidden, pack[0], NT)
+        back = term if back is None else back + term
+    back_ref[...] = back.astype(BF)
+
+
+def source_back(info, cot, near, far, values, norm, slope_near, slope_far, pack_near, pack_far):
     length, model = values.shape
+    hidden = pack_near.shape[2]
+    unit = shape((length, hidden), BF)
     return pl.pallas_call(
         source_back_kernel,
         grid=(length // TILE,),
-        out_shape=(shape((length, model), F32), shape((length, model), BF), shape((2, model), F32)),
-        in_specs=[scalars(), row_spec(model), fixed_spec(near.shape), fixed_spec(far.shape)]
-        + [row_spec(model), fixed_spec((2, model))],
-        out_specs=(row_spec(model), row_spec(model), fixed_spec((2, model))),
-        compiler_params=params(),
-        cost_estimate=cost(length * model * 20, length * model * 18),
-    )(info, cot, near, far, values, norm)
-
-
-def gelu_parts(hidden):
-    half = 0.5 * (1.0 + lax.erf(hidden * math.sqrt(0.5)))
-    slope = half + hidden * jnp.exp(-0.5 * hidden * hidden) * (1.0 / math.sqrt(2.0 * math.pi))
-    return hidden * half, slope
-
-
-def feed_forward_kernel(has_sum, info, normed, pack, *refs):
-    previous = refs[0] if has_sum else None
-    sum_ref, active_ref, slope_ref = refs[1 if has_sum else 0 :]
-
-    @pl.when(info[ROLE] == ENCODER)
-    def _():
-        active, slope = gelu_parts(mm(normed[...], pack[0], NN))
-        active = active.astype(BF)
-        active_ref[...] = active
-        slope_ref[...] = slope
-        value = mm(active, pack[1], NN)
-        if has_sum:
-            value = value + previous[...]
-        sum_ref[...] = value.astype(sum_ref.dtype)
-
-
-def feed_forward(info, normed, pack, previous):
-    length, model = normed.shape
-    hidden = pack.shape[2]
-    has_sum = previous is not None
-    operands = [info, normed, pack] + ([previous] if has_sum else [])
-    return pl.pallas_call(
-        functools.partial(feed_forward_kernel, has_sum),
-        grid=(length // TILE,),
         out_shape=(
-            shape((length, model), BF if has_sum else F32),
-            shape((length, hidden), BF),
-            shape((length, hidden), F32),
+            shape((length, model), F32),
+            shape((length, model), BF),
+            shape((2, model), F32),
+            shape((length, model), BF),
+            unit,
+            unit,
         ),
-        in_specs=[scalars(), row_spec(model), fixed_spec(pack.shape)]
-        + ([row_spec(model)] if has_sum else []),
-        out_specs=(row_spec(model), row_spec(hidden), row_spec(hidden)),
-        compiler_params=params(),
-        cost_estimate=cost(4 * length * model * hidden, length * model * 12),
-    )(*operands)
-
-
-def feed_both_kernel(info, normed, cot, pack_near, pack_far, *refs):
-    sum_ref, back_ref = refs[:2]
-
-    @pl.when(info[ROLE] == DECODER)
-    def _():
-        value, back = None, None
-        for pack, active_ref, grad_ref in ((pack_near, *refs[2:4]), (pack_far, *refs[4:6])):
-            active, slope = gelu_parts(mm(normed[...], pack[0], NN))
-            active = active.astype(BF)
-            active_ref[...] = active
-            term = mm(active, pack[1], NN)
-            value = term if value is None else value + term
-            grad = (mm(cot[...], pack[1], NT) * slope).astype(BF)
-            grad_ref[...] = grad
-            term = mm(grad, pack[0], NT)
-            back = term if back is None else back + term
-        sum_ref[...] = value.astype(BF)
-        back_ref[...] = back.astype(BF)
-
-
-def feed_both(info, normed, cot, pack_near, pack_far):
-    length, model = normed.shape
-    hidden = pack_near.shape[2]
-    out, unit = shape((length, model), BF), shape((length, hidden), BF)
-    return pl.pallas_call(
-        feed_both_kernel,
-        grid=(length // TILE,),
-        out_shape=(out, out, unit, unit, unit, unit),
         in_specs=[
             scalars(),
             row_spec(model),
+            fixed_spec(near.shape),
+            fixed_spec(far.shape),
             row_spec(model),
-            fixed_spec(pack_near.shape),
-            fixed_spec(pack_far.shape),
-        ],
-        out_specs=(row_spec(model),) * 2 + (row_spec(hidden),) * 4,
-        compiler_params=params(),
-        cost_estimate=cost(16 * length * model * hidden, length * model * 20),
-    )(info, normed, cot, pack_near, pack_far)
-
-
-def feed_back_kernel(above, slope_near, slope_far, pack_near, pack_far, back_ref, *grad_refs):
-    back = None
-    for pack, slope, grad_ref in (
-        (pack_near, slope_near, grad_refs[0]),
-        (pack_far, slope_far, grad_refs[1]),
-    ):
-        grad = (mm(above[...], pack[1], NT) * slope[...]).astype(BF)
-        grad_ref[...] = grad
-        term = mm(grad, pack[0], NT)
-        back = term if back is None else back + term
-    back_ref[...] = back.astype(BF)
-
-
-def feed_back(above, slope_near, slope_far, pack_near, pack_far):
-    length, model = above.shape
-    hidden = pack_near.shape[2]
-    unit = shape((length, hidden), BF)
-    return pl.pallas_call(
-        feed_back_kernel,
-        grid=(length // TILE,),
-        out_shape=(shape((length, model), BF), unit, unit),
-        in_specs=[
-            row_spec(model),
+            fixed_spec((2, model)),
             row_spec(hidden),
             row_spec(hidden),
             fixed_spec(pack_near.shape),
             fixed_spec(pack_far.shape),
         ],
-        out_specs=(row_spec(model), row_spec(hidden), row_spec(hidden)),
-        compiler_params=params(),
-        cost_estimate=cost(8 * length * model * hidden, length * model * 16),
-    )(above, slope_near, slope_far, pack_near, pack_far)
+        out_specs=(
+            row_spec(model),
+            row_spec(model),
+            fixed_spec((2, model)),
+            row_spec(model),
+            row_spec(hidden),
+            row_spec(hidden),
+        ),
+        compiler_params=params(),
+        cost_estimate=cost(8 * length * model * hidden, length * model * 30),
+    )(info, cot, near, far, values, norm, slope_near, slope_far, pack_near, pack_far)
 
 
 def product_kernel(left_near, left_far, right_near, right_far, near_ref, far_ref):
@@ -849,26 +836,38 @@
     return lax.ppermute(value, "section", [(DECODER, ENCODER)])
 
 
-def line_total(value):
-    if lax.axis_size("dp") != 4:
-        return lax.psum(value, "dp")
-    place = lax.axis_index("dp")
-    inner = (place == 1) | (place == 2)
-    value = value + lax.ppermute(value, "dp", [(0, 1), (3, 2)])
-    value = value + lax.ppermute(value, "dp", [(1, 2), (2, 1)])
-    return jnp.where(inner, value, lax.ppermute(value, "dp", [(1, 0), (2, 3)]))
-
-
-def exchange_total(value):
-    if lax.axis_size("dp") != value.shape[0]:
-        return lax.psum(value, "dp")
-    parts = lax.all_to_all(value, "dp", 0, 0, tiled=True)
-    total = jnp.sum(parts.astype(F32), 0, keepdims=True).astype(BF)
-    return lax.all_to_all(jnp.broadcast_to(total, value.shape), "dp", 0, 0, tiled=True)
-
-
-def far_added(own, other):
-    return (own + across(other).astype(F32)).astype(BF)
+class Line:
+    def __init__(self, value):
+        self.four = lax.axis_size("dp") == 4
+        self.value = value
+        self.done = 0
+
+    def inward(self, behind=None):
+        if self.four:
+            arrived = lax.ppermute(self.value, "dp", [(0, 1), (3, 2)])
+            self.value = self.value + (arrived if behind is None else after(arrived, behind))
+        self.done = 1
+
+    def swap(self):
+        if self.four:
+            self.value = self.value + lax.ppermute(self.value, "dp", [(1, 2), (2, 1)])
+        self.done = 2
+
+    def total(self):
+        if not self.four:
+            return lax.psum(self.value, "dp").astype(F32)
+        if self.done < 1:
+            self.inward()
+        if self.done < 2:
+            self.swap()
+        place = lax.axis_index("dp")
+        inner = (place == 1) | (place == 2)
+        outward = lax.ppermute(self.value, "dp", [(1, 0), (2, 3)])
+        return jnp.where(inner, self.value, outward).astype(F32)
+
+
+def near_added(own, other):
+    return (own + other.astype(F32)).astype(BF)
 
 
 def after(value, done):
@@ -913,13 +912,14 @@
     frame_mine = pick(frames, pair)
     frame_far = across(pick(frames, 1 - pair))
     rel_far = across(rel_table[0])
-    self_far = across(after(self_near, frame_far))
+    self_far = across(after(self_near, rel_far))
     pair_source = to_decoder(pair_own)
-    feed_far_e = across_in(after(feed_near, self_far), ENCODER)
-    cross_near = jnp.concatenate([pair_own, after(pair_source, self_far)])
-    cross_far = across_in(cross_near, DECODER)
-    cot_far = across(after(pick(cotangent, 1 - pair), cross_far))
-    feed_far_d = across_in(after(feed_near, cot_far), DECODER)
+    feed_far_e = across_in(after(feed_near, frame_far), ENCODER)
+    cross_near = jnp.concatenate([pair_own, pair_source]).reshape(4 * width, model)
+    pack_near = jnp.concatenate([cross_near, ffn_out[0]])
+    pack_far = across_in(after(pack_near, frame_far), DECODER)
+    up_far_d = across_in(after(ffn_in[0], pack_far), DECODER)
+    cot_mine, cot_other = pick(cotangent, pair), pick(cotangent, 1 - pair)
 
     def quarters(mine, far):
         both = beside(jnp.stack([mine, far]))
@@ -940,32 +940,37 @@
     rows, normed_one = enter(info, quarters(frame_mine, frame_far), norms[0, 0])
     part, *saved_near = self_forward(info, normed_one, self_near, table_near, None)
     part, *saved_far = self_forward(
-        info, normed_one, after(self_far, pair_source), table_far, part
-    )
-    stream_one, normed_two = add_norm(rows, part, beside(part), norms[0, 1])
+        info, normed_one, after(self_far, pack_near), table_far, part
+    )
+    stream_one, normed_two = add_norm(
+        rows, part, beside(part), norms[0, 1]
+    )
 
     part, active_e_near, slope_near = feed_forward(
-        info, after(normed_two, cross_far), feed_near, None
-    )
-    part, active_e_far, slope_far = feed_forward(info, normed_two, feed_far_e, part)
-    cot = masked_rows(info, quarters(pick(cotangent, pair), cot_far))
+        info, normed_two, feed_near, None
+    )
+    part, active_e_far, slope_far = feed_forward(
+        info, normed_two, after(feed_far_e, pack_far), part
+    )
     stream_e, sent, squares = source_out(
-        info, after(stream_one, cot), part, beside(part), norms[0, 2]
+        info, stream_one, part, beside(part), norms[0, 2]
     )
     sent_near = to_decoder(lax.dynamic_slice_in_dim(sent, core * half, half, 0))
     sent_far = beside(sent_near)
-    normed_cross = after(normed_two, feed_far_d)
+    cot = masked_rows(info, quarters(cot_mine, across(after(cot_other, sent))))
+    hidden_pre = feed_above(info, cot, ffn_out[0], pack_far)
+    normed_cross = after(normed_two, (hidden_pre, up_far_d))
 
     part, joint_near, joint_far = cross_forward(
-        info, normed_cross, sent_near, sent_far, cross_near, cross_far
+        info, normed_cross, sent_near, sent_far, cross_near, pack_far
     )
     stream_d, normed_three = add_norm(stream_one, part, beside(part), norms[0, 2])
-    part_d, back, active_d_near, hidden_d_near, active_d_far, hidden_d_far = feed_both(
-        info, normed_three, cot, feed_near, feed_far_d
+    back, active_d_near, hidden_d_near, active_d_far, hidden_d_far = feed_both(
+        info, normed_three, hidden_pre, ffn_in[0], up_far_d
     )
     grad_d, above_d, norm_d = norm_backward(cot, back, beside(back), stream_d, norms[0, 2])
     back_d, returned, d_joint_near, d_joint_far = cross_backward(
-        info, joint_near, joint_far, above_d, cross_near, cross_far
+        info, joint_near, joint_far, above_d, cross_near, pack_far
     )
     returned_mine = lax.dynamic_slice_in_dim(returned, core * half, half, 0)
     returned_theirs = lax.dynamic_slice_in_dim(returned, (1 - core) * half, half, 0)
@@ -974,6 +979,41 @@
     returned_near = to_encoder(returned)
     returned_far = beside(returned_near)
 
+    grad_two, above_feed, norm_grad_three, back, hidden_near, hidden_far = lax.cond(
+        decoder,
+        lambda: (grad_d, cot, norm_d, back_d, hidden_d_near, hidden_d_far),
+        lambda: source_back(
+            info,
+            cot,
+            returned_near,
+            returned_far,
+            stream_e,
+            norms[0, 2],
+            slope_near,
+            slope_far,
+            feed_near,
+            feed_far_e,
+        ),
+    )
+    down_near, down_far = lax.cond(
+        decoder,
+        lambda: feed_weights(active_d_near, active_d_far, above_feed, above_feed),
+        lambda: feed_weights(active_e_near, active_e_far, above_feed, above_feed),
+    )
+    down_other = across(down_far)
+    grad_one, above_one, norm_grad_two = norm_backward(
+        grad_two, back, beside(back), stream_one, norms[0, 1]
+    )
+    up_near, up_far = lax.cond(
+        decoder,
+        lambda: feed_weights(normed_three, normed_three, hidden_near, hidden_far),
+        lambda: feed_weights(normed_two, normed_two, hidden_near, hidden_far),
+    )
+    up_other = across(up_far)
+
+    back, attn_far, spread_far = self_backward(
+        info, saved_far, after(above_one, up_far), normed_one, self_far, table_far, None, BF
+    )
     pair_near, pair_far = cross_weights(
         info,
         d_joint_near,
@@ -981,53 +1021,39 @@
         joint_near[1],
         joint_far[1],
         normed_two,
-        after(above_d, returned),
+        after(above_d, attn_far),
         sent_near,
         sent_far,
     )
+    attn_other = across(attn_far)
+    d_down = Line(near_added(down_near, after(down_other, attn_far)))
+    above_near = after(above_one, d_down.value)
+    back, attn_near, spread_near = self_backward(
+        info, saved_near, above_near, normed_one, self_near, table_near, back, F32
+    )
+
+    d_down.inward(attn_near)
+    d_up = Line(near_added(up_near, after(up_other, attn_near)))
+    d_up.inward()
+    d_down.swap()
+    d_attn = Line(near_added(attn_near, after(attn_other, d_down.value)))
+    d_attn.inward()
+    d_up.value = after(d_up.value, d_down.value)
+    d_up.swap()
+    grad_rows, _, norm_grad_one = norm_backward(grad_one, back, beside(back), rows, norms[0, 0])
+    d_ffn_out = d_down.total()
+    d_attn.swap()
     d_pair = (pair_near + across_in(pair_far, DECODER).astype(F32)).astype(BF)
     d_source = to_encoder(d_pair[2:])
-
-    grad_two, above_e, norm_grad_three = lax.cond(
-        decoder,
-        lambda: (grad_d, above_d, norm_d),
-        lambda: source_back(info, cot, returned_near, returned_far, stream_e, norms[0, 2]),
-    )
-    down_near, down_far = lax.cond(
-        decoder,
-        lambda: feed_weights(active_d_near, active_d_far, cot, cot),
-        lambda: feed_weights(active_e_near, active_e_far, above_e, above_e),
-    )
-    d_down = far_added(down_near, down_far)
-    d_ffn_out = line_total(d_down).astype(F32)
-    back, hidden_near, hidden_far = lax.cond(
-        decoder,
-        lambda: (back_d, hidden_d_near, hidden_d_far),
-        lambda: feed_back(above_e, slope_near, slope_far, feed_near, feed_far_e),
-    )
-    grad_one, above_one, norm_grad_two = norm_backward(
-        grad_two, back, beside(back), stream_one, norms[0, 1]
-    )
-    up_near, up_far = lax.cond(
-        decoder,
-        lambda: feed_weights(normed_three, normed_three, hidden_near, hidden_far),
-        lambda: feed_weights(normed_two, normed_two, hidden_near, hidden_far),
-    )
-    d_up = far_added(up_near, up_far)
-    d_ffn_in = line_total(d_up).astype(F32)
-
-    back, attn_far, spread_far = self_backward(
-        info, saved_far, above_one, normed_one, self_far, table_far, None, BF
-    )
-    back, attn_near, spread_near = self_backward(
-        info, saved_near, after(above_one, d_down), normed_one, self_near, table_near, back, F32
-    )
-    grad_rows, _, norm_grad_one = norm_backward(grad_one, back, beside(back), rows, norms[0, 0])
-    d_attn = exchange_total(far_added(attn_near, attn_far)).astype(F32)
-    d_pair = jnp.where(decoder, d_pair[:2], d_source)
-    d_pair = line_total(d_pair).astype(F32)
-
-    part_d = after(part_d, returned)
+    d_pair = Line(after(jnp.where(decoder, d_pair[:2], d_source), d_up.value))
+    d_ffn_in = d_up.total()
+    reached = d_attn.value
+    d_attn = d_attn.total()
+    d_pair = d_pair.total()
+
+    part_d = feed_value(
+        info, after(active_d_near, hidden_near), active_d_far, ffn_out[0], pack_far
+    )
     result, squares = finish(info, stream_d, part_d, beside(part_d), sent, squares)
 
     def placed(value):
@@ -1057,7 +1083,7 @@
     )
     small = jnp.concatenate([shared, table_rows(d_table[:, :heads])])
     small = small + across(jnp.concatenate([shared, table_rows(d_table[:, heads:])]))
-    small = line_total(small)
+    small = Line(after(small, reached)).total()
     d_table = small[8:].reshape(-1)[: buckets * heads].reshape(buckets, heads)
     stats = jnp.sqrt(small[6, :1] / (small[7, :1] * model))
     return (

time: 576 us -> 508 us (0.88)
  waiting for transfers between devices: 232 us -> 200 us
  Pallas kernels: 165 us -> 146 us
  starting transfers between devices: 80.1 us -> 74.3 us
    ppermute x2, waiting for transfers between devices: 96.6 us -> 73.7 us  [to_encoder(): return lax.ppermute(value, 'section', [(DECODER, ENCODER)])]
    pallas_call x2, Pallas kernels: 52.1 us -> 34.5 us  [self_backward(): pl.pallas_call(functools.partial(self_backward_kernel, has_sum), out_shap...]
    ppermute x2, waiting for transfers between devices: 17.3 us -> 5.81 us  [to_decoder(): return lax.ppermute(value, 'section', [(ENCODER, DECODER)])]
    all_to_all x2 -> x0, starting transfers between devices: 9.2 us -> none  [the longest x1 4.91 us: exchange_total(): lax.all_to_all(jnp.broadcast_to(total, value.shape), 'dp', 0, 0, tiled=True)]
    pallas_call x1 -> x2, Pallas kernels: 11 us -> 2.83 us  [the longest x1 2.19 us: feed_value(): pl.pallas_call(feed_value_kernel, grid=(length // TILE,), out_shape=shape...]
    ppermute x12 -> x15, waiting for transfers between devices: 56 us -> 49.4 us  [the longest x5 34.8 us: total(): outward = lax.ppermute(self.value, 'dp', [(1, 0), (2, 3)])]
    pallas_call x1, Pallas kernels: 6.71 us -> 13.2 us  [source_back(): pl.pallas_call(source_back_kernel, grid=(length // TILE,), out_shape=(sha...]
    ppermute x12 -> x15, starting transfers between devices: 39.2 us -> 44.8 us  [the longest x5 32.7 us: inward(): arrived = lax.ppermute(self.value, 'dp', [(0, 1), (3, 2)])]
  transfers between devices with their start and end apart: 44 -> 45, of which waited for: 17 -> 18; matrix products, arithmetic and copies ran while one was open for 11% -> 9% of each run, Pallas kernels for 25% -> 20%
where the time goes in v4:
time: 508 us; the launch traced here: 501 us
  waiting for transfers between devices  200 us (39%)
  Pallas kernels  146 us (29%)
  starting transfers between devices  74.3 us (15%)
  local copies, waits for them, and re-layouts  41.4 us (8%)
  other arithmetic  32.3 us (6%)
  between operations  5.44 us (1%)
    ppermute x2, waiting for transfers between devices, to_encoder(): return lax.ppermute(value, 'section', [(DECODER, ENCODER)])  73.7 us
    ppermute x5, waiting for transfers between devices, total(): outward = lax.ppermute(self.value, 'dp', [(1, 0), (2, 3)])  34.8 us
    pallas_call x2, Pallas kernels, self_backward(): pl.pallas_call(functools.partial(self_backward_kernel, has_sum), out_shap...  34.5 us
    ppermute x5, starting transfers between devices, inward(): arrived = lax.ppermute(self.value, 'dp', [(0, 1), (3, 2)])  32.7 us
    ppermute x10, waiting for transfers between devices, across(): return lax.ppermute(value, 'tensor', [(0, 2), (1, 3), (2, 0), (3, 1)])  27.9 us
    ppermute x4, waiting for transfers between devices, across_in(): lax.ppermute(value, ('section', 'tensor'), [(role * 4 + a, role * 4 + b)...  24.6 us
    unnamed x199, local copies, waits for them, and re-layouts  23 us
    pallas_call x2, Pallas kernels, self_forward(): pl.pallas_call(functools.partial(self_forward_kernel, has_sum), out_shape...  20.6 us
  transfers between devices with their start and end apart: 45, of which 18 were waited for; matrix products, arithmetic and copies ran while one was open for 9% of the time, Pallas kernels for 20%

profile of v4, /device:TPU:0, one launch (start us, length us, event | category | flops | bytes accessed | tf_op | source)
XLA Modules:
  0.0 501.4 jit_solution(10206830187680272771)
XLA Ops:
  0.7 2.2 dynamic-slice_bitcast_fusion.6
  2.9 2.9 collective-permute-start
  5.9 4.7 collective-permute-start.4
  15.9 1.8 stack.74.info
  22.2 2.4 collective-permute-start.6
  27.1 1.7 shard_map.186
  28.9 11.2 %shard_map.189 = (f32[1024,768]{1,0:T(8,128)S(1)}, bf16[3,192,1024]{2,1,0:T(8,128)(2,1)S(1)}, f32[192,1024]{1,0:T(8,128)S(1)}, f32[8,1024]{1,0:T(8,128)S(1)}) custom-call(s32[8]{0:T(128)S(1)} %copy-done.87, bf16[1024,768]{1,0:T(8,128)(2,1)S(1)} %get-tuple-element.177.normed, bf16[4,192,768]{2,1,0:T(8,128)(2,1)} %pad_maximum_fusion.1.weights, ...), custom_call_target="tpu_custom_call" | custom-call | flops 8858370048 | bytes 12582912 | tf_op jit(solution)/shard_map/pallas_call | solution.py:221
  42.0 6.8 %collective-permute-done.3.weights = bf16[4,192,768]{2,1,0:T(8,128)(2,1)S(1)} collective-permute-done((bf16[4,192,768]{2,1,0:T(8,128)(2,1)}, bf16[4,192,768]{2,1,0:T(8,128)(2,1)S(1)}, u32[]{:S(2)}, u32[]{:S(2)}) %collective-permute-start.3) | collective-permute-done | bytes 1179680 | tf_op jit(solution)/shard_map/ppermute | solution.py:817
  48.8 9.4 %shard_map.190 = (bf16[1024,768]{1,0:T(8,128)(2,1)S(1)}, bf16[3,192,1024]{2,1,0:T(8,128)(2,1)S(1)}, f32[192,1024]{1,0:T(8,128)S(1)}, f32[8,1024]{1,0:T(8,128)S(1)}) custom-call(s32[8]{0:T(128)S(1)} %copy-done.87, bf16[1024,768]{1,0:T(8,128)(2,1)S(1)} %get-tuple-element.177.normed, bf16[4,192,768]{2,1,0:T(8,128)(2,1)S(1)} %collective-permute-done.3.weights, ...), custom_call_target="tpu_custom_call" | custom-call | flops 8858370048 | bytes 12582912 | tf_op jit(solution)/shard_map/pallas_call | solution.py:221
  60.2 3.4 collective-permute-done.5.far
  63.6 2.6 shard_map.191
  66.2 8.2 %shard_map.192 = (f32[1024,768]{1,0:T(8,128)S(1)}, bf16[1024,768]{1,0:T(8,128)(2,1)}, bf16[1024,768]{1,0:T(8,128)(2,1)}) custom-call(s32[8]{0:T(128)S(1)} %copy-done.87, bf16[1024,768]{1,0:T(8,128)(2,1)} %get-tuple-element.194.normed, bf16[2,768,768]{2,1,0:T(8,128)(2,1)} %constant_dynamic-update-slice_fusion.pack), custom_call_target="tpu_custom_call" | custom-call | flops 48318384 | bytes 188743 | tf_op jit(solution)/shard_map/pallas_call | solution.py:612
  74.4 24.5 %collective-permute-done.6.pack = bf16[2,768,768]{2,1,0:T(8,128)(2,1)S(1)} collective-permute-done((bf16[2,768,768]{2,1,0:T(8,128)(2,1)}, bf16[2,768,768]{2,1,0:T(8,128)(2,1)S(1)}, u32[]{:S(2)}, u32[]{:S(2)}) %collective-permute-start.6) | collective-permute-done | bytes 2359328 | tf_op jit(solution)/shard_map/ppermute | solution.py:822
  99.0 6.8 %shard_map.193 = (bf16[1024,768]{1,0:T(8,128)(2,1)}, bf16[1024,768]{1,0:T(8,128)(2,1)}, bf16[1024,768]{1,0:T(8,128)(2,1)}) custom-call(s32[8]{0:T(128)S(1)} %copy-done.87, bf16[1024,768]{1,0:T(8,128)(2,1)} %get-tuple-element.194.normed, bf16[2,768,768]{2,1,0:T(8,128)(2,1)S(1)} %collective-permute-done.6.pack, f32[1024,768]{1,0:T(8,128)S(1)} %get-tuple-element.187.refs_0_), custom_call_target="tpu_custom_call" | custom-call | flops 48318384 | bytes 188743 | tf_op jit(solution)/shard_map/pallas_call | solution.py:612
  105.8 3.7 collective-permute-done.8.far
  109.5 1.9 copy-done.1
  111.4 4.8 shard_map.194
  120.4 8.9 %collective-permute-done.9.far = bf16[256,768]{1,0:T(8,128)(2,1)S(1)} collective-permute-done((bf16[256,768]{1,0:T(8,128)(2,1)S(1)}, bf16[256,768]{1,0:T(8,128)(2,1)S(1)}, u32[]{:S(2)}, u32[]{:S(2)}) %collective-permute-start.9) | collective-permute-done | bytes 393248 | tf_op jit(solution)/shard_map/ppermute | solution.py:817
  129.5 5.8 %collective-permute-done.12.near.refs_0_ = bf16[512,768]{1,0:T(8,128)(2,1)S(1)} collective-permute-done((bf16[512,768]{1,0:T(8,128)(2,1)S(1)}, bf16[512,768]{1,0:T(8,128)(2,1)S(1)}, u32[]{:S(2)}, u32[]{:S(2)}) %collective-permute-start.12) | collective-permute-done | bytes 786464 | tf_op jit(solution)/shard_map/ppermute | solution.py:832
  138.0 1.9 shard_map.197
  140.4 3.1 collective-permute-done.14.far
  145.0 1.7 copy-done.7
  146.7 3.8 shard_map.199
  150.8 3.5 collective-permute-done.15.far
  154.3 1.9 copy-done.8
  156.2 5.9 %shard_map.200 = (f32[1024,768]{1,0:T(8,128)}, bf16[1024,768]{1,0:T(8,128)(2,1)S(1)}, f32[2,768]{1,0:T(2,128)}) custom-call(bf16[1024,768]{1,0:T(8,128)(2,1)} %copy-done.70, bf16[1024,768]{1,0:T(8,128)(2,1)} %get-tuple-element.205.near, bf16[1024,768]{1,0:T(8,128)(2,1)} %collective-permute-done.15.far, f32[1024,768]{1,0:T(8,128)S(1)} %copy-done.8, ...), custom_call_target="tpu_custom_call" | custom-call | flops 314572 | bytes 283115 | tf_op jit(solution)/shard_map/pallas_call | solution.py:574
  162.2 6.5 %shard_map.201 = (bf16[1024,768]{1,0:T(8,128)(2,1)}, bf16[1024,768]{1,0:T(8,128)(2,1)S(1)}, bf16[3,192,1024]{2,1,0:T(8,128)(2,1)S(1)}, bf16[3,192,1024]{2,1,0:T(8,128)(2,1)S(1)}) custom-call(s32[8]{0:T(128)S(1)} %copy-done.89, bf16[3,192,1024]{2,1,0:T(8,128)(2,1)S(1)} %copy-done.42, f32[192,1024]{1,0:T(8,128)S(1)} %copy-done.19, f32[8,1024]{1,0:T(8,128)S(1)} %copy-done.49, ...), custom_call_target="tpu_custom_call" | custom-call | flops 370440928 | bytes 125829 | tf_op jit(solution)/shard_map/pallas_call | solution.py:400
  169.1 2.0 collective-permute-done.16
  172.6 73.7 %collective-permute-done.17 = bf16[512,768]{1,0:T(8,128)(2,1)S(1)} collective-permute-done((bf16[512,768]{1,0:T(8,128)(2,1)S(1)}, bf16[512,768]{1,0:T(8,128)(2,1)S(1)}, u32[]{:S(2)}, u32[]{:S(2)}) %collective-permute-start.17) | collective-permute-done | bytes 786464 | tf_op jit(solution)/shard_map/ppermute | solution.py:836
  246.3 2.4 collective-permute-done.18
  248.7 15.4 %conditional.3 = ((f32[1024,768]{1,0:T(8,128)}, bf16[1024,768]{1,0:T(8,128)(2,1)}, f32[2,768]{1,0:T(2,128)}, bf16[1024,768]{1,0:T(8,128)(2,1)}, bf16[1024,768]{1,0:T(8,128)(2,1)}, /*index=5*/bf16[1024,768]{1,0:T(8,128)(2,1)})) conditional(s32[]{:T(128)} %convert_element_type.58, (f32[1,3,2,768]{3,2,1,0:T(2,128)}, s32[8]{0:T(128)S(1)}, ...), branch_computations={%region_0.1_spmd, %region_1.2_spmd} | conditional | flops 96636768 | bytes 13067095 | solution.py:982
  251.0 13.2 %branch_0_fun.3 = (f32[1024,768]{1,0:T(8,128)}, bf16[1024,768]{1,0:T(8,128)(2,1)}, f32[2,768]{1,0:T(2,128)}, bf16[1024,768]{1,0:T(8,128)(2,1)}, bf16[1024,768]{1,0:T(8,128)(2,1)}, /*index=5*/bf16[1024,768]{1,0:T(8,128)(2,1)}) custom-call(s32[8]{0:T(128)S(1)} %get-tuple-element.56.info, bf16[1024,768]{1,0:T(8,128)(2,1)S(1)} %copy.49.cot, ...), custom_call_target="tpu_custom_call" | custom-call | flops 96636768 | bytes 471859 | tf_op jit(solution)/shard_map/cond/branch_0_fun/pallas_call | solution.py:758
  264.4 6.6 %conditional.4 = ((f32[768,768]{1,0:T(8,128)}, bf16[768,768]{1,0:T(8,128)(2,1)})) conditional(s32[]{:T(128)} %convert_element_type.58, (bf16[1024,768]{1,0:T(8,128)(2,1)}, bf16[1024,768]{1,0:T(8,128)(2,1)}, bf16[1024,768]{1,0:T(8,128)(2,1)}) %tuple.56, (bf16[1024,768]{1,0:T(8,128)(2,1)}, bf16[1024,768]{1,0:T(8,128)(2,1)}, ...), branch_computations={%region_2.3_spmd, %region_3.4_spmd} | conditional | flops 48318384 | bytes 188751 | solution.py:998
  264.4 6.6 %branch_0_fun.4 = (f32[768,768]{1,0:T(8,128)}, bf16[768,768]{1,0:T(8,128)(2,1)}) custom-call(bf16[1024,768]{1,0:T(8,128)(2,1)} %get-tuple-element.66.left_near, bf16[1024,768]{1,0:T(8,128)(2,1)} %get-tuple-element.67.left_far, bf16[1024,768]{1,0:T(8,128)(2,1)} %get-tuple-element.68.right_near.right_far, bf16[1024,768]{1,0:T(8,128)(2,1)} %get-tuple-element.68.right_near.right_far), custom_call_target="tpu_custom_call" | custom-call | flops 48318384 | bytes 188743 | tf_op jit(solution)/shard_map/cond/branch_0_fun/pallas_call | solution.py:805
  272.5 6.8 %conditional.5 = ((f32[768,768]{1,0:T(8,128)}, bf16[768,768]{1,0:T(8,128)(2,1)})) conditional(s32[]{:T(128)} %convert_element_type.58, (bf16[1024,768]{1,0:T(8,128)(2,1)}, bf16[1024,768]{1,0:T(8,128)(2,1)}, bf16[1024,768]{1,0:T(8,128)(2,1)}) %tuple.58, (bf16[1024,768]{1,0:T(8,128)(2,1)}, bf16[1024,768]{1,0:T(8,128)(2,1)}, ...), branch_computations={%region_4.5_spmd, %region_5.6_spmd} | conditional | flops 48318384 | bytes 188751 | solution.py:1007
  272.5 6.4 %branch_0_fun.5 = (f32[768,768]{1,0:T(8,128)}, bf16[768,768]{1,0:T(8,128)(2,1)}) custom-call(bf16[1024,768]{1,0:T(8,128)(2,1)} %get-tuple-element.72.left_near.left_far, bf16[1024,768]{1,0:T(8,128)(2,1)} %get-tuple-element.72.left_near.left_far, bf16[1024,768]{1,0:T(8,128)(2,1)} %get-tuple-element.73.right_near, bf16[1024,768]{1,0:T(8,128)(2,1)} %get-tuple-element.74.right_far), custom_call_target="tpu_custom_call" | custom-call | flops 48318384 | bytes 188743 | tf_op jit(solution)/shard_map/cond/branch_0_fun/pallas_call | solution.py:805
  279.9 1.9 copy-done.3
  281.8 5.6 %shard_map.204 = (f32[1024,768]{1,0:T(8,128)S(1)}, bf16[1024,768]{1,0:T(8,128)(2,1)S(1)}, f32[2,768]{1,0:T(2,128)S(1)}) custom-call(f32[1024,768]{1,0:T(8,128)} %get-tuple-element.221.residual, bf16[1024,768]{1,0:T(8,128)(2,1)} %get-tuple-element.222.near, bf16[1024,768]{1,0:T(8,128)(2,1)} %collective-permute-done.21.far, f32[1024,768]{1,0:T(8,128)S(1)} %copy-done.3, ...), custom_call_target="tpu_custom_call" | custom-call | flops 314572 | bytes 283115 | tf_op jit(solution)/shard_map/pallas_call | solution.py:574
  289.2 16.3 %shard_map.205 = (f32[1024,768]{1,0:T(8,128)S(1)}, bf16[4,192,768]{2,1,0:T(8,128)(2,1)S(1)}, f32[3,2048]{1,0:T(4,128)S(1)}) custom-call(s32[8]{0:T(128)S(1)} %copy-done.90, bf16[3,192,1024]{2,1,0:T(8,128)(2,1)S(1)} %copy-done.59, f32[192,1024]{1,0:T(8,128)S(1)} %copy-done.63, f32[8,1024]{1,0:T(8,128)S(1)} %copy-done.67, ...), custom_call_target="tpu_custom_call" | custom-call | flops 20937965568 | bytes 12582912 | tf_op jit(solution)/shard_map/pallas_call | solution.py:345
  307.2 3.7 collective-permute-start.27
  311.0 18.2 %shard_map.206 = (bf16[1024,768]{1,0:T(8,128)(2,1)}, f32[4,192,768]{2,1,0:T(8,128)S(1)}, f32[3,2048]{1,0:T(4,128)S(1)}) custom-call(s32[8]{0:T(128)S(1)} %copy-done.90, bf16[3,192,1024]{2,1,0:T(8,128)(2,1)S(1)} %copy-done.61, f32[192,1024]{1,0:T(8,128)S(1)} %copy-done.65, f32[8,1024]{1,0:T(8,128)S(1)} %copy-done.69, ...), custom_call_target="tpu_custom_call" | custom-call | flops 20937965568 | bytes 12582912 | tf_op jit(solution)/shard_map/pallas_call | solution.py:345
  329.2 6.6 %collective-permute-done.27 = bf16[768,768]{1,0:T(8,128)(2,1)S(1)} collective-permute-done((bf16[768,768]{1,0:T(8,128)(2,1)S(1)}, bf16[768,768]{1,0:T(8,128)(2,1)S(1)}, u32[]{:S(2)}, u32[]{:S(2)}) %collective-permute-start.27) | collective-permute-done | bytes 1179680 | tf_op jit(solution)/shard_map/ppermute | solution.py:847
  338.9 7.5 %collective-permute-start.38 = (bf16[768,768]{1,0:T(8,128)(2,1)S(1)}, bf16[768,768]{1,0:T(8,128)(2,1)S(1)}, u32[]{:S(2)}, u32[]{:S(2)}) collective-permute-start(bf16[768,768]{1,0:T(8,128)(2,1)S(1)} %add_convert_fusion), channel_id=1, source_target_pairs={{0,4},{12,8},{1,5},{13,9},{2,6},{14,10},{3,7},{15,11},{16,20},{28,... | collective-permute-start | bytes 3538952 | tf_op jit(solution)/shard_map/ppermute | solution.py:847
  346.5 1.8 shard_map.208
  349.2 2.2 shard_map.202.near
  352.7 11.2 %collective-permute-done.26 = bf16[4,192,768]{2,1,0:T(8,128)(2,1)S(1)} collective-permute-done((bf16[4,192,768]{2,1,0:T(8,128)(2,1)S(1)}, bf16[4,192,768]{2,1,0:T(8,128)(2,1)S(1)}, u32[]{:S(2)}, u32[]{:S(2)}) %collective-permute-start.26) | collective-permute-done | bytes 1179680 | tf_op jit(solution)/shard_map/ppermute | solution.py:817
  365.2 7.9 %collective-permute-start.29 = (bf16[4,192,768]{2,1,0:T(8,128)(2,1)}, bf16[4,192,768]{2,1,0:T(8,128)(2,1)}, u32[]{:S(2)}, u32[]{:S(2)}) collective-permute-start(bf16[4,192,768]{2,1,0:T(8,128)(2,1)} %add_convert_fusion.2), channel_id=1, source_target_pairs={{0,4},{12,8},{1,5},{13,9},{2,6},{14,10},{3,7},{15,11},{16,20},{28,... | collective-permute-start | bytes 3538952 | tf_op jit(solution)/shard_map/ppermute | solution.py:847
  381.5 2.6 shard_map.203
  387.7 8.0 %collective-permute-done.29 = bf16[4,192,768]{2,1,0:T(8,128)(2,1)} collective-permute-done((bf16[4,192,768]{2,1,0:T(8,128)(2,1)}, bf16[4,192,768]{2,1,0:T(8,128)(2,1)}, u32[]{:S(2)}, u32[]{:S(2)}) %collective-permute-start.29) | collective-permute-done | bytes 1179680 | tf_op jit(solution)/shard_map/ppermute | solution.py:847
  396.9 2.9 add.103
  399.9 1.7 collective-permute-start.30
  401.6 2.0 slice_select_fusion
  403.5 3.0 add.110
  406.6 8.2 %collective-permute-start.40 = (bf16[2,192,768]{2,1,0:T(8,128)(2,1)}, bf16[2,192,768]{2,1,0:T(8,128)(2,1)}, u32[]{:S(2)}, u32[]{:S(2)}) collective-permute-start(bf16[2,192,768]{2,1,0:T(8,128)(2,1)} %slice_select_fusion), channel_id=1, source_target_pairs={{0,4},{12,8},{1,5},{13,9},{2,6},{14,10},{3,7},{15,11},{16,20},{28,... | collective-permute-start | bytes 1769480 | tf_op jit(solution)/shard_map/ppermute | solution.py:847
  415.7 1.9 copy-done.29
  417.6 5.3 %shard_map.207 = (f32[1024,768]{1,0:T(8,128)S(1)}, bf16[1024,768]{1,0:T(8,128)(2,1)}, f32[2,768]{1,0:T(2,128)S(1)}) custom-call(f32[1024,768]{1,0:T(8,128)S(1)} %copy-done.29, bf16[1024,768]{1,0:T(8,128)(2,1)} %get-tuple-element.243.near, bf16[1024,768]{1,0:T(8,128)(2,1)} %collective-permute-done.23.far, bf16[1024,768]{1,0:T(8,128)(2,1)S(1)} %copy-done.11, ...), custom_call_target="tpu_custom_call" | custom-call | flops 314572 | bytes 283115 | tf_op jit(solution)/shard_map/pallas_call | solution.py:574
  422.9 1.7 copy-done.45
  431.9 2.1 maximum_select_fusion.1
  437.8 1.9 add.104
  439.7 5.4 %collective-permute-start.31 = (f32[10,768]{1,0:T(8,128)S(1)}, f32[10,768]{1,0:T(8,128)S(1)}, u32[]{:S(2)}, u32[]{:S(2)}) collective-permute-start(f32[10,768]{1,0:T(8,128)S(1)} %add.99), channel_id=1, source_target_pairs={{0,4},{12,8},{1,5},{13,9},{2,6},{14,10},{3,7},{15,11},{16,20},{28,... | collective-permute-start | bytes 92168 | tf_op jit(solution)/shard_map/ppermute | solution.py:847
  448.4 2.8 bitcast_convert_fusion
  454.1 3.9 collective-permute-done.43
  458.0 3.0 bitcast_convert_fusion.1
  461.0 30.9 %collective-permute-done.33 = f32[10,768]{1,0:T(8,128)S(1)} collective-permute-done((f32[10,768]{1,0:T(8,128)S(1)}, f32[10,768]{1,0:T(8,128)S(1)}, u32[]{:S(2)}, u32[]{:S(2)}) %collective-permute-start.33) | collective-permute-done | bytes 30752 | tf_op jit(solution)/shard_map/ppermute | solution.py:865
  (329 shorter events, 78.7 us)
Async XLA Ops:
  0.7 10.0 %copy-start.91 = (f32[1,3,2,768]{3,2,1,0:T(2,128)S(1)}, f32[1,3,2,768]{3,2,1,0:T(2,128)}, u32[]{:S(2)}) copy-start(f32[1,3,2,768]{3,2,1,0:T(2,128)} %param.21) | copy-start | bytes 55300
  0.7 10.6 %copy-start.14 = (bf16[1,768,768]{2,1,0:T(8,128)(2,1)S(1)}, bf16[1,768,768]{2,1,0:T(8,128)(2,1)}, u32[]{:S(2)}) copy-start(bf16[1,768,768]{2,1,0:T(8,128)(2,1)} %param.25) | copy-start | bytes 3538948
  2.9 9.4 %copy-start.82 = (bf16[1,3,768,192]{2,3,1,0:T(8,128)(2,1)S(1)}, bf16[1,3,768,192]{2,3,1,0:T(8,128)(2,1)}, u32[]{:S(2)}) copy-start(bf16[1,3,768,192]{2,3,1,0:T(8,128)(2,1)} %param.22) | copy-start | bytes 2654212
  2.9 9.4 %copy-start.86 = (bf16[1,192,768]{2,1,0:T(8,128)(2,1)S(1)}, bf16[1,192,768]{2,1,0:T(8,128)(2,1)}, u32[]{:S(2)}) copy-start(bf16[1,192,768]{2,1,0:T(8,128)(2,1)} %param.23) | copy-start | bytes 884740
  2.9 15.7 %collective-permute-start = (bf16[256,768]{1,0:T(8,128)(2,1)}, bf16[256,768]{1,0:T(8,128)(2,1)S(1)}, u32[]{:S(2)}, u32[]{:S(2)}) collective-permute-start(bf16[256,768]{1,0:T(8,128)(2,1)} %get-tuple-element.284), channel_id=1, source_target_pairs={{0,2},{1,3},{2,0},{3,1},{4,6},{5,7},{6,4},{7,5},{8,10},{9,11},{10,... | collective-permute-start | bytes 1179656 | tf_op jit(solution)/shard_map/ppermute | solution.py:817
  5.9 11.9 %collective-permute-start.2 = (f32[320,3]{0,1:T(4,128)S(1)}, f32[320,3]{0,1:T(4,128)S(1)}, u32[]{:S(2)}, u32[]{:S(2)}) collective-permute-start(f32[320,3]{0,1:T(4,128)S(1)} %bitcast.91), channel_id=1, source_target_pairs={{0,2},{1,3},{2,0},{3,1},{4,6},{5,7},{6,4},{7,5},{8,10},{9,11},{10,... | collective-permute-start | bytes 11528 | tf_op jit(solution)/shard_map/ppermute | solution.py:817
  5.9 18.7 %collective-permute-start.4 = (bf16[2,192,768]{2,1,0:T(8,128)(2,1)S(1)}, bf16[2,192,768]{2,1,0:T(8,128)(2,1)}, u32[]{:S(2)}, u32[]{:S(2)}) collective-permute-start(bf16[2,192,768]{2,1,0:T(8,128)(2,1)S(1)} %bitcast.88), channel_id=1, source_target_pairs={{0,16},{1,17},{2,18},{3,19},{4,20},{5,21},{6,22},{7,23},{8,24},{9,... | collective-permute-start | bytes 1769480 | tf_op jit(solution)/shard_map/ppermute | solution.py:832
  18.7 8.2 %collective-permute-start.1 = (bf16[2,256,768]{2,1,0:T(8,128)(2,1)S(1)}, bf16[2,256,768]{2,1,0:T(8,128)(2,1)S(1)}, u32[]{:S(2)}, u32[]{:S(2)}) collective-permute-start(bf16[2,256,768]{2,1,0:T(8,128)(2,1)S(1)} %pad_maximum_fusion.3), channel_id=1, source_target_pairs={{0,1},{1,0},{2,3},{3,2},{4,5},{5,4},{6,7},{7,6},{8,9},{9,8},{10,11... | collective-permute-start | bytes 2359304 | tf_op jit(solution)/shard_map/ppermute | solution.py:828
  19.8 29.0 %collective-permute-start.3 = (bf16[4,192,768]{2,1,0:T(8,128)(2,1)}, bf16[4,192,768]{2,1,0:T(8,128)(2,1)S(1)}, u32[]{:S(2)}, u32[]{:S(2)}) collective-permute-start(bf16[4,192,768]{2,1,0:T(8,128)(2,1)} %pad_maximum_fusion.1.weights), channel_id=1, source_target_pairs={{0,2},{1,3},{2,0},{3,1},{4,6},{5,7},{6,4},{7,5},{8,10},{9,11},{10,... | collective-permute-start | bytes 3538952 | tf_op jit(solution)/shard_map/ppermute | solution.py:817
  22.2 26.6 %copy-start.26 = (f32[3,128,2048]{2,1,0:T(8,128)}, f32[3,128,2048]{2,1,0:T(8,128)S(1)}, u32[]{:S(2)}) copy-start(f32[3,128,2048]{2,1,0:T(8,128)S(1)} %shard_map.187.table) | copy-start | bytes 9437188
  22.2 76.8 %collective-permute-start.6 = (bf16[2,768,768]{2,1,0:T(8,128)(2,1)}, bf16[2,768,768]{2,1,0:T(8,128)(2,1)S(1)}, u32[]{:S(2)}, u32[]{:S(2)}) collective-permute-start(bf16[2,768,768]{2,1,0:T(8,128)(2,1)} %constant_dynamic-update-slice_fusion.pack), channel_id=1, source_target_pairs={{0,2},{1,3},{2,0},{3,1},{4,6},{5,7},{6,4},{7,5},{8,10},{9,11},{10,... | collective-permute-start | bytes 7077896 | tf_op jit(solution)/shard_map/ppermute | solution.py:822
  26.0 72.9 %collective-permute-start.7 = (bf16[1536,768]{1,0:T(8,128)(2,1)S(1)}, bf16[1536,768]{1,0:T(8,128)(2,1)S(1)}, u32[]{:S(2)}, u32[]{:S(2)}) collective-permute-start(bf16[1536,768]{1,0:T(8,128)(2,1)S(1)} %pad_maximum_fusion), channel_id=1, source_target_pairs={{16,18},{17,19},{18,16},{19,17},{20,22},{21,23},{22,20},{23,21},{2... | collective-permute-start | bytes 7077896 | tf_op jit(solution)/shard_map/ppermute | solution.py:822
  28.8 20.0 %copy-start.54 = (bf16[1024,768]{1,0:T(8,128)(2,1)}, bf16[1024,768]{1,0:T(8,128)(2,1)S(1)}, u32[]{:S(2)}) copy-start(bf16[1024,768]{1,0:T(8,128)(2,1)S(1)} %get-tuple-element.177.normed) | copy-start | bytes 4718596
  28.9 34.8 %copy-start.10 = (bf16[1024,768]{1,0:T(8,128)(2,1)}, bf16[1024,768]{1,0:T(8,128)(2,1)S(1)}, u32[]{:S(2)}) copy-start(bf16[1024,768]{1,0:T(8,128)(2,1)S(1)} %get-tuple-element.176.stream.values) | copy-start | bytes 4718596
  42.0 16.3 %copy-start.68 = (f32[8,1024]{1,0:T(8,128)}, f32[8,1024]{1,0:T(8,128)S(1)}, u32[]{:S(2)}) copy-start(f32[8,1024]{1,0:T(8,128)S(1)} %get-tuple-element.226.lse) | copy-start | bytes 98308
  48.8 9.5 %copy-start.56 = (bf16[4,192,768]{2,1,0:T(8,128)(2,1)}, bf16[4,192,768]{2,1,0:T(8,128)(2,1)S(1)}, u32[]{:S(2)}) copy-start(bf16[4,192,768]{2,1,0:T(8,128)(2,1)S(1)} %collective-permute-done.3.weights) | copy-start | bytes 3538948
  48.8 14.8 %copy-start.46 = (f32[2,768]{1,0:T(2,128)S(1)}, f32[2,768]{1,0:T(2,128)}, u32[]{:S(2)}) copy-start(f32[2,768]{1,0:T(2,128)} %get-tuple-element.291.norm_ref) | copy-start | bytes 18436
  60.2 3.4 collective-permute-start.5
  105.8 3.8 collective-permute-start.8
  116.3 18.9 %collective-permute-start.12 = (bf16[512,768]{1,0:T(8,128)(2,1)S(1)}, bf16[512,768]{1,0:T(8,128)(2,1)S(1)}, u32[]{:S(2)}, u32[]{:S(2)}) collective-permute-start(bf16[512,768]{1,0:T(8,128)(2,1)S(1)} %constant_dynamic-slice_fusion.2), channel_id=1, source_target_pairs={{0,16},{1,17},{2,18},{3,19},{4,20},{5,21},{6,22},{7,23},{8,24},{9,... | collective-permute-start | bytes 2359304 | tf_op jit(solution)/shard_map/ppermute | solution.py:832
  118.1 11.2 %collective-permute-start.9 = (bf16[256,768]{1,0:T(8,128)(2,1)S(1)}, bf16[256,768]{1,0:T(8,128)(2,1)S(1)}, u32[]{:S(2)}, u32[]{:S(2)}) collective-permute-start(bf16[256,768]{1,0:T(8,128)(2,1)S(1)} %get-tuple-element.190), channel_id=1, source_target_pairs={{0,2},{1,3},{2,0},{3,1},{4,6},{5,7},{6,4},{7,5},{8,10},{9,11},{10,... | collective-permute-start | bytes 1179656 | tf_op jit(solution)/shard_map/ppermute | solution.py:817
  119.6 17.9 %collective-permute-start.11 = (bf16[768,768]{1,0:T(8,128)(2,1)S(1)}, bf16[768,768]{1,0:T(8,128)(2,1)S(1)}, u32[]{:S(2)}, u32[]{:S(2)}) collective-permute-start(bf16[768,768]{1,0:T(8,128)(2,1)S(1)} %bitcast.83), channel_id=1, source_target_pairs={{16,18},{17,19},{18,16},{19,17},{20,22},{21,23},{22,20},{23,21},{2... | collective-permute-start | bytes 3538952 | tf_op jit(solution)/shard_map/ppermute | solution.py:822
  129.4 5.9 %collective-permute-start.10 = (bf16[2,256,768]{2,1,0:T(8,128)(2,1)S(1)}, bf16[2,256,768]{2,1,0:T(8,128)(2,1)S(1)}, u32[]{:S(2)}, u32[]{:S(2)}) collective-permute-start(bf16[2,256,768]{2,1,0:T(8,128)(2,1)S(1)} %pad_maximum_fusion.4), channel_id=1, source_target_pairs={{0,1},{1,0},{2,3},{3,2},{4,5},{5,4},{6,7},{7,6},{8,9},{9,8},{10,11... | collective-permute-start | bytes 2359304 | tf_op jit(solution)/shard_map/ppermute | solution.py:828
  135.3 2.7 collective-permute-start.13
  140.0 3.5 collective-permute-start.14
  150.5 3.8 collective-permute-start.15
  168.8 80.0 %copy-start.90 = (s32[8]{0:T(128)S(1)}, s32[8]{0:T(128)}, u32[]{:S(2)}) copy-start(s32[8]{0:T(128)} %stack.74.info) | copy-start | bytes 100
  168.8 2.4 collective-permute-start.16
  171.3 75.0 %collective-permute-start.17 = (bf16[512,768]{1,0:T(8,128)(2,1)S(1)}, bf16[512,768]{1,0:T(8,128)(2,1)S(1)}, u32[]{:S(2)}, u32[]{:S(2)}) collective-permute-start(bf16[512,768]{1,0:T(8,128)(2,1)S(1)} %add_convert_fusion.4), channel_id=1, source_target_pairs={{16,0},{17,1},{18,2},{19,3},{20,4},{21,5},{22,6},{23,7},{24,8},{25... | collective-permute-start | bytes 2359304 | tf_op jit(solution)/shard_map/ppermute | solution.py:836
  246.3 2.4 collective-permute-start.18
  264.2 15.8 %collective-permute-start.21 = (bf16[1024,768]{1,0:T(8,128)(2,1)}, bf16[1024,768]{1,0:T(8,128)(2,1)}, u32[]{:S(2)}, u32[]{:S(2)}) collective-permute-start(bf16[1024,768]{1,0:T(8,128)(2,1)} %get-tuple-element.222.near), channel_id=1, source_target_pairs={{0,1},{1,0},{2,3},{3,2},{4,5},{5,4},{6,7},{7,6},{8,9},{9,8},{10,11... | collective-permute-start | bytes 4718600 | tf_op jit(solution)/shard_map/ppermute | solution.py:828
  271.0 34.5 %collective-permute-start.22 = (bf16[768,768]{1,0:T(8,128)(2,1)}, bf16[768,768]{1,0:T(8,128)(2,1)}, u32[]{:S(2)}, u32[]{:S(2)}) collective-permute-start(bf16[768,768]{1,0:T(8,128)(2,1)} %get-tuple-element.232), channel_id=1, source_target_pairs={{0,2},{1,3},{2,0},{3,1},{4,6},{5,7},{6,4},{7,5},{8,10},{9,11},{10,... | collective-permute-start | bytes 3538952 | tf_op jit(solution)/shard_map/ppermute | solution.py:817
  279.3 59.3 %collective-permute-start.37 = (bf16[768,768]{1,0:T(8,128)(2,1)}, bf16[768,768]{1,0:T(8,128)(2,1)S(1)}, u32[]{:S(2)}, u32[]{:S(2)}) collective-permute-start(bf16[768,768]{1,0:T(8,128)(2,1)} %get-tuple-element.237), channel_id=1, source_target_pairs={{0,2},{1,3},{2,0},{3,1},{4,6},{5,7},{6,4},{7,5},{8,10},{9,11},{10,... | collective-permute-start | bytes 3538952 | tf_op jit(solution)/shard_map/ppermute | solution.py:817
  289.2 16.4 %copy-start.80 = (f32[768,768]{1,0:T(8,128)S(1)}, f32[768,768]{1,0:T(8,128)}, u32[]{:S(2)}) copy-start(f32[768,768]{1,0:T(8,128)} %get-tuple-element.231) | copy-start | bytes 7077892
  289.2 21.8 %copy-start.65 = (f32[192,1024]{1,0:T(8,128)S(1)}, f32[192,1024]{1,0:T(8,128)}, u32[]{:S(2)}) copy-start(f32[192,1024]{1,0:T(8,128)} %copy-done.64) | copy-start | bytes 2359300
  307.2 28.6 %collective-permute-start.27 = (bf16[768,768]{1,0:T(8,128)(2,1)S(1)}, bf16[768,768]{1,0:T(8,128)(2,1)S(1)}, u32[]{:S(2)}, u32[]{:S(2)}) collective-permute-start(bf16[768,768]{1,0:T(8,128)(2,1)S(1)} %add_convert_fusion.3), channel_id=1, source_target_pairs={{0,4},{12,8},{1,5},{13,9},{2,6},{14,10},{3,7},{15,11},{16,20},{28,... | collective-permute-start | bytes 3538952 | tf_op jit(solution)/shard_map/ppermute | solution.py:847
  311.0 27.6 %copy-start.81 = (f32[768,768]{1,0:T(8,128)S(1)}, f32[768,768]{1,0:T(8,128)}, u32[]{:S(2)}) copy-start(f32[768,768]{1,0:T(8,128)} %get-tuple-element.260) | copy-start | bytes 7077892
  335.9 10.5 %copy-start.38 = (bf16[3,192,1024]{2,1,0:T(8,128)(2,1)S(1)}, bf16[3,192,1024]{2,1,0:T(8,128)(2,1)}, u32[]{:S(2)}) copy-start(bf16[3,192,1024]{2,1,0:T(8,128)(2,1)} %copy-done.37) | copy-start | bytes 3538948
  335.9 10.5 %copy-start.40 = (bf16[3,192,1024]{2,1,0:T(8,128)(2,1)S(1)}, bf16[3,192,1024]{2,1,0:T(8,128)(2,1)}, u32[]{:S(2)}) copy-start(bf16[3,192,1024]{2,1,0:T(8,128)(2,1)} %copy-done.39) | copy-start | bytes 3538948
  336.2 15.2 %collective-permute-start.28 = (bf16[768,768]{1,0:T(8,128)(2,1)S(1)}, bf16[768,768]{1,0:T(8,128)(2,1)S(1)}, u32[]{:S(2)}, u32[]{:S(2)}) collective-permute-start(bf16[768,768]{1,0:T(8,128)(2,1)S(1)} %add.100), channel_id=1, source_target_pairs={{4,8},{8,4},{5,9},{9,5},{6,10},{10,6},{7,11},{11,7},{20,24},{24,20... | collective-permute-start | bytes 3538952 | tf_op jit(solution)/shard_map/ppermute | solution.py:853
  337.1 26.8 %collective-permute-start.26 = (bf16[4,192,768]{2,1,0:T(8,128)(2,1)S(1)}, bf16[4,192,768]{2,1,0:T(8,128)(2,1)S(1)}, u32[]{:S(2)}, u32[]{:S(2)}) collective-permute-start(bf16[4,192,768]{2,1,0:T(8,128)(2,1)S(1)} %get-tuple-element.239), channel_id=1, source_target_pairs={{0,2},{1,3},{2,0},{3,1},{4,6},{5,7},{6,4},{7,5},{8,10},{9,11},{10,... | collective-permute-start | bytes 3538952 | tf_op jit(solution)/shard_map/ppermute | solution.py:817
  338.9 34.1 %collective-permute-start.38 = (bf16[768,768]{1,0:T(8,128)(2,1)S(1)}, bf16[768,768]{1,0:T(8,128)(2,1)S(1)}, u32[]{:S(2)}, u32[]{:S(2)}) collective-permute-start(bf16[768,768]{1,0:T(8,128)(2,1)S(1)} %add_convert_fusion), channel_id=1, source_target_pairs={{0,4},{12,8},{1,5},{13,9},{2,6},{14,10},{3,7},{15,11},{16,20},{28,... | collective-permute-start | bytes 3538952 | tf_op jit(solution)/shard_map/ppermute | solution.py:847
  348.3 27.7 %collective-permute-start.35 = (bf16[4,192,768]{2,1,0:T(8,128)(2,1)S(1)}, bf16[4,192,768]{2,1,0:T(8,128)(2,1)S(1)}, u32[]{:S(2)}, u32[]{:S(2)}) collective-permute-start(bf16[4,192,768]{2,1,0:T(8,128)(2,1)S(1)} %get-tuple-element.259), channel_id=1, source_target_pairs={{16,18},{17,19},{18,16},{19,17},{20,22},{21,23},{22,20},{23,21},{2... | collective-permute-start | bytes 3538952 | tf_op jit(solution)/shard_map/ppermute | solution.py:822
  351.4 28.7 %collective-permute-start.19 = (bf16[1024,768]{1,0:T(8,128)(2,1)}, bf16[1024,768]{1,0:T(8,128)(2,1)}, u32[]{:S(2)}, u32[]{:S(2)}) collective-permute-start(bf16[1024,768]{1,0:T(8,128)(2,1)} %shard_map.202.near), channel_id=1, source_target_pairs={{0,1},{1,0},{2,3},{3,2},{4,5},{5,4},{6,7},{7,6},{8,9},{9,8},{10,11... | collective-permute-start | bytes 4718600 | tf_op jit(solution)/shard_map/ppermute | solution.py:828
  365.2 30.5 %collective-permute-start.29 = (bf16[4,192,768]{2,1,0:T(8,128)(2,1)}, bf16[4,192,768]{2,1,0:T(8,128)(2,1)}, u32[]{:S(2)}, u32[]{:S(2)}) collective-permute-start(bf16[4,192,768]{2,1,0:T(8,128)(2,1)} %add_convert_fusion.2), channel_id=1, source_target_pairs={{0,4},{12,8},{1,5},{13,9},{2,6},{14,10},{3,7},{15,11},{16,20},{28,... | collective-permute-start | bytes 3538952 | tf_op jit(solution)/shard_map/ppermute | solution.py:847
  373.0 42.6 %collective-permute-start.23 = (bf16[1024,768]{1,0:T(8,128)(2,1)}, bf16[1024,768]{1,0:T(8,128)(2,1)}, u32[]{:S(2)}, u32[]{:S(2)}) collective-permute-start(bf16[1024,768]{1,0:T(8,128)(2,1)} %get-tuple-element.243.near), channel_id=1, source_target_pairs={{0,1},{1,0},{2,3},{3,2},{4,5},{5,4},{6,7},{7,6},{8,9},{9,8},{10,11... | collective-permute-start | bytes 4718600 | tf_op jit(solution)/shard_map/ppermute | solution.py:828
  374.4 29.2 %collective-permute-start.39 = (bf16[768,768]{1,0:T(8,128)(2,1)}, bf16[768,768]{1,0:T(8,128)(2,1)}, u32[]{:S(2)}, u32[]{:S(2)}) collective-permute-start(bf16[768,768]{1,0:T(8,128)(2,1)} %add.109), channel_id=1, source_target_pairs={{4,8},{8,4},{5,9},{9,5},{6,10},{10,6},{7,11},{11,7},{20,24},{24,20... | collective-permute-start | bytes 3538952 | tf_op jit(solution)/shard_map/ppermute | solution.py:853
  378.2 21.7 %collective-permute-start.36 = (bf16[2,192,768]{2,1,0:T(8,128)(2,1)}, bf16[2,192,768]{2,1,0:T(8,128)(2,1)}, u32[]{:S(2)}, u32[]{:S(2)}) collective-permute-start(bf16[2,192,768]{2,1,0:T(8,128)(2,1)} %slice.105), channel_id=1, source_target_pairs={{16,0},{17,1},{18,2},{19,3},{20,4},{21,5},{22,6},{23,7},{24,8},{25... | collective-permute-start | bytes 1769480 | tf_op jit(solution)/shard_map/ppermute | solution.py:836
  384.2 11.5 %copy-start.76 = (bf16[768,768]{1,0:T(8,128)(2,1)S(1)}, bf16[768,768]{1,0:T(8,128)(2,1)}, u32[]{:S(2)}) copy-start(bf16[768,768]{1,0:T(8,128)(2,1)} %add.101) | copy-start | bytes 3538948
  385.0 41.9 %collective-permute-start.20 = (bf16[256,768]{1,0:T(8,128)(2,1)}, bf16[256,768]{1,0:T(8,128)(2,1)}, u32[]{:S(2)}, u32[]{:S(2)}) collective-permute-start(bf16[256,768]{1,0:T(8,128)(2,1)} %get-tuple-element.275), channel_id=1, source_target_pairs={{0,2},{1,3},{2,0},{3,1},{4,6},{5,7},{6,4},{7,5},{8,10},{9,11},{10,... | collective-permute-start | bytes 1179656 | tf_op jit(solution)/shard_map/ppermute | solution.py:817
  387.7 13.9 %copy-start.79 = (bf16[4,192,768]{2,1,0:T(8,128)(2,1)S(1)}, bf16[4,192,768]{2,1,0:T(8,128)(2,1)}, u32[]{:S(2)}) copy-start(bf16[4,192,768]{2,1,0:T(8,128)(2,1)} %copy-done.78) | copy-start | bytes 3538948
  395.7 52.7 %collective-permute-start.44 = (bf16[768,768]{1,0:T(8,128)(2,1)S(1)}, bf16[768,768]{1,0:T(8,128)(2,1)}, u32[]{:S(2)}, u32[]{:S(2)}) collective-permute-start(bf16[768,768]{1,0:T(8,128)(2,1)S(1)} %copy-done.76), channel_id=1, source_target_pairs={{4,0},{8,12},{5,1},{9,13},{6,2},{10,14},{7,3},{11,15},{20,16},{24,... | collective-permute-start | bytes 3538952 | tf_op jit(solution)/shard_map/ppermute | solution.py:865
  399.9 37.9 %collective-permute-start.30 = (bf16[4,192,768]{2,1,0:T(8,128)(2,1)}, bf16[4,192,768]{2,1,0:T(8,128)(2,1)}, u32[]{:S(2)}, u32[]{:S(2)}) collective-permute-start(bf16[4,192,768]{2,1,0:T(8,128)(2,1)} %add.103), channel_id=1, source_target_pairs={{4,8},{8,4},{5,9},{9,5},{6,10},{10,6},{7,11},{11,7},{20,24},{24,20... | collective-permute-start | bytes 3538952 | tf_op jit(solution)/shard_map/ppermute | solution.py:853
  403.5 12.2 %copy-start.11 = (bf16[1024,768]{1,0:T(8,128)(2,1)S(1)}, bf16[1024,768]{1,0:T(8,128)(2,1)}, u32[]{:S(2)}) copy-start(bf16[1024,768]{1,0:T(8,128)(2,1)} %copy-done.10) | copy-start | bytes 4718596
  406.6 28.7 %collective-permute-start.40 = (bf16[2,192,768]{2,1,0:T(8,128)(2,1)}, bf16[2,192,768]{2,1,0:T(8,128)(2,1)}, u32[]{:S(2)}, u32[]{:S(2)}) collective-permute-start(bf16[2,192,768]{2,1,0:T(8,128)(2,1)} %slice_select_fusion), channel_id=1, source_target_pairs={{0,4},{12,8},{1,5},{13,9},{2,6},{14,10},{3,7},{15,11},{16,20},{28,... | collective-permute-start | bytes 1769480 | tf_op jit(solution)/shard_map/ppermute | solution.py:847
  425.3 4.7 collective-permute-start.25
  426.9 31.1 %collective-permute-start.43 = (bf16[768,768]{1,0:T(8,128)(2,1)}, bf16[768,768]{1,0:T(8,128)(2,1)}, u32[]{:S(2)}, u32[]{:S(2)}) collective-permute-start(bf16[768,768]{1,0:T(8,128)(2,1)} %add.110), channel_id=1, source_target_pairs={{4,0},{8,12},{5,1},{9,13},{6,2},{10,14},{7,3},{11,15},{20,16},{24,... | collective-permute-start | bytes 3538952 | tf_op jit(solution)/shard_map/ppermute | solution.py:865
  430.0 7.8 %collective-permute-start.24 = (bf16[256,768]{1,0:T(8,128)(2,1)S(1)}, bf16[256,768]{1,0:T(8,128)(2,1)S(1)}, u32[]{:S(2)}, u32[]{:S(2)}) collective-permute-start(bf16[256,768]{1,0:T(8,128)(2,1)S(1)} %dynamic-slice_convert_fusion), channel_id=1, source_target_pairs={{0,2},{1,3},{2,0},{3,1},{4,6},{5,7},{6,4},{7,5},{8,10},{9,11},{10,... | collective-permute-start | bytes 1179656 | tf_op jit(solution)/shard_map/ppermute | solution.py:817
  436.7 14.5 %collective-permute-start.41 = (bf16[2,192,768]{2,1,0:T(8,128)(2,1)S(1)}, bf16[2,192,768]{2,1,0:T(8,128)(2,1)S(1)}, u32[]{:S(2)}, u32[]{:S(2)}) collective-permute-start(bf16[2,192,768]{2,1,0:T(8,128)(2,1)S(1)} %add.111), channel_id=1, source_target_pairs={{4,8},{8,4},{5,9},{9,5},{6,10},{10,6},{7,11},{11,7},{20,24},{24,20... | collective-permute-start | bytes 1769480 | tf_op jit(solution)/shard_map/ppermute | solution.py:853
  439.7 7.9 %collective-permute-start.31 = (f32[10,768]{1,0:T(8,128)S(1)}, f32[10,768]{1,0:T(8,128)S(1)}, u32[]{:S(2)}, u32[]{:S(2)}) collective-permute-start(f32[10,768]{1,0:T(8,128)S(1)} %add.99), channel_id=1, source_target_pairs={{0,4},{12,8},{1,5},{13,9},{2,6},{14,10},{3,7},{15,11},{16,20},{28,... | collective-permute-start | bytes 92168 | tf_op jit(solution)/shard_map/ppermute | solution.py:847
  446.4 50.1 %collective-permute-start.34 = (bf16[4,192,768]{2,1,0:T(8,128)(2,1)S(1)}, bf16[4,192,768]{2,1,0:T(8,128)(2,1)}, u32[]{:S(2)}, u32[]{:S(2)}) collective-permute-start(bf16[4,192,768]{2,1,0:T(8,128)(2,1)S(1)} %add.104), channel_id=1, source_target_pairs={{4,0},{8,12},{5,1},{9,13},{6,2},{10,14},{7,3},{11,15},{20,16},{24,... | collective-permute-start | bytes 3538952 | tf_op jit(solution)/shard_map/ppermute | solution.py:865
  447.7 5.1 %collective-permute-start.32 = (f32[10,768]{1,0:T(8,128)S(1)}, f32[10,768]{1,0:T(8,128)S(1)}, u32[]{:S(2)}, u32[]{:S(2)}) collective-permute-start(f32[10,768]{1,0:T(8,128)S(1)} %add.105), channel_id=1, source_target_pairs={{4,8},{8,4},{5,9},{9,5},{6,10},{10,6},{7,11},{11,7},{20,24},{24,20... | collective-permute-start | bytes 92168 | tf_op jit(solution)/shard_map/ppermute | solution.py:853
  451.3 44.0 %collective-permute-start.42 = (bf16[2,192,768]{2,1,0:T(8,128)(2,1)S(1)}, bf16[2,192,768]{2,1,0:T(8,128)(2,1)S(1)}, u32[]{:S(2)}, u32[]{:S(2)}) collective-permute-start(bf16[2,192,768]{2,1,0:T(8,128)(2,1)S(1)} %add.112), channel_id=1, source_target_pairs={{4,0},{8,12},{5,1},{9,13},{6,2},{10,14},{7,3},{11,15},{20,16},{24,... | collective-permute-start | bytes 1769480 | tf_op jit(solution)/shard_map/ppermute | solution.py:865
  452.8 39.1 %collective-permute-start.33 = (f32[10,768]{1,0:T(8,128)S(1)}, f32[10,768]{1,0:T(8,128)S(1)}, u32[]{:S(2)}, u32[]{:S(2)}) collective-permute-start(f32[10,768]{1,0:T(8,128)S(1)} %add.106), channel_id=1, source_target_pairs={{4,0},{8,12},{5,1},{9,13},{6,2},{10,14},{7,3},{11,15},{20,16},{24,... | collective-permute-start | bytes 92168 | tf_op jit(solution)/shard_map/ppermute | solution.py:865
  (79 other events, 333.6 us)

commit v5 on v4

--- a/solution.py
+++ b/solution.py
@@ -337,7 +337,7 @@
         spread_ref[head : head + 1, :] = unskewed(band[head])
 
 
-def self_backward(info, saved, above, normed, weights, table, previous, weight_type):
+def self_backward(info, saved, above, normed, weights, table, previous, weight_type, hides):
     length, model = above.shape
     width = weights.shape[1]
     has_sum = previous is not None
@@ -357,7 +357,7 @@
             pltpu.VMEM((3, width, length), BF),
         ],
         compiler_params=params(),
-        cost_estimate=attention_cost(length, width, model, 5, 8, HIDES_MUCH),
+        cost_estimate=attention_cost(length, width, model, 5, 8, hides),
     )(*operands)
 
 
@@ -1012,7 +1012,15 @@
     up_other = across(up_far)
 
     back, attn_far, spread_far = self_backward(
-        info, saved_far, after(above_one, up_far), normed_one, self_far, table_far, None, BF
+        info,
+        saved_far,
+        after(above_one, up_far),
+        normed_one,
+        self_far,
+        table_far,
+        None,
+        BF,
+        HIDES_MUCH,
     )
     pair_near, pair_far = cross_weights(
         info,
@@ -1029,7 +1037,7 @@
     d_down = Line(near_added(down_near, after(down_other, attn_far)))
     above_near = after(above_one, d_down.value)
     back, attn_near, spread_near = self_backward(
-        info, saved_near, above_near, normed_one, self_near, table_near, back, F32
+        info, saved_near, above_near, normed_one, self_near, table_near, back, F32, HIDES_LITTLE
     )
 
     d_down.inward(attn_near)
@@ -1042,6 +1050,7 @@
     d_up.swap()
     grad_rows, _, norm_grad_one = norm_backward(grad_one, back, beside(back), rows, norms[0, 0])
     d_ffn_out = d_down.total()
+    d_attn.value = after(d_attn.value, d_ffn_out)
     d_attn.swap()
     d_pair = (pair_near + across_in(pair_far, DECODER).astype(F32)).astype(BF)
     d_source = to_encoder(d_pair[2:])

time: 508 us -> 502 us (0.988)
    ppermute x5, waiting for transfers between devices: 34.8 us -> 25.6 us  [total(): outward = lax.ppermute(self.value, 'dp', [(1, 0), (2, 3)])]
    unnamed x199 -> x205, local copies, waits for them, and re-layouts: 23 us -> 22.7 us
  transfers between devices with their start and end apart: 45 -> 45, of which waited for: 18 -> 18; matrix products, arithmetic and copies ran while one was open for 9% -> 10% of each run, Pallas kernels for 20% -> 20%
where the time goes in v5:
time: 502 us; the launch traced here: 495 us
  waiting for transfers between devices  197 us (39%)
  Pallas kernels  142 us (28%)
  starting transfers between devices  72.4 us (14%)
  local copies, waits for them, and re-layouts  40.7 us (8%)
  other arithmetic  35.3 us (7%)
  between operations  5.49 us (1%)
    ppermute x2, waiting for transfers between devices, to_encoder(): return lax.ppermute(value, 'section', [(DECODER, ENCODER)])  73.5 us
    pallas_call x2, Pallas kernels, self_backward(): pl.pallas_call(functools.partial(self_backward_kernel, has_sum), out_shap...  34.5 us
    ppermute x5, starting transfers between devices, inward(): arrived = lax.ppermute(self.value, 'dp', [(0, 1), (3, 2)])  32.5 us
    ppermute x10, waiting for transfers between devices, across(): return lax.ppermute(value, 'tensor', [(0, 2), (1, 3), (2, 0), (3, 1)])  31.7 us
    ppermute x5, waiting for transfers between devices, total(): outward = lax.ppermute(self.value, 'dp', [(1, 0), (2, 3)])  25.6 us
    ppermute x4, waiting for transfers between devices, across_in(): lax.ppermute(value, ('section', 'tensor'), [(role * 4 + a, role * 4 + b)...  24.8 us
    unnamed x205, local copies, waits for them, and re-layouts  22.7 us
    pallas_call x2, Pallas kernels, self_forward(): pl.pallas_call(functools.partial(self_forward_kernel, has_sum), out_shape...  20.7 us
  transfers between devices with their start and end apart: 45, of which 18 were waited for; matrix products, arithmetic and copies ran while one was open for 10% of the time, Pallas kernels for 20%

profile of v5, /device:TPU:0, one launch (start us, length us, event | category | flops | bytes accessed | tf_op | source)
XLA Modules:
  0.0 495.4 jit_solution(15641010551869907305)
XLA Ops:
  0.7 2.2 dynamic-slice_bitcast_fusion.6
  2.9 2.9 collective-permute-start
  5.9 4.7 collective-permute-start.4
  15.9 1.9 stack.74.info
  22.2 2.4 collective-permute-start.6
  27.2 1.7 shard_map.186
  28.9 11.2 %shard_map.189 = (f32[1024,768]{1,0:T(8,128)S(1)}, bf16[3,192,1024]{2,1,0:T(8,128)(2,1)S(1)}, f32[192,1024]{1,0:T(8,128)S(1)}, f32[8,1024]{1,0:T(8,128)S(1)}) custom-call(s32[8]{0:T(128)S(1)} %copy-done.89, bf16[1024,768]{1,0:T(8,128)(2,1)S(1)} %get-tuple-element.178.normed, bf16[4,192,768]{2,1,0:T(8,128)(2,1)} %pad_maximum_fusion.1.weights, ...), custom_call_target="tpu_custom_call" | custom-call | flops 8858370048 | bytes 12582912 | tf_op jit(solution)/shard_map/pallas_call | solution.py:221
  41.6 7.2 %collective-permute-done.3.weights = bf16[4,192,768]{2,1,0:T(8,128)(2,1)S(1)} collective-permute-done((bf16[4,192,768]{2,1,0:T(8,128)(2,1)}, bf16[4,192,768]{2,1,0:T(8,128)(2,1)S(1)}, u32[]{:S(2)}, u32[]{:S(2)}) %collective-permute-start.3) | collective-permute-done | bytes 1179680 | tf_op jit(solution)/shard_map/ppermute | solution.py:817
  48.9 9.4 %shard_map.190 = (bf16[1024,768]{1,0:T(8,128)(2,1)S(1)}, bf16[3,192,1024]{2,1,0:T(8,128)(2,1)S(1)}, f32[192,1024]{1,0:T(8,128)S(1)}, f32[8,1024]{1,0:T(8,128)S(1)}) custom-call(s32[8]{0:T(128)S(1)} %copy-done.89, bf16[1024,768]{1,0:T(8,128)(2,1)S(1)} %get-tuple-element.178.normed, bf16[4,192,768]{2,1,0:T(8,128)(2,1)S(1)} %collective-permute-done.3.weights, ...), custom_call_target="tpu_custom_call" | custom-call | flops 8858370048 | bytes 12582912 | tf_op jit(solution)/shard_map/pallas_call | solution.py:221
  60.0 3.4 collective-permute-done.5.far
  63.4 2.6 shard_map.191
  66.0 8.2 %shard_map.192 = (f32[1024,768]{1,0:T(8,128)S(1)}, bf16[1024,768]{1,0:T(8,128)(2,1)}, bf16[1024,768]{1,0:T(8,128)(2,1)}) custom-call(s32[8]{0:T(128)S(1)} %copy-done.89, bf16[1024,768]{1,0:T(8,128)(2,1)} %get-tuple-element.195.normed, bf16[2,768,768]{2,1,0:T(8,128)(2,1)} %constant_dynamic-update-slice_fusion.pack), custom_call_target="tpu_custom_call" | custom-call | flops 48318384 | bytes 188743 | tf_op jit(solution)/shard_map/pallas_call | solution.py:612
  74.2 24.8 %collective-permute-done.6.pack = bf16[2,768,768]{2,1,0:T(8,128)(2,1)S(1)} collective-permute-done((bf16[2,768,768]{2,1,0:T(8,128)(2,1)}, bf16[2,768,768]{2,1,0:T(8,128)(2,1)S(1)}, u32[]{:S(2)}, u32[]{:S(2)}) %collective-permute-start.6) | collective-permute-done | bytes 2359328 | tf_op jit(solution)/shard_map/ppermute | solution.py:822
  99.0 6.8 %shard_map.193 = (bf16[1024,768]{1,0:T(8,128)(2,1)}, bf16[1024,768]{1,0:T(8,128)(2,1)}, bf16[1024,768]{1,0:T(8,128)(2,1)}) custom-call(s32[8]{0:T(128)S(1)} %copy-done.89, bf16[1024,768]{1,0:T(8,128)(2,1)} %get-tuple-element.195.normed, bf16[2,768,768]{2,1,0:T(8,128)(2,1)S(1)} %collective-permute-done.6.pack, f32[1024,768]{1,0:T(8,128)S(1)} %get-tuple-element.188.refs_0_), custom_call_target="tpu_custom_call" | custom-call | flops 48318384 | bytes 188743 | tf_op jit(solution)/shard_map/pallas_call | solution.py:612
  105.8 3.7 collective-permute-done.8.far
  109.5 1.9 copy-done.1
  111.4 4.9 shard_map.194
  120.4 8.9 %collective-permute-done.9.far = bf16[256,768]{1,0:T(8,128)(2,1)S(1)} collective-permute-done((bf16[256,768]{1,0:T(8,128)(2,1)S(1)}, bf16[256,768]{1,0:T(8,128)(2,1)S(1)}, u32[]{:S(2)}, u32[]{:S(2)}) %collective-permute-start.9) | collective-permute-done | bytes 393248 | tf_op jit(solution)/shard_map/ppermute | solution.py:817
  129.5 5.8 %collective-permute-done.12.near.refs_0_ = bf16[512,768]{1,0:T(8,128)(2,1)S(1)} collective-permute-done((bf16[512,768]{1,0:T(8,128)(2,1)S(1)}, bf16[512,768]{1,0:T(8,128)(2,1)S(1)}, u32[]{:S(2)}, u32[]{:S(2)}) %collective-permute-start.12) | collective-permute-done | bytes 786464 | tf_op jit(solution)/shard_map/ppermute | solution.py:832
  138.1 1.9 shard_map.197
  140.5 3.1 collective-permute-done.14.far
  145.1 1.7 copy-done.7
  146.8 3.9 shard_map.199
  151.0 3.5 collective-permute-done.15.far
  154.4 1.9 copy-done.8
  156.4 5.8 %shard_map.200 = (f32[1024,768]{1,0:T(8,128)}, bf16[1024,768]{1,0:T(8,128)(2,1)S(1)}, f32[2,768]{1,0:T(2,128)}) custom-call(bf16[1024,768]{1,0:T(8,128)(2,1)} %copy-done.73, bf16[1024,768]{1,0:T(8,128)(2,1)} %get-tuple-element.206.near, bf16[1024,768]{1,0:T(8,128)(2,1)} %collective-permute-done.15.far, f32[1024,768]{1,0:T(8,128)S(1)} %copy-done.8, ...), custom_call_target="tpu_custom_call" | custom-call | flops 314572 | bytes 283115 | tf_op jit(solution)/shard_map/pallas_call | solution.py:574
  162.3 6.5 %shard_map.201 = (bf16[1024,768]{1,0:T(8,128)(2,1)}, bf16[1024,768]{1,0:T(8,128)(2,1)S(1)}, bf16[3,192,1024]{2,1,0:T(8,128)(2,1)S(1)}, bf16[3,192,1024]{2,1,0:T(8,128)(2,1)S(1)}) custom-call(s32[8]{0:T(128)S(1)} %copy-done.91, bf16[3,192,1024]{2,1,0:T(8,128)(2,1)S(1)} %copy-done.50, f32[192,1024]{1,0:T(8,128)S(1)} %copy-done.23, f32[8,1024]{1,0:T(8,128)S(1)} %copy-done.60, ...), custom_call_target="tpu_custom_call" | custom-call | flops 370440928 | bytes 125829 | tf_op jit(solution)/shard_map/pallas_call | solution.py:400
  169.2 2.0 collective-permute-done.16
  172.7 73.5 %collective-permute-done.17 = bf16[512,768]{1,0:T(8,128)(2,1)S(1)} collective-permute-done((bf16[512,768]{1,0:T(8,128)(2,1)S(1)}, bf16[512,768]{1,0:T(8,128)(2,1)S(1)}, u32[]{:S(2)}, u32[]{:S(2)}) %collective-permute-start.17) | collective-permute-done | bytes 786464 | tf_op jit(solution)/shard_map/ppermute | solution.py:836
  246.3 2.4 collective-permute-done.18
  248.7 15.4 %conditional.3 = ((f32[1024,768]{1,0:T(8,128)}, bf16[1024,768]{1,0:T(8,128)(2,1)}, f32[2,768]{1,0:T(2,128)}, bf16[1024,768]{1,0:T(8,128)(2,1)}, bf16[1024,768]{1,0:T(8,128)(2,1)}, /*index=5*/bf16[1024,768]{1,0:T(8,128)(2,1)})) conditional(s32[]{:T(128)} %convert_element_type.60, (f32[1,3,2,768]{3,2,1,0:T(2,128)}, s32[8]{0:T(128)S(1)}, ...), branch_computations={%region_0.1_spmd, %region_1.2_spmd} | conditional | flops 96636768 | bytes 13067095 | solution.py:982
  250.9 13.2 %branch_0_fun.3 = (f32[1024,768]{1,0:T(8,128)}, bf16[1024,768]{1,0:T(8,128)(2,1)}, f32[2,768]{1,0:T(2,128)}, bf16[1024,768]{1,0:T(8,128)(2,1)}, bf16[1024,768]{1,0:T(8,128)(2,1)}, /*index=5*/bf16[1024,768]{1,0:T(8,128)(2,1)}) custom-call(s32[8]{0:T(128)S(1)} %get-tuple-element.56.info, bf16[1024,768]{1,0:T(8,128)(2,1)S(1)} %copy.49.cot, ...), custom_call_target="tpu_custom_call" | custom-call | flops 96636768 | bytes 471859 | tf_op jit(solution)/shard_map/cond/branch_0_fun/pallas_call | solution.py:758
  264.3 6.7 %conditional.4 = ((f32[768,768]{1,0:T(8,128)}, bf16[768,768]{1,0:T(8,128)(2,1)})) conditional(s32[]{:T(128)} %convert_element_type.60, (bf16[1024,768]{1,0:T(8,128)(2,1)}, bf16[1024,768]{1,0:T(8,128)(2,1)}, bf16[1024,768]{1,0:T(8,128)(2,1)}) %tuple.57, (bf16[1024,768]{1,0:T(8,128)(2,1)}, bf16[1024,768]{1,0:T(8,128)(2,1)}, ...), branch_computations={%region_2.3_spmd, %region_3.4_spmd} | conditional | flops 48318384 | bytes 188751 | solution.py:998
  264.3 6.6 %branch_0_fun.4 = (f32[768,768]{1,0:T(8,128)}, bf16[768,768]{1,0:T(8,128)(2,1)}) custom-call(bf16[1024,768]{1,0:T(8,128)(2,1)} %get-tuple-element.66.left_near, bf16[1024,768]{1,0:T(8,128)(2,1)} %get-tuple-element.67.left_far, bf16[1024,768]{1,0:T(8,128)(2,1)} %get-tuple-element.68.right_near.right_far, bf16[1024,768]{1,0:T(8,128)(2,1)} %get-tuple-element.68.right_near.right_far), custom_call_target="tpu_custom_call" | custom-call | flops 48318384 | bytes 188743 | tf_op jit(solution)/shard_map/cond/branch_0_fun/pallas_call | solution.py:805
  272.5 6.8 %conditional.5 = ((f32[768,768]{1,0:T(8,128)}, bf16[768,768]{1,0:T(8,128)(2,1)})) conditional(s32[]{:T(128)} %convert_element_type.60, (bf16[1024,768]{1,0:T(8,128)(2,1)}, bf16[1024,768]{1,0:T(8,128)(2,1)}, bf16[1024,768]{1,0:T(8,128)(2,1)}) %tuple.59, (bf16[1024,768]{1,0:T(8,128)(2,1)}, bf16[1024,768]{1,0:T(8,128)(2,1)}, ...), branch_computations={%region_4.5_spmd, %region_5.6_spmd} | conditional | flops 48318384 | bytes 188751 | solution.py:1007
  272.5 6.4 %branch_0_fun.5 = (f32[768,768]{1,0:T(8,128)}, bf16[768,768]{1,0:T(8,128)(2,1)}) custom-call(bf16[1024,768]{1,0:T(8,128)(2,1)} %get-tuple-element.72.left_near.left_far, bf16[1024,768]{1,0:T(8,128)(2,1)} %get-tuple-element.72.left_near.left_far, bf16[1024,768]{1,0:T(8,128)(2,1)} %get-tuple-element.73.right_near, bf16[1024,768]{1,0:T(8,128)(2,1)} %get-tuple-element.74.right_far), custom_call_target="tpu_custom_call" | custom-call | flops 48318384 | bytes 188743 | tf_op jit(solution)/shard_map/cond/branch_0_fun/pallas_call | solution.py:805
  279.4 1.9 copy-done.3
  281.3 5.6 %shard_map.204 = (f32[1024,768]{1,0:T(8,128)S(1)}, bf16[1024,768]{1,0:T(8,128)(2,1)S(1)}, f32[2,768]{1,0:T(2,128)S(1)}) custom-call(f32[1024,768]{1,0:T(8,128)} %get-tuple-element.222.residual, bf16[1024,768]{1,0:T(8,128)(2,1)} %get-tuple-element.223.near, bf16[1024,768]{1,0:T(8,128)(2,1)} %collective-permute-done.21.far, f32[1024,768]{1,0:T(8,128)S(1)} %copy-done.3, ...), custom_call_target="tpu_custom_call" | custom-call | flops 314572 | bytes 283115 | tf_op jit(solution)/shard_map/pallas_call | solution.py:574
  286.9 1.7 copy-done.30
  288.6 16.3 %shard_map.205 = (f32[1024,768]{1,0:T(8,128)S(1)}, bf16[4,192,768]{2,1,0:T(8,128)(2,1)S(1)}, f32[3,2048]{1,0:T(4,128)S(1)}) custom-call(s32[8]{0:T(128)S(1)} %copy-done.92, bf16[3,192,1024]{2,1,0:T(8,128)(2,1)S(1)} %copy-done.68, f32[192,1024]{1,0:T(8,128)S(1)} %copy-done.70, f32[8,1024]{1,0:T(8,128)S(1)} %copy-done.72, ...), custom_call_target="tpu_custom_call" | custom-call | flops 20937965568 | bytes 12582912 | tf_op jit(solution)/shard_map/pallas_call | solution.py:345
  305.0 1.7 add_convert_fusion.3
  306.7 3.7 collective-permute-start.27
  311.1 18.2 %shard_map.206 = (bf16[1024,768]{1,0:T(8,128)(2,1)}, f32[4,192,768]{2,1,0:T(8,128)S(1)}, f32[3,2048]{1,0:T(4,128)S(1)}) custom-call(s32[8]{0:T(128)S(1)} %copy-done.92, bf16[3,192,1024]{2,1,0:T(8,128)(2,1)S(1)} %copy-done.44, f32[192,1024]{1,0:T(8,128)S(1)} %copy-done.54, f32[8,1024]{1,0:T(8,128)S(1)} %copy-done.58, ...), custom_call_target="tpu_custom_call" | custom-call | flops 209379648 | bytes 125829 | tf_op jit(solution)/shard_map/pallas_call | solution.py:345
  329.2 6.4 %collective-permute-done.27 = bf16[768,768]{1,0:T(8,128)(2,1)S(1)} collective-permute-done((bf16[768,768]{1,0:T(8,128)(2,1)S(1)}, bf16[768,768]{1,0:T(8,128)(2,1)S(1)}, u32[]{:S(2)}, u32[]{:S(2)}) %collective-permute-start.27) | collective-permute-done | bytes 1179680 | tf_op jit(solution)/shard_map/ppermute | solution.py:847
  339.4 7.7 %collective-permute-start.39 = (bf16[768,768]{1,0:T(8,128)(2,1)S(1)}, bf16[768,768]{1,0:T(8,128)(2,1)S(1)}, u32[]{:S(2)}, u32[]{:S(2)}) collective-permute-start(bf16[768,768]{1,0:T(8,128)(2,1)S(1)} %add_convert_fusion), channel_id=1, source_target_pairs={{0,4},{12,8},{1,5},{13,9},{2,6},{14,10},{3,7},{15,11},{16,20},{28,... | collective-permute-start | bytes 3538952 | tf_op jit(solution)/shard_map/ppermute | solution.py:847
  350.6 13.4 %collective-permute-done.26 = bf16[4,192,768]{2,1,0:T(8,128)(2,1)S(1)} collective-permute-done((bf16[4,192,768]{2,1,0:T(8,128)(2,1)S(1)}, bf16[4,192,768]{2,1,0:T(8,128)(2,1)S(1)}, u32[]{:S(2)}, u32[]{:S(2)}) %collective-permute-start.26) | collective-permute-done | bytes 1179680 | tf_op jit(solution)/shard_map/ppermute | solution.py:817
  365.2 7.9 %collective-permute-start.29 = (bf16[4,192,768]{2,1,0:T(8,128)(2,1)}, bf16[4,192,768]{2,1,0:T(8,128)(2,1)}, u32[]{:S(2)}, u32[]{:S(2)}) collective-permute-start(bf16[4,192,768]{2,1,0:T(8,128)(2,1)} %add_convert_fusion.2), channel_id=1, source_target_pairs={{0,4},{12,8},{1,5},{13,9},{2,6},{14,10},{3,7},{15,11},{16,20},{28,... | collective-permute-start | bytes 3538952 | tf_op jit(solution)/shard_map/ppermute | solution.py:847
  375.9 1.7 collective-permute-start.40
  387.1 10.0 %collective-permute-done.29 = bf16[4,192,768]{2,1,0:T(8,128)(2,1)} collective-permute-done((bf16[4,192,768]{2,1,0:T(8,128)(2,1)}, bf16[4,192,768]{2,1,0:T(8,128)(2,1)}, u32[]{:S(2)}, u32[]{:S(2)}) %collective-permute-start.29) | collective-permute-done | bytes 1179680 | tf_op jit(solution)/shard_map/ppermute | solution.py:847
  397.2 2.9 add.103
  401.2 2.8 select_convert_fusion.1
  404.0 1.7 collective-permute-start.31
  405.7 2.0 slice_select_fusion
  407.7 3.1 add.110
  410.7 5.7 %collective-permute-start.41 = (bf16[2,192,768]{2,1,0:T(8,128)(2,1)}, bf16[2,192,768]{2,1,0:T(8,128)(2,1)}, u32[]{:S(2)}, u32[]{:S(2)}) collective-permute-start(bf16[2,192,768]{2,1,0:T(8,128)(2,1)} %slice_select_fusion), channel_id=1, source_target_pairs={{0,4},{12,8},{1,5},{13,9},{2,6},{14,10},{3,7},{15,11},{16,20},{28,... | collective-permute-start | bytes 1769480 | tf_op jit(solution)/shard_map/ppermute | solution.py:847
  420.8 5.3 %shard_map.207 = (f32[1024,768]{1,0:T(8,128)S(1)}, bf16[1024,768]{1,0:T(8,128)(2,1)}, f32[2,768]{1,0:T(2,128)S(1)}) custom-call(f32[1024,768]{1,0:T(8,128)S(1)} %copy-done.31, bf16[1024,768]{1,0:T(8,128)(2,1)} %get-tuple-element.244.near, bf16[1024,768]{1,0:T(8,128)(2,1)} %collective-permute-done.23.far, bf16[1024,768]{1,0:T(8,128)(2,1)S(1)} %copy-done.15, ...), custom_call_target="tpu_custom_call" | custom-call | flops 314572 | bytes 283115 | tf_op jit(solution)/shard_map/pallas_call | solution.py:574
  429.3 2.2 add.111
  433.0 2.4 maximum_select_fusion.1
  438.0 2.2 collective-permute-done.25
  440.2 2.0 add.104
  443.5 7.6 %collective-permute-start.32 = (f32[10,768]{1,0:T(8,128)S(1)}, f32[10,768]{1,0:T(8,128)S(1)}, u32[]{:S(2)}, u32[]{:S(2)}) collective-permute-start(f32[10,768]{1,0:T(8,128)S(1)} %add.99), channel_id=1, source_target_pairs={{0,4},{12,8},{1,5},{13,9},{2,6},{14,10},{3,7},{15,11},{16,20},{28,... | collective-permute-start | bytes 92168 | tf_op jit(solution)/shard_map/ppermute | solution.py:847
  458.8 2.8 bitcast_convert_fusion
  461.6 24.5 %collective-permute-done.34 = f32[10,768]{1,0:T(8,128)S(1)} collective-permute-done((f32[10,768]{1,0:T(8,128)S(1)}, f32[10,768]{1,0:T(8,128)S(1)}, u32[]{:S(2)}, u32[]{:S(2)}) %collective-permute-start.34) | collective-permute-done | bytes 30752 | tf_op jit(solution)/shard_map/ppermute | solution.py:865
  489.6 2.2 convert_bitcast_fusion
  (335 shorter events, 76.9 us)
Async XLA Ops:
  0.7 10.0 %copy-start.93 = (f32[1,3,2,768]{3,2,1,0:T(2,128)S(1)}, f32[1,3,2,768]{3,2,1,0:T(2,128)}, u32[]{:S(2)}) copy-start(f32[1,3,2,768]{3,2,1,0:T(2,128)} %param.21) | copy-start | bytes 55300
  0.7 10.6 %copy-start.18 = (bf16[1,768,768]{2,1,0:T(8,128)(2,1)S(1)}, bf16[1,768,768]{2,1,0:T(8,128)(2,1)}, u32[]{:S(2)}) copy-start(bf16[1,768,768]{2,1,0:T(8,128)(2,1)} %param.25) | copy-start | bytes 3538948
  2.9 9.4 %copy-start.88 = (bf16[1,192,768]{2,1,0:T(8,128)(2,1)S(1)}, bf16[1,192,768]{2,1,0:T(8,128)(2,1)}, u32[]{:S(2)}) copy-start(bf16[1,192,768]{2,1,0:T(8,128)(2,1)} %param.23) | copy-start | bytes 884740
  2.9 15.8 %collective-permute-start = (bf16[256,768]{1,0:T(8,128)(2,1)}, bf16[256,768]{1,0:T(8,128)(2,1)S(1)}, u32[]{:S(2)}, u32[]{:S(2)}) collective-permute-start(bf16[256,768]{1,0:T(8,128)(2,1)} %get-tuple-element.286), channel_id=1, source_target_pairs={{0,2},{1,3},{2,0},{3,1},{4,6},{5,7},{6,4},{7,5},{8,10},{9,11},{10,... | collective-permute-start | bytes 1179656 | tf_op jit(solution)/shard_map/ppermute | solution.py:817
  5.9 11.9 %collective-permute-start.2 = (f32[320,3]{0,1:T(4,128)S(1)}, f32[320,3]{0,1:T(4,128)S(1)}, u32[]{:S(2)}, u32[]{:S(2)}) collective-permute-start(f32[320,3]{0,1:T(4,128)S(1)} %bitcast.90), channel_id=1, source_target_pairs={{0,2},{1,3},{2,0},{3,1},{4,6},{5,7},{6,4},{7,5},{8,10},{9,11},{10,... | collective-permute-start | bytes 11528 | tf_op jit(solution)/shard_map/ppermute | solution.py:817
  5.9 18.8 %collective-permute-start.4 = (bf16[2,192,768]{2,1,0:T(8,128)(2,1)S(1)}, bf16[2,192,768]{2,1,0:T(8,128)(2,1)}, u32[]{:S(2)}, u32[]{:S(2)}) collective-permute-start(bf16[2,192,768]{2,1,0:T(8,128)(2,1)S(1)} %bitcast.87), channel_id=1, source_target_pairs={{0,16},{1,17},{2,18},{3,19},{4,20},{5,21},{6,22},{7,23},{8,24},{9,... | collective-permute-start | bytes 1769480 | tf_op jit(solution)/shard_map/ppermute | solution.py:832
  18.8 8.2 %collective-permute-start.1 = (bf16[2,256,768]{2,1,0:T(8,128)(2,1)S(1)}, bf16[2,256,768]{2,1,0:T(8,128)(2,1)S(1)}, u32[]{:S(2)}, u32[]{:S(2)}) collective-permute-start(bf16[2,256,768]{2,1,0:T(8,128)(2,1)S(1)} %pad_maximum_fusion.3), channel_id=1, source_target_pairs={{0,1},{1,0},{2,3},{3,2},{4,5},{5,4},{6,7},{7,6},{8,9},{9,8},{10,11... | collective-permute-start | bytes 2359304 | tf_op jit(solution)/shard_map/ppermute | solution.py:828
  19.8 29.0 %collective-permute-start.3 = (bf16[4,192,768]{2,1,0:T(8,128)(2,1)}, bf16[4,192,768]{2,1,0:T(8,128)(2,1)S(1)}, u32[]{:S(2)}, u32[]{:S(2)}) collective-permute-start(bf16[4,192,768]{2,1,0:T(8,128)(2,1)} %pad_maximum_fusion.1.weights), channel_id=1, source_target_pairs={{0,2},{1,3},{2,0},{3,1},{4,6},{5,7},{6,4},{7,5},{8,10},{9,11},{10,... | collective-permute-start | bytes 3538952 | tf_op jit(solution)/shard_map/ppermute | solution.py:817
  22.2 26.6 %copy-start.28 = (f32[3,128,2048]{2,1,0:T(8,128)}, f32[3,128,2048]{2,1,0:T(8,128)S(1)}, u32[]{:S(2)}) copy-start(f32[3,128,2048]{2,1,0:T(8,128)S(1)} %shard_map.187.table) | copy-start | bytes 9437188
  22.2 76.8 %collective-permute-start.6 = (bf16[2,768,768]{2,1,0:T(8,128)(2,1)}, bf16[2,768,768]{2,1,0:T(8,128)(2,1)S(1)}, u32[]{:S(2)}, u32[]{:S(2)}) collective-permute-start(bf16[2,768,768]{2,1,0:T(8,128)(2,1)} %constant_dynamic-update-slice_fusion.pack), channel_id=1, source_target_pairs={{0,2},{1,3},{2,0},{3,1},{4,6},{5,7},{6,4},{7,5},{8,10},{9,11},{10,... | collective-permute-start | bytes 7077896 | tf_op jit(solution)/shard_map/ppermute | solution.py:822
  26.1 72.9 %collective-permute-start.7 = (bf16[1536,768]{1,0:T(8,128)(2,1)S(1)}, bf16[1536,768]{1,0:T(8,128)(2,1)S(1)}, u32[]{:S(2)}, u32[]{:S(2)}) collective-permute-start(bf16[1536,768]{1,0:T(8,128)(2,1)S(1)} %pad_maximum_fusion), channel_id=1, source_target_pairs={{16,18},{17,19},{18,16},{19,17},{20,22},{21,23},{22,20},{23,21},{2... | collective-permute-start | bytes 7077896 | tf_op jit(solution)/shard_map/ppermute | solution.py:822
  28.9 20.0 %copy-start.36 = (bf16[1024,768]{1,0:T(8,128)(2,1)}, bf16[1024,768]{1,0:T(8,128)(2,1)S(1)}, u32[]{:S(2)}) copy-start(bf16[1024,768]{1,0:T(8,128)(2,1)S(1)} %get-tuple-element.178.normed) | copy-start | bytes 4718596
  28.9 34.5 %copy-start.14 = (bf16[1024,768]{1,0:T(8,128)(2,1)}, bf16[1024,768]{1,0:T(8,128)(2,1)S(1)}, u32[]{:S(2)}) copy-start(bf16[1024,768]{1,0:T(8,128)(2,1)S(1)} %get-tuple-element.177.stream.values) | copy-start | bytes 4718596
  41.6 16.7 %copy-start.43 = (bf16[3,192,1024]{2,1,0:T(8,128)(2,1)}, bf16[3,192,1024]{2,1,0:T(8,128)(2,1)S(1)}, u32[]{:S(2)}) copy-start(bf16[3,192,1024]{2,1,0:T(8,128)(2,1)S(1)} %get-tuple-element.225.qkv) | copy-start | bytes 3538948
  48.8 9.5 %copy-start.65 = (bf16[4,192,768]{2,1,0:T(8,128)(2,1)}, bf16[4,192,768]{2,1,0:T(8,128)(2,1)S(1)}, u32[]{:S(2)}) copy-start(bf16[4,192,768]{2,1,0:T(8,128)(2,1)S(1)} %collective-permute-done.3.weights) | copy-start | bytes 3538948
  48.9 14.5 %copy-start.55 = (f32[2,768]{1,0:T(2,128)S(1)}, f32[2,768]{1,0:T(2,128)}, u32[]{:S(2)}) copy-start(f32[2,768]{1,0:T(2,128)} %get-tuple-element.293.norm_ref) | copy-start | bytes 18436
  60.0 3.4 collective-permute-start.5
  105.8 3.8 collective-permute-start.8
  116.4 18.9 %collective-permute-start.12 = (bf16[512,768]{1,0:T(8,128)(2,1)S(1)}, bf16[512,768]{1,0:T(8,128)(2,1)S(1)}, u32[]{:S(2)}, u32[]{:S(2)}) collective-permute-start(bf16[512,768]{1,0:T(8,128)(2,1)S(1)} %constant_dynamic-slice_fusion.2), channel_id=1, source_target_pairs={{0,16},{1,17},{2,18},{3,19},{4,20},{5,21},{6,22},{7,23},{8,24},{9,... | collective-permute-start | bytes 2359304 | tf_op jit(solution)/shard_map/ppermute | solution.py:832
  118.2 11.2 %collective-permute-start.9 = (bf16[256,768]{1,0:T(8,128)(2,1)S(1)}, bf16[256,768]{1,0:T(8,128)(2,1)S(1)}, u32[]{:S(2)}, u32[]{:S(2)}) collective-permute-start(bf16[256,768]{1,0:T(8,128)(2,1)S(1)} %get-tuple-element.191), channel_id=1, source_target_pairs={{0,2},{1,3},{2,0},{3,1},{4,6},{5,7},{6,4},{7,5},{8,10},{9,11},{10,... | collective-permute-start | bytes 1179656 | tf_op jit(solution)/shard_map/ppermute | solution.py:817
  119.7 17.9 %collective-permute-start.11 = (bf16[768,768]{1,0:T(8,128)(2,1)S(1)}, bf16[768,768]{1,0:T(8,128)(2,1)S(1)}, u32[]{:S(2)}, u32[]{:S(2)}) collective-permute-start(bf16[768,768]{1,0:T(8,128)(2,1)S(1)} %bitcast.81), channel_id=1, source_target_pairs={{16,18},{17,19},{18,16},{19,17},{20,22},{21,23},{22,20},{23,21},{2... | collective-permute-start | bytes 3538952 | tf_op jit(solution)/shard_map/ppermute | solution.py:822
  129.5 5.9 %collective-permute-start.10 = (bf16[2,256,768]{2,1,0:T(8,128)(2,1)S(1)}, bf16[2,256,768]{2,1,0:T(8,128)(2,1)S(1)}, u32[]{:S(2)}, u32[]{:S(2)}) collective-permute-start(bf16[2,256,768]{2,1,0:T(8,128)(2,1)S(1)} %pad_maximum_fusion.4), channel_id=1, source_target_pairs={{0,1},{1,0},{2,3},{3,2},{4,5},{5,4},{6,7},{7,6},{8,9},{9,8},{10,11... | collective-permute-start | bytes 2359304 | tf_op jit(solution)/shard_map/ppermute | solution.py:828
  135.3 2.7 collective-permute-start.13
  140.1 3.5 collective-permute-start.14
  150.7 3.8 collective-permute-start.15
  168.9 79.8 %copy-start.92 = (s32[8]{0:T(128)S(1)}, s32[8]{0:T(128)}, u32[]{:S(2)}) copy-start(s32[8]{0:T(128)} %stack.74.info) | copy-start | bytes 100
  168.9 2.4 collective-permute-start.16
  171.4 74.8 %collective-permute-start.17 = (bf16[512,768]{1,0:T(8,128)(2,1)S(1)}, bf16[512,768]{1,0:T(8,128)(2,1)S(1)}, u32[]{:S(2)}, u32[]{:S(2)}) collective-permute-start(bf16[512,768]{1,0:T(8,128)(2,1)S(1)} %add_convert_fusion.4), channel_id=1, source_target_pairs={{16,0},{17,1},{18,2},{19,3},{20,4},{21,5},{22,6},{23,7},{24,8},{25... | collective-permute-start | bytes 2359304 | tf_op jit(solution)/shard_map/ppermute | solution.py:836
  246.3 2.4 collective-permute-start.18
  264.1 15.2 %collective-permute-start.21 = (bf16[1024,768]{1,0:T(8,128)(2,1)}, bf16[1024,768]{1,0:T(8,128)(2,1)}, u32[]{:S(2)}, u32[]{:S(2)}) collective-permute-start(bf16[1024,768]{1,0:T(8,128)(2,1)} %get-tuple-element.223.near), channel_id=1, source_target_pairs={{0,1},{1,0},{2,3},{3,2},{4,5},{5,4},{6,7},{7,6},{8,9},{9,8},{10,11... | collective-permute-start | bytes 4718600 | tf_op jit(solution)/shard_map/ppermute | solution.py:828
  271.0 34.0 %collective-permute-start.22 = (bf16[768,768]{1,0:T(8,128)(2,1)}, bf16[768,768]{1,0:T(8,128)(2,1)}, u32[]{:S(2)}, u32[]{:S(2)}) collective-permute-start(bf16[768,768]{1,0:T(8,128)(2,1)} %get-tuple-element.233), channel_id=1, source_target_pairs={{0,2},{1,3},{2,0},{3,1},{4,6},{5,7},{6,4},{7,5},{8,10},{9,11},{10,... | collective-permute-start | bytes 3538952 | tf_op jit(solution)/shard_map/ppermute | solution.py:817
  288.6 16.4 %copy-start.82 = (f32[768,768]{1,0:T(8,128)S(1)}, f32[768,768]{1,0:T(8,128)}, u32[]{:S(2)}) copy-start(f32[768,768]{1,0:T(8,128)} %get-tuple-element.232) | copy-start | bytes 7077892
  288.6 21.8 %copy-start.100 = (bf16[768,768]{1,0:T(8,128)(2,1)S(1)}, bf16[768,768]{1,0:T(8,128)(2,1)}, u32[]{:S(2)}) copy-start(bf16[768,768]{1,0:T(8,128)(2,1)} %get-tuple-element.238) | copy-start | bytes 3538948
  288.6 22.4 %copy-start.54 = (f32[192,1024]{1,0:T(8,128)S(1)}, f32[192,1024]{1,0:T(8,128)}, u32[]{:S(2)}) copy-start(f32[192,1024]{1,0:T(8,128)} %copy-done.53) | copy-start | bytes 2359300
  306.7 28.9 %collective-permute-start.27 = (bf16[768,768]{1,0:T(8,128)(2,1)S(1)}, bf16[768,768]{1,0:T(8,128)(2,1)S(1)}, u32[]{:S(2)}, u32[]{:S(2)}) collective-permute-start(bf16[768,768]{1,0:T(8,128)(2,1)S(1)} %add_convert_fusion.3), channel_id=1, source_target_pairs={{0,4},{12,8},{1,5},{13,9},{2,6},{14,10},{3,7},{15,11},{16,20},{28,... | collective-permute-start | bytes 3538952 | tf_op jit(solution)/shard_map/ppermute | solution.py:847
  310.4 27.8 %collective-permute-start.38 = (bf16[768,768]{1,0:T(8,128)(2,1)S(1)}, bf16[768,768]{1,0:T(8,128)(2,1)S(1)}, u32[]{:S(2)}, u32[]{:S(2)}) collective-permute-start(bf16[768,768]{1,0:T(8,128)(2,1)S(1)} %copy-done.100), channel_id=1, source_target_pairs={{0,2},{1,3},{2,0},{3,1},{4,6},{5,7},{6,4},{7,5},{8,10},{9,11},{10,... | collective-permute-start | bytes 3538952 | tf_op jit(solution)/shard_map/ppermute | solution.py:817
  311.0 26.4 %copy-start.78 = (bf16[1024,768]{1,0:T(8,128)(2,1)S(1)}, bf16[1024,768]{1,0:T(8,128)(2,1)}, u32[]{:S(2)}) copy-start(bf16[1024,768]{1,0:T(8,128)(2,1)} %get-tuple-element.219.active_far) | copy-start | bytes 4718596
  335.9 13.4 %collective-permute-start.28 = (bf16[768,768]{1,0:T(8,128)(2,1)S(1)}, bf16[768,768]{1,0:T(8,128)(2,1)S(1)}, u32[]{:S(2)}, u32[]{:S(2)}) collective-permute-start(bf16[768,768]{1,0:T(8,128)(2,1)S(1)} %add.100), channel_id=1, source_target_pairs={{4,8},{8,4},{5,9},{9,5},{6,10},{10,6},{7,11},{11,7},{20,24},{24,20... | collective-permute-start | bytes 3538952 | tf_op jit(solution)/shard_map/ppermute | solution.py:853
  336.8 27.2 %collective-permute-start.26 = (bf16[4,192,768]{2,1,0:T(8,128)(2,1)S(1)}, bf16[4,192,768]{2,1,0:T(8,128)(2,1)S(1)}, u32[]{:S(2)}, u32[]{:S(2)}) collective-permute-start(bf16[4,192,768]{2,1,0:T(8,128)(2,1)S(1)} %get-tuple-element.240), channel_id=1, source_target_pairs={{0,2},{1,3},{2,0},{3,1},{4,6},{5,7},{6,4},{7,5},{8,10},{9,11},{10,... | collective-permute-start | bytes 3538952 | tf_op jit(solution)/shard_map/ppermute | solution.py:817
  337.4 9.6 %copy-start.46 = (bf16[3,192,1024]{2,1,0:T(8,128)(2,1)S(1)}, bf16[3,192,1024]{2,1,0:T(8,128)(2,1)}, u32[]{:S(2)}) copy-start(bf16[3,192,1024]{2,1,0:T(8,128)(2,1)} %copy-done.45) | copy-start | bytes 3538948
  337.4 9.6 %copy-start.48 = (bf16[3,192,1024]{2,1,0:T(8,128)(2,1)S(1)}, bf16[3,192,1024]{2,1,0:T(8,128)(2,1)}, u32[]{:S(2)}) copy-start(bf16[3,192,1024]{2,1,0:T(8,128)(2,1)} %copy-done.47) | copy-start | bytes 3538948
  338.1 40.5 %collective-permute-start.19 = (bf16[1024,768]{1,0:T(8,128)(2,1)S(1)}, bf16[1024,768]{1,0:T(8,128)(2,1)S(1)}, u32[]{:S(2)}, u32[]{:S(2)}) collective-permute-start(bf16[1024,768]{1,0:T(8,128)(2,1)S(1)} %shard_map.202.near), channel_id=1, source_target_pairs={{0,1},{1,0},{2,3},{3,2},{4,5},{5,4},{6,7},{7,6},{8,9},{9,8},{10,11... | collective-permute-start | bytes 4718600 | tf_op jit(solution)/shard_map/ppermute | solution.py:828
  339.4 35.1 %collective-permute-start.39 = (bf16[768,768]{1,0:T(8,128)(2,1)S(1)}, bf16[768,768]{1,0:T(8,128)(2,1)S(1)}, u32[]{:S(2)}, u32[]{:S(2)}) collective-permute-start(bf16[768,768]{1,0:T(8,128)(2,1)S(1)} %add_convert_fusion), channel_id=1, source_target_pairs={{0,4},{12,8},{1,5},{13,9},{2,6},{14,10},{3,7},{15,11},{16,20},{28,... | collective-permute-start | bytes 3538952 | tf_op jit(solution)/shard_map/ppermute | solution.py:847
  348.6 27.3 %collective-permute-start.36 = (bf16[4,192,768]{2,1,0:T(8,128)(2,1)S(1)}, bf16[4,192,768]{2,1,0:T(8,128)(2,1)S(1)}, u32[]{:S(2)}, u32[]{:S(2)}) collective-permute-start(bf16[4,192,768]{2,1,0:T(8,128)(2,1)S(1)} %get-tuple-element.261), channel_id=1, source_target_pairs={{16,18},{17,19},{18,16},{19,17},{20,22},{21,23},{22,20},{23,21},{2... | collective-permute-start | bytes 3538952 | tf_op jit(solution)/shard_map/ppermute | solution.py:822
  365.2 31.9 %collective-permute-start.29 = (bf16[4,192,768]{2,1,0:T(8,128)(2,1)}, bf16[4,192,768]{2,1,0:T(8,128)(2,1)}, u32[]{:S(2)}, u32[]{:S(2)}) collective-permute-start(bf16[4,192,768]{2,1,0:T(8,128)(2,1)} %add_convert_fusion.2), channel_id=1, source_target_pairs={{0,4},{12,8},{1,5},{13,9},{2,6},{14,10},{3,7},{15,11},{16,20},{28,... | collective-permute-start | bytes 3538952 | tf_op jit(solution)/shard_map/ppermute | solution.py:847
  373.1 28.0 %collective-permute-start.30 = (bf16[768,768]{1,0:T(8,128)(2,1)}, bf16[768,768]{1,0:T(8,128)(2,1)}, u32[]{:S(2)}, u32[]{:S(2)}) collective-permute-start(bf16[768,768]{1,0:T(8,128)(2,1)} %add.101), channel_id=1, source_target_pairs={{4,0},{8,12},{5,1},{9,13},{6,2},{10,14},{7,3},{11,15},{20,16},{24,... | collective-permute-start | bytes 3538952 | tf_op jit(solution)/shard_map/ppermute | solution.py:865
  374.4 46.3 %collective-permute-start.23 = (bf16[1024,768]{1,0:T(8,128)(2,1)}, bf16[1024,768]{1,0:T(8,128)(2,1)}, u32[]{:S(2)}, u32[]{:S(2)}) collective-permute-start(bf16[1024,768]{1,0:T(8,128)(2,1)} %get-tuple-element.244.near), channel_id=1, source_target_pairs={{0,1},{1,0},{2,3},{3,2},{4,5},{5,4},{6,7},{7,6},{8,9},{9,8},{10,11... | collective-permute-start | bytes 4718600 | tf_op jit(solution)/shard_map/ppermute | solution.py:828
  375.9 31.8 %collective-permute-start.40 = (bf16[768,768]{1,0:T(8,128)(2,1)}, bf16[768,768]{1,0:T(8,128)(2,1)}, u32[]{:S(2)}, u32[]{:S(2)}) collective-permute-start(bf16[768,768]{1,0:T(8,128)(2,1)} %add.109), channel_id=1, source_target_pairs={{4,8},{8,4},{5,9},{9,5},{6,10},{10,6},{7,11},{11,7},{20,24},{24,20... | collective-permute-start | bytes 3538952 | tf_op jit(solution)/shard_map/ppermute | solution.py:853
  380.2 25.5 %collective-permute-start.37 = (bf16[2,192,768]{2,1,0:T(8,128)(2,1)}, bf16[2,192,768]{2,1,0:T(8,128)(2,1)}, u32[]{:S(2)}, u32[]{:S(2)}) collective-permute-start(bf16[2,192,768]{2,1,0:T(8,128)(2,1)} %slice.105), channel_id=1, source_target_pairs={{16,0},{17,1},{18,2},{19,3},{20,4},{21,5},{22,6},{23,7},{24,8},{25... | collective-permute-start | bytes 1769480 | tf_op jit(solution)/shard_map/ppermute | solution.py:836
  404.0 36.2 %collective-permute-start.31 = (bf16[4,192,768]{2,1,0:T(8,128)(2,1)}, bf16[4,192,768]{2,1,0:T(8,128)(2,1)}, u32[]{:S(2)}, u32[]{:S(2)}) collective-permute-start(bf16[4,192,768]{2,1,0:T(8,128)(2,1)} %add.103), channel_id=1, source_target_pairs={{4,8},{8,4},{5,9},{9,5},{6,10},{10,6},{7,11},{11,7},{20,24},{24,20... | collective-permute-start | bytes 3538952 | tf_op jit(solution)/shard_map/ppermute | solution.py:853
  407.7 13.1 %copy-start.31 = (f32[1024,768]{1,0:T(8,128)S(1)}, f32[1024,768]{1,0:T(8,128)}, u32[]{:S(2)}) copy-start(f32[1024,768]{1,0:T(8,128)} %copy-done.30) | copy-start | bytes 9437188
  410.7 10.0 %copy-start.15 = (bf16[1024,768]{1,0:T(8,128)(2,1)S(1)}, bf16[1024,768]{1,0:T(8,128)(2,1)}, u32[]{:S(2)}) copy-start(bf16[1024,768]{1,0:T(8,128)(2,1)} %copy-done.14) | copy-start | bytes 4718596
  410.7 18.5 %collective-permute-start.41 = (bf16[2,192,768]{2,1,0:T(8,128)(2,1)}, bf16[2,192,768]{2,1,0:T(8,128)(2,1)}, u32[]{:S(2)}, u32[]{:S(2)}) collective-permute-start(bf16[2,192,768]{2,1,0:T(8,128)(2,1)} %slice_select_fusion), channel_id=1, source_target_pairs={{0,4},{12,8},{1,5},{13,9},{2,6},{14,10},{3,7},{15,11},{16,20},{28,... | collective-permute-start | bytes 1769480 | tf_op jit(solution)/shard_map/ppermute | solution.py:847
  417.3 15.6 %collective-permute-start.20 = (bf16[256,768]{1,0:T(8,128)(2,1)}, bf16[256,768]{1,0:T(8,128)(2,1)}, u32[]{:S(2)}, u32[]{:S(2)}) collective-permute-start(bf16[256,768]{1,0:T(8,128)(2,1)} %get-tuple-element.277), channel_id=1, source_target_pairs={{0,2},{1,3},{2,0},{3,1},{4,6},{5,7},{6,4},{7,5},{8,10},{9,11},{10,... | collective-permute-start | bytes 1179656 | tf_op jit(solution)/shard_map/ppermute | solution.py:817
  418.3 40.5 %collective-permute-start.44 = (bf16[768,768]{1,0:T(8,128)(2,1)}, bf16[768,768]{1,0:T(8,128)(2,1)}, u32[]{:S(2)}, u32[]{:S(2)}) collective-permute-start(bf16[768,768]{1,0:T(8,128)(2,1)} %add.110), channel_id=1, source_target_pairs={{4,0},{8,12},{5,1},{9,13},{6,2},{10,14},{7,3},{11,15},{20,16},{24,... | collective-permute-start | bytes 3538952 | tf_op jit(solution)/shard_map/ppermute | solution.py:865
  426.9 24.2 %collective-permute-start.24 = (bf16[256,768]{1,0:T(8,128)(2,1)}, bf16[256,768]{1,0:T(8,128)(2,1)}, u32[]{:S(2)}, u32[]{:S(2)}) collective-permute-start(bf16[256,768]{1,0:T(8,128)(2,1)} %dynamic-slice_convert_fusion), channel_id=1, source_target_pairs={{0,2},{1,3},{2,0},{3,1},{4,6},{5,7},{6,4},{7,5},{8,10},{9,11},{10,... | collective-permute-start | bytes 1179656 | tf_op jit(solution)/shard_map/ppermute | solution.py:817
  431.5 23.3 %collective-permute-start.42 = (bf16[2,192,768]{2,1,0:T(8,128)(2,1)}, bf16[2,192,768]{2,1,0:T(8,128)(2,1)}, u32[]{:S(2)}, u32[]{:S(2)}) collective-permute-start(bf16[2,192,768]{2,1,0:T(8,128)(2,1)} %add.111), channel_id=1, source_target_pairs={{4,8},{8,4},{5,9},{9,5},{6,10},{10,6},{7,11},{11,7},{20,24},{24,20... | collective-permute-start | bytes 1769480 | tf_op jit(solution)/shard_map/ppermute | solution.py:853
  436.1 4.1 collective-permute-start.25
  440.2 13.3 %copy-start.81 = (f32[1,1,1,256,768]{4,3,2,1,0:T(8,128)S(1)}, f32[1,1,1,256,768]{4,3,2,1,0:T(8,128)}, u32[]{:S(2)}) copy-start(f32[1,1,1,256,768]{4,3,2,1,0:T(8,128)} %dynamic-slice_bitcast_fusion) | copy-start | bytes 2359300
  442.2 49.5 %collective-permute-start.35 = (bf16[4,192,768]{2,1,0:T(8,128)(2,1)S(1)}, bf16[4,192,768]{2,1,0:T(8,128)(2,1)S(1)}, u32[]{:S(2)}, u32[]{:S(2)}) collective-permute-start(bf16[4,192,768]{2,1,0:T(8,128)(2,1)S(1)} %add.104), channel_id=1, source_target_pairs={{4,0},{8,12},{5,1},{9,13},{6,2},{10,14},{7,3},{11,15},{20,16},{24,... | collective-permute-start | bytes 3538952 | tf_op jit(solution)/shard_map/ppermute | solution.py:865
  443.5 9.3 %collective-permute-start.32 = (f32[10,768]{1,0:T(8,128)S(1)}, f32[10,768]{1,0:T(8,128)S(1)}, u32[]{:S(2)}, u32[]{:S(2)}) collective-permute-start(f32[10,768]{1,0:T(8,128)S(1)} %add.99), channel_id=1, source_target_pairs={{0,4},{12,8},{1,5},{13,9},{2,6},{14,10},{3,7},{15,11},{16,20},{28,... | collective-permute-start | bytes 92168 | tf_op jit(solution)/shard_map/ppermute | solution.py:847
  452.8 4.6 collective-permute-start.33
  456.1 33.4 %collective-permute-start.43 = (bf16[2,192,768]{2,1,0:T(8,128)(2,1)S(1)}, bf16[2,192,768]{2,1,0:T(8,128)(2,1)}, u32[]{:S(2)}, u32[]{:S(2)}) collective-permute-start(bf16[2,192,768]{2,1,0:T(8,128)(2,1)S(1)} %add.112), channel_id=1, source_target_pairs={{4,0},{8,12},{5,1},{9,13},{6,2},{10,14},{7,3},{11,15},{20,16},{24,... | collective-permute-start | bytes 1769480 | tf_op jit(solution)/shard_map/ppermute | solution.py:865
  457.5 28.6 %collective-permute-start.34 = (f32[10,768]{1,0:T(8,128)S(1)}, f32[10,768]{1,0:T(8,128)S(1)}, u32[]{:S(2)}, u32[]{:S(2)}) collective-permute-start(f32[10,768]{1,0:T(8,128)S(1)} %add.106), channel_id=1, source_target_pairs={{4,0},{8,12},{5,1},{9,13},{6,2},{10,14},{7,3},{11,15},{20,16},{24,... | collective-permute-start | bytes 92168 | tf_op jit(solution)/shard_map/ppermute | solution.py:865
  (82 other events, 349.3 us)

commit v6 on v5

--- a/solution.py
+++ b/solution.py
@@ -1054,9 +1054,9 @@
     d_attn.swap()
     d_pair = (pair_near + across_in(pair_far, DECODER).astype(F32)).astype(BF)
     d_source = to_encoder(d_pair[2:])
-    d_pair = Line(after(jnp.where(decoder, d_pair[:2], d_source), d_up.value))
     d_ffn_in = d_up.total()
     reached = d_attn.value
+    d_pair = Line(after(jnp.where(decoder, d_pair[:2], d_source), reached))
     d_attn = d_attn.total()
     d_pair = d_pair.total()
 

time: 502 us -> 511 us (1.018)
  starting transfers between devices: 72.4 us -> 79.8 us
  local copies, waits for them, and re-layouts: 40.7 us -> 47.2 us
    ppermute x5, starting transfers between devices: 32.5 us -> 39.4 us  [inward(): arrived = lax.ppermute(self.value, 'dp', [(0, 1), (3, 2)])]
    unnamed x205 -> x213, local copies, waits for them, and re-layouts: 22.7 us -> 26.1 us
  transfers between devices with their start and end apart: 45 -> 45, of which waited for: 18 -> 19; matrix products, arithmetic and copies ran while one was open for 10% -> 10% of each run, Pallas kernels for 20% -> 20%
where the time goes in v6:
time: 511 us; the launch traced here: 504 us
  waiting for transfers between devices  192 us (38%)
  Pallas kernels  143 us (28%)
  starting transfers between devices  79.8 us (16%)
  local copies, waits for them, and re-layouts  47.2 us (9%)
  other arithmetic  33.6 us (7%)
  between operations  5.42 us (1%)
    ppermute x2, waiting for transfers between devices, to_encoder(): return lax.ppermute(value, 'section', [(DECODER, ENCODER)])  73.1 us
    ppermute x5, starting transfers between devices, inward(): arrived = lax.ppermute(self.value, 'dp', [(0, 1), (3, 2)])  39.4 us
    pallas_call x2, Pallas kernels, self_backward(): pl.pallas_call(functools.partial(self_backward_kernel, has_sum), out_shap...  34.6 us
    ppermute x10, waiting for transfers between devices, across(): return lax.ppermute(value, 'tensor', [(0, 2), (1, 3), (2, 0), (3, 1)])  32.1 us
    unnamed x213, local copies, waits for them, and re-layouts  26.1 us
    ppermute x4, waiting for transfers between devices, across_in(): lax.ppermute(value, ('section', 'tensor'), [(role * 4 + a, role * 4 + b)...  24.8 us
    ppermute x5, waiting for transfers between devices, total(): outward = lax.ppermute(self.value, 'dp', [(1, 0), (2, 3)])  22.3 us
    pallas_call x2, Pallas kernels, self_forward(): pl.pallas_call(functools.partial(self_forward_kernel, has_sum), out_shape...  20.6 us
  transfers between devices with their start and end apart: 45, of which 19 were waited for; matrix products, arithmetic and copies ran while one was open for 10% of the time, Pallas kernels for 20%

profile of v6, /device:TPU:0, one launch (start us, length us, event | category | flops | bytes accessed | tf_op | source)
XLA Modules:
  0.0 504.1 jit_solution(9108768007534303268)
XLA Ops:
  0.7 2.2 dynamic-slice_bitcast_fusion.6
  2.9 2.9 collective-permute-start
  5.9 4.7 collective-permute-start.4
  16.0 2.0 stack.74.info
  22.4 2.4 collective-permute-start.6
  27.3 1.7 shard_map.186
  29.1 11.2 %shard_map.189 = (f32[1024,768]{1,0:T(8,128)S(1)}, bf16[3,192,1024]{2,1,0:T(8,128)(2,1)S(1)}, f32[192,1024]{1,0:T(8,128)S(1)}, f32[8,1024]{1,0:T(8,128)S(1)}) custom-call(s32[8]{0:T(128)S(1)} %copy-done.92, bf16[1024,768]{1,0:T(8,128)(2,1)S(1)} %get-tuple-element.178.normed, bf16[4,192,768]{2,1,0:T(8,128)(2,1)} %pad_maximum_fusion.1.weights, ...), custom_call_target="tpu_custom_call" | custom-call | flops 8858370048 | bytes 12582912 | tf_op jit(solution)/shard_map/pallas_call | solution.py:221
  41.8 7.2 %collective-permute-done.3.weights = bf16[4,192,768]{2,1,0:T(8,128)(2,1)S(1)} collective-permute-done((bf16[4,192,768]{2,1,0:T(8,128)(2,1)}, bf16[4,192,768]{2,1,0:T(8,128)(2,1)S(1)}, u32[]{:S(2)}, u32[]{:S(2)}) %collective-permute-start.3) | collective-permute-done | bytes 1179680 | tf_op jit(solution)/shard_map/ppermute | solution.py:817
  49.0 9.4 %shard_map.190 = (bf16[1024,768]{1,0:T(8,128)(2,1)S(1)}, bf16[3,192,1024]{2,1,0:T(8,128)(2,1)S(1)}, f32[192,1024]{1,0:T(8,128)S(1)}, f32[8,1024]{1,0:T(8,128)S(1)}) custom-call(s32[8]{0:T(128)S(1)} %copy-done.92, bf16[1024,768]{1,0:T(8,128)(2,1)S(1)} %get-tuple-element.178.normed, bf16[4,192,768]{2,1,0:T(8,128)(2,1)S(1)} %collective-permute-done.3.weights, ...), custom_call_target="tpu_custom_call" | custom-call | flops 8858370048 | bytes 12582912 | tf_op jit(solution)/shard_map/pallas_call | solution.py:221
  60.1 3.4 collective-permute-done.5.far
  63.5 2.6 shard_map.191
  66.1 8.2 %shard_map.192 = (f32[1024,768]{1,0:T(8,128)S(1)}, bf16[1024,768]{1,0:T(8,128)(2,1)}, bf16[1024,768]{1,0:T(8,128)(2,1)}) custom-call(s32[8]{0:T(128)S(1)} %copy-done.92, bf16[1024,768]{1,0:T(8,128)(2,1)} %get-tuple-element.195.normed, bf16[2,768,768]{2,1,0:T(8,128)(2,1)} %constant_dynamic-update-slice_fusion.pack), custom_call_target="tpu_custom_call" | custom-call | flops 48318384 | bytes 188743 | tf_op jit(solution)/shard_map/pallas_call | solution.py:612
  74.4 24.8 %collective-permute-done.6.pack = bf16[2,768,768]{2,1,0:T(8,128)(2,1)S(1)} collective-permute-done((bf16[2,768,768]{2,1,0:T(8,128)(2,1)}, bf16[2,768,768]{2,1,0:T(8,128)(2,1)S(1)}, u32[]{:S(2)}, u32[]{:S(2)}) %collective-permute-start.6) | collective-permute-done | bytes 2359328 | tf_op jit(solution)/shard_map/ppermute | solution.py:822
  99.2 6.8 %shard_map.193 = (bf16[1024,768]{1,0:T(8,128)(2,1)}, bf16[1024,768]{1,0:T(8,128)(2,1)}, bf16[1024,768]{1,0:T(8,128)(2,1)}) custom-call(s32[8]{0:T(128)S(1)} %copy-done.92, bf16[1024,768]{1,0:T(8,128)(2,1)} %get-tuple-element.195.normed, bf16[2,768,768]{2,1,0:T(8,128)(2,1)S(1)} %collective-permute-done.6.pack, f32[1024,768]{1,0:T(8,128)S(1)} %get-tuple-element.188.refs_0_), custom_call_target="tpu_custom_call" | custom-call | flops 48318384 | bytes 188743 | tf_op jit(solution)/shard_map/pallas_call | solution.py:612
  106.0 3.7 collective-permute-done.8.far
  109.7 1.9 copy-done.1
  111.6 4.9 shard_map.194
  121.2 8.9 %collective-permute-done.9.far = bf16[256,768]{1,0:T(8,128)(2,1)S(1)} collective-permute-done((bf16[256,768]{1,0:T(8,128)(2,1)S(1)}, bf16[256,768]{1,0:T(8,128)(2,1)S(1)}, u32[]{:S(2)}, u32[]{:S(2)}) %collective-permute-start.9) | collective-permute-done | bytes 393248 | tf_op jit(solution)/shard_map/ppermute | solution.py:817
  130.3 5.8 %collective-permute-done.12.near.refs_0_ = bf16[512,768]{1,0:T(8,128)(2,1)S(1)} collective-permute-done((bf16[512,768]{1,0:T(8,128)(2,1)S(1)}, bf16[512,768]{1,0:T(8,128)(2,1)S(1)}, u32[]{:S(2)}, u32[]{:S(2)}) %collective-permute-start.12) | collective-permute-done | bytes 786464 | tf_op jit(solution)/shard_map/ppermute | solution.py:832
  138.8 1.9 shard_map.197
  142.3 3.1 collective-permute-done.14.far
  146.9 1.7 copy-done.7
  148.6 3.9 shard_map.199
  152.8 3.5 collective-permute-done.15.far
  156.2 1.9 copy-done.8
  158.2 5.9 %shard_map.200 = (f32[1024,768]{1,0:T(8,128)}, bf16[1024,768]{1,0:T(8,128)(2,1)S(1)}, f32[2,768]{1,0:T(2,128)}) custom-call(bf16[1024,768]{1,0:T(8,128)(2,1)} %copy-done.76, bf16[1024,768]{1,0:T(8,128)(2,1)} %get-tuple-element.206.near, bf16[1024,768]{1,0:T(8,128)(2,1)} %collective-permute-done.15.far, f32[1024,768]{1,0:T(8,128)S(1)} %copy-done.8, ...), custom_call_target="tpu_custom_call" | custom-call | flops 314572 | bytes 283115 | tf_op jit(solution)/shard_map/pallas_call | solution.py:574
  164.1 6.5 %shard_map.201 = (bf16[1024,768]{1,0:T(8,128)(2,1)}, bf16[1024,768]{1,0:T(8,128)(2,1)S(1)}, bf16[3,192,1024]{2,1,0:T(8,128)(2,1)S(1)}, bf16[3,192,1024]{2,1,0:T(8,128)(2,1)S(1)}) custom-call(s32[8]{0:T(128)S(1)} %copy-done.94, bf16[3,192,1024]{2,1,0:T(8,128)(2,1)S(1)} %copy-done.52, f32[192,1024]{1,0:T(8,128)S(1)} %copy-done.23, f32[8,1024]{1,0:T(8,128)S(1)} %copy-done.63, ...), custom_call_target="tpu_custom_call" | custom-call | flops 370440928 | bytes 125829 | tf_op jit(solution)/shard_map/pallas_call | solution.py:400
  171.0 2.0 collective-permute-done.16
  174.5 73.1 %collective-permute-done.17 = bf16[512,768]{1,0:T(8,128)(2,1)S(1)} collective-permute-done((bf16[512,768]{1,0:T(8,128)(2,1)S(1)}, bf16[512,768]{1,0:T(8,128)(2,1)S(1)}, u32[]{:S(2)}, u32[]{:S(2)}) %collective-permute-start.17) | collective-permute-done | bytes 786464 | tf_op jit(solution)/shard_map/ppermute | solution.py:836
  247.7 2.4 collective-permute-done.18
  250.1 15.4 %conditional.3 = ((f32[1024,768]{1,0:T(8,128)}, bf16[1024,768]{1,0:T(8,128)(2,1)}, f32[2,768]{1,0:T(2,128)}, bf16[1024,768]{1,0:T(8,128)(2,1)}, bf16[1024,768]{1,0:T(8,128)(2,1)}, /*index=5*/bf16[1024,768]{1,0:T(8,128)(2,1)})) conditional(s32[]{:T(128)} %convert_element_type.60, (f32[1,3,2,768]{3,2,1,0:T(2,128)}, s32[8]{0:T(128)S(1)}, ...), branch_computations={%region_0.1_spmd, %region_1.2_spmd} | conditional | flops 96636768 | bytes 13067095 | solution.py:982
  252.3 13.1 %branch_0_fun.3 = (f32[1024,768]{1,0:T(8,128)}, bf16[1024,768]{1,0:T(8,128)(2,1)}, f32[2,768]{1,0:T(2,128)}, bf16[1024,768]{1,0:T(8,128)(2,1)}, bf16[1024,768]{1,0:T(8,128)(2,1)}, /*index=5*/bf16[1024,768]{1,0:T(8,128)(2,1)}) custom-call(s32[8]{0:T(128)S(1)} %get-tuple-element.56.info, bf16[1024,768]{1,0:T(8,128)(2,1)S(1)} %copy.49.cot, ...), custom_call_target="tpu_custom_call" | custom-call | flops 96636768 | bytes 471859 | tf_op jit(solution)/shard_map/cond/branch_0_fun/pallas_call | solution.py:758
  265.7 6.6 %conditional.4 = ((f32[768,768]{1,0:T(8,128)}, bf16[768,768]{1,0:T(8,128)(2,1)})) conditional(s32[]{:T(128)} %convert_element_type.60, (bf16[1024,768]{1,0:T(8,128)(2,1)}, bf16[1024,768]{1,0:T(8,128)(2,1)}, bf16[1024,768]{1,0:T(8,128)(2,1)}) %tuple.57, (bf16[1024,768]{1,0:T(8,128)(2,1)}, bf16[1024,768]{1,0:T(8,128)(2,1)}, ...), branch_computations={%region_2.3_spmd, %region_3.4_spmd} | conditional | flops 48318384 | bytes 188751 | solution.py:998
  265.7 6.6 %branch_0_fun.4 = (f32[768,768]{1,0:T(8,128)}, bf16[768,768]{1,0:T(8,128)(2,1)}) custom-call(bf16[1024,768]{1,0:T(8,128)(2,1)} %get-tuple-element.66.left_near, bf16[1024,768]{1,0:T(8,128)(2,1)} %get-tuple-element.67.left_far, bf16[1024,768]{1,0:T(8,128)(2,1)} %get-tuple-element.68.right_near.right_far, bf16[1024,768]{1,0:T(8,128)(2,1)} %get-tuple-element.68.right_near.right_far), custom_call_target="tpu_custom_call" | custom-call | flops 48318384 | bytes 188743 | tf_op jit(solution)/shard_map/cond/branch_0_fun/pallas_call | solution.py:805
  273.8 6.8 %conditional.5 = ((f32[768,768]{1,0:T(8,128)}, bf16[768,768]{1,0:T(8,128)(2,1)})) conditional(s32[]{:T(128)} %convert_element_type.60, (bf16[1024,768]{1,0:T(8,128)(2,1)}, bf16[1024,768]{1,0:T(8,128)(2,1)}, bf16[1024,768]{1,0:T(8,128)(2,1)}) %tuple.59, (bf16[1024,768]{1,0:T(8,128)(2,1)}, bf16[1024,768]{1,0:T(8,128)(2,1)}, ...), branch_computations={%region_4.5_spmd, %region_5.6_spmd} | conditional | flops 48318384 | bytes 188751 | solution.py:1007
  273.8 6.4 %branch_0_fun.5 = (f32[768,768]{1,0:T(8,128)}, bf16[768,768]{1,0:T(8,128)(2,1)}) custom-call(bf16[1024,768]{1,0:T(8,128)(2,1)} %get-tuple-element.72.left_near.left_far, bf16[1024,768]{1,0:T(8,128)(2,1)} %get-tuple-element.72.left_near.left_far, bf16[1024,768]{1,0:T(8,128)(2,1)} %get-tuple-element.73.right_near, bf16[1024,768]{1,0:T(8,128)(2,1)} %get-tuple-element.74.right_far), custom_call_target="tpu_custom_call" | custom-call | flops 48318384 | bytes 188743 | tf_op jit(solution)/shard_map/cond/branch_0_fun/pallas_call | solution.py:805
  280.7 1.9 copy-done.3
  282.6 5.6 %shard_map.204 = (f32[1024,768]{1,0:T(8,128)S(1)}, bf16[1024,768]{1,0:T(8,128)(2,1)S(1)}, f32[2,768]{1,0:T(2,128)S(1)}) custom-call(f32[1024,768]{1,0:T(8,128)} %get-tuple-element.222.residual, bf16[1024,768]{1,0:T(8,128)(2,1)} %get-tuple-element.223.near, bf16[1024,768]{1,0:T(8,128)(2,1)} %collective-permute-done.21.far, f32[1024,768]{1,0:T(8,128)S(1)} %copy-done.3, ...), custom_call_target="tpu_custom_call" | custom-call | flops 314572 | bytes 283115 | tf_op jit(solution)/shard_map/pallas_call | solution.py:574
  289.9 16.3 %shard_map.205 = (f32[1024,768]{1,0:T(8,128)S(1)}, bf16[4,192,768]{2,1,0:T(8,128)(2,1)S(1)}, f32[3,2048]{1,0:T(4,128)S(1)}) custom-call(s32[8]{0:T(128)S(1)} %copy-done.95, bf16[3,192,1024]{2,1,0:T(8,128)(2,1)S(1)} %copy-done.71, f32[192,1024]{1,0:T(8,128)S(1)} %copy-done.73, f32[8,1024]{1,0:T(8,128)S(1)} %copy-done.75, ...), custom_call_target="tpu_custom_call" | custom-call | flops 20937965568 | bytes 12582912 | tf_op jit(solution)/shard_map/pallas_call | solution.py:345
  308.0 3.7 collective-permute-start.27
  312.3 18.3 %shard_map.206 = (bf16[1024,768]{1,0:T(8,128)(2,1)}, f32[4,192,768]{2,1,0:T(8,128)S(1)}, f32[3,2048]{1,0:T(4,128)S(1)}) custom-call(s32[8]{0:T(128)S(1)} %copy-done.95, bf16[3,192,1024]{2,1,0:T(8,128)(2,1)S(1)} %copy-done.46, f32[192,1024]{1,0:T(8,128)S(1)} %copy-done.56, f32[8,1024]{1,0:T(8,128)S(1)} %copy-done.61, ...), custom_call_target="tpu_custom_call" | custom-call | flops 209379648 | bytes 125829 | tf_op jit(solution)/shard_map/pallas_call | solution.py:345
  330.6 6.3 %collective-permute-done.27 = bf16[768,768]{1,0:T(8,128)(2,1)S(1)} collective-permute-done((bf16[768,768]{1,0:T(8,128)(2,1)S(1)}, bf16[768,768]{1,0:T(8,128)(2,1)S(1)}, u32[]{:S(2)}, u32[]{:S(2)}) %collective-permute-start.27) | collective-permute-done | bytes 1179680 | tf_op jit(solution)/shard_map/ppermute | solution.py:847
  340.6 7.4 %collective-permute-start.42 = (bf16[768,768]{1,0:T(8,128)(2,1)S(1)}, bf16[768,768]{1,0:T(8,128)(2,1)S(1)}, u32[]{:S(2)}, u32[]{:S(2)}) collective-permute-start(bf16[768,768]{1,0:T(8,128)(2,1)S(1)} %add_convert_fusion), channel_id=1, source_target_pairs={{0,4},{12,8},{1,5},{13,9},{2,6},{14,10},{3,7},{15,11},{16,20},{28,... | collective-permute-start | bytes 3538952 | tf_op jit(solution)/shard_map/ppermute | solution.py:847
  349.5 15.8 %collective-permute-done.26 = bf16[4,192,768]{2,1,0:T(8,128)(2,1)S(1)} collective-permute-done((bf16[4,192,768]{2,1,0:T(8,128)(2,1)S(1)}, bf16[4,192,768]{2,1,0:T(8,128)(2,1)S(1)}, u32[]{:S(2)}, u32[]{:S(2)}) %collective-permute-start.26) | collective-permute-done | bytes 1179680 | tf_op jit(solution)/shard_map/ppermute | solution.py:817
  366.5 8.0 %collective-permute-start.29 = (bf16[4,192,768]{2,1,0:T(8,128)(2,1)}, bf16[4,192,768]{2,1,0:T(8,128)(2,1)}, u32[]{:S(2)}, u32[]{:S(2)}) collective-permute-start(bf16[4,192,768]{2,1,0:T(8,128)(2,1)} %add_convert_fusion.2), channel_id=1, source_target_pairs={{0,4},{12,8},{1,5},{13,9},{2,6},{14,10},{3,7},{15,11},{16,20},{28,... | collective-permute-start | bytes 3538952 | tf_op jit(solution)/shard_map/ppermute | solution.py:847
  375.9 2.4 shard_map.208
  378.3 1.8 collective-permute-start.36
  382.6 1.7 collective-permute-start.43
  390.0 8.1 %collective-permute-done.29 = bf16[4,192,768]{2,1,0:T(8,128)(2,1)} collective-permute-done((bf16[4,192,768]{2,1,0:T(8,128)(2,1)}, bf16[4,192,768]{2,1,0:T(8,128)(2,1)}, u32[]{:S(2)}, u32[]{:S(2)}) %collective-permute-start.29) | collective-permute-done | bytes 1179680 | tf_op jit(solution)/shard_map/ppermute | solution.py:847
  398.1 2.9 add.103
  402.6 2.8 select_convert_fusion.1
  405.5 1.7 collective-permute-start.31
  413.7 2.0 add.112
  419.5 1.9 copy-done.31
  421.4 5.3 %shard_map.207 = (f32[1024,768]{1,0:T(8,128)S(1)}, bf16[1024,768]{1,0:T(8,128)(2,1)}, f32[2,768]{1,0:T(2,128)S(1)}) custom-call(f32[1024,768]{1,0:T(8,128)S(1)} %copy-done.31, bf16[1024,768]{1,0:T(8,128)(2,1)} %get-tuple-element.244.near, bf16[1024,768]{1,0:T(8,128)(2,1)} %collective-permute-done.23.far, bf16[1024,768]{1,0:T(8,128)(2,1)S(1)} %copy-done.15, ...), custom_call_target="tpu_custom_call" | custom-call | flops 314572 | bytes 283115 | tf_op jit(solution)/shard_map/pallas_call | solution.py:574
  428.2 1.9 slice_select_fusion
  430.2 1.9 add.104
  432.1 14.6 %collective-permute-start.38 = (bf16[2,192,768]{2,1,0:T(8,128)(2,1)}, bf16[2,192,768]{2,1,0:T(8,128)(2,1)}, u32[]{:S(2)}, u32[]{:S(2)}) collective-permute-start(bf16[2,192,768]{2,1,0:T(8,128)(2,1)} %slice_select_fusion), channel_id=1, source_target_pairs={{0,4},{12,8},{1,5},{13,9},{2,6},{14,10},{3,7},{15,11},{16,20},{28,... | collective-permute-start | bytes 1769480 | tf_op jit(solution)/shard_map/ppermute | solution.py:847
  446.7 2.2 maximum_select_fusion.1
  452.8 2.1 dynamic-slice_bitcast_fusion
  455.1 5.6 %collective-permute-start.32 = (f32[10,768]{1,0:T(8,128)S(1)}, f32[10,768]{1,0:T(8,128)S(1)}, u32[]{:S(2)}, u32[]{:S(2)}) collective-permute-start(f32[10,768]{1,0:T(8,128)S(1)} %add.99), channel_id=1, source_target_pairs={{0,4},{12,8},{1,5},{13,9},{2,6},{14,10},{3,7},{15,11},{16,20},{28,... | collective-permute-start | bytes 92168 | tf_op jit(solution)/shard_map/ppermute | solution.py:847
  468.5 2.8 bitcast_convert_fusion
  471.4 10.1 %collective-permute-done.34 = f32[10,768]{1,0:T(8,128)S(1)} collective-permute-done((f32[10,768]{1,0:T(8,128)S(1)}, f32[10,768]{1,0:T(8,128)S(1)}, u32[]{:S(2)}, u32[]{:S(2)}) %collective-permute-start.34) | collective-permute-done | bytes 30752 | tf_op jit(solution)/shard_map/ppermute | solution.py:865
  491.1 10.5 %collective-permute-done.40 = bf16[2,192,768]{2,1,0:T(8,128)(2,1)S(1)} collective-permute-done((bf16[2,192,768]{2,1,0:T(8,128)(2,1)S(1)}, bf16[2,192,768]{2,1,0:T(8,128)(2,1)S(1)}, u32[]{:S(2)}, u32[]{:S(2)}) %collective-permute-start.40) | collective-permute-done | bytes 589856 | tf_op jit(solution)/shard_map/ppermute | solution.py:865
  (343 shorter events, 85.6 us)
Async XLA Ops:
  0.7 10.0 %copy-start.96 = (f32[1,3,2,768]{3,2,1,0:T(2,128)S(1)}, f32[1,3,2,768]{3,2,1,0:T(2,128)}, u32[]{:S(2)}) copy-start(f32[1,3,2,768]{3,2,1,0:T(2,128)} %param.21) | copy-start | bytes 55300
  0.7 10.6 %copy-start.18 = (bf16[1,768,768]{2,1,0:T(8,128)(2,1)S(1)}, bf16[1,768,768]{2,1,0:T(8,128)(2,1)}, u32[]{:S(2)}) copy-start(bf16[1,768,768]{2,1,0:T(8,128)(2,1)} %param.25) | copy-start | bytes 3538948
  2.9 16.0 %collective-permute-start = (bf16[256,768]{1,0:T(8,128)(2,1)}, bf16[256,768]{1,0:T(8,128)(2,1)S(1)}, u32[]{:S(2)}, u32[]{:S(2)}) collective-permute-start(bf16[256,768]{1,0:T(8,128)(2,1)} %get-tuple-element.286), channel_id=1, source_target_pairs={{0,2},{1,3},{2,0},{3,1},{4,6},{5,7},{6,4},{7,5},{8,10},{9,11},{10,... | collective-permute-start | bytes 1179656 | tf_op jit(solution)/shard_map/ppermute | solution.py:817
  5.9 12.1 %collective-permute-start.2 = (f32[320,3]{0,1:T(4,128)S(1)}, f32[320,3]{0,1:T(4,128)S(1)}, u32[]{:S(2)}, u32[]{:S(2)}) collective-permute-start(f32[320,3]{0,1:T(4,128)S(1)} %bitcast.90), channel_id=1, source_target_pairs={{0,2},{1,3},{2,0},{3,1},{4,6},{5,7},{6,4},{7,5},{8,10},{9,11},{10,... | collective-permute-start | bytes 11528 | tf_op jit(solution)/shard_map/ppermute | solution.py:817
  5.9 18.9 %collective-permute-start.4 = (bf16[2,192,768]{2,1,0:T(8,128)(2,1)S(1)}, bf16[2,192,768]{2,1,0:T(8,128)(2,1)}, u32[]{:S(2)}, u32[]{:S(2)}) collective-permute-start(bf16[2,192,768]{2,1,0:T(8,128)(2,1)S(1)} %bitcast.87), channel_id=1, source_target_pairs={{0,16},{1,17},{2,18},{3,19},{4,20},{5,21},{6,22},{7,23},{8,24},{9,... | collective-permute-start | bytes 1769480 | tf_op jit(solution)/shard_map/ppermute | solution.py:832
  19.0 8.2 %collective-permute-start.1 = (bf16[2,256,768]{2,1,0:T(8,128)(2,1)S(1)}, bf16[2,256,768]{2,1,0:T(8,128)(2,1)S(1)}, u32[]{:S(2)}, u32[]{:S(2)}) collective-permute-start(bf16[2,256,768]{2,1,0:T(8,128)(2,1)S(1)} %pad_maximum_fusion.3), channel_id=1, source_target_pairs={{0,1},{1,0},{2,3},{3,2},{4,5},{5,4},{6,7},{7,6},{8,9},{9,8},{10,11... | collective-permute-start | bytes 2359304 | tf_op jit(solution)/shard_map/ppermute | solution.py:828
  20.0 29.0 %collective-permute-start.3 = (bf16[4,192,768]{2,1,0:T(8,128)(2,1)}, bf16[4,192,768]{2,1,0:T(8,128)(2,1)S(1)}, u32[]{:S(2)}, u32[]{:S(2)}) collective-permute-start(bf16[4,192,768]{2,1,0:T(8,128)(2,1)} %pad_maximum_fusion.1.weights), channel_id=1, source_target_pairs={{0,2},{1,3},{2,0},{3,1},{4,6},{5,7},{6,4},{7,5},{8,10},{9,11},{10,... | collective-permute-start | bytes 3538952 | tf_op jit(solution)/shard_map/ppermute | solution.py:817
  22.4 26.6 %copy-start.28 = (f32[3,128,2048]{2,1,0:T(8,128)}, f32[3,128,2048]{2,1,0:T(8,128)S(1)}, u32[]{:S(2)}) copy-start(f32[3,128,2048]{2,1,0:T(8,128)S(1)} %shard_map.187.table) | copy-start | bytes 9437188
  22.4 76.8 %collective-permute-start.6 = (bf16[2,768,768]{2,1,0:T(8,128)(2,1)}, bf16[2,768,768]{2,1,0:T(8,128)(2,1)S(1)}, u32[]{:S(2)}, u32[]{:S(2)}) collective-permute-start(bf16[2,768,768]{2,1,0:T(8,128)(2,1)} %constant_dynamic-update-slice_fusion.pack), channel_id=1, source_target_pairs={{0,2},{1,3},{2,0},{3,1},{4,6},{5,7},{6,4},{7,5},{8,10},{9,11},{10,... | collective-permute-start | bytes 7077896 | tf_op jit(solution)/shard_map/ppermute | solution.py:822
  26.3 72.9 %collective-permute-start.7 = (bf16[1536,768]{1,0:T(8,128)(2,1)S(1)}, bf16[1536,768]{1,0:T(8,128)(2,1)S(1)}, u32[]{:S(2)}, u32[]{:S(2)}) collective-permute-start(bf16[1536,768]{1,0:T(8,128)(2,1)S(1)} %pad_maximum_fusion), channel_id=1, source_target_pairs={{16,18},{17,19},{18,16},{19,17},{20,22},{21,23},{22,20},{23,21},{2... | collective-permute-start | bytes 7077896 | tf_op jit(solution)/shard_map/ppermute | solution.py:822
  29.1 20.0 %copy-start.38 = (bf16[1024,768]{1,0:T(8,128)(2,1)}, bf16[1024,768]{1,0:T(8,128)(2,1)S(1)}, u32[]{:S(2)}) copy-start(bf16[1024,768]{1,0:T(8,128)(2,1)S(1)} %get-tuple-element.178.normed) | copy-start | bytes 4718596
  29.1 34.5 %copy-start.14 = (bf16[1024,768]{1,0:T(8,128)(2,1)}, bf16[1024,768]{1,0:T(8,128)(2,1)S(1)}, u32[]{:S(2)}) copy-start(bf16[1024,768]{1,0:T(8,128)(2,1)S(1)} %get-tuple-element.177.stream.values) | copy-start | bytes 4718596
  41.8 16.6 %copy-start.45 = (bf16[3,192,1024]{2,1,0:T(8,128)(2,1)}, bf16[3,192,1024]{2,1,0:T(8,128)(2,1)S(1)}, u32[]{:S(2)}) copy-start(bf16[3,192,1024]{2,1,0:T(8,128)(2,1)S(1)} %get-tuple-element.225.qkv) | copy-start | bytes 3538948
  49.0 14.5 %copy-start.58 = (f32[2,768]{1,0:T(2,128)S(1)}, f32[2,768]{1,0:T(2,128)}, u32[]{:S(2)}) copy-start(f32[2,768]{1,0:T(2,128)} %get-tuple-element.293.norm_ref) | copy-start | bytes 18436
  60.1 3.4 collective-permute-start.5
  106.0 3.8 collective-permute-start.8
  117.1 18.9 %collective-permute-start.12 = (bf16[512,768]{1,0:T(8,128)(2,1)S(1)}, bf16[512,768]{1,0:T(8,128)(2,1)S(1)}, u32[]{:S(2)}, u32[]{:S(2)}) collective-permute-start(bf16[512,768]{1,0:T(8,128)(2,1)S(1)} %constant_dynamic-slice_fusion.2), channel_id=1, source_target_pairs={{0,16},{1,17},{2,18},{3,19},{4,20},{5,21},{6,22},{7,23},{8,24},{9,... | collective-permute-start | bytes 2359304 | tf_op jit(solution)/shard_map/ppermute | solution.py:832
  118.9 11.2 %collective-permute-start.9 = (bf16[256,768]{1,0:T(8,128)(2,1)S(1)}, bf16[256,768]{1,0:T(8,128)(2,1)S(1)}, u32[]{:S(2)}, u32[]{:S(2)}) collective-permute-start(bf16[256,768]{1,0:T(8,128)(2,1)S(1)} %get-tuple-element.191), channel_id=1, source_target_pairs={{0,2},{1,3},{2,0},{3,1},{4,6},{5,7},{6,4},{7,5},{8,10},{9,11},{10,... | collective-permute-start | bytes 1179656 | tf_op jit(solution)/shard_map/ppermute | solution.py:817
  120.4 17.9 %collective-permute-start.11 = (bf16[768,768]{1,0:T(8,128)(2,1)S(1)}, bf16[768,768]{1,0:T(8,128)(2,1)S(1)}, u32[]{:S(2)}, u32[]{:S(2)}) collective-permute-start(bf16[768,768]{1,0:T(8,128)(2,1)S(1)} %bitcast.81), channel_id=1, source_target_pairs={{16,18},{17,19},{18,16},{19,17},{20,22},{21,23},{22,20},{23,21},{2... | collective-permute-start | bytes 3538952 | tf_op jit(solution)/shard_map/ppermute | solution.py:822
  130.2 5.9 %collective-permute-start.10 = (bf16[2,256,768]{2,1,0:T(8,128)(2,1)S(1)}, bf16[2,256,768]{2,1,0:T(8,128)(2,1)S(1)}, u32[]{:S(2)}, u32[]{:S(2)}) collective-permute-start(bf16[2,256,768]{2,1,0:T(8,128)(2,1)S(1)} %pad_maximum_fusion.4), channel_id=1, source_target_pairs={{0,1},{1,0},{2,3},{3,2},{4,5},{5,4},{6,7},{7,6},{8,9},{9,8},{10,11... | collective-permute-start | bytes 2359304 | tf_op jit(solution)/shard_map/ppermute | solution.py:828
  136.1 2.7 collective-permute-start.13
  142.0 3.5 collective-permute-start.14
  152.5 3.8 collective-permute-start.15
  170.7 79.4 %copy-start.95 = (s32[8]{0:T(128)S(1)}, s32[8]{0:T(128)}, u32[]{:S(2)}) copy-start(s32[8]{0:T(128)} %stack.74.info) | copy-start | bytes 100
  170.7 2.4 collective-permute-start.16
  173.2 74.4 %collective-permute-start.17 = (bf16[512,768]{1,0:T(8,128)(2,1)S(1)}, bf16[512,768]{1,0:T(8,128)(2,1)S(1)}, u32[]{:S(2)}, u32[]{:S(2)}) collective-permute-start(bf16[512,768]{1,0:T(8,128)(2,1)S(1)} %add_convert_fusion.4), channel_id=1, source_target_pairs={{16,0},{17,1},{18,2},{19,3},{20,4},{21,5},{22,6},{23,7},{24,8},{25... | collective-permute-start | bytes 2359304 | tf_op jit(solution)/shard_map/ppermute | solution.py:836
  247.6 2.4 collective-permute-start.18
  265.5 15.1 %collective-permute-start.21 = (bf16[1024,768]{1,0:T(8,128)(2,1)}, bf16[1024,768]{1,0:T(8,128)(2,1)}, u32[]{:S(2)}, u32[]{:S(2)}) collective-permute-start(bf16[1024,768]{1,0:T(8,128)(2,1)} %get-tuple-element.223.near), channel_id=1, source_target_pairs={{0,1},{1,0},{2,3},{3,2},{4,5},{5,4},{6,7},{7,6},{8,9},{9,8},{10,11... | collective-permute-start | bytes 4718600 | tf_op jit(solution)/shard_map/ppermute | solution.py:828
  272.3 34.0 %collective-permute-start.22 = (bf16[768,768]{1,0:T(8,128)(2,1)}, bf16[768,768]{1,0:T(8,128)(2,1)}, u32[]{:S(2)}, u32[]{:S(2)}) collective-permute-start(bf16[768,768]{1,0:T(8,128)(2,1)} %get-tuple-element.233), channel_id=1, source_target_pairs={{0,2},{1,3},{2,0},{3,1},{4,6},{5,7},{6,4},{7,5},{8,10},{9,11},{10,... | collective-permute-start | bytes 3538952 | tf_op jit(solution)/shard_map/ppermute | solution.py:817
  289.9 16.4 %copy-start.85 = (f32[768,768]{1,0:T(8,128)S(1)}, f32[768,768]{1,0:T(8,128)}, u32[]{:S(2)}) copy-start(f32[768,768]{1,0:T(8,128)} %get-tuple-element.232) | copy-start | bytes 7077892
  289.9 21.8 %copy-start.104 = (bf16[768,768]{1,0:T(8,128)(2,1)S(1)}, bf16[768,768]{1,0:T(8,128)(2,1)}, u32[]{:S(2)}) copy-start(bf16[768,768]{1,0:T(8,128)(2,1)} %get-tuple-element.238) | copy-start | bytes 3538948
  289.9 22.4 %copy-start.56 = (f32[192,1024]{1,0:T(8,128)S(1)}, f32[192,1024]{1,0:T(8,128)}, u32[]{:S(2)}) copy-start(f32[192,1024]{1,0:T(8,128)} %copy-done.55) | copy-start | bytes 2359300
  308.0 28.9 %collective-permute-start.27 = (bf16[768,768]{1,0:T(8,128)(2,1)S(1)}, bf16[768,768]{1,0:T(8,128)(2,1)S(1)}, u32[]{:S(2)}, u32[]{:S(2)}) collective-permute-start(bf16[768,768]{1,0:T(8,128)(2,1)S(1)} %add_convert_fusion.3), channel_id=1, source_target_pairs={{0,4},{12,8},{1,5},{13,9},{2,6},{14,10},{3,7},{15,11},{16,20},{28,... | collective-permute-start | bytes 3538952 | tf_op jit(solution)/shard_map/ppermute | solution.py:847
  311.7 27.7 %collective-permute-start.41 = (bf16[768,768]{1,0:T(8,128)(2,1)S(1)}, bf16[768,768]{1,0:T(8,128)(2,1)S(1)}, u32[]{:S(2)}, u32[]{:S(2)}) collective-permute-start(bf16[768,768]{1,0:T(8,128)(2,1)S(1)} %copy-done.104), channel_id=1, source_target_pairs={{0,2},{1,3},{2,0},{3,1},{4,6},{5,7},{6,4},{7,5},{8,10},{9,11},{10,... | collective-permute-start | bytes 3538952 | tf_op jit(solution)/shard_map/ppermute | solution.py:817
  312.3 26.4 %copy-start.81 = (bf16[1024,768]{1,0:T(8,128)(2,1)S(1)}, bf16[1024,768]{1,0:T(8,128)(2,1)}, u32[]{:S(2)}) copy-start(bf16[1024,768]{1,0:T(8,128)(2,1)} %get-tuple-element.219.active_far) | copy-start | bytes 4718596
  337.2 10.9 %collective-permute-start.28 = (bf16[768,768]{1,0:T(8,128)(2,1)S(1)}, bf16[768,768]{1,0:T(8,128)(2,1)S(1)}, u32[]{:S(2)}, u32[]{:S(2)}) collective-permute-start(bf16[768,768]{1,0:T(8,128)(2,1)S(1)} %add.100), channel_id=1, source_target_pairs={{4,8},{8,4},{5,9},{9,5},{6,10},{10,6},{7,11},{11,7},{20,24},{24,20... | collective-permute-start | bytes 3538952 | tf_op jit(solution)/shard_map/ppermute | solution.py:853
  338.1 27.2 %collective-permute-start.26 = (bf16[4,192,768]{2,1,0:T(8,128)(2,1)S(1)}, bf16[4,192,768]{2,1,0:T(8,128)(2,1)S(1)}, u32[]{:S(2)}, u32[]{:S(2)}) collective-permute-start(bf16[4,192,768]{2,1,0:T(8,128)(2,1)S(1)} %get-tuple-element.240), channel_id=1, source_target_pairs={{0,2},{1,3},{2,0},{3,1},{4,6},{5,7},{6,4},{7,5},{8,10},{9,11},{10,... | collective-permute-start | bytes 3538952 | tf_op jit(solution)/shard_map/ppermute | solution.py:817
  339.4 42.0 %collective-permute-start.19 = (bf16[1024,768]{1,0:T(8,128)(2,1)S(1)}, bf16[1024,768]{1,0:T(8,128)(2,1)S(1)}, u32[]{:S(2)}, u32[]{:S(2)}) collective-permute-start(bf16[1024,768]{1,0:T(8,128)(2,1)S(1)} %shard_map.202.near), channel_id=1, source_target_pairs={{0,1},{1,0},{2,3},{3,2},{4,5},{5,4},{6,7},{7,6},{8,9},{9,8},{10,11... | collective-permute-start | bytes 4718600 | tf_op jit(solution)/shard_map/ppermute | solution.py:828
  340.6 39.5 %collective-permute-start.42 = (bf16[768,768]{1,0:T(8,128)(2,1)S(1)}, bf16[768,768]{1,0:T(8,128)(2,1)S(1)}, u32[]{:S(2)}, u32[]{:S(2)}) collective-permute-start(bf16[768,768]{1,0:T(8,128)(2,1)S(1)} %add_convert_fusion), channel_id=1, source_target_pairs={{0,4},{12,8},{1,5},{13,9},{2,6},{14,10},{3,7},{15,11},{16,20},{28,... | collective-permute-start | bytes 3538952 | tf_op jit(solution)/shard_map/ppermute | solution.py:847
  348.1 27.7 %copy-start.48 = (bf16[3,192,1024]{2,1,0:T(8,128)(2,1)S(1)}, bf16[3,192,1024]{2,1,0:T(8,128)(2,1)}, u32[]{:S(2)}) copy-start(bf16[3,192,1024]{2,1,0:T(8,128)(2,1)} %copy-done.47) | copy-start | bytes 3538948
  348.1 27.7 %copy-start.50 = (bf16[3,192,1024]{2,1,0:T(8,128)(2,1)S(1)}, bf16[3,192,1024]{2,1,0:T(8,128)(2,1)}, u32[]{:S(2)}) copy-start(bf16[3,192,1024]{2,1,0:T(8,128)(2,1)} %copy-done.49) | copy-start | bytes 3538948
  349.5 26.4 %copy-start.17 = (bf16[1024,768]{1,0:T(8,128)(2,1)S(1)}, bf16[1024,768]{1,0:T(8,128)(2,1)}, u32[]{:S(2)}) copy-start(bf16[1024,768]{1,0:T(8,128)(2,1)} %copy-done.16) | copy-start | bytes 4718596
  349.5 26.4 %copy-start.24 = (f32[192,1024]{1,0:T(8,128)S(1)}, f32[192,1024]{1,0:T(8,128)}, u32[]{:S(2)}) copy-start(f32[192,1024]{1,0:T(8,128)} %copy-done.22) | copy-start | bytes 2359300
  349.5 26.4 %copy-start.27 = (f32[192,1024]{1,0:T(8,128)S(1)}, f32[192,1024]{1,0:T(8,128)}, u32[]{:S(2)}) copy-start(f32[192,1024]{1,0:T(8,128)} %copy-done.25) | copy-start | bytes 2359300
  349.5 26.4 %copy-start.33 = (bf16[512,768]{1,0:T(8,128)(2,1)S(1)}, bf16[512,768]{1,0:T(8,128)(2,1)}, u32[]{:S(2)}) copy-start(bf16[512,768]{1,0:T(8,128)(2,1)} %copy-done.32) | copy-start | bytes 2359300
  349.5 26.4 %copy-start.35 = (bf16[512,768]{1,0:T(8,128)(2,1)S(1)}, bf16[512,768]{1,0:T(8,128)(2,1)}, u32[]{:S(2)}) copy-start(bf16[512,768]{1,0:T(8,128)(2,1)} %copy-done.34) | copy-start | bytes 2359300
  366.5 31.6 %collective-permute-start.29 = (bf16[4,192,768]{2,1,0:T(8,128)(2,1)}, bf16[4,192,768]{2,1,0:T(8,128)(2,1)}, u32[]{:S(2)}, u32[]{:S(2)}) collective-permute-start(bf16[4,192,768]{2,1,0:T(8,128)(2,1)} %add_convert_fusion.2), channel_id=1, source_target_pairs={{0,4},{12,8},{1,5},{13,9},{2,6},{14,10},{3,7},{15,11},{16,20},{28,... | collective-permute-start | bytes 3538952 | tf_op jit(solution)/shard_map/ppermute | solution.py:847
  374.5 28.1 %collective-permute-start.30 = (bf16[768,768]{1,0:T(8,128)(2,1)}, bf16[768,768]{1,0:T(8,128)(2,1)}, u32[]{:S(2)}, u32[]{:S(2)}) collective-permute-start(bf16[768,768]{1,0:T(8,128)(2,1)} %add.101), channel_id=1, source_target_pairs={{4,0},{8,12},{5,1},{9,13},{6,2},{10,14},{7,3},{11,15},{20,16},{24,... | collective-permute-start | bytes 3538952 | tf_op jit(solution)/shard_map/ppermute | solution.py:865
  378.3 28.8 %collective-permute-start.36 = (bf16[4,192,768]{2,1,0:T(8,128)(2,1)}, bf16[4,192,768]{2,1,0:T(8,128)(2,1)}, u32[]{:S(2)}, u32[]{:S(2)}) collective-permute-start(bf16[4,192,768]{2,1,0:T(8,128)(2,1)} %get-tuple-element.261), channel_id=1, source_target_pairs={{16,18},{17,19},{18,16},{19,17},{20,22},{21,23},{22,20},{23,21},{2... | collective-permute-start | bytes 3538952 | tf_op jit(solution)/shard_map/ppermute | solution.py:822
  380.1 39.4 %collective-permute-start.23 = (bf16[1024,768]{1,0:T(8,128)(2,1)}, bf16[1024,768]{1,0:T(8,128)(2,1)}, u32[]{:S(2)}, u32[]{:S(2)}) collective-permute-start(bf16[1024,768]{1,0:T(8,128)(2,1)} %get-tuple-element.244.near), channel_id=1, source_target_pairs={{0,1},{1,0},{2,3},{3,2},{4,5},{5,4},{6,7},{7,6},{8,9},{9,8},{10,11... | collective-permute-start | bytes 4718600 | tf_op jit(solution)/shard_map/ppermute | solution.py:828
  382.6 31.1 %collective-permute-start.43 = (bf16[768,768]{1,0:T(8,128)(2,1)}, bf16[768,768]{1,0:T(8,128)(2,1)}, u32[]{:S(2)}, u32[]{:S(2)}) collective-permute-start(bf16[768,768]{1,0:T(8,128)(2,1)} %add.111), channel_id=1, source_target_pairs={{4,8},{8,4},{5,9},{9,5},{6,10},{10,6},{7,11},{11,7},{20,24},{24,20... | collective-permute-start | bytes 3538952 | tf_op jit(solution)/shard_map/ppermute | solution.py:853
  405.5 24.7 %collective-permute-start.31 = (bf16[4,192,768]{2,1,0:T(8,128)(2,1)}, bf16[4,192,768]{2,1,0:T(8,128)(2,1)}, u32[]{:S(2)}, u32[]{:S(2)}) collective-permute-start(bf16[4,192,768]{2,1,0:T(8,128)(2,1)} %add.103), channel_id=1, source_target_pairs={{4,8},{8,4},{5,9},{9,5},{6,10},{10,6},{7,11},{11,7},{20,24},{24,20... | collective-permute-start | bytes 3538952 | tf_op jit(solution)/shard_map/ppermute | solution.py:853
  409.8 18.5 %collective-permute-start.37 = (bf16[2,192,768]{2,1,0:T(8,128)(2,1)}, bf16[2,192,768]{2,1,0:T(8,128)(2,1)}, u32[]{:S(2)}, u32[]{:S(2)}) collective-permute-start(bf16[2,192,768]{2,1,0:T(8,128)(2,1)} %slice.105), channel_id=1, source_target_pairs={{16,0},{17,1},{18,2},{19,3},{20,4},{21,5},{22,6},{23,7},{24,8},{25... | collective-permute-start | bytes 1769480 | tf_op jit(solution)/shard_map/ppermute | solution.py:836
  411.9 34.8 %collective-permute-start.20 = (bf16[256,768]{1,0:T(8,128)(2,1)}, bf16[256,768]{1,0:T(8,128)(2,1)}, u32[]{:S(2)}, u32[]{:S(2)}) collective-permute-start(bf16[256,768]{1,0:T(8,128)(2,1)} %get-tuple-element.277), channel_id=1, source_target_pairs={{0,2},{1,3},{2,0},{3,1},{4,6},{5,7},{6,4},{7,5},{8,10},{9,11},{10,... | collective-permute-start | bytes 1179656 | tf_op jit(solution)/shard_map/ppermute | solution.py:817
  415.7 52.8 %collective-permute-start.44 = (bf16[768,768]{1,0:T(8,128)(2,1)S(1)}, bf16[768,768]{1,0:T(8,128)(2,1)}, u32[]{:S(2)}, u32[]{:S(2)}) collective-permute-start(bf16[768,768]{1,0:T(8,128)(2,1)S(1)} %add.112), channel_id=1, source_target_pairs={{4,0},{8,12},{5,1},{9,13},{6,2},{10,14},{7,3},{11,15},{20,16},{24,... | collective-permute-start | bytes 3538952 | tf_op jit(solution)/shard_map/ppermute | solution.py:865
  426.7 33.9 %collective-permute-start.24 = (bf16[256,768]{1,0:T(8,128)(2,1)S(1)}, bf16[256,768]{1,0:T(8,128)(2,1)S(1)}, u32[]{:S(2)}, u32[]{:S(2)}) collective-permute-start(bf16[256,768]{1,0:T(8,128)(2,1)S(1)} %dynamic-slice_convert_fusion), channel_id=1, source_target_pairs={{0,2},{1,3},{2,0},{3,1},{4,6},{5,7},{6,4},{7,5},{8,10},{9,11},{10,... | collective-permute-start | bytes 1179656 | tf_op jit(solution)/shard_map/ppermute | solution.py:817
  432.1 33.6 %collective-permute-start.38 = (bf16[2,192,768]{2,1,0:T(8,128)(2,1)}, bf16[2,192,768]{2,1,0:T(8,128)(2,1)}, u32[]{:S(2)}, u32[]{:S(2)}) collective-permute-start(bf16[2,192,768]{2,1,0:T(8,128)(2,1)} %slice_select_fusion), channel_id=1, source_target_pairs={{0,4},{12,8},{1,5},{13,9},{2,6},{14,10},{3,7},{15,11},{16,20},{28,... | collective-permute-start | bytes 1769480 | tf_op jit(solution)/shard_map/ppermute | solution.py:847
  451.0 4.1 collective-permute-start.25
  451.5 35.9 %collective-permute-start.35 = (bf16[4,192,768]{2,1,0:T(8,128)(2,1)S(1)}, bf16[4,192,768]{2,1,0:T(8,128)(2,1)}, u32[]{:S(2)}, u32[]{:S(2)}) collective-permute-start(bf16[4,192,768]{2,1,0:T(8,128)(2,1)S(1)} %add.104), channel_id=1, source_target_pairs={{4,0},{8,12},{5,1},{9,13},{6,2},{10,14},{7,3},{11,15},{20,16},{24,... | collective-permute-start | bytes 3538952 | tf_op jit(solution)/shard_map/ppermute | solution.py:865
  455.1 7.3 %collective-permute-start.32 = (f32[10,768]{1,0:T(8,128)S(1)}, f32[10,768]{1,0:T(8,128)S(1)}, u32[]{:S(2)}, u32[]{:S(2)}) collective-permute-start(f32[10,768]{1,0:T(8,128)S(1)} %add.99), channel_id=1, source_target_pairs={{0,4},{12,8},{1,5},{13,9},{2,6},{14,10},{3,7},{15,11},{16,20},{28,... | collective-permute-start | bytes 92168 | tf_op jit(solution)/shard_map/ppermute | solution.py:847
  462.4 1.9 collective-permute-start.33
  464.4 17.1 %collective-permute-start.34 = (f32[10,768]{1,0:T(8,128)S(1)}, f32[10,768]{1,0:T(8,128)S(1)}, u32[]{:S(2)}, u32[]{:S(2)}) collective-permute-start(f32[10,768]{1,0:T(8,128)S(1)} %add.106), channel_id=1, source_target_pairs={{4,0},{8,12},{5,1},{9,13},{6,2},{10,14},{7,3},{11,15},{20,16},{24,... | collective-permute-start | bytes 92168 | tf_op jit(solution)/shard_map/ppermute | solution.py:865
  467.1 17.9 %collective-permute-start.39 = (bf16[2,192,768]{2,1,0:T(8,128)(2,1)S(1)}, bf16[2,192,768]{2,1,0:T(8,128)(2,1)}, u32[]{:S(2)}, u32[]{:S(2)}) collective-permute-start(bf16[2,192,768]{2,1,0:T(8,128)(2,1)S(1)} %add.108), channel_id=1, source_target_pairs={{4,8},{8,4},{5,9},{9,5},{6,10},{10,6},{7,11},{11,7},{20,24},{24,20... | collective-permute-start | bytes 1769480 | tf_op jit(solution)/shard_map/ppermute | solution.py:853
  486.1 15.5 %collective-permute-start.40 = (bf16[2,192,768]{2,1,0:T(8,128)(2,1)S(1)}, bf16[2,192,768]{2,1,0:T(8,128)(2,1)S(1)}, u32[]{:S(2)}, u32[]{:S(2)}) collective-permute-start(bf16[2,192,768]{2,1,0:T(8,128)(2,1)S(1)} %add.109), channel_id=1, source_target_pairs={{4,0},{8,12},{5,1},{9,13},{6,2},{10,14},{7,3},{11,15},{20,16},{24,... | collective-permute-start | bytes 1769480 | tf_op jit(solution)/shard_map/ppermute | solution.py:865
  (86 other events, 355.1 us)
